TPU v7x, 128 devices: a whole 4x4x4 slice. The times are simulated.
128 devices in a mesh: req: 64 (over y, z, x_hi, core), tp: 2 (over x_lo).
Axes of the slice: x: 4 (x_hi: 2, x_lo: 2; x = x_hi * 2 + x_lo), y: 4, z: 4, core: 2. Of those that a mesh axis runs over, the one named last changes fastest.
Arguments:
- residual: bfloat16 [8192, 2048], P('req'), may hold values from -6 to 6
- queries: bfloat16 [8192, 1024], P('req', 'tp'), may hold values from -6 to 6
- new_keys: bfloat16 [8192, 1024], P('req', 'tp'), may hold values from -6 to 6
- new_values: bfloat16 [8192, 1024], P('req', 'tp'), may hold values from -6 to 6
- request_ids: int32 [8192], P('req'), may hold values from 0 to 3, as said below
- page_store: bfloat16 [512, 2, 128, 1024], P('req', None, None, 'tp'), may hold values from -6 to 6
- page_sends: int32 [64, 64], P('req'), may hold values from 0 to 7
- page_users: int32 [64, 64], P('req'), may hold values from -1 to 3
- expert_ids: int32 [8192, 4], P('req'), may hold values from 0 to 63, all different within a row; in each aligned block of 128 rows (0 to 127, 128 to 255, ...) at most 12 rows name the same one
- expert_weights: float32 [8192, 4], P('req'), may hold values from 0.1 to 1
- output_weight: bfloat16 [1024, 2048], P('tp'), may hold values from -0.1875 to 0.1875
- norm_gain: float32 [2048], replicated, may hold values from 0.1 to 1.9
- gate_weight: bfloat16 [64, 2048, 1408], P('req', None, 'tp'), may hold values from -0.125 to 0.125
- up_weight: bfloat16 [64, 2048, 1408], P('req', None, 'tp'), may hold values from -0.125 to 0.125
- down_weight: bfloat16 [64, 1408, 2048], P('req', 'tp'), may hold values from -0.15625 to 0.15625
Outputs:
- layer_out: bfloat16 [8192, 2048], P('req', 'tp')
Inputs may be any that keep to these rules, and one draw needn't show every extreme that they name: `request_ids`: within each device's 128 tokens the local requests 0 to 3 each appear, in order, in whole runs of 16 tokens that start at multiples of 16. `page_users`: -1 marks a fetched page that no local request uses. `expert_ids`: the 4 experts of a token differ; within the 128 rows of one device no expert is named more than 12 times.
All inputs are finite; a program needn't handle non-finite values.
Results may differ from a plain program's by a relative error of at most 0.0054.
Values may be sent and summed in bfloat16 or wider, within the bound.
No kernel may reach another device: no remote copies, remote signals or barrier semaphores. Data moves between devices by JAX's collectives and lax.ppermute only.
A program may use at most 192 MiB of HBM per device.

v0:
```python
import math

import jax
import jax.numpy as jnp
from jax import lax
from jax.sharding import PartitionSpec as P

HD = 128
TOP = 4


norm_eps = 1e-06


def shards(
    residual,
    queries,
    new_keys,
    new_values,
    request_ids,
    page_store,
    page_sends,
    page_users,
    expert_ids,
    expert_weights,
    output_weight,
    norm_gain,
    gate_weight,
    up_weight,
    down_weight,
):
    peer_count = lax.axis_size("req")
    tok_rows = residual.shape[0]
    model_width = residual.shape[1]
    half_width = model_width // lax.axis_size("tp")
    tp_index = lax.axis_index("tp")
    local_heads = queries.shape[1] // HD
    page_rows = page_store.shape[2]
    inv_scale = 1.0 / math.sqrt(HD)
    query_heads = queries.reshape(tok_rows, local_heads, HD)
    own_keys = new_keys.reshape(tok_rows, local_heads, HD)
    own_values = new_values.reshape(tok_rows, local_heads, HD)
    held_pages = jnp.take(page_store, page_sends[0], axis=0)
    arrived = lax.all_to_all(held_pages, "req", split_axis=0, concat_axis=0, tiled=True)
    prefix_keys = arrived[:, 0].reshape(peer_count * page_rows, local_heads, HD)
    prefix_values = arrived[:, 1].reshape(peer_count * page_rows, local_heads, HD)
    all_keys = jnp.concatenate([prefix_keys, own_keys], 0)
    all_values = jnp.concatenate([prefix_values, own_values], 0)
    key_request = jnp.concatenate([jnp.repeat(page_users[0], page_rows), request_ids])
    key_place = jnp.concatenate(
        [jnp.full((peer_count * page_rows,), -1, jnp.int32), jnp.arange(tok_rows, dtype=jnp.int32)]
    )
    query_place = jnp.arange(tok_rows, dtype=jnp.int32)
    allowed = (key_request[None, :] == request_ids[:, None]) & (
        key_place[None, :] <= query_place[:, None]
    )
    scores = (
        jnp.einsum("qhd,khd->hqk", query_heads, all_keys, preferred_element_type=jnp.float32)
        * inv_scale
    )
    masked = jnp.where(allowed[None], scores, -1e30)
    top_score = jnp.max(masked, axis=2, keepdims=True)
    shifted = jnp.where(allowed[None], jnp.exp(masked - top_score), 0.0)
    totals = jnp.sum(shifted, axis=2, keepdims=True)
    attn_probs = (shifted / totals).astype(jnp.bfloat16)
    attended = jnp.einsum(
        "hqk,khd->qhd", attn_probs, all_values, preferred_element_type=jnp.float32
    )
    attended = attended.astype(jnp.bfloat16).reshape(tok_rows, local_heads * HD)
    partial_value = jnp.dot(attended, output_weight, preferred_element_type=jnp.float32)
    attn_full = lax.psum(partial_value, "tp")
    mixed_rows = residual.astype(jnp.float32) + attn_full
    scale_row = lax.rsqrt(jnp.mean(mixed_rows * mixed_rows, axis=1, keepdims=True) + norm_eps)
    normed = (mixed_rows * scale_row * norm_gain).astype(jnp.bfloat16)
    residual_half = lax.dynamic_slice_in_dim(mixed_rows, tp_index * half_width, half_width, 1)
    capacity = max(2, tok_rows * TOP * 3 // (2 * peer_count))
    flat_ids = expert_ids.reshape(-1)
    onehot = (flat_ids[:, None] == jnp.arange(peer_count, dtype=jnp.int32)[None, :]).astype(
        jnp.int32
    )
    before = jnp.cumsum(onehot, axis=0) - onehot
    slot_index = jnp.sum(before * onehot, axis=1)
    token_of = jnp.arange(tok_rows * TOP, dtype=jnp.int32) // TOP
    outgoing_rows = (
        jnp.zeros((peer_count, capacity, normed.shape[1]), jnp.bfloat16)
        .at[flat_ids, slot_index]
        .set(normed[token_of])
    )
    arrived_rows = lax.all_to_all(outgoing_rows, "req", split_axis=0, concat_axis=0, tiled=True)
    item_count = arrived_rows.shape[1]
    flat_rows = arrived_rows.reshape(peer_count * item_count, model_width)
    gate_act = jnp.dot(flat_rows, gate_weight[0], preferred_element_type=jnp.float32)
    up_act = jnp.dot(flat_rows, up_weight[0], preferred_element_type=jnp.float32)
    hidden = (jax.nn.silu(gate_act) * up_act).astype(jnp.bfloat16)
    result = jnp.dot(hidden, down_weight[0], preferred_element_type=jnp.float32).reshape(
        peer_count, item_count, model_width
    )
    returned = lax.all_to_all(result, "req", split_axis=0, concat_axis=0, tiled=True)
    picked = returned[flat_ids, slot_index]
    weighted = picked * expert_weights.reshape(-1)[:, None]
    combined = jnp.sum(weighted.reshape(tok_rows, TOP, picked.shape[1]), axis=1)
    moe_half = lax.psum_scatter(combined, "tp", scatter_dimension=1, tiled=True)
    return (residual_half + moe_half).astype(jnp.bfloat16)


def solution(mesh):
    placed = (
        P("req", None),
        P("req", "tp"),
        P("req", "tp"),
        P("req", "tp"),
        P("req"),
        P("req", None, None, "tp"),
        P("req", None),
        P("req", None),
        P("req", None),
        P("req", None),
        P("tp", None),
        P(),
        P("req", None, "tp"),
        P("req", None, "tp"),
        P("req", "tp", None),
    )
    return jax.shard_map(
        shards, mesh=mesh, in_specs=placed, out_specs=P("req", "tp"), check_vma=False
    )
```

profile of v0, /device:TPU:1, one launch (start us, length us, event | category | flops | bytes accessed | tf_op | source)
XLA Modules:
  0.0 823.1 jit_solution(14570764709166166487)
XLA Ops:
  8.1 9.1 %gather_fusion = bf16[64,2,128,512]{3,2,1,0:T(8,128)(2,1)} fusion(bf16[8,2,128,512]{3,2,1,0:T(8,128)(2,1)} %param.20, s32[1024]{0:T(1024)S(1)} %pad_clamp_fusion.1), kind=kCustom, calls=%fused_computation | custom fusion | bytes 33554688 | tf_op jit(solution)/shard_map/jit(_take)/gather | solution.py:43
  17.2 14.2 %broadcast_select_fusion = bf16[64,2,128,512]{3,2,1,0:T(8,128)(2,1)} fusion(bf16[64,2,128,512]{3,2,1,0:T(8,128)(2,1)} %gather_fusion, pred[64]{0:T(512)(128)(4,1)S(1)} %compare_and_fusion), kind=kLoop, calls=%fused_computation.7 | loop fusion | flops 8388608 | bytes 33554496 | tf_op jit(solution)/shard_map/jit(_take)/select_n | solution.py:43
  31.4 12.8 %all-to-all-start = ((bf16[64,2,128,512]{3,2,1,0:T(8,128)(2,1)}), bf16[64,2,128,512]{3,2,1,0:T(8,128)(2,1)}, u32[]{:S(2)}, u32[]{:S(2)}) async-start(bf16[64,2,128,512]{3,2,1,0:T(8,128)(2,1)} %broadcast_select_fusion), calls=%async_computation | async-start | bytes 33554432 | tf_op jit(solution)/shard_map/all_to_all | solution.py:44
  44.9 6.2 fusion.11
  51.1 203.0 %all-to-all-done = bf16[64,2,128,512]{3,2,1,0:T(8,128)(2,1)} async-done(((bf16[64,2,128,512]{3,2,1,0:T(8,128)(2,1)}), bf16[64,2,128,512]{3,2,1,0:T(8,128)(2,1)}, u32[]{:S(2)}, u32[]{:S(2)}) %all-to-all-start) | async-done | bytes 16777248 | tf_op jit(solution)/shard_map/all_to_all | solution.py:44
  254.1 11.6 %fusion.38 = (bf16[64,1,128,512]{3,2,1,0:T(8,128)(2,1)}, bf16[64,1,128,512]{3,2,1,0:T(8,128)(2,1)}) fusion(bf16[64,2,128,512]{3,2,1,0:T(8,128)(2,1)} %all-to-all-done), kind=kLoop, calls=%fused_computation.71 | loop fusion | bytes 33554432 | tf_op jit(solution)/shard_map/slice | solution.py:46
  265.7 12.5 %reshape.264 = bf16[8192,4,128]{2,1,0:T(4,128)(2,1)} reshape(bf16[64,1,128,512]{3,2,1,0:T(8,128)(2,1)} %get-tuple-element.10) | data formatting | bytes 16777216 | tf_op jit(solution)/shard_map/reshape;squeeze | solution.py:45
  278.3 7.7 copy.42
  285.9 12.5 %reshape.263 = bf16[8192,4,128]{2,1,0:T(4,128)(2,1)} reshape(bf16[64,1,128,512]{3,2,1,0:T(8,128)(2,1)} %get-tuple-element.9) | data formatting | bytes 16777216 | tf_op jit(solution)/shard_map/reshape;squeeze | solution.py:46
  298.5 13.9 %copy.57 = bf16[8192,4,128]{0,2,1:T(8,128)(2,1)} copy(bf16[8192,4,128]{2,1,0:T(4,128)(2,1)} %reshape.263) | data formatting | bytes 16777216 | tf_op jit(solution)/shard_map/reshape;squeeze | solution.py:46
  312.3 13.2 %fusion = (f32[4,128]{1,0:T(4,128)S(1)}, f32[4,8320,128]{2,1,0:T(8,128)}) fusion(pred[128,8320]{0,1:T(8,128)(4,1)} %fusion.11, bf16[128,4,128]{2,0,1:T(8,128)(2,1)S(1)} %copy.43, bf16[8192,4,128]{2,0,1:T(8,128)(2,1)} %copy.42, bf16[128,512]{1,0:T(8,128)(2,1)S(1)} %copy-done.15), kind=kOutput, calls=%fused_computation.8 | convolution fusion | flops 1120337408 | bytes 26757120 | tf_op jit(solution)/shard_map/qhd,khd->hqk/dot_general | solution.py:58
  325.6 8.3 %fusion.1 = f32[4,128]{1,0:T(4,128)S(1)} fusion(f32[4,8320,128]{2,1,0:T(8,128)} %get-tuple-element.12, f32[4,128]{1,0:T(4,128)S(1)} %get-tuple-element.11, pred[128,8320]{0,1:T(8,128)(4,1)S(1)} %copy-done.3), kind=kLoop, calls=%fused_computation.9 | loop fusion | flops 21298688 | bytes 18108416 | tf_op jit(solution)/shard_map/reduce_sum | solution.py:64
  333.9 11.3 %fusion.21 = bf16[4,128,128]{2,1,0:T(8,128)(2,1)S(1)} fusion(f32[4,8320,128]{2,1,0:T(8,128)} %get-tuple-element.12, f32[4,128]{1,0:T(4,128)S(1)} %fusion.1, f32[4,128]{1,0:T(4,128)S(1)} %get-tuple-element.11, pred[128,8320]{0,1:T(8,128)(4,1)S(1)} %copy-done.3, bf16[128,4,128]{0,2,1:T(8,128)(2,1)S(1)} %bitcast.83, bf16[8192,4,128]{0,2,1:T(8,128)(2,1)S(1)} %copy-done.1), kind=kOutput, calls=%fused_computation.30 | convolution fusion | flops 1133182976 | bytes 26759168 | tf_op jit(solution)/shard_map/hqk,khd->qhd/dot_general | solution.py:66
  348.9 84.0 %all-reduce.2.cloned.1.call-done = f32[128,2048]{1,0:T(8,128)} async-done(((f32[128,2048]{1,0:T(8,128)}), f32[128,2048]{1,0:T(8,128)}) %all-reduce.2.cloned.1.call-update) | async-done | bytes 1048592 | tf_op jit(solution)/shard_map/psum | solution.py:71
  441.0 93.2 %scatter_fusion = bf16[64,12,2048]{2,0,1:T(8,128)(2,1)} fusion(bf16[64,12,2048]{2,0,1:T(8,128)(2,1)} %broadcast_in_dim.57, s32[512]{0:T(512)S(1)} %bitcast.80, bf16[512,2048]{1,0:T(8,128)(2,1)} %gather_fusion.1), kind=kCustom, calls=%fused_computation.3 | custom fusion | bytes 6295552 | tf_op jit(solution)/shard_map/scatter | solution.py:87
  537.8 63.4 %all_to_all.15 = bf16[64,12,2048]{2,1,0:T(8,128)(2,1)} all-to-all(bf16[64,12,2048]{2,1,0:T(8,128)(2,1)S(1)} %copy.50), channel_id=1, replica_groups=mesh['req'=64,'tp'=2] {'req'}, dimensions={0} | all-to-all | bytes 6291456 | tf_op jit(solution)/shard_map/all_to_all | solution.py:89
  601.3 6.2 reshape.233
  626.1 6.9 copy.53
  633.1 6.6 all-to-all-start.2
  640.0 102.7 %all-to-all-done.2 = f32[64,12,2048]{2,1,0:T(8,128)} async-done(((f32[64,12,2048]{2,1,0:T(8,128)}), f32[64,12,2048]{2,1,0:T(8,128)}, u32[]{:S(2)}, u32[]{:S(2)}) %all-to-all-start.2) | async-done | bytes 6291488 | tf_op jit(solution)/shard_map/all_to_all | solution.py:98
  742.7 9.7 %copy.54 = f32[64,12,2048]{2,0,1:T(8,128)} copy(f32[64,12,2048]{2,1,0:T(8,128)} %all-to-all-done.2) | data formatting | bytes 12582912 | tf_op jit(solution)/shard_map/all_to_all | solution.py:98
  752.4 13.0 %gather_fusion.2 = f32[512,2048]{1,0:T(8,128)} fusion(f32[64,12,2048]{2,0,1:T(8,128)} %copy.54, s32[512]{0:T(512)S(1)} %bitcast.79), kind=kCustom, calls=%fused_computation.2 | custom fusion | bytes 8392704 | tf_op jit(solution)/shard_map/gather | solution.py:99
  770.6 6.3 multiply_reduce_fusion
  776.9 37.2 %reduce-scatter.2.cloned.1.call-done = f32[128,1024]{1,0:T(8,128)} async-done(((f32[128,2048]{1,0:T(8,128)}), f32[128,1024]{1,0:T(8,128)}) %reduce-scatter.2.cloned.1.call-update) | async-done | bytes 524304 | tf_op jit(solution)/shard_map/reduce_scatter | solution.py:102
  (72 shorter events, 43.7 us)
Async XLA Ops:
  6.5 615.6 %copy-start = (bf16[1,704,2048]{2,1,0:T(8,128)(2,1)S(1)}, bf16[1,704,2048]{2,1,0:T(8,128)(2,1)}, u32[]{:S(2)}) copy-start(bf16[1,704,2048]{2,1,0:T(8,128)(2,1)} %param.29) | copy-start | bytes 8650756
  31.4 13.0 %copy-start.6 = (bf16[128,512]{1,0:T(8,128)(2,1)S(1)}, bf16[128,512]{1,0:T(8,128)(2,1)}, u32[]{:S(2)}) copy-start(bf16[128,512]{1,0:T(8,128)(2,1)} %param.17) | copy-start | bytes 393220
  31.4 13.3 %copy-start.7 = (bf16[128,512]{1,0:T(8,128)(2,1)S(1)}, bf16[128,512]{1,0:T(8,128)(2,1)}, u32[]{:S(2)}) copy-start(bf16[128,512]{1,0:T(8,128)(2,1)} %param.18) | copy-start | bytes 393220
  31.4 13.4 %copy-start.13 = (s32[1,64]{1,0:T(1,128)S(1)}, s32[1,64]{1,0:T(1,128)}, u32[]{:S(2)}) copy-start(s32[1,64]{1,0:T(1,128)} %param.22) | copy-start | bytes 772
  31.4 13.5 %copy-start.10 = (s32[128]{0:T(128)S(1)}, s32[128]{0:T(128)}, u32[]{:S(2)}) copy-start(s32[128]{0:T(128)} %param.19) | copy-start | bytes 1540
  31.4 13.5 %copy-start.8 = (s32[8320]{0:T(1024)S(1)}, s32[8320]{0:T(1024)}, u32[]{:S(2)}) copy-start(s32[8320]{0:T(1024)} %constant.36.clone.1) | copy-start | bytes 99844
  31.4 222.7 %all-to-all-start = ((bf16[64,2,128,512]{3,2,1,0:T(8,128)(2,1)}), bf16[64,2,128,512]{3,2,1,0:T(8,128)(2,1)}, u32[]{:S(2)}, u32[]{:S(2)}) async-start(bf16[64,2,128,512]{3,2,1,0:T(8,128)(2,1)} %broadcast_select_fusion), calls=%async_computation | async-start | bytes 33554432 | tf_op jit(solution)/shard_map/all_to_all | solution.py:44
  44.2 388.7 %all-reduce.2.cloned.1.call-start = ((), (), s32[]{:S(2)}) async-start(), calls=%async_computation.4 | async-start | bytes 2097152 | tf_op jit(solution)/shard_map/psum | solution.py:71
  298.5 13.9 %copy-start.15 = (bf16[128,512]{1,0:T(8,128)(2,1)S(1)}, bf16[128,512]{1,0:T(8,128)(2,1)}, u32[]{:S(2)}) copy-start(bf16[128,512]{1,0:T(8,128)(2,1)} %param.16) | copy-start | bytes 393220
  312.3 13.2 %copy-start.3 = (pred[128,8320]{0,1:T(8,128)(4,1)S(1)}, pred[128,8320]{0,1:T(8,128)(4,1)}, u32[]{:S(2)}) copy-start(pred[128,8320]{0,1:T(8,128)(4,1)} %fusion.11) | copy-start | bytes 3194884
  325.6 8.3 %copy-start.1 = (bf16[8192,4,128]{0,2,1:T(8,128)(2,1)S(1)}, bf16[8192,4,128]{0,2,1:T(8,128)(2,1)}, u32[]{:S(2)}) copy-start(bf16[8192,4,128]{0,2,1:T(8,128)(2,1)} %copy.57) | copy-start | bytes 25165828
  333.9 11.3 %copy-start.5 = (bf16[512,2048]{1,0:T(8,128)(2,1)S(1)}, bf16[512,2048]{1,0:T(8,128)(2,1)}, u32[]{:S(2)}) copy-start(bf16[512,2048]{1,0:T(8,128)(2,1)} %param.25) | copy-start | bytes 6291460
  345.2 1.6 copy-start.11
  345.2 90.3 %copy-start.9 = (f32[2048]{0:T(1024)S(1)}, f32[2048]{0:T(1024)}, u32[]{:S(2)}) copy-start(f32[2048]{0:T(1024)} %param.26) | copy-start | bytes 24580
  434.5 1.0 copy-start.2
  607.4 5.4 copy-start.4
  607.4 5.4 copy-start.14
  633.1 6.9 copy-start.12
  633.1 109.6 %all-to-all-start.2 = ((f32[64,12,2048]{2,1,0:T(8,128)}), f32[64,12,2048]{2,1,0:T(8,128)}, u32[]{:S(2)}, u32[]{:S(2)}) async-start(f32[64,12,2048]{2,1,0:T(8,128)} %copy.53), calls=%async_computation.2 | async-start | bytes 16777216 | tf_op jit(solution)/shard_map/all_to_all | solution.py:98
  639.7 174.4 %reduce-scatter.2.cloned.1.call-start = ((), (), s32[]{:S(2)}) async-start(), calls=%async_computation.5 | async-start | bytes 1572864 | tf_op jit(solution)/shard_map/reduce_scatter | solution.py:102
Sparse Core Ops, SparseCore 0:
  346.9 85.9 all-reduce.1
  777.0 37.0 reduce-scatter.1
where the time goes:
time: 835 us; the launch traced here: 823 us
  waiting for transfers between devices  427 us (51%)
  local copies, waits for them, and re-layouts  218 us (26%)
  blocking collectives  63.4 us (8%)
  other arithmetic  41.6 us (5%)
  matrix products  38.9 us (5%)
  starting transfers between devices  19.8 us (2%)
  between operations  13.9 us (2%)
    all_to_all x1, waiting for transfers between devices, shards(): lax.all_to_all(held_pages, 'req', split_axis=0, concat_axis=0, tiled=True)  203 us
    all_to_all x1, waiting for transfers between devices, shards(): lax.all_to_all(result, 'req', split_axis=0, concat_axis=0, tiled=True)  103 us
    scatter x2, local copies, waits for them, and re-layouts, shards(): outgoing_rows = jnp.zeros((peer_count, capacity, normed.shape[1]), jnp.bf...  96.8 us
    psum x1, waiting for transfers between devices, shards(): attn_full = lax.psum(partial_value, 'tp')  84 us
    all_to_all x1, blocking collectives, shards(): lax.all_to_all(outgoing_rows, 'req', split_axis=0, concat_axis=0, tiled=T...  63.4 us
    reduce_scatter x1, waiting for transfers between devices, shards(): moe_half = lax.psum_scatter(combined, 'tp', scatter_dimension=1, tiled=True)  37.2 us
    another operation x2, local copies, waits for them, and re-layouts, shards(): arrived[:, 1].reshape(peer_count * page_rows, local_heads, HD)  26.4 us
    another operation x2, local copies, waits for them, and re-layouts, shards(): prefix_keys = arrived[:, 0].reshape(peer_count * page_rows, local_heads, HD)  20.2 us
  transfers between devices with their start and end apart: 4, of which 4 were waited for; matrix products, arithmetic and copies ran while one was open for 1% of the time, Pallas kernels for 0%

commit v1 on v0

v1 whole, which is shorter than its diff:
```python
import math

import jax
import jax.numpy as jnp
import numpy as np
from jax import lax
from jax.experimental import pallas as pl
from jax.experimental.pallas import tpu as pltpu
from jax.sharding import PartitionSpec as P

HD = 128
TOP = 4
HEADS = 4
PAGE = 128
TOK = 128
REQS = 4
WIN = 80
CAP = 12
STAT = HEADS * WIN
BLOCK = STAT + 8
GROUPS = WIN // 8
QROWS = TOK + 8
NORM_EPS = 1e-06
SCALE = 1.0 / math.sqrt(HD)
NEG = -1e30
F32 = jnp.float32
BF16 = jnp.bfloat16

NY, NZ, NX, NC = 4, 4, 2, 2
NREQ = NY * NZ * NX * NC


def req_index(y, z, x, c):
    return ((y * NZ + z) * NX + x) * NC + c


def all_coords():
    return [
        (y, z, x, c) for y in range(NY) for z in range(NZ) for x in range(NX) for c in range(NC)
    ]


def perm_x():
    return [(req_index(y, z, x, c), req_index(y, z, 1 - x, c)) for y, z, x, c in all_coords()]


def perm_core():
    return [(req_index(y, z, x, c), req_index(y, z, x, 1 - c)) for y, z, x, c in all_coords()]


def perm_ring(stage, step):
    pairs = []
    for y, z, x, c in all_coords():
        if (c + stage) % 2 == 0:
            to = req_index((y + step) % NY, z, x, c)
        else:
            to = req_index(y, (z + step) % NZ, x, c)
        pairs.append((req_index(y, z, x, c), to))
    return pairs


def source_table():
    table = np.zeros((NREQ, NREQ), np.int32)
    for y, z, x, c in all_coords():
        row = []
        for swap in range(2):
            core = c ^ swap
            for d1 in range(4):
                for d0 in range(4):
                    for dx in range(2):
                        dy, dz = (d0, d1) if core == 0 else (d1, d0)
                        row.append(req_index((y - dy) % NY, (z - dz) % NZ, x ^ dx, core))
        table[req_index(y, z, x, c)] = row
    return table


def gather_blocks(block):
    pair = jnp.stack([block, lax.ppermute(block, "req", perm_x())])
    line = jnp.stack(
        [pair] + [lax.ppermute(pair, "req", perm_ring(0, step)) for step in (1, 2, 3)]
    ).reshape(8, *block.shape)
    own = [line] + [lax.ppermute(line, "req", perm_ring(1, step)) for step in (1, 2, 3)]
    other = [lax.ppermute(piece, "req", perm_core()) for piece in own]
    return own + other


def attend(query_of, key_of, value_of, mask=None):
    outs, sums = [], []
    for head in range(HEADS):
        scores = lax.dot_general(
            query_of(head), key_of(head), (((1,), (0,)), ((), ())), preferred_element_type=F32
        )
        if mask is not None:
            scores = jnp.where(mask, scores, NEG)
        top = jnp.max(scores, axis=1, keepdims=True)
        probs = jnp.exp((scores - top) * SCALE).astype(BF16)
        both = jnp.dot(probs, value_of(head), preferred_element_type=F32)
        total = both[:, HD:]
        outs.append(both[:, :HD] / total)
        sums.append(top * SCALE + jnp.log(total))
    return outs, sums


def pack_sums(sums):
    lane = lax.broadcasted_iota(jnp.int32, (WIN, 128), 1)
    head = lane % 4
    mixed = jnp.where(head == 0, sums[0], sums[1])
    mixed = jnp.where(head == 2, sums[2], mixed)
    mixed = jnp.where(head == 3, sums[3], mixed)
    group = (lax.broadcasted_iota(jnp.int32, (8, 128), 1) % 40) // 4
    tile = mixed[0:8]
    for g in range(1, GROUPS):
        tile = jnp.where(group == g, mixed[8 * g : 8 * g + 8], tile)
    return tile


def split_sums(tile):
    lane = lax.broadcasted_iota(jnp.int32, (8, 128), 1)
    first = tile.astype(BF16).astype(F32)
    rest = tile - first
    second = rest.astype(BF16).astype(F32)
    third = rest - second
    return jnp.where(lane < 40, first, jnp.where(lane < 80, second, third)).astype(BF16)


def page_kernel(src, page_of, win_of, *refs):
    pieces, (pages, out, keys_t, values_1) = refs[:8], refs[8:]
    ones = jnp.ones((PAGE, HD), BF16)
    for page in range(8):
        for head in range(HEADS):
            cols = slice(head * HD, (head + 1) * HD)
            keys_t[page, head] = pages[page, 0, :, cols].T
            values_1[page, head, :, :HD] = pages[page, 1, :, cols]
            values_1[page, head, :, HD:] = ones
    for index, piece in enumerate(pieces):

        def step(i, carry, index=index, piece=piece):
            b = index * 8 + i
            page = page_of[b]
            first = pl.multiple_of(win_of[b] * 16, 16)
            to = src[b]
            outs, sums = attend(
                lambda h: piece[i, pl.ds(first, WIN), h * HD : (h + 1) * HD],
                lambda h: keys_t[page, h],
                lambda h: values_1[page, h],
            )
            for head in range(HEADS):
                out[to, head * WIN : (head + 1) * WIN, :] = outs[head].astype(BF16)
            out[to, STAT:BLOCK, :] = split_sums(pack_sums(sums))
            return carry

        lax.fori_loop(0, 8, step, 0)


def smem():
    return pl.BlockSpec(memory_space=pltpu.SMEM)


def vmem():
    return pl.BlockSpec(memory_space=pltpu.VMEM)


def partial_attention(src, page_of, win_of, pieces, pages):
    return pl.pallas_call(
        page_kernel,
        out_shape=jax.ShapeDtypeStruct((NREQ, BLOCK, HD), BF16),
        in_specs=[smem()] * 3 + [vmem()] * 9,
        out_specs=vmem(),
        scratch_shapes=[
            pltpu.VMEM((8, HEADS, HD, PAGE), BF16),
            pltpu.VMEM((8, HEADS, PAGE, 2 * HD), BF16),
        ],
        compiler_params=pltpu.CompilerParams(vmem_limit_bytes=48 << 20),
        cost_estimate=pl.CostEstimate(
            flops=NREQ * HEADS * 6 * WIN * HD * HD, bytes_accessed=18 << 20, transcendentals=3 << 20
        ),
        name="page_attention",
    )(src, page_of, win_of, *pieces, pages)


def spread(tile, head, k):
    halves = []
    for g in (2 * k, 2 * k + 1):
        lane = g * 4 + head
        halves.append(jnp.broadcast_to(tile[:, lane : lane + 1], (8, 128)))
    return jnp.concatenate(halves, axis=0)


def merge_kernel(
    users, win_of, first_of, end_of, arrived, queries, keys, values, out, acc, tiles, top, low, rows
):
    lane = lax.broadcasted_iota(jnp.int32, (8, 128), 1)
    row_of = ((lane % 40) // 4) * 8 + lax.broadcasted_iota(jnp.int32, (8, 128), 0)

    def window(user):
        return jnp.minimum(first_of[user], TOK - WIN)

    def held(user):
        token = row_of + window(user)
        return (token >= first_of[user]) & (token < end_of[user])

    def rows_of(head, k):
        return slice(head * WIN + 16 * k, head * WIN + 16 * k + 16)

    ones = jnp.ones((TOK, HD), BF16)
    keys_t = [keys[:, h * HD : (h + 1) * HD].T for h in range(HEADS)]
    values_1 = [
        jnp.concatenate([values[:, h * HD : (h + 1) * HD], ones], axis=1) for h in range(HEADS)
    ]
    own = []
    for user in range(REQS):
        first = pl.multiple_of(window(user), 16)
        token = lax.broadcasted_iota(jnp.int32, (WIN, TOK), 0) + first
        key = lax.broadcasted_iota(jnp.int32, (WIN, TOK), 1)
        outs, sums = attend(
            lambda h: queries[pl.ds(first, WIN), h * HD : (h + 1) * HD],
            lambda h: keys_t[h],
            lambda h: values_1[h],
            (key <= token) & (key >= first_of[user]),
        )
        for head in range(HEADS):
            acc[user, head * WIN : (head + 1) * WIN, :] = outs[head]
        tile = pack_sums(sums)
        own.append(tile)
        top[user] = tile

    def collect(p, carry):
        user = users[p]

        @pl.when(user >= 0)
        def _():
            tile = arrived[p, STAT:BLOCK, :].astype(F32)
            tile = (tile + pltpu.roll(tile, 88, 1)) + pltpu.roll(tile, 48, 1)
            tiles[p] = tile
            top[user] = jnp.maximum(top[user], tile)

        return carry

    lax.fori_loop(0, NREQ, collect, 0)

    for user in range(REQS):
        share = jnp.where(held(user), jnp.exp(own[user] - top[user]), 0.0)
        low[user] = share
        for head in range(HEADS):
            for k in range(WIN // 16):
                acc[user, rows_of(head, k), :] *= spread(share, head, k)

    def add(p, carry):
        user = users[p]

        @pl.when(user >= 0)
        def _():
            share = jnp.where(held(user), jnp.exp(tiles[p] - top[user]), 0.0)
            low[user] += share
            for head in range(HEADS):
                for k in range(WIN // 16):
                    part = arrived[p, rows_of(head, k), :].astype(F32)
                    acc[user, rows_of(head, k), :] += part * spread(share, head, k)

        return carry

    lax.fori_loop(0, NREQ, add, 0)

    rows[...] = jnp.zeros_like(rows)
    for user in range(REQS):
        inside = held(user)
        factor = jnp.where(inside, 1.0 / jnp.where(inside, low[user], 1.0), 0.0)
        first = window(user)
        for head in range(HEADS):
            for k in range(WIN // 16):
                at = pl.ds(pl.multiple_of(first + 16 * k, 16), 16)
                rows[head, at, :] += acc[user, rows_of(head, k), :] * spread(factor, head, k)
    for head in range(HEADS):
        out[:, head * HD : (head + 1) * HD] = rows[head].astype(BF16)


def merge_attention(users, win_of, first_of, end_of, arrived, queries, keys, values):
    return pl.pallas_call(
        merge_kernel,
        out_shape=jax.ShapeDtypeStruct((TOK, HEADS * HD), BF16),
        in_specs=[smem()] * 4 + [vmem()] * 4,
        out_specs=vmem(),
        scratch_shapes=[
            pltpu.VMEM((REQS, STAT, HD), F32),
            pltpu.VMEM((NREQ, 8, 128), F32),
            pltpu.VMEM((REQS, 8, 128), F32),
            pltpu.VMEM((REQS, 8, 128), F32),
            pltpu.VMEM((HEADS, TOK, HD), F32),
        ],
        compiler_params=pltpu.CompilerParams(vmem_limit_bytes=32 << 20),
        cost_estimate=pl.CostEstimate(
            flops=64 << 20, bytes_accessed=6 << 20, transcendentals=1 << 18
        ),
        name="merge_attention",
    )(users, win_of, first_of, end_of, arrived, queries, keys, values)


def project_kernel(att, att_far, weight, weight_far, residual, gain, picks, mixed, sent, both):
    half = residual.shape[1] // 2
    total = residual[...].astype(F32)
    total += jnp.dot(att[...], weight[...], preferred_element_type=F32)
    total += jnp.dot(att_far[...], weight_far[...], preferred_element_type=F32)
    mixed[...] = total
    scale = lax.rsqrt(jnp.mean(total * total, axis=1, keepdims=True) + NORM_EPS)
    normed = (total * scale * gain[...]).astype(BF16)
    both[:TOK] = normed[:, :half]
    both[TOK:] = normed[:, half:]
    step = 256
    for row in range(0, sent.shape[0], step):
        sent[row : row + step] = jnp.dot(
            picks[row : row + step], both[...], preferred_element_type=F32
        ).astype(BF16)


def project(att, att_far, weight, weight_far, residual, gain, picks):
    width = residual.shape[1]
    return pl.pallas_call(
        project_kernel,
        out_shape=(
            jax.ShapeDtypeStruct((TOK, width), F32),
            jax.ShapeDtypeStruct((picks.shape[0], width // 2), BF16),
        ),
        in_specs=[vmem()] * 7,
        out_specs=(vmem(), vmem()),
        scratch_shapes=[pltpu.VMEM((2 * TOK, width // 2), BF16)],
        compiler_params=pltpu.CompilerParams(vmem_limit_bytes=32 << 20),
        cost_estimate=pl.CostEstimate(
            flops=4 * TOK * 512 * width + 2 * picks.shape[0] * 256 * width // 2,
            bytes_accessed=10 << 20,
            transcendentals=TOK,
        ),
        name="project_dispatch",
    )(att, att_far, weight, weight_far, residual, gain, picks)


def expert_kernel(rows, gate, up, down, out):
    count = rows.shape[0]
    width = gate.shape[0]
    half, quarter = width // 2, width // 4
    wide = rows[...].astype(F32)
    upper = lax.broadcasted_iota(jnp.int32, (count // 2, 8, half), 1) < 4
    tail = wide[:, 16:24].reshape(count // 2, 2, 8, half)
    even, odd = tail[:, 0], tail[:, 1]
    tail_0 = jnp.where(upper, even, pltpu.roll(odd, 4, 1))
    tail_1 = jnp.where(upper, pltpu.roll(even, 4, 1), odd)
    left = jnp.concatenate(
        [wide[:, 0:8].reshape(count * 8, half), tail_0.reshape(count * 4, half)], axis=0
    )
    right = jnp.concatenate(
        [wide[:, 8:16].reshape(count * 8, half), tail_1.reshape(count * 4, half)], axis=0
    )
    tokens = jnp.concatenate([left.astype(BF16), right.astype(BF16)], axis=1)
    gate_act = jnp.dot(tokens, gate[...], preferred_element_type=F32)
    up_act = jnp.dot(tokens, up[...], preferred_element_type=F32)
    hidden = (gate_act / (1.0 + jnp.exp(-gate_act)) * up_act).astype(BF16)
    result = jnp.dot(hidden, down[...], preferred_element_type=F32)
    upper = lax.broadcasted_iota(jnp.int32, (count // 2, 8, quarter), 1) < 4
    for side in range(2):
        cols = [slice((2 * side + q) * quarter, (2 * side + q + 1) * quarter) for q in range(2)]
        main = [result[: count * 8, c].reshape(count, 8, quarter) for c in cols]
        tail = [result[count * 8 :, c].reshape(count // 2, 8, quarter) for c in cols]
        even = jnp.where(upper, tail[0], pltpu.roll(tail[1], 4, 1))
        odd = jnp.where(upper, pltpu.roll(tail[0], 4, 1), tail[1])
        last = jnp.stack([even, odd], axis=1).reshape(count, 8, quarter)
        out[:, side] = jnp.concatenate(main + [last], axis=1).astype(BF16)


def run_expert(rows, gate, up, down, steps=2):
    count = rows.shape[0] // steps
    width, hidden = gate.shape
    once = pl.Buffered(1)
    return pl.pallas_call(
        expert_kernel,
        grid=(steps,),
        out_shape=jax.ShapeDtypeStruct((rows.shape[0], 2, 2 * CAP, width // 4), BF16),
        in_specs=[
            pl.BlockSpec((count, 2 * CAP, width // 2), lambda i: (i, 0, 0)),
            pl.BlockSpec((width, hidden), lambda i: (0, 0), pipeline_mode=once),
            pl.BlockSpec((width, hidden), lambda i: (0, 0), pipeline_mode=once),
            pl.BlockSpec((hidden, width), lambda i: (0, 0), pipeline_mode=once),
        ],
        out_specs=pl.BlockSpec((count, 2, 2 * CAP, width // 4), lambda i: (i, 0, 0, 0)),
        compiler_params=pltpu.CompilerParams(vmem_limit_bytes=56 << 20),
        cost_estimate=pl.CostEstimate(
            flops=6 * rows.shape[0] * CAP * width * hidden,
            bytes_accessed=15 << 20,
            transcendentals=rows.shape[0] * CAP * hidden,
        ),
        name="expert",
    )(rows, gate, up, down)


def combine_kernel(mixed, shares, shares_low, rows, out):
    total = jnp.dot(shares[...], rows[...], preferred_element_type=F32)
    total += jnp.dot(shares_low[...], rows[...], preferred_element_type=F32)
    width = rows.shape[1]
    out[:, :width] = (mixed[:, :width] + total[:TOK]).astype(BF16)
    out[:, width:] = (mixed[:, width:] + total[TOK:]).astype(BF16)


def combine(mixed, shares, shares_low, rows):
    return pl.pallas_call(
        combine_kernel,
        out_shape=jax.ShapeDtypeStruct(mixed.shape, BF16),
        in_specs=[vmem()] * 4,
        out_specs=vmem(),
        compiler_params=pltpu.CompilerParams(vmem_limit_bytes=32 << 20),
        cost_estimate=pl.CostEstimate(
            flops=4 * shares.shape[0] * rows.shape[0] * rows.shape[1],
            bytes_accessed=8 << 20,
            transcendentals=0,
        ),
        name="combine",
    )(mixed, shares, shares_low, rows)


def slot_rows():
    slot = np.array(list(range(8)) * 2 + list(range(8, 12)) * 2, np.int32)
    part = np.array([0] * 8 + [1] * 8 + [0] * 4 + [1] * 4, np.int32)
    return slot, part


def routing(expert_ids, expert_weights):
    flat = expert_ids.reshape(-1)
    count = flat.shape[0]
    onehot = (flat[:, None] == jnp.arange(NREQ, dtype=jnp.int32)[None, :]).astype(BF16)
    earlier = (
        jnp.arange(count, dtype=jnp.int32)[None, :] < jnp.arange(count, dtype=jnp.int32)[:, None]
    ).astype(BF16)
    before = jnp.dot(earlier, onehot, preferred_element_type=F32)
    slot = jnp.sum(before * onehot.astype(F32), axis=1).astype(jnp.int32)
    place = (flat * CAP + slot).reshape(TOK, TOP)

    slot_at, part_at = slot_rows()
    row_place = (np.arange(NREQ, dtype=np.int32)[:, None] * CAP + slot_at[None, :]).reshape(-1)
    row_part = np.tile(part_at, NREQ)
    col_place = jnp.concatenate([place, place], axis=0)
    col_part = np.repeat(np.arange(2, dtype=np.int32), TOK)
    hit = jnp.zeros((row_place.shape[0], 2 * TOK), jnp.bool_)
    for k in range(TOP):
        hit = hit | (col_place[None, :, k] == row_place[:, None])
    picks = (hit & (row_part[:, None] == col_part[None, :])).astype(BF16)

    back_place = np.repeat(row_place.reshape(NREQ, 1, -1), 2, axis=1).reshape(-1)
    back_part = np.tile(part_at, 2 * NREQ)
    col_weight = jnp.concatenate([expert_weights, expert_weights], axis=0)
    shares = jnp.zeros((2 * TOK, back_place.shape[0]), F32)
    for k in range(TOP):
        shares = shares + jnp.where(
            col_place[:, k, None] == back_place[None, :], col_weight[:, k, None], 0.0
        )
    shares = jnp.where(back_part[None, :] == col_part[:, None], shares, 0.0)
    high = lax.reduce_precision(shares, 8, 7)
    return picks, high.astype(BF16), (shares - high).astype(BF16)


def shards(
    residual,
    queries,
    new_keys,
    new_values,
    request_ids,
    page_store,
    page_sends,
    page_users,
    expert_ids,
    expert_weights,
    output_weight,
    norm_gain,
    gate_weight,
    up_weight,
    down_weight,
):
    me = lax.axis_index("req")
    tp_index = lax.axis_index("tp")
    width = residual.shape[1]
    half = width // 2
    swap = [(0, 1), (1, 0)]

    users = page_users[0]
    counts = jnp.sum(
        (request_ids[:, None] == jnp.arange(REQS, dtype=jnp.int32)[None, :]).astype(jnp.int32), 0
    )
    end_of = jnp.cumsum(counts)
    first_of = end_of - counts
    win_of_user = jnp.minimum(first_of, TOK - WIN) // 16
    sent_win = jnp.sum(
        jnp.where(
            users[:, None] == jnp.arange(REQS, dtype=jnp.int32)[None, :], win_of_user[None, :], 0
        ),
        1,
    )
    note = jnp.zeros((8, queries.shape[1]), BF16).at[0, :NREQ].set(sent_win.astype(BF16))
    pieces = gather_blocks(jnp.concatenate([queries, note], axis=0))
    src = lax.dynamic_index_in_dim(jnp.asarray(source_table()), me, 0, keepdims=False)
    page_of = page_sends[0][src]
    notes = jnp.concatenate([piece[:, TOK, :NREQ] for piece in pieces], axis=0)
    win_of = lax.dynamic_index_in_dim(notes, me, 1, keepdims=False).astype(jnp.int32)

    parts = partial_attention(src, page_of, win_of, pieces, page_store)
    arrived = lax.all_to_all(parts, "req", 0, 0, tiled=True)
    attended = merge_attention(
        users, sent_win, first_of, end_of, arrived, queries, new_keys, new_values
    )
    weight_far = lax.ppermute(output_weight, "tp", swap)
    picks, shares, shares_low = routing(expert_ids, expert_weights)
    attended_far = lax.ppermute(attended, "tp", swap)
    mixed, sent = project(
        attended, attended_far, output_weight, weight_far, residual, norm_gain[None, :], picks
    )
    rows = lax.all_to_all(sent.reshape(NREQ, 2 * CAP, half), "req", 0, 0, tiled=True)
    result = run_expert(rows, gate_weight[0], up_weight[0], down_weight[0])
    returned = lax.all_to_all(
        result.reshape(2 * NREQ, 2 * CAP, width // 4), ("req", "tp"), 0, 0, tiled=True
    )
    mixed_half = lax.dynamic_slice_in_dim(mixed, tp_index * half, half, 1)
    return combine(mixed_half, shares, shares_low, returned.reshape(-1, width // 4))


def solution(mesh):
    placed = (
        P("req", None),
        P("req", "tp"),
        P("req", "tp"),
        P("req", "tp"),
        P("req"),
        P("req", None, None, "tp"),
        P("req", None),
        P("req", None),
        P("req", None),
        P("req", None),
        P("tp", None),
        P(),
        P("req", None, "tp"),
        P("req", None, "tp"),
        P("req", "tp", None),
    )
    return jax.shard_map(
        shards, mesh=mesh, in_specs=placed, out_specs=P("req", "tp"), check_vma=False
    )
```

time: 835 us -> 341 us (0.41); the launches traced: 823 us -> 340 us
  waiting for transfers between devices: 427 us -> 181 us
  local copies, waits for them, and re-layouts: 218 us -> 20.9 us
  Pallas kernels: 0 us -> 73.3 us
  blocking collectives: 63.4 us -> 0 us
  matrix products: 38.9 us -> 0.29 us
  starting transfers between devices: 19.8 us -> 56 us
  other arithmetic: 41.6 us -> 8.97 us
  between operations: 13.9 us -> 0.33 us
    all_to_all x2 -> x3, waiting for transfers between devices: 306 us -> 135 us  [the longest x1 65.9 us: shards(): arrived = lax.all_to_all(parts, 'req', 0, 0, tiled=True)]
    scatter x2 -> x0, local copies, waits for them, and re-layouts: 96.8 us -> none  [shards(): outgoing_rows = jnp.zeros((peer_count, capacity, normed.shape[1]), jnp.bf...]
    psum x1 -> x0, waiting for transfers between devices: 84 us -> none  [shards(): attn_full = lax.psum(partial_value, 'tp')]
    pallas_call x0 -> x5, Pallas kernels: none -> 73.3 us  [the longest x1 34.2 us: partial_attention(): pl.pallas_call(page_kernel, out_shape=jax.ShapeDtypeStruct((NREQ, BLOCK,...]
    all_to_all x1 -> x0, blocking collectives: 63.4 us -> none  [shards(): lax.all_to_all(outgoing_rows, 'req', split_axis=0, concat_axis=0, tiled=T...]
    another operation x5 -> x0, local copies, waits for them, and re-layouts: 46.6 us -> none  [the longest x2 26.4 us: shards(): arrived[:, 1].reshape(peer_count * page_rows, local_heads, HD)]
    ppermute x0 -> x13, waiting for transfers between devices: none -> 45.8 us  [the longest x3 15.6 us: gather_blocks(): lax.ppermute(line, 'req', perm_ring(1, step))]
    dot_general x6 -> x1, matrix products: 38.9 us -> 0.29 us  [routing(): before = jnp.dot(earlier, onehot, preferred_element_type=F32)]
  transfers between devices with their start and end apart: 4 -> 16, of which waited for: 4 -> 12; matrix products, arithmetic and copies ran while one was open for 1% -> 6% of each run, Pallas kernels for 0% -> 5%
where the time goes in v1:
time: 341 us; the launch traced here: 340 us
  waiting for transfers between devices  181 us (53%)
  Pallas kernels  73.3 us (21%)
  starting transfers between devices  56 us (16%)
  local copies, waits for them, and re-layouts  20.9 us (6%)
  other arithmetic  8.97 us (3%)
    all_to_all x1, waiting for transfers between devices, shards(): arrived = lax.all_to_all(parts, 'req', 0, 0, tiled=True)  65.9 us
    all_to_all x1, waiting for transfers between devices, shards(): lax.all_to_all(result.reshape(2 * NREQ, 2 * CAP, width // 4), ('req', 'tp...  36.1 us
    pallas_call x1, Pallas kernels, partial_attention(): pl.pallas_call(page_kernel, out_shape=jax.ShapeDtypeStruct((NREQ, BLOCK,...  34.2 us
    all_to_all x1, waiting for transfers between devices, shards(): lax.all_to_all(sent.reshape(NREQ, 2 * CAP, half), 'req', 0, 0, tiled=True)  33 us
    pallas_call x1, Pallas kernels, merge_attention(): pl.pallas_call(merge_kernel, out_shape=jax.ShapeDtypeStruct((TOK, HEADS *...  18.6 us
    unnamed x55, local copies, waits for them, and re-layouts  16.8 us
    ppermute x3, waiting for transfers between devices, gather_blocks(): lax.ppermute(line, 'req', perm_ring(1, step))  15.6 us
    ppermute x1, waiting for transfers between devices, shards(): weight_far = lax.ppermute(output_weight, 'tp', swap)  15.3 us
  transfers between devices with their start and end apart: 16, of which 12 were waited for; matrix products, arithmetic and copies ran while one was open for 6% of the time, Pallas kernels for 5%

profile of v1, /device:TPU:1, one launch (start us, length us, event | category | flops | bytes accessed | tf_op | source)
XLA Modules:
  0.0 340.5 jit_solution(5592341012956052480)
XLA Ops:
  2.7 3.7 %collective-permute-start = (bf16[136,512]{1,0:T(8,128)(2,1)S(1)}, bf16[136,512]{1,0:T(8,128)(2,1)S(1)}, u32[]{:S(2)}, u32[]{:S(2)}) collective-permute-start(bf16[136,512]{1,0:T(8,128)(2,1)S(1)} %get-tuple-element.28), channel_id=1, source_target_pairs={{0,4},{2,6},{4,0},{6,2},{8,12},{10,14},{12,8},{14,10},{16,20},{18,... | collective-permute-start | bytes 417800 | tf_op jit(solution)/shard_map/ppermute | solution.py:78
  6.3 2.9 collective-permute-done
  11.4 3.3 collective-permute-start.2
  17.7 4.2 %collective-permute-done.2 = bf16[2,136,512]{2,1,0:T(8,128)(2,1)S(1)} collective-permute-done((bf16[2,136,512]{2,1,0:T(8,128)(2,1)S(1)}, bf16[2,136,512]{2,1,0:T(8,128)(2,1)S(1)}, u32[]{:S(2)}, u32[]{:S(2)}) %collective-permute-start.2) | collective-permute-done | bytes 278560 | tf_op jit(solution)/shard_map/ppermute | solution.py:80
  26.8 3.2 collective-permute-start.7
  32.2 5.8 %collective-permute-done.4.refs_1_ = bf16[8,136,512]{2,1,0:T(8,128)(2,1)S(1)} collective-permute-done((bf16[8,136,512]{2,1,0:T(8,128)(2,1)S(1)}, bf16[8,136,512]{2,1,0:T(8,128)(2,1)S(1)}, u32[]{:S(2)}, u32[]{:S(2)}) %collective-permute-start.4) | collective-permute-done | bytes 1114144 | tf_op jit(solution)/shard_map/ppermute | solution.py:82
  37.9 3.0 collective-permute-start.8
  41.0 9.8 %collective-permute-done.5.refs_2_ = bf16[8,136,512]{2,1,0:T(8,128)(2,1)S(1)} collective-permute-done((bf16[8,136,512]{2,1,0:T(8,128)(2,1)S(1)}, bf16[8,136,512]{2,1,0:T(8,128)(2,1)S(1)}, u32[]{:S(2)}, u32[]{:S(2)}) %collective-permute-start.5) | collective-permute-done | bytes 1114144 | tf_op jit(solution)/shard_map/ppermute | solution.py:82
  50.8 3.6 %collective-permute-start.9 = (bf16[8,136,512]{2,1,0:T(8,128)(2,1)S(1)}, bf16[8,136,512]{2,1,0:T(8,128)(2,1)S(1)}, u32[]{:S(2)}, u32[]{:S(2)}) collective-permute-start(bf16[8,136,512]{2,1,0:T(8,128)(2,1)S(1)} %collective-permute-done.5.refs_2_), channel_id=1, source_target_pairs={{0,2},{2,0},{4,6},{6,4},{8,10},{10,8},{12,14},{14,12},{16,18},{18,... | collective-permute-start | bytes 3342344 | tf_op jit(solution)/shard_map/ppermute | solution.py:83
  59.6 34.2 %page_attention.1 = bf16[64,328,128]{2,1,0:T(8,128)(2,1)} custom-call(s32[64]{0:T(128)S(1)} %fusion.10.src, s32[64]{0:T(128)S(1)} %gather_fusion, s32[64]{0:T(128)S(1)} %convert_reduce_fusion.win_of, bf16[8,136,512]{2,1,0:T(8,128)(2,1)S(1)} %bitcast.61, bf16[8,136,512]{2,1,0:T(8,128)(2,1)S(1)} %collective-permute-done.4.refs_1_, ...), custom_call_target="tpu_custom_call" | custom-call | flops 2013265920 | bytes 18874368 | tf_op jit(solution)/shard_map/page_attention/pallas_call | solution.py:164
  93.9 9.3 %all-to-all-start = ((bf16[64,328,128]{2,1,0:T(8,128)(2,1)}), bf16[64,328,128]{2,1,0:T(8,128)(2,1)}, u32[]{:S(2)}, u32[]{:S(2)}) async-start(bf16[64,328,128]{2,1,0:T(8,128)(2,1)} %page_attention.1), calls=%async_computation | async-start | bytes 10747904 | tf_op jit(solution)/shard_map/all_to_all | solution.py:501
  104.3 65.9 %all-to-all-done.arrived = bf16[64,328,128]{2,1,0:T(8,128)(2,1)} async-done(((bf16[64,328,128]{2,1,0:T(8,128)(2,1)}), bf16[64,328,128]{2,1,0:T(8,128)(2,1)}, u32[]{:S(2)}, u32[]{:S(2)}) %all-to-all-start) | async-done | bytes 5373984 | tf_op jit(solution)/shard_map/all_to_all | solution.py:501
  170.2 18.6 %merge_attention.1.att = bf16[128,512]{1,0:T(8,128)(2,1)S(1)} custom-call(s32[64]{0:T(128)S(1)} %bitcast.65, s32[64]{0:T(128)S(1)} %select_reduce_fusion.win_of, s32[4]{0:T(128)S(1)} %get-tuple-element.22.first_of, s32[4]{0:T(128)S(1)} %bitcast.63, bf16[64,328,128]{2,1,0:T(8,128)(2,1)} %all-to-all-done.arrived, bf16[128,512]{1,0:T(8,128)(2,1)S(1)} %copy-done.5, ...), custom_call_target="tpu_custom_call" | custom-call | flops 67108864 | bytes 6291456 | tf_op jit(solution)/shard_map/merge_attention/pallas_call | solution.py:278
  191.6 15.3 %collective-permute-done.12.weight_far = bf16[512,2048]{1,0:T(8,128)(2,1)} collective-permute-done((bf16[512,2048]{1,0:T(8,128)(2,1)S(1)}, bf16[512,2048]{1,0:T(8,128)(2,1)}, u32[]{:S(2)}, u32[]{:S(2)}) %collective-permute-start.12) | collective-permute-done | bytes 2097184 | tf_op jit(solution)/shard_map/ppermute | solution.py:505
  206.9 2.8 collective-permute-done.11.att_far
  209.7 5.0 %project_dispatch.1 = (f32[128,2048]{1,0:T(8,128)S(1)}, bf16[1536,1024]{1,0:T(8,128)(2,1)}) custom-call(bf16[128,512]{1,0:T(8,128)(2,1)S(1)} %merge_attention.1.att, bf16[128,512]{1,0:T(8,128)(2,1)S(1)} %collective-permute-done.11.att_far, bf16[512,2048]{1,0:T(8,128)(2,1)S(1)} %copy-done.4, bf16[512,2048]{1,0:T(8,128)(2,1)} %collective-permute-done.12.weight_far, ...), custom_call_target="tpu_custom_call" | custom-call | flops 1342177280 | bytes 10485760 | tf_op jit(solution)/shard_map/project_dispatch/pallas_call | solution.py:317
  215.8 14.6 %all-to-all-start.1 = ((bf16[64,24,1024]{2,1,0:T(8,128)(2,1)}), bf16[64,24,1024]{2,1,0:T(8,128)(2,1)S(1)}, u32[]{:S(2)}, u32[]{:S(2)}) async-start(bf16[64,24,1024]{2,1,0:T(8,128)(2,1)} %bitcast.24), calls=%async_computation.1 | async-start | bytes 6291456 | tf_op jit(solution)/shard_map/all_to_all | solution.py:511
  230.4 4.6 %copy.121 = bf16[1,2048,704]{2,1,0:T(8,128)(2,1)} copy(bf16[1,2048,704]{1,2,0:T(8,128)(2,1)} %param.40) | data formatting | bytes 5767168 | tf_op args[12]
  235.0 4.6 %copy.122 = bf16[1,2048,704]{2,1,0:T(8,128)(2,1)} copy(bf16[1,2048,704]{1,2,0:T(8,128)(2,1)} %param.41) | data formatting | bytes 5767168 | tf_op args[13]
  239.6 33.0 %all-to-all-done.1.rows = bf16[64,24,1024]{2,1,0:T(8,128)(2,1)S(1)} async-done(((bf16[64,24,1024]{2,1,0:T(8,128)(2,1)}), bf16[64,24,1024]{2,1,0:T(8,128)(2,1)S(1)}, u32[]{:S(2)}, u32[]{:S(2)}) %all-to-all-start.1) | async-done | bytes 3145760 | tf_op jit(solution)/shard_map/all_to_all | solution.py:511
  274.3 13.0 %expert.1 = bf16[64,2,24,512]{3,2,1,0:T(8,128)(2,1)} custom-call(bf16[64,24,1024]{2,1,0:T(8,128)(2,1)} %copy-done.13, bf16[2048,704]{1,0:T(8,128)(2,1)} %bitcast.67, bf16[2048,704]{1,0:T(8,128)(2,1)} %bitcast.68, bf16[704,2048]{1,0:T(8,128)(2,1)} %bitcast.86), custom_call_target="tpu_custom_call" | custom-call | flops 6643777536 | bytes 15728640 | tf_op jit(solution)/shard_map/expert/pallas_call | solution.py:372
  287.3 5.3 %all-to-all-start.2 = ((bf16[128,24,512]{2,1,0:T(8,128)(2,1)}), bf16[128,24,512]{2,1,0:T(8,128)(2,1)S(1)}, u32[]{:S(2)}, u32[]{:S(2)}) async-start(bf16[128,24,512]{2,1,0:T(8,128)(2,1)} %bitcast.66), calls=%async_computation.2 | async-start | bytes 6291456 | tf_op jit(solution)/shard_map/all_to_all | solution.py:513
  292.7 4.6 %fusion = (bf16[256,3072]{1,0:T(8,128)(2,1)}, bf16[256,3072]{1,0:T(8,128)(2,1)}) fusion(pred[256,3072]{1,0:T(32,128)(4,1)} %constant.90.clone, f32[256]{0:T(256)S(1)} %bitcast.82, f32[256]{0:T(256)S(1)} %bitcast.83, f32[256]{0:T(256)S(1)} %bitcast.84, f32[256]{0:T(256)S(1)} %bitcast.81, s32[3072]{0:T(1024)S(1)} %copy-done.18, s32[256]{0:T(256)S(1)} %bitcast.76, ...), kind=kLoop, calls=%fused_computation.3 | loop fusion | flops 12582912 | bytes 3952640 | tf_op jit(solution)/shard_map/convert_element_type | solution.py:454
  298.1 36.1 %all-to-all-done.2 = bf16[128,24,512]{2,1,0:T(8,128)(2,1)S(1)} async-done(((bf16[128,24,512]{2,1,0:T(8,128)(2,1)}), bf16[128,24,512]{2,1,0:T(8,128)(2,1)S(1)}, u32[]{:S(2)}, u32[]{:S(2)}) %all-to-all-start.2) | async-done | bytes 3145760 | tf_op jit(solution)/shard_map/all_to_all | solution.py:513
  (102 shorter events, 33.8 us)
Async XLA Ops:
  0.0 30.7 %copy-start = (s32[1,64]{1,0:T(1,128)S(1)}, s32[1,64]{1,0:T(1,128)}, u32[]{:S(2)}) copy-start(s32[1,64]{1,0:T(1,128)} %param.34) | copy-start | bytes 772
  2.7 6.6 %collective-permute-start = (bf16[136,512]{1,0:T(8,128)(2,1)S(1)}, bf16[136,512]{1,0:T(8,128)(2,1)S(1)}, u32[]{:S(2)}, u32[]{:S(2)}) collective-permute-start(bf16[136,512]{1,0:T(8,128)(2,1)S(1)} %get-tuple-element.28), channel_id=1, source_target_pairs={{0,4},{2,6},{4,0},{6,2},{8,12},{10,14},{12,8},{14,10},{16,20},{18,... | collective-permute-start | bytes 417800 | tf_op jit(solution)/shard_map/ppermute | solution.py:78
  9.3 8.4 %collective-permute-start.1 = (bf16[2,136,512]{2,1,0:T(8,128)(2,1)S(1)}, bf16[2,136,512]{2,1,0:T(8,128)(2,1)S(1)}, u32[]{:S(2)}, u32[]{:S(2)}) collective-permute-start(bf16[2,136,512]{2,1,0:T(8,128)(2,1)S(1)} %get-tuple-element.26), channel_id=1, source_target_pairs={{0,32},{2,10},{4,36},{6,14},{8,40},{10,18},{12,44},{14,22},{16,48}... | collective-permute-start | bytes 835592 | tf_op jit(solution)/shard_map/ppermute | solution.py:80
  11.4 10.5 %collective-permute-start.2 = (bf16[2,136,512]{2,1,0:T(8,128)(2,1)S(1)}, bf16[2,136,512]{2,1,0:T(8,128)(2,1)S(1)}, u32[]{:S(2)}, u32[]{:S(2)}) collective-permute-start(bf16[2,136,512]{2,1,0:T(8,128)(2,1)S(1)} %get-tuple-element.26), channel_id=1, source_target_pairs={{0,64},{2,18},{4,68},{6,22},{8,72},{10,26},{12,76},{14,30},{16,80}... | collective-permute-start | bytes 835592 | tf_op jit(solution)/shard_map/ppermute | solution.py:80
  14.7 7.2 %collective-permute-start.3 = (bf16[2,136,512]{2,1,0:T(8,128)(2,1)S(1)}, bf16[2,136,512]{2,1,0:T(8,128)(2,1)S(1)}, u32[]{:S(2)}, u32[]{:S(2)}) collective-permute-start(bf16[2,136,512]{2,1,0:T(8,128)(2,1)S(1)} %get-tuple-element.26), channel_id=1, source_target_pairs={{0,96},{2,26},{4,100},{6,30},{8,104},{10,2},{12,108},{14,6},{16,11... | collective-permute-start | bytes 835592 | tf_op jit(solution)/shard_map/ppermute | solution.py:80
  22.0 15.9 %collective-permute-start.4 = (bf16[8,136,512]{2,1,0:T(8,128)(2,1)S(1)}, bf16[8,136,512]{2,1,0:T(8,128)(2,1)S(1)}, u32[]{:S(2)}, u32[]{:S(2)}) collective-permute-start(bf16[8,136,512]{2,1,0:T(8,128)(2,1)S(1)} %bitcast.56), channel_id=1, source_target_pairs={{0,8},{2,34},{4,12},{6,38},{8,16},{10,42},{12,20},{14,46},{16,24},... | collective-permute-start | bytes 3342344 | tf_op jit(solution)/shard_map/ppermute | solution.py:82
  23.1 27.7 %collective-permute-start.5 = (bf16[8,136,512]{2,1,0:T(8,128)(2,1)S(1)}, bf16[8,136,512]{2,1,0:T(8,128)(2,1)S(1)}, u32[]{:S(2)}, u32[]{:S(2)}) collective-permute-start(bf16[8,136,512]{2,1,0:T(8,128)(2,1)S(1)} %bitcast.57), channel_id=1, source_target_pairs={{0,16},{2,66},{4,20},{6,70},{8,24},{10,74},{12,28},{14,78},{16,0},... | collective-permute-start | bytes 3342344 | tf_op jit(solution)/shard_map/ppermute | solution.py:82
  25.7 28.7 %collective-permute-start.6 = (bf16[8,136,512]{2,1,0:T(8,128)(2,1)S(1)}, bf16[8,136,512]{2,1,0:T(8,128)(2,1)}, u32[]{:S(2)}, u32[]{:S(2)}) collective-permute-start(bf16[8,136,512]{2,1,0:T(8,128)(2,1)S(1)} %bitcast.58), channel_id=1, source_target_pairs={{0,24},{2,98},{4,28},{6,102},{8,0},{10,106},{12,4},{14,110},{16,8}... | collective-permute-start | bytes 3342344 | tf_op jit(solution)/shard_map/ppermute | solution.py:82
  26.8 28.4 %collective-permute-start.7 = (bf16[8,136,512]{2,1,0:T(8,128)(2,1)S(1)}, bf16[8,136,512]{2,1,0:T(8,128)(2,1)}, u32[]{:S(2)}, u32[]{:S(2)}) collective-permute-start(bf16[8,136,512]{2,1,0:T(8,128)(2,1)S(1)} %bitcast.59), channel_id=1, source_target_pairs={{0,2},{2,0},{4,6},{6,4},{8,10},{10,8},{12,14},{14,12},{16,18},{18,... | collective-permute-start | bytes 3342344 | tf_op jit(solution)/shard_map/ppermute | solution.py:83
  37.9 18.0 %collective-permute-start.8 = (bf16[8,136,512]{2,1,0:T(8,128)(2,1)S(1)}, bf16[8,136,512]{2,1,0:T(8,128)(2,1)S(1)}, u32[]{:S(2)}, u32[]{:S(2)}) collective-permute-start(bf16[8,136,512]{2,1,0:T(8,128)(2,1)S(1)} %collective-permute-done.4.refs_1_), channel_id=1, source_target_pairs={{0,2},{2,0},{4,6},{6,4},{8,10},{10,8},{12,14},{14,12},{16,18},{18,... | collective-permute-start | bytes 3342344 | tf_op jit(solution)/shard_map/ppermute | solution.py:83
  50.8 5.9 %collective-permute-start.9 = (bf16[8,136,512]{2,1,0:T(8,128)(2,1)S(1)}, bf16[8,136,512]{2,1,0:T(8,128)(2,1)S(1)}, u32[]{:S(2)}, u32[]{:S(2)}) collective-permute-start(bf16[8,136,512]{2,1,0:T(8,128)(2,1)S(1)} %collective-permute-done.5.refs_2_), channel_id=1, source_target_pairs={{0,2},{2,0},{4,6},{6,4},{8,10},{10,8},{12,14},{14,12},{16,18},{18,... | collective-permute-start | bytes 3342344 | tf_op jit(solution)/shard_map/ppermute | solution.py:83
  55.1 3.4 %collective-permute-start.10 = (bf16[8,136,512]{2,1,0:T(8,128)(2,1)}, bf16[8,136,512]{2,1,0:T(8,128)(2,1)S(1)}, u32[]{:S(2)}, u32[]{:S(2)}) collective-permute-start(bf16[8,136,512]{2,1,0:T(8,128)(2,1)} %collective-permute-done.6.refs_3_), channel_id=1, source_target_pairs={{0,2},{2,0},{4,6},{6,4},{8,10},{10,8},{12,14},{14,12},{16,18},{18,... | collective-permute-start | bytes 3342344 | tf_op jit(solution)/shard_map/ppermute | solution.py:83
  93.8 76.4 %copy-start.5 = (bf16[128,512]{1,0:T(8,128)(2,1)S(1)}, bf16[128,512]{1,0:T(8,128)(2,1)}, u32[]{:S(2)}) copy-start(bf16[128,512]{1,0:T(8,128)(2,1)} %queries.1) | copy-start | bytes 393220
  93.8 76.4 %copy-start.9 = (bf16[128,512]{1,0:T(8,128)(2,1)S(1)}, bf16[128,512]{1,0:T(8,128)(2,1)}, u32[]{:S(2)}) copy-start(bf16[128,512]{1,0:T(8,128)(2,1)} %keys.1) | copy-start | bytes 393220
  93.8 76.3 %copy-start.10 = (bf16[128,512]{1,0:T(8,128)(2,1)S(1)}, bf16[128,512]{1,0:T(8,128)(2,1)}, u32[]{:S(2)}) copy-start(bf16[128,512]{1,0:T(8,128)(2,1)} %values.1) | copy-start | bytes 393220
  93.8 76.3 %copy-start.12 = (s32[1,64]{1,0:T(1,128)S(1)}, s32[1,64]{1,0:T(1,128)}, u32[]{:S(2)}) copy-start(s32[1,64]{1,0:T(1,128)} %param.35) | copy-start | bytes 772
  93.9 76.3 %all-to-all-start = ((bf16[64,328,128]{2,1,0:T(8,128)(2,1)}), bf16[64,328,128]{2,1,0:T(8,128)(2,1)}, u32[]{:S(2)}, u32[]{:S(2)}) async-start(bf16[64,328,128]{2,1,0:T(8,128)(2,1)} %page_attention.1), calls=%async_computation | async-start | bytes 10747904 | tf_op jit(solution)/shard_map/all_to_all | solution.py:501
  103.1 103.8 %collective-permute-start.12 = (bf16[512,2048]{1,0:T(8,128)(2,1)S(1)}, bf16[512,2048]{1,0:T(8,128)(2,1)}, u32[]{:S(2)}, u32[]{:S(2)}) collective-permute-start(bf16[512,2048]{1,0:T(8,128)(2,1)S(1)} %copy-done.4), channel_id=1, source_target_pairs={{0,1},{1,0},{2,3},{3,2},{4,5},{5,4},{6,7},{7,6},{8,9},{9,8},{10,11... | collective-permute-start | bytes 6291464 | tf_op jit(solution)/shard_map/ppermute | solution.py:505
  170.2 20.7 %copy-start.17 = (pred[1536,256]{1,0:T(32,128)(4,1)S(1)}, pred[1536,256]{1,0:T(32,128)(4,1)}, u32[]{:S(2)}) copy-start(pred[1536,256]{1,0:T(32,128)(4,1)} %constant.88.clone) | copy-start | bytes 1179652
  170.2 39.5 %copy-start.6 = (bf16[128,2048]{1,0:T(8,128)(2,1)S(1)}, bf16[128,2048]{1,0:T(8,128)(2,1)}, u32[]{:S(2)}) copy-start(bf16[128,2048]{1,0:T(8,128)(2,1)} %residual.1) | copy-start | bytes 1572868
  170.2 39.5 %copy-start.11 = (f32[2048]{0:T(1024)S(1)}, f32[2048]{0:T(1024)}, u32[]{:S(2)}) copy-start(f32[2048]{0:T(1024)} %param.39) | copy-start | bytes 24580
  188.8 20.9 %collective-permute-start.11 = (bf16[128,512]{1,0:T(8,128)(2,1)S(1)}, bf16[128,512]{1,0:T(8,128)(2,1)S(1)}, u32[]{:S(2)}, u32[]{:S(2)}) collective-permute-start(bf16[128,512]{1,0:T(8,128)(2,1)S(1)} %merge_attention.1.att), channel_id=1, source_target_pairs={{0,1},{1,0},{2,3},{3,2},{4,5},{5,4},{6,7},{7,6},{8,9},{9,8},{10,11... | collective-permute-start | bytes 393224 | tf_op jit(solution)/shard_map/ppermute | solution.py:507
  215.8 56.8 %all-to-all-start.1 = ((bf16[64,24,1024]{2,1,0:T(8,128)(2,1)}), bf16[64,24,1024]{2,1,0:T(8,128)(2,1)S(1)}, u32[]{:S(2)}, u32[]{:S(2)}) async-start(bf16[64,24,1024]{2,1,0:T(8,128)(2,1)} %bitcast.24), calls=%async_computation.1 | async-start | bytes 6291456 | tf_op jit(solution)/shard_map/all_to_all | solution.py:511
  287.3 46.9 %all-to-all-start.2 = ((bf16[128,24,512]{2,1,0:T(8,128)(2,1)}), bf16[128,24,512]{2,1,0:T(8,128)(2,1)S(1)}, u32[]{:S(2)}, u32[]{:S(2)}) async-start(bf16[128,24,512]{2,1,0:T(8,128)(2,1)} %bitcast.66), calls=%async_computation.2 | async-start | bytes 6291456 | tf_op jit(solution)/shard_map/all_to_all | solution.py:513
  (14 other events, 67.5 us)

commit v2 on v1

v2 whole, which is shorter than its diff:
```python
import math

import jax
import jax.numpy as jnp
import numpy as np
from jax import lax
from jax.experimental import pallas as pl
from jax.experimental.pallas import tpu as pltpu
from jax.sharding import PartitionSpec as P

HD = 128
TOP = 4
HEADS = 4
PAGE = 128
TOK = 128
CAP = 12
SLOTS = 6
ROWS = SLOTS * 16
STAT = HEADS * ROWS
BLOCK = STAT + 16
NORM_EPS = 1e-06
SCALE = 1.0 / math.sqrt(HD)
LOG2E = math.log2(math.e)
NEG = -1e30
F32 = jnp.float32
BF16 = jnp.bfloat16

NY, NZ, NX, NC = 4, 4, 2, 2
NREQ = NY * NZ * NX * NC
NCHIP = NY * NZ * NX


def req_index(y, z, x, c):
    return ((y * NZ + z) * NX + x) * NC + c


def all_coords():
    return [
        (y, z, x, c) for y in range(NY) for z in range(NZ) for x in range(NX) for c in range(NC)
    ]


def perm_x():
    return [(req_index(y, z, x, c), req_index(y, z, 1 - x, c)) for y, z, x, c in all_coords()]


def perm_core():
    return [(req_index(y, z, x, c), req_index(y, z, x, 1 - c)) for y, z, x, c in all_coords()]


def perm_ring(stage, step):
    pairs = []
    for y, z, x, c in all_coords():
        if (c + stage) % 2 == 0:
            to = req_index((y + step) % NY, z, x, c)
        else:
            to = req_index(y, (z + step) % NZ, x, c)
        pairs.append((req_index(y, z, x, c), to))
    return pairs


def chip_table():
    table = np.zeros((NREQ, NCHIP), np.int32)
    for y, z, x, c in all_coords():
        row = []
        for d1 in range(4):
            for d0 in range(4):
                for dx in range(2):
                    dy, dz = (d0, d1) if c == 0 else (d1, d0)
                    row.append(req_index((y - dy) % NY, (z - dz) % NZ, x ^ dx, 0) // NC)
        table[req_index(y, z, x, c)] = row
    return table


def core_groups():
    return [[chip * NC + core for chip in range(NCHIP)] for core in range(NC)]


def gather_blocks(block, weight):
    pair = jnp.stack([block, lax.ppermute(block, "req", perm_x())])
    pair, weight = lax.optimization_barrier((pair, weight))
    weight_far = lax.ppermute(weight, "tp", [(0, 1), (1, 0)])
    line = jnp.stack(
        [pair] + [lax.ppermute(pair, "req", perm_ring(0, step)) for step in (1, 2, 3)]
    ).reshape(8, *block.shape)
    return [line] + [
        lax.ppermute(line, "req", perm_ring(1, step)) for step in (1, 3, 2)
    ], weight_far


def attend(query, key_t, value_1, shift):
    scores = jnp.dot(query, key_t, preferred_element_type=F32)
    scores = shift(scores)
    top = jnp.max(scores, axis=1, keepdims=True)
    probs = jnp.exp2((scores - top) * (SCALE * LOG2E)).astype(BF16)
    both = jnp.dot(probs, value_1, preferred_element_type=F32)
    total = both[:, HD:]
    return both[:, :HD] / total, top * SCALE + jnp.log(total)


def by_head(rows):
    head = lax.broadcasted_iota(jnp.int32, (8, 128), 0) % HEADS
    tile = jnp.where(head == 0, rows[0], rows[1])
    tile = jnp.where(head == 2, rows[2], tile)
    return jnp.where(head == 3, rows[3], tile)


def keys_kernel(pages, out):
    for page in range(pages.shape[0]):
        for head in range(HEADS):
            out[page, head] = pages[page, 0, :, head * HD : (head + 1) * HD].T


def turn_keys(pages):
    count = pages.shape[0]
    return pl.pallas_call(
        keys_kernel,
        out_shape=jax.ShapeDtypeStruct((count, HEADS, HD, PAGE), BF16),
        in_specs=[vmem()],
        out_specs=vmem(),
        cost_estimate=pl.CostEstimate(
            flops=32 << 20, bytes_accessed=3 << 20, transcendentals=0
        ),
        compiler_params=pltpu.CompilerParams(vmem_limit_bytes=16 << 20),
        name="turn_keys",
    )(pages)


def page_kernel(chip_of, page_a, page_b, codes, blocks, keys_a, keys_b, pages_a, pages_b, *refs):
    out, held, sems = refs[-3:]
    row = lax.broadcasted_iota(jnp.int32, (16, 128), 0)
    offset = lax.broadcasted_iota(jnp.int32, (16, 128), 1) - row
    sub = lax.broadcasted_iota(jnp.int32, (8, 128), 0)
    ones = jnp.ones((PAGE, HD), BF16)

    def copy(i):
        return pltpu.make_async_copy(held.at[i], out.at[chip_of[i]], sems.at[i])

    def step(i, carry):
        pa, pb = page_a[i], page_b[i]
        code = [codes[i * SLOTS + j] for j in range(SLOTS)]
        first = [pl.multiple_of((c & 7) * 16, 16) for c in code]
        bias = jnp.concatenate(
            [
                jnp.concatenate(
                    [
                        jnp.full((16, PAGE), jnp.where((c & bit) != 0, 0.0, NEG), F32)
                        for bit in (8, 16)
                    ],
                    axis=1,
                )
                for c in code
            ],
            axis=0,
        )
        mine = [offset == jnp.where(c >= 8, (c & 7) * 16, -1024) for c in code]
        sums = []
        for head in range(HEADS):
            cols = slice(head * HD, (head + 1) * HD)
            query = jnp.concatenate(
                [blocks[i, pl.ds(first[j], 16), cols] for j in range(SLOTS)], axis=0
            )
            key_t = jnp.concatenate([keys_a[pa, head], keys_b[pb, head]], axis=1)
            value_1 = jnp.concatenate(
                [
                    jnp.concatenate([pages_a[pa, 1, :, cols], ones], axis=1),
                    jnp.concatenate([pages_b[pb, 1, :, cols], ones], axis=1),
                ],
                axis=0,
            )
            got, total = attend(query, key_t, value_1, lambda s: s + bias)
            held[i, head * ROWS : (head + 1) * ROWS, :] = got.astype(BF16)
            here = jnp.where(mine[0], total[:16], NEG)
            for j in range(1, SLOTS):
                here = jnp.maximum(here, jnp.where(mine[j], total[16 * j : 16 * j + 16], NEG))
            sums.append(jnp.max(here, axis=0, keepdims=True))
        tile = by_head(sums)
        high = tile.astype(BF16).astype(F32)
        rest = tile - high
        middle = rest.astype(BF16).astype(F32)
        upper = jnp.where(sub < HEADS, high, middle)
        lower = jnp.where(sub < HEADS, rest - middle, 0.0)
        held[i, STAT:BLOCK, :] = jnp.concatenate([upper, lower], axis=0).astype(BF16)
        copy(i).start()
        return carry

    count = blocks.shape[0]
    lax.fori_loop(0, count, step, 0, unroll=2)
    lax.fori_loop(0, count, lambda i, carry: (copy(i).wait(), carry)[1], 0)


def page_attention(chip_of, page_a, page_b, codes, blocks, keys_a, keys_b, pages_a, pages_b, last):
    count = blocks.shape[0]
    before = [] if last is None else [last]
    return pl.pallas_call(
        page_kernel,
        out_shape=jax.ShapeDtypeStruct((NCHIP, BLOCK, HD), BF16),
        in_specs=[smem()] * 4
        + [vmem()] * 5
        + [pl.BlockSpec(memory_space=pl.ANY)] * len(before),
        out_specs=pl.BlockSpec(memory_space=pl.ANY),
        input_output_aliases={9: 0} if before else {},
        scratch_shapes=[
            pltpu.VMEM((count, BLOCK, HD), BF16),
            pltpu.SemaphoreType.DMA((count,)),
        ],
        compiler_params=pltpu.CompilerParams(vmem_limit_bytes=24 << 20),
        cost_estimate=pl.CostEstimate(
            flops=count * HEADS * 12 * ROWS * HD * HD * 8,
            bytes_accessed=6 << 20,
            transcendentals=count * HEADS * ROWS * 2 * PAGE,
        ),
        name="page_attention",
    )(chip_of, page_a, page_b, codes, blocks, keys_a, keys_b, pages_a, pages_b, *before)


def smem():
    return pl.BlockSpec(memory_space=pltpu.SMEM)


def vmem():
    return pl.BlockSpec(memory_space=pltpu.VMEM)


def own_kernel(request_col, request_row, queries, keys, values, out, total):
    token = lax.broadcasted_iota(jnp.int32, (TOK, TOK), 0)
    key = lax.broadcasted_iota(jnp.int32, (TOK, TOK), 1)
    mask = (request_col[...] == request_row[...]) & (key <= token)
    ones = jnp.ones((TOK, HD), BF16)
    sums = []
    for head in range(HEADS):
        cols = slice(head * HD, (head + 1) * HD)
        got, low = attend(
            queries[:, cols],
            keys[:, cols].T,
            jnp.concatenate([values[:, cols], ones], axis=1),
            lambda s: jnp.where(mask, s, NEG),
        )
        out[head] = got
        sums.append(jnp.max(jnp.where(token == key, low, NEG), axis=0, keepdims=True))
    total[...] = by_head(sums)


def own_attention(request_ids, queries, keys, values):
    return pl.pallas_call(
        own_kernel,
        out_shape=(
            jax.ShapeDtypeStruct((HEADS, TOK, HD), F32),
            jax.ShapeDtypeStruct((8, TOK), F32),
        ),
        in_specs=[vmem()] * 5,
        out_specs=(vmem(), vmem()),
        compiler_params=pltpu.CompilerParams(vmem_limit_bytes=16 << 20),
        cost_estimate=pl.CostEstimate(
            flops=64 << 20, bytes_accessed=1 << 20, transcendentals=HEADS * TOK * TOK
        ),
        name="own_attention",
    )(request_ids[:, None], request_ids[None, :], queries, keys, values)


def merge_kernel(codes, arrived, own, own_sums, out, acc, tiles):
    row = lax.broadcasted_iota(jnp.int32, (16, TOK), 0)
    offset = lax.broadcasted_iota(jnp.int32, (16, TOK), 1) - row
    ones = jnp.ones((2 * TOK, HD), BF16)

    def halves(tile):
        high = tile.astype(BF16).astype(F32)
        return high, tile - high

    def on_rows(parts, masks):
        blocks = []
        for head in range(HEADS):
            for mask in masks:
                blocks.append(
                    jnp.concatenate(
                        [
                            jnp.where(mask, jnp.broadcast_to(p[head : head + 1], (16, TOK)), 0.0)
                            for p in parts
                        ],
                        axis=1,
                    )
                )
        picked = jnp.concatenate(blocks, axis=0).astype(BF16)
        return jnp.dot(picked, ones, preferred_element_type=F32)

    def collect(p, top):
        tile = arrived[p, STAT:BLOCK, :].astype(F32)
        tile = (tile[:8] + pltpu.roll(tile[:8], HEADS, 0)) + tile[8:]
        tiles[p] = tile
        return jnp.maximum(top, tile)

    top = lax.fori_loop(0, NCHIP, collect, own_sums[...], unroll=4)
    whole = [offset == 16 * g for g in range(TOK // 16)]
    share = jnp.exp(own_sums[...] - top)
    acc[...] = own[...] * on_rows(halves(share), whole).reshape(HEADS, TOK, HD)

    def add(p, low):
        share = jnp.exp(tiles[p] - top)
        code = [codes[p * SLOTS + j] for j in range(SLOTS)]
        masks = [offset == jnp.where(c >= 8, (c & 7) * 16, -1024) for c in code]
        factor = on_rows(halves(share), masks)
        for j in range(SLOTS):
            at = pl.ds(pl.multiple_of((code[j] & 7) * 16, 16), 16)
            for head in range(HEADS):
                start = head * ROWS + 16 * j
                part = arrived[p, start : start + 16, :].astype(F32)
                acc[head, at, :] += part * factor[start : start + 16]
        return low + share

    low = lax.fori_loop(0, NCHIP, add, share)
    factor = on_rows(halves(1.0 / low), whole)
    for head in range(HEADS):
        out[:, head * HD : (head + 1) * HD] = (
            acc[head] * factor[head * TOK : (head + 1) * TOK]
        ).astype(BF16)


def merge_attention(codes, arrived, own, own_sums):
    return pl.pallas_call(
        merge_kernel,
        out_shape=jax.ShapeDtypeStruct((TOK, HEADS * HD), BF16),
        in_specs=[smem()] + [vmem()] * 3,
        out_specs=vmem(),
        scratch_shapes=[
            pltpu.VMEM((HEADS, TOK, HD), F32),
            pltpu.VMEM((NCHIP, 8, TOK), F32),
        ],
        compiler_params=pltpu.CompilerParams(vmem_limit_bytes=24 << 20),
        cost_estimate=pl.CostEstimate(
            flops=64 << 20, bytes_accessed=4 << 20, transcendentals=1 << 18
        ),
        name="merge_attention",
    )(codes, arrived, own, own_sums)


def project_kernel(att, att_far, weight, weight_far, residual, gain, picks, mixed, sent, both):
    half = residual.shape[1] // 2
    total = residual[...].astype(F32)
    total += jnp.dot(att[...], weight[...], preferred_element_type=F32)
    total += jnp.dot(att_far[...], weight_far[...], preferred_element_type=F32)
    mixed[...] = total
    scale = lax.rsqrt(jnp.mean(total * total, axis=1, keepdims=True) + NORM_EPS)
    normed = (total * scale * gain[...]).astype(BF16)
    both[:TOK] = normed[:, :half]
    both[TOK:] = normed[:, half:]
    step = 256
    for row in range(0, sent.shape[0], step):
        sent[row : row + step] = jnp.dot(
            picks[row : row + step], both[...], preferred_element_type=F32
        ).astype(BF16)


def project(att, att_far, weight, weight_far, residual, gain, picks):
    width = residual.shape[1]
    return pl.pallas_call(
        project_kernel,
        out_shape=(
            jax.ShapeDtypeStruct((TOK, width), F32),
            jax.ShapeDtypeStruct((picks.shape[0], width // 2), BF16),
        ),
        in_specs=[vmem()] * 7,
        out_specs=(vmem(), vmem()),
        scratch_shapes=[pltpu.VMEM((2 * TOK, width // 2), BF16)],
        compiler_params=pltpu.CompilerParams(vmem_limit_bytes=32 << 20),
        cost_estimate=pl.CostEstimate(
            flops=4 * TOK * 512 * width + 2 * picks.shape[0] * 256 * width // 2,
            bytes_accessed=10 << 20,
            transcendentals=TOK,
        ),
        name="project_dispatch",
    )(att, att_far, weight, weight_far, residual, gain, picks)


def expert_kernel(rows, gate, up, down, out):
    count = rows.shape[0]
    width = gate.shape[0]
    half, quarter = width // 2, width // 4
    wide = rows[...].astype(F32)
    upper = lax.broadcasted_iota(jnp.int32, (count // 2, 8, half), 1) < 4
    tail = wide[:, 16:24].reshape(count // 2, 2, 8, half)
    even, odd = tail[:, 0], tail[:, 1]
    tail_0 = jnp.where(upper, even, pltpu.roll(odd, 4, 1))
    tail_1 = jnp.where(upper, pltpu.roll(even, 4, 1), odd)
    left = jnp.concatenate(
        [wide[:, 0:8].reshape(count * 8, half), tail_0.reshape(count * 4, half)], axis=0
    )
    right = jnp.concatenate(
        [wide[:, 8:16].reshape(count * 8, half), tail_1.reshape(count * 4, half)], axis=0
    )
    tokens = jnp.concatenate([left.astype(BF16), right.astype(BF16)], axis=1)
    gate_act = jnp.dot(tokens, gate[...], preferred_element_type=F32)
    up_act = jnp.dot(tokens, up[...], preferred_element_type=F32)
    hidden = (gate_act / (1.0 + jnp.exp(-gate_act)) * up_act).astype(BF16)
    result = jnp.dot(hidden, down[...], preferred_element_type=F32)
    upper = lax.broadcasted_iota(jnp.int32, (count // 2, 8, quarter), 1) < 4
    for side in range(2):
        cols = [slice((2 * side + q) * quarter, (2 * side + q + 1) * quarter) for q in range(2)]
        main = [result[: count * 8, c].reshape(count, 8, quarter) for c in cols]
        tail = [result[count * 8 :, c].reshape(count // 2, 8, quarter) for c in cols]
        even = jnp.where(upper, tail[0], pltpu.roll(tail[1], 4, 1))
        odd = jnp.where(upper, pltpu.roll(tail[0], 4, 1), tail[1])
        last = jnp.stack([even, odd], axis=1).reshape(count, 8, quarter)
        out[:, side] = jnp.concatenate(main + [last], axis=1).astype(BF16)


def run_expert(rows, gate, up, down, steps=2):
    count = rows.shape[0] // steps
    width, hidden = gate.shape
    once = pl.Buffered(1)
    return pl.pallas_call(
        expert_kernel,
        grid=(steps,),
        out_shape=jax.ShapeDtypeStruct((rows.shape[0], 2, 2 * CAP, width // 4), BF16),
        in_specs=[
            pl.BlockSpec((count, 2 * CAP, width // 2), lambda i: (i, 0, 0)),
            pl.BlockSpec((width, hidden), lambda i: (0, 0), pipeline_mode=once),
            pl.BlockSpec((width, hidden), lambda i: (0, 0), pipeline_mode=once),
            pl.BlockSpec((hidden, width), lambda i: (0, 0), pipeline_mode=once),
        ],
        out_specs=pl.BlockSpec((count, 2, 2 * CAP, width // 4), lambda i: (i, 0, 0, 0)),
        compiler_params=pltpu.CompilerParams(vmem_limit_bytes=56 << 20),
        cost_estimate=pl.CostEstimate(
            flops=6 * rows.shape[0] * CAP * width * hidden,
            bytes_accessed=15 << 20,
            transcendentals=rows.shape[0] * CAP * hidden,
        ),
        name="expert",
    )(rows, gate, up, down)


def combine_kernel(mixed, shares, shares_low, rows, out):
    total = jnp.dot(shares[...], rows[...], preferred_element_type=F32)
    total += jnp.dot(shares_low[...], rows[...], preferred_element_type=F32)
    width = rows.shape[1]
    out[:, :width] = (mixed[:, :width] + total[:TOK]).astype(BF16)
    out[:, width:] = (mixed[:, width:] + total[TOK:]).astype(BF16)


def combine(mixed, shares, shares_low, rows):
    return pl.pallas_call(
        combine_kernel,
        out_shape=jax.ShapeDtypeStruct(mixed.shape, BF16),
        in_specs=[vmem()] * 4,
        out_specs=vmem(),
        compiler_params=pltpu.CompilerParams(vmem_limit_bytes=32 << 20),
        cost_estimate=pl.CostEstimate(
            flops=4 * shares.shape[0] * rows.shape[0] * rows.shape[1],
            bytes_accessed=8 << 20,
            transcendentals=0,
        ),
        name="combine",
    )(mixed, shares, shares_low, rows)


def slot_rows():
    slot = np.array(list(range(8)) * 2 + list(range(8, 12)) * 2, np.int32)
    part = np.array([0] * 8 + [1] * 8 + [0] * 4 + [1] * 4, np.int32)
    return slot, part


def routing(expert_ids, expert_weights):
    flat = expert_ids.reshape(-1)
    count = flat.shape[0]
    onehot = (flat[:, None] == jnp.arange(NREQ, dtype=jnp.int32)[None, :]).astype(BF16)
    earlier = (
        jnp.arange(count, dtype=jnp.int32)[None, :] < jnp.arange(count, dtype=jnp.int32)[:, None]
    ).astype(BF16)
    before = jnp.dot(earlier, onehot, preferred_element_type=F32)
    slot = jnp.sum(before * onehot.astype(F32), axis=1).astype(jnp.int32)
    place = (flat * CAP + slot).reshape(TOK, TOP)

    slot_at, part_at = slot_rows()
    row_place = (np.arange(NREQ, dtype=np.int32)[:, None] * CAP + slot_at[None, :]).reshape(-1)
    row_part = np.tile(part_at, NREQ)
    col_place = jnp.concatenate([place, place], axis=0)
    col_part = np.repeat(np.arange(2, dtype=np.int32), TOK)
    hit = jnp.zeros((row_place.shape[0], 2 * TOK), jnp.bool_)
    for k in range(TOP):
        hit = hit | (col_place[None, :, k] == row_place[:, None])
    picks = (hit & (row_part[:, None] == col_part[None, :])).astype(BF16)

    back_place = np.repeat(row_place.reshape(NREQ, 1, -1), 2, axis=1).reshape(-1)
    back_part = np.tile(part_at, 2 * NREQ)
    col_weight = jnp.concatenate([expert_weights, expert_weights], axis=0)
    shares = jnp.zeros((2 * TOK, back_place.shape[0]), F32)
    for k in range(TOP):
        shares = shares + jnp.where(
            col_place[:, k, None] == back_place[None, :], col_weight[:, k, None], 0.0
        )
    shares = jnp.where(back_part[None, :] == col_part[:, None], shares, 0.0)
    high = lax.reduce_precision(shares, 8, 7)
    return picks, high.astype(BF16), (shares - high).astype(BF16)


def shards(
    residual,
    queries,
    new_keys,
    new_values,
    request_ids,
    page_store,
    page_sends,
    page_users,
    expert_ids,
    expert_weights,
    output_weight,
    norm_gain,
    gate_weight,
    up_weight,
    down_weight,
):
    me = lax.axis_index("req")
    tp_index = lax.axis_index("tp")
    width = residual.shape[1]
    half = width // 2
    swap = [(0, 1), (1, 0)]

    core = me % NC
    users = page_users[0].reshape(NCHIP, NC)
    user_a = jnp.where(core == 0, users[:, 0], users[:, 1])[:, None]
    user_b = jnp.where(core == 0, users[:, 1], users[:, 0])[:, None]
    group = jnp.arange(TOK // 16, dtype=jnp.int32)
    group_user = request_ids.reshape(TOK // 16, 16)[:, 0][None, :]
    hit_a, hit_b = group_user == user_a, group_user == user_b
    needed = (hit_a | hit_b).astype(jnp.int32)
    rank = jnp.sum(needed[:, None, :] * (group[None, :] < group[:, None]), axis=2)
    value = needed * (group[None, :] + 8 * hit_a + 16 * hit_b)
    slot = jnp.arange(SLOTS, dtype=jnp.int32)
    codes = jnp.sum(jnp.where(rank[:, None, :] == slot[None, :, None], value[:, None, :], 0), 2)

    note = jnp.zeros((8, queries.shape[1]), BF16)
    note = note.at[0, : NCHIP * SLOTS].set(codes.T.reshape(-1).astype(BF16))
    pieces, weight_far = gather_blocks(
        jnp.concatenate([queries, note], axis=0), output_weight
    )
    pages_far = lax.ppermute(page_store, "req", perm_core())
    sends_far = lax.ppermute(page_sends, "req", perm_core())
    keys_a, keys_b = turn_keys(page_store), turn_keys(pages_far)
    own, own_sums = own_attention(request_ids, queries, new_keys, new_values)

    table = chip_table()
    order = np.array([0, 1, 3, 2])
    chips = lax.dynamic_index_in_dim(
        jnp.asarray(table.reshape(NREQ, 4, 8)[:, order].reshape(NREQ, NCHIP)), me, 0, keepdims=False
    )
    page_a = page_sends[0][chips * NC + core]
    page_b = sends_far[0][chips * NC + core]
    parts = None
    for index, piece in enumerate(pieces):
        if index == 3:
            piece, weight_far = lax.optimization_barrier((piece, weight_far))
        asked = piece[:, TOK, : NCHIP * SLOTS].reshape(8, SLOTS, NCHIP)
        asked = lax.dynamic_index_in_dim(asked, me // NC, 2, keepdims=False)
        rows = slice(8 * index, 8 * index + 8)
        parts = page_attention(
            chips[rows],
            page_a[rows],
            page_b[rows],
            asked.astype(jnp.int32).reshape(-1),
            piece,
            keys_a,
            keys_b,
            page_store,
            pages_far,
            parts,
        )
    arrived = lax.all_to_all(
        parts, "req", 0, 0, tiled=True, axis_index_groups=core_groups()
    )
    attended = merge_attention(codes.reshape(-1), arrived, own, own_sums)
    picks, shares, shares_low = routing(expert_ids, expert_weights)
    attended_far = lax.ppermute(attended, "tp", swap)
    mixed, sent = project(
        attended, attended_far, output_weight, weight_far, residual, norm_gain[None, :], picks
    )
    rows = lax.all_to_all(sent.reshape(NREQ, 2 * CAP, half), "req", 0, 0, tiled=True)
    result = run_expert(rows, gate_weight[0], up_weight[0], down_weight[0])
    returned = lax.all_to_all(
        result.reshape(2 * NREQ, 2 * CAP, width // 4), ("req", "tp"), 0, 0, tiled=True
    )
    mixed_half = lax.dynamic_slice_in_dim(mixed, tp_index * half, half, 1)
    return combine(mixed_half, shares, shares_low, returned.reshape(-1, width // 4))


def solution(mesh):
    placed = (
        P("req", None),
        P("req", "tp"),
        P("req", "tp"),
        P("req", "tp"),
        P("req"),
        P("req", None, None, "tp"),
        P("req", None),
        P("req", None),
        P("req", None),
        P("req", None),
        P("tp", None),
        P(),
        P("req", None, "tp"),
        P("req", None, "tp"),
        P("req", "tp", None),
    )
    return jax.shard_map(
        shards, mesh=mesh, in_specs=placed, out_specs=P("req", "tp"), check_vma=False
    )
```

time: 341 us -> 295 us (0.87)
  waiting for transfers between devices: 181 us -> 125 us
  local copies, waits for them, and re-layouts: 20.9 us -> 38.1 us
  Pallas kernels: 73.3 us -> 66.5 us
    all_to_all x1, waiting for transfers between devices: 65.9 us -> 33.9 us  [shards(): lax.all_to_all(parts, 'req', 0, 0, tiled=True, axis_index_groups=core_gro...]
    ppermute x3, waiting for transfers between devices: 15.6 us -> 2.44 us  [gather_blocks(): lax.ppermute(line, 'req', perm_ring(1, step))]
    unnamed x55 -> x69, local copies, waits for them, and re-layouts: 16.8 us -> 28 us
    ppermute x5 -> x3, waiting for transfers between devices: 17.9 us -> 7.43 us  [the longest x1 7.43 us: gather_blocks(): weight_far = lax.ppermute(weight, 'tp', [(0, 1), (1, 0)])]
    pallas_call x1, Pallas kernels: 18.6 us -> 8.34 us  [merge_attention(): pl.pallas_call(merge_kernel, out_shape=jax.ShapeDtypeStruct((TOK, HEADS *...]
    all_to_all x1, starting transfers between devices: 14.6 us -> 9.5 us  [shards(): lax.all_to_all(sent.reshape(NREQ, 2 * CAP, half), 'req', 0, 0, tiled=True)]
    ppermute x5 -> x3, starting transfers between devices: 10.2 us -> 5.29 us  [the longest x1 2.65 us: shards(): sends_far = lax.ppermute(page_sends, 'req', perm_core())]
    ppermute x1, starting transfers between devices: 2.06 us -> 6.11 us  [shards(): attended_far = lax.ppermute(attended, 'tp', swap)]
  transfers between devices with their start and end apart: 16 -> 14, of which waited for: 12 -> 9; matrix products, arithmetic and copies ran while one was open for 6% -> 10% of each run, Pallas kernels for 5% -> 10%
where the time goes in v2:
time: 295 us; the launch traced here: 294 us
  waiting for transfers between devices  125 us (42%)
  Pallas kernels  66.5 us (23%)
  starting transfers between devices  53.2 us (18%)
  local copies, waits for them, and re-layouts  38.1 us (13%)
  other arithmetic  10.8 us (4%)
    all_to_all x1, waiting for transfers between devices, shards(): lax.all_to_all(result.reshape(2 * NREQ, 2 * CAP, width // 4), ('req', 'tp...  36.1 us
    pallas_call x4, Pallas kernels, page_attention(): pl.pallas_call(page_kernel, out_shape=jax.ShapeDtypeStruct((NCHIP, BLOCK,...  34.1 us
    all_to_all x1, waiting for transfers between devices, shards(): lax.all_to_all(parts, 'req', 0, 0, tiled=True, axis_index_groups=core_gro...  33.9 us
    all_to_all x1, waiting for transfers between devices, shards(): lax.all_to_all(sent.reshape(NREQ, 2 * CAP, half), 'req', 0, 0, tiled=True)  32.9 us
    unnamed x69, local copies, waits for them, and re-layouts  28 us
    pallas_call x1, Pallas kernels, run_expert(): pl.pallas_call(expert_kernel, grid=(steps,), out_shape=jax.ShapeDtypeStru...  13 us
    all_to_all x1, starting transfers between devices, shards(): lax.all_to_all(parts, 'req', 0, 0, tiled=True, axis_index_groups=core_gro...  12.4 us
    all_to_all x1, starting transfers between devices, shards(): lax.all_to_all(sent.reshape(NREQ, 2 * CAP, half), 'req', 0, 0, tiled=True)  9.5 us
  transfers between devices with their start and end apart: 14, of which 9 were waited for; matrix products, arithmetic and copies ran while one was open for 10% of the time, Pallas kernels for 10%

profile of v2, /device:TPU:1, one launch (start us, length us, event | category | flops | bytes accessed | tf_op | source)
XLA Modules:
  0.0 294.0 jit_solution(16439350078712052074)
XLA Ops:
  5.7 2.9 collective-permute-start.1
  8.6 3.9 %collective-permute-done.1 = bf16[136,512]{1,0:T(8,128)(2,1)S(1)} collective-permute-done((bf16[136,512]{1,0:T(8,128)(2,1)S(1)}, bf16[136,512]{1,0:T(8,128)(2,1)S(1)}, u32[]{:S(2)}, u32[]{:S(2)}) %collective-permute-start.1) | collective-permute-done | bytes 139296 | tf_op jit(solution)/shard_map/ppermute | solution.py:80
  12.6 3.7 %collective-permute-start.3 = (bf16[2,136,512]{2,1,0:T(8,128)(2,1)S(1)}, bf16[2,136,512]{2,1,0:T(8,128)(2,1)S(1)}, u32[]{:S(2)}, u32[]{:S(2)}) collective-permute-start(bf16[2,136,512]{2,1,0:T(8,128)(2,1)S(1)} %pad_maximum_fusion.1), channel_id=1, source_target_pairs={{0,64},{2,18},{4,68},{6,22},{8,72},{10,26},{12,76},{14,30},{16,80}... | collective-permute-start | bytes 835592 | tf_op jit(solution)/shard_map/ppermute | solution.py:84
  17.8 2.8 collective-permute-done.3
  20.5 3.8 %collective-permute-done.4 = bf16[2,136,512]{2,1,0:T(8,128)(2,1)S(1)} collective-permute-done((bf16[2,136,512]{2,1,0:T(8,128)(2,1)S(1)}, bf16[2,136,512]{2,1,0:T(8,128)(2,1)S(1)}, u32[]{:S(2)}, u32[]{:S(2)}) %collective-permute-start.4) | collective-permute-done | bytes 278560 | tf_op jit(solution)/shard_map/ppermute | solution.py:84
  28.1 2.6 collective-permute-start
  46.1 8.6 %page_attention.4.refs_0_ = bf16[32,400,128]{2,1,0:T(8,128)(2,1)S(1)} custom-call(s32[8]{0:T(128)S(1)} %get-tuple-element.55.chip_of, s32[8]{0:T(128)S(1)} %get-tuple-element.64.page_a, s32[8]{0:T(128)S(1)} %get-tuple-element.47.page_b, s32[48]{0:T(128)S(1)} %reshape.248.codes, bf16[8,136,512]{2,1,0:T(8,128)(2,1)} %bitcast.12.blocks, ...), custom_call_target="tpu_custom_call" | custom-call | flops 4831838208 | bytes 6291456 | tf_op jit(solution)/shard_map/page_attention/pallas_call | solution.py:195
  54.7 8.7 %page_attention.5.refs_0_ = bf16[32,400,128]{2,1,0:T(8,128)(2,1)S(1)} custom-call(s32[8]{0:T(128)S(1)} %get-tuple-element.56.chip_of, s32[8]{0:T(128)S(1)} %get-tuple-element.63.page_a, s32[8]{0:T(128)S(1)} %get-tuple-element.48.page_b, s32[48]{0:T(128)S(1)} %reshape.247.codes, ...), custom_call_target="tpu_custom_call", output_to_operand_aliasing={{}: (9, {})} | custom-call | flops 4831838208 | bytes 6291456 | tf_op jit(solution)/shard_map/page_attention/pallas_call | solution.py:195
  63.4 8.3 %page_attention.6.refs_0_ = bf16[32,400,128]{2,1,0:T(8,128)(2,1)S(1)} custom-call(s32[8]{0:T(128)S(1)} %get-tuple-element.57.chip_of, s32[8]{0:T(128)S(1)} %get-tuple-element.62.page_a, s32[8]{0:T(128)S(1)} %get-tuple-element.49.page_b, s32[48]{0:T(128)S(1)} %reshape.246.codes, bf16[8,136,512]{2,1,0:T(8,128)(2,1)S(1)} %copy-done.24, ...), custom_call_target="tpu_custom_call", output_to_operand_aliasing={{}: (9, {})} | custom-call | flops 4831838208 | bytes 6291456 | tf_op jit(solution)/shard_map/page_attention/pallas_call | solution.py:195
  71.7 7.4 %collective-permute-done.6.weight_far = bf16[512,2048]{1,0:T(8,128)(2,1)} collective-permute-done((bf16[512,2048]{1,0:T(8,128)(2,1)}, bf16[512,2048]{1,0:T(8,128)(2,1)}, u32[]{:S(2)}, u32[]{:S(2)}) %collective-permute-start.6) | collective-permute-done | bytes 2097184 | tf_op jit(solution)/shard_map/ppermute | solution.py:82
  84.4 8.6 %page_attention.7 = bf16[32,400,128]{2,1,0:T(8,128)(2,1)S(1)} custom-call(s32[8]{0:T(128)S(1)} %get-tuple-element.58.chip_of, s32[8]{0:T(128)S(1)} %get-tuple-element.61.page_a, s32[8]{0:T(128)S(1)} %get-tuple-element.50.page_b, s32[48]{0:T(128)S(1)} %reshape.245.codes, ...), custom_call_target="tpu_custom_call", output_to_operand_aliasing={{}: (9, {})} | custom-call | flops 4831838208 | bytes 6291456 | tf_op jit(solution)/shard_map/page_attention/pallas_call | solution.py:195
  94.7 12.4 %all-to-all-start = ((bf16[32,400,128]{2,1,0:T(8,128)(2,1)}), bf16[32,400,128]{2,1,0:T(8,128)(2,1)S(1)}, u32[]{:S(2)}, u32[]{:S(2)}) async-start(bf16[32,400,128]{2,1,0:T(8,128)(2,1)} %copy-done.2), calls=%async_computation | async-start | bytes 6553600 | tf_op jit(solution)/shard_map/all_to_all | solution.py:567
  114.7 33.9 %all-to-all-done.arrived = bf16[32,400,128]{2,1,0:T(8,128)(2,1)S(1)} async-done(((bf16[32,400,128]{2,1,0:T(8,128)(2,1)}), bf16[32,400,128]{2,1,0:T(8,128)(2,1)S(1)}, u32[]{:S(2)}, u32[]{:S(2)}) %all-to-all-start) | async-done | bytes 3276832 | tf_op jit(solution)/shard_map/all_to_all | solution.py:567
  149.8 8.3 %merge_attention.1.att = bf16[128,512]{1,0:T(8,128)(2,1)S(1)} custom-call(s32[192]{0:T(256)S(1)} %reshape.240.codes, bf16[32,400,128]{2,1,0:T(8,128)(2,1)S(1)} %all-to-all-done.arrived, f32[4,128,128]{2,1,0:T(8,128)S(1)} %copy-done.16, f32[8,128]{1,0:T(8,128)S(1)} %get-tuple-element.29.own_sums), custom_call_target="tpu_custom_call" | custom-call | flops 67108864 | bytes 4194304 | tf_op jit(solution)/shard_map/merge_attention/pallas_call | solution.py:319
  158.1 6.1 %collective-permute-start.10 = (bf16[128,512]{1,0:T(8,128)(2,1)S(1)}, bf16[128,512]{1,0:T(8,128)(2,1)S(1)}, u32[]{:S(2)}, u32[]{:S(2)}) collective-permute-start(bf16[128,512]{1,0:T(8,128)(2,1)S(1)} %merge_attention.1.att), channel_id=1, source_target_pairs={{0,1},{1,0},{2,3},{3,2},{4,5},{5,4},{6,7},{7,6},{8,9},{9,8},{10,11... | collective-permute-start | bytes 393224 | tf_op jit(solution)/shard_map/ppermute | solution.py:572
  166.6 5.0 %project_dispatch.1 = (f32[128,2048]{1,0:T(8,128)S(1)}, bf16[1536,1024]{1,0:T(8,128)(2,1)}) custom-call(bf16[128,512]{1,0:T(8,128)(2,1)S(1)} %merge_attention.1.att, bf16[128,512]{1,0:T(8,128)(2,1)S(1)} %collective-permute-done.10.att_far, bf16[512,2048]{1,0:T(8,128)(2,1)S(1)} %copy-done.7, bf16[512,2048]{1,0:T(8,128)(2,1)} %collective-permute-done.6.weight_far, ...), custom_call_target="tpu_custom_call" | custom-call | flops 1342177280 | bytes 10485760 | tf_op jit(solution)/shard_map/project_dispatch/pallas_call | solution.py:355
  172.7 9.5 %all-to-all-start.1 = ((bf16[64,24,1024]{2,1,0:T(8,128)(2,1)}), bf16[64,24,1024]{2,1,0:T(8,128)(2,1)S(1)}, u32[]{:S(2)}, u32[]{:S(2)}) async-start(bf16[64,24,1024]{2,1,0:T(8,128)(2,1)} %bitcast.27), calls=%async_computation.1 | async-start | bytes 6291456 | tf_op jit(solution)/shard_map/all_to_all | solution.py:576
  182.2 4.6 %copy.73 = bf16[1,2048,704]{2,1,0:T(8,128)(2,1)} copy(bf16[1,2048,704]{1,2,0:T(8,128)(2,1)} %param.40) | data formatting | bytes 5767168 | tf_op args[12]
  186.8 4.7 %copy.74 = bf16[1,2048,704]{2,1,0:T(8,128)(2,1)} copy(bf16[1,2048,704]{1,2,0:T(8,128)(2,1)} %param.41) | data formatting | bytes 5767168 | tf_op args[13]
  191.5 32.9 %all-to-all-done.1.rows = bf16[64,24,1024]{2,1,0:T(8,128)(2,1)S(1)} async-done(((bf16[64,24,1024]{2,1,0:T(8,128)(2,1)}), bf16[64,24,1024]{2,1,0:T(8,128)(2,1)S(1)}, u32[]{:S(2)}, u32[]{:S(2)}) %all-to-all-start.1) | async-done | bytes 3145760 | tf_op jit(solution)/shard_map/all_to_all | solution.py:576
  226.1 13.0 %expert.1 = bf16[64,2,24,512]{3,2,1,0:T(8,128)(2,1)} custom-call(bf16[64,24,1024]{2,1,0:T(8,128)(2,1)} %copy-done.26, bf16[2048,704]{1,0:T(8,128)(2,1)} %bitcast.48, bf16[2048,704]{1,0:T(8,128)(2,1)} %bitcast.49, bf16[704,2048]{1,0:T(8,128)(2,1)} %bitcast.67), custom_call_target="tpu_custom_call" | custom-call | flops 6643777536 | bytes 15728640 | tf_op jit(solution)/shard_map/expert/pallas_call | solution.py:410
  239.0 7.1 %all-to-all-start.2 = ((bf16[128,24,512]{2,1,0:T(8,128)(2,1)}), bf16[128,24,512]{2,1,0:T(8,128)(2,1)S(1)}, u32[]{:S(2)}, u32[]{:S(2)}) async-start(bf16[128,24,512]{2,1,0:T(8,128)(2,1)} %bitcast.47), calls=%async_computation.2 | async-start | bytes 6291456 | tf_op jit(solution)/shard_map/all_to_all | solution.py:578
  246.2 4.5 %fusion = (bf16[256,3072]{1,0:T(8,128)(2,1)}, bf16[256,3072]{1,0:T(8,128)(2,1)}) fusion(pred[256,3072]{1,0:T(32,128)(4,1)} %constant.114.clone, f32[256]{0:T(256)S(1)} %bitcast.64, f32[256]{0:T(256)S(1)} %bitcast.65, f32[256]{0:T(256)S(1)} %bitcast.66, f32[256]{0:T(256)S(1)} %bitcast.63, s32[3072]{0:T(1024)S(1)} %copy-done.28, s32[256]{0:T(256)S(1)} %bitcast.58, ...), kind=kLoop, calls=%fused_computation.4 | loop fusion | flops 12582912 | bytes 3952640 | tf_op jit(solution)/shard_map/convert_element_type | solution.py:492
  251.6 36.1 %all-to-all-done.2 = bf16[128,24,512]{2,1,0:T(8,128)(2,1)S(1)} async-done(((bf16[128,24,512]{2,1,0:T(8,128)(2,1)}), bf16[128,24,512]{2,1,0:T(8,128)(2,1)S(1)}, u32[]{:S(2)}, u32[]{:S(2)}) %all-to-all-start.2) | async-done | bytes 3145760 | tf_op jit(solution)/shard_map/all_to_all | solution.py:578
  (136 shorter events, 54.1 us)
Async XLA Ops:
  0.0 33.5 %copy-start.3 = (bf16[8,2,128,512]{3,2,1,0:T(8,128)(2,1)S(1)}, bf16[8,2,128,512]{3,2,1,0:T(8,128)(2,1)}, u32[]{:S(2)}) copy-start(bf16[8,2,128,512]{3,2,1,0:T(8,128)(2,1)} %pages_a.7) | copy-start | bytes 6291460
  0.0 28.1 %copy-start.25 = (s32[1,64]{1,0:T(1,128)S(1)}, s32[1,64]{1,0:T(1,128)}, u32[]{:S(2)}) copy-start(s32[1,64]{1,0:T(1,128)} %param.34) | copy-start | bytes 772
  0.0 43.6 %collective-permute-start.7 = (bf16[8,2,128,512]{3,2,1,0:T(8,128)(2,1)}, bf16[8,2,128,512]{3,2,1,0:T(8,128)(2,1)}, u32[]{:S(2)}, u32[]{:S(2)}) collective-permute-start(bf16[8,2,128,512]{3,2,1,0:T(8,128)(2,1)} %pages_a.7), channel_id=1, source_target_pairs={{0,2},{2,0},{4,6},{6,4},{8,10},{10,8},{12,14},{14,12},{16,18},{18,... | collective-permute-start | bytes 6291464 | tf_op jit(solution)/shard_map/ppermute | solution.py:536
  5.7 6.8 %collective-permute-start.1 = (bf16[136,512]{1,0:T(8,128)(2,1)S(1)}, bf16[136,512]{1,0:T(8,128)(2,1)S(1)}, u32[]{:S(2)}, u32[]{:S(2)}) collective-permute-start(bf16[136,512]{1,0:T(8,128)(2,1)S(1)} %get-tuple-element.38), channel_id=1, source_target_pairs={{0,4},{2,6},{4,0},{6,2},{8,12},{10,14},{12,8},{14,10},{16,20},{18,... | collective-permute-start | bytes 417800 | tf_op jit(solution)/shard_map/ppermute | solution.py:80
  12.6 8.0 %collective-permute-start.3 = (bf16[2,136,512]{2,1,0:T(8,128)(2,1)S(1)}, bf16[2,136,512]{2,1,0:T(8,128)(2,1)S(1)}, u32[]{:S(2)}, u32[]{:S(2)}) collective-permute-start(bf16[2,136,512]{2,1,0:T(8,128)(2,1)S(1)} %pad_maximum_fusion.1), channel_id=1, source_target_pairs={{0,64},{2,18},{4,68},{6,22},{8,72},{10,26},{12,76},{14,30},{16,80}... | collective-permute-start | bytes 835592 | tf_op jit(solution)/shard_map/ppermute | solution.py:84
  16.3 8.0 %collective-permute-start.4 = (bf16[2,136,512]{2,1,0:T(8,128)(2,1)S(1)}, bf16[2,136,512]{2,1,0:T(8,128)(2,1)S(1)}, u32[]{:S(2)}, u32[]{:S(2)}) collective-permute-start(bf16[2,136,512]{2,1,0:T(8,128)(2,1)S(1)} %pad_maximum_fusion.1), channel_id=1, source_target_pairs={{0,96},{2,26},{4,100},{6,30},{8,104},{10,2},{12,108},{14,6},{16,11... | collective-permute-start | bytes 835592 | tf_op jit(solution)/shard_map/ppermute | solution.py:84
  16.7 7.6 %collective-permute-start.2 = (bf16[2,136,512]{2,1,0:T(8,128)(2,1)S(1)}, bf16[2,136,512]{2,1,0:T(8,128)(2,1)S(1)}, u32[]{:S(2)}, u32[]{:S(2)}) collective-permute-start(bf16[2,136,512]{2,1,0:T(8,128)(2,1)S(1)} %pad_maximum_fusion.1), channel_id=1, source_target_pairs={{0,32},{2,10},{4,36},{6,14},{8,40},{10,18},{12,44},{14,22},{16,48}... | collective-permute-start | bytes 835592 | tf_op jit(solution)/shard_map/ppermute | solution.py:84
  25.4 16.2 %collective-permute-start.9 = (bf16[8,136,512]{2,1,0:T(8,128)(2,1)}, bf16[8,136,512]{2,1,0:T(8,128)(2,1)}, u32[]{:S(2)}, u32[]{:S(2)}) collective-permute-start(bf16[8,136,512]{2,1,0:T(8,128)(2,1)} %bitcast.12.blocks), channel_id=1, source_target_pairs={{0,8},{2,34},{4,12},{6,38},{8,16},{10,42},{12,20},{14,46},{16,24},... | collective-permute-start | bytes 3342344 | tf_op jit(solution)/shard_map/ppermute | solution.py:87
  26.7 16.3 %collective-permute-start.8 = (bf16[8,136,512]{2,1,0:T(8,128)(2,1)}, bf16[8,136,512]{2,1,0:T(8,128)(2,1)S(1)}, u32[]{:S(2)}, u32[]{:S(2)}) collective-permute-start(bf16[8,136,512]{2,1,0:T(8,128)(2,1)} %bitcast.12.blocks), channel_id=1, source_target_pairs={{0,24},{2,98},{4,28},{6,102},{8,0},{10,106},{12,4},{14,110},{16,8}... | collective-permute-start | bytes 3342344 | tf_op jit(solution)/shard_map/ppermute | solution.py:87
  28.1 7.4 %collective-permute-start = (s32[1,64]{1,0:T(1,128)S(1)}, s32[1,64]{1,0:T(1,128)S(1)}, u32[]{:S(2)}, u32[]{:S(2)}) collective-permute-start(s32[1,64]{1,0:T(1,128)S(1)} %copy-done.25), channel_id=1, source_target_pairs={{0,2},{2,0},{4,6},{6,4},{8,10},{10,8},{12,14},{14,12},{16,18},{18,... | collective-permute-start | bytes 776 | tf_op jit(solution)/shard_map/ppermute | solution.py:537
  31.5 47.6 %collective-permute-start.6 = (bf16[512,2048]{1,0:T(8,128)(2,1)}, bf16[512,2048]{1,0:T(8,128)(2,1)}, u32[]{:S(2)}, u32[]{:S(2)}) collective-permute-start(bf16[512,2048]{1,0:T(8,128)(2,1)} %weight.1), channel_id=1, source_target_pairs={{0,1},{1,0},{2,3},{3,2},{4,5},{5,4},{6,7},{7,6},{8,9},{9,8},{10,11... | collective-permute-start | bytes 6291464 | tf_op jit(solution)/shard_map/ppermute | solution.py:82
  36.3 35.4 %collective-permute-start.5 = (bf16[8,136,512]{2,1,0:T(8,128)(2,1)}, bf16[8,136,512]{2,1,0:T(8,128)(2,1)}, u32[]{:S(2)}, u32[]{:S(2)}) collective-permute-start(bf16[8,136,512]{2,1,0:T(8,128)(2,1)} %bitcast.12.blocks), channel_id=1, source_target_pairs={{0,16},{2,66},{4,20},{6,70},{8,24},{10,74},{12,28},{14,78},{16,0},... | collective-permute-start | bytes 3342344 | tf_op jit(solution)/shard_map/ppermute | solution.py:87
  45.7 17.7 %copy-start.11 = (bf16[8,4,128,128]{3,2,1,0:T(8,128)(2,1)}, bf16[8,4,128,128]{3,2,1,0:T(8,128)(2,1)S(1)}, u32[]{:S(2)}) copy-start(bf16[8,4,128,128]{3,2,1,0:T(8,128)(2,1)S(1)} %turn_keys.3.keys_b) | copy-start | bytes 3145732
  94.7 12.7 %copy-start.30 = (s32[128,4]{0,1:T(4,128)S(1)}, s32[128,4]{0,1:T(4,128)}, u32[]{:S(2)}) copy-start(s32[128,4]{0,1:T(4,128)} %param.36) | copy-start | bytes 6148
  94.7 16.4 %copy-start.13 = (bf16[128,512]{1,0:T(8,128)(2,1)S(1)}, bf16[128,512]{1,0:T(8,128)(2,1)}, u32[]{:S(2)}) copy-start(bf16[128,512]{1,0:T(8,128)(2,1)} %queries.1) | copy-start | bytes 393220
  94.7 53.9 %all-to-all-start = ((bf16[32,400,128]{2,1,0:T(8,128)(2,1)}), bf16[32,400,128]{2,1,0:T(8,128)(2,1)S(1)}, u32[]{:S(2)}, u32[]{:S(2)}) async-start(bf16[32,400,128]{2,1,0:T(8,128)(2,1)} %copy-done.2), calls=%async_computation | async-start | bytes 6553600 | tf_op jit(solution)/shard_map/all_to_all | solution.py:567
  107.1 57.1 %copy-start.29 = (s32[1536]{0:T(1024)S(1)}, s32[1536]{0:T(1024)}, u32[]{:S(2)}) copy-start(s32[1536]{0:T(1024)} %constant.123) | copy-start | bytes 18436
  107.1 59.5 %copy-start.21 = (f32[2048]{0:T(1024)S(1)}, f32[2048]{0:T(1024)}, u32[]{:S(2)}) copy-start(f32[2048]{0:T(1024)} %param.39) | copy-start | bytes 24580
  148.7 17.9 %copy-start.7 = (bf16[512,2048]{1,0:T(8,128)(2,1)S(1)}, bf16[512,2048]{1,0:T(8,128)(2,1)}, u32[]{:S(2)}) copy-start(bf16[512,2048]{1,0:T(8,128)(2,1)} %weight.1) | copy-start | bytes 6291460
  148.7 17.9 %copy-start.14 = (bf16[128,2048]{1,0:T(8,128)(2,1)S(1)}, bf16[128,2048]{1,0:T(8,128)(2,1)}, u32[]{:S(2)}) copy-start(bf16[128,2048]{1,0:T(8,128)(2,1)} %residual.1) | copy-start | bytes 1572868
  149.8 14.5 %copy-start.27 = (pred[1536,256]{1,0:T(32,128)(4,1)S(1)}, pred[1536,256]{1,0:T(32,128)(4,1)}, u32[]{:S(2)}) copy-start(pred[1536,256]{1,0:T(32,128)(4,1)} %constant.112.clone) | copy-start | bytes 1179652
  158.1 8.5 %collective-permute-start.10 = (bf16[128,512]{1,0:T(8,128)(2,1)S(1)}, bf16[128,512]{1,0:T(8,128)(2,1)S(1)}, u32[]{:S(2)}, u32[]{:S(2)}) collective-permute-start(bf16[128,512]{1,0:T(8,128)(2,1)S(1)} %merge_attention.1.att), channel_id=1, source_target_pairs={{0,1},{1,0},{2,3},{3,2},{4,5},{5,4},{6,7},{7,6},{8,9},{9,8},{10,11... | collective-permute-start | bytes 393224 | tf_op jit(solution)/shard_map/ppermute | solution.py:572
  172.7 51.7 %all-to-all-start.1 = ((bf16[64,24,1024]{2,1,0:T(8,128)(2,1)}), bf16[64,24,1024]{2,1,0:T(8,128)(2,1)S(1)}, u32[]{:S(2)}, u32[]{:S(2)}) async-start(bf16[64,24,1024]{2,1,0:T(8,128)(2,1)} %bitcast.27), calls=%async_computation.1 | async-start | bytes 6291456 | tf_op jit(solution)/shard_map/all_to_all | solution.py:576
  239.0 48.6 %all-to-all-start.2 = ((bf16[128,24,512]{2,1,0:T(8,128)(2,1)}), bf16[128,24,512]{2,1,0:T(8,128)(2,1)S(1)}, u32[]{:S(2)}, u32[]{:S(2)}) async-start(bf16[128,24,512]{2,1,0:T(8,128)(2,1)} %bitcast.47), calls=%async_computation.2 | async-start | bytes 6291456 | tf_op jit(solution)/shard_map/all_to_all | solution.py:578
  (22 other events, 64.5 us)

commit v3 on v2

--- a/solution.py
+++ b/solution.py
@@ -18,6 +18,7 @@
 ROWS = SLOTS * 16
 STAT = HEADS * ROWS
 BLOCK = STAT + 16
+MERGE_PARTS = 2
 NORM_EPS = 1e-06
 SCALE = 1.0 / math.sqrt(HD)
 LOG2E = math.log2(math.e)
@@ -76,16 +77,19 @@
     return [[chip * NC + core for chip in range(NCHIP)] for core in range(NC)]
 
 
-def gather_blocks(block, weight):
-    pair = jnp.stack([block, lax.ppermute(block, "req", perm_x())])
-    pair, weight = lax.optimization_barrier((pair, weight))
+def gather_blocks(block, weight, pages, sends):
+    near = lax.ppermute(block, "req", perm_x())
+    pages = lax.ppermute(pages, "req", perm_core())
+    sends = lax.ppermute(sends, "req", perm_core())
+    near, weight, pages, sends = lax.optimization_barrier((near, weight, pages, sends))
+    pair = jnp.stack([block, near])
     weight_far = lax.ppermute(weight, "tp", [(0, 1), (1, 0)])
     line = jnp.stack(
         [pair] + [lax.ppermute(pair, "req", perm_ring(0, step)) for step in (1, 2, 3)]
     ).reshape(8, *block.shape)
     return [line] + [
         lax.ppermute(line, "req", perm_ring(1, step)) for step in (1, 3, 2)
-    ], weight_far
+    ], (weight_far, pages, sends)
 
 
 def attend(query, key_t, value_1, shift):
@@ -116,22 +120,39 @@
     return pl.pallas_call(
         keys_kernel,
         out_shape=jax.ShapeDtypeStruct((count, HEADS, HD, PAGE), BF16),
-        in_specs=[vmem()],
-        out_specs=vmem(),
+        in_specs=[pl.BlockSpec(pages.shape, lambda i: (0, 0, 0, 0))],
+        out_specs=pl.BlockSpec((count, HEADS, HD, PAGE), lambda i: (0, 0, 0, 0)),
+        grid=(1,),
         cost_estimate=pl.CostEstimate(
             flops=32 << 20, bytes_accessed=3 << 20, transcendentals=0
         ),
-        compiler_params=pltpu.CompilerParams(vmem_limit_bytes=16 << 20),
+        compiler_params=pltpu.CompilerParams(vmem_limit_bytes=62 << 20),
         name="turn_keys",
     )(pages)
 
 
-def page_kernel(chip_of, page_a, page_b, codes, blocks, keys_a, keys_b, pages_a, pages_b, *refs):
-    out, held, sems = refs[-3:]
+def page_kernel(chip_of, page_a, page_b, codes, blocks_in, keys_a_in, keys_b_in, pages_a_in, pages_b_in, *refs):
+    out, blocks, keys_a, keys_b, values_a, values_b, held, sems, load_sems = refs[-9:]
+    loads = [
+        pltpu.make_async_copy(source, target, load_sems.at[n])
+        for n, (source, target) in enumerate(
+            (
+                (keys_a_in, keys_a),
+                (keys_b_in, keys_b),
+                (blocks_in, blocks),
+                (pages_a_in.at[:, 1], values_a),
+                (pages_b_in.at[:, 1], values_b),
+            )
+        )
+    ]
+    for load in loads:
+        load.start()
     row = lax.broadcasted_iota(jnp.int32, (16, 128), 0)
     offset = lax.broadcasted_iota(jnp.int32, (16, 128), 1) - row
     sub = lax.broadcasted_iota(jnp.int32, (8, 128), 0)
     ones = jnp.ones((PAGE, HD), BF16)
+    for load in loads:
+        load.wait()
 
     def copy(i):
         return pltpu.make_async_copy(held.at[i], out.at[chip_of[i]], sems.at[i])
@@ -154,22 +175,35 @@
             axis=0,
         )
         mine = [offset == jnp.where(c >= 8, (c & 7) * 16, -1024) for c in code]
-        sums = []
+        scores = []
         for head in range(HEADS):
             cols = slice(head * HD, (head + 1) * HD)
             query = jnp.concatenate(
                 [blocks[i, pl.ds(first[j], 16), cols] for j in range(SLOTS)], axis=0
             )
             key_t = jnp.concatenate([keys_a[pa, head], keys_b[pb, head]], axis=1)
+            scores.append(jnp.dot(query, key_t, preferred_element_type=F32) + bias)
+        tops = [jnp.max(s, axis=1, keepdims=True) for s in scores]
+        probs = [
+            jnp.exp2((s - t) * (SCALE * LOG2E)).astype(BF16) for s, t in zip(scores, tops)
+        ]
+        boths = []
+        for head in range(HEADS):
+            cols = slice(head * HD, (head + 1) * HD)
             value_1 = jnp.concatenate(
                 [
-                    jnp.concatenate([pages_a[pa, 1, :, cols], ones], axis=1),
-                    jnp.concatenate([pages_b[pb, 1, :, cols], ones], axis=1),
+                    jnp.concatenate([values_a[pa, :, cols], ones], axis=1),
+                    jnp.concatenate([values_b[pb, :, cols], ones], axis=1),
                 ],
                 axis=0,
             )
-            got, total = attend(query, key_t, value_1, lambda s: s + bias)
+            boths.append(jnp.dot(probs[head], value_1, preferred_element_type=F32))
+        sums = []
+        for head in range(HEADS):
+            total = boths[head][:, HD:]
+            got = boths[head][:, :HD] / total
             held[i, head * ROWS : (head + 1) * ROWS, :] = got.astype(BF16)
+            total = tops[head] * SCALE + jnp.log(total)
             here = jnp.where(mine[0], total[:16], NEG)
             for j in range(1, SLOTS):
                 here = jnp.maximum(here, jnp.where(mine[j], total[16 * j : 16 * j + 16], NEG))
@@ -185,7 +219,7 @@
         return carry
 
     count = blocks.shape[0]
-    lax.fori_loop(0, count, step, 0, unroll=2)
+    lax.fori_loop(0, count, step, 0, unroll=4)
     lax.fori_loop(0, count, lambda i, carry: (copy(i).wait(), carry)[1], 0)
 
 
@@ -196,15 +230,20 @@
         page_kernel,
         out_shape=jax.ShapeDtypeStruct((NCHIP, BLOCK, HD), BF16),
         in_specs=[smem()] * 4
-        + [vmem()] * 5
-        + [pl.BlockSpec(memory_space=pl.ANY)] * len(before),
-        out_specs=pl.BlockSpec(memory_space=pl.ANY),
+        + [hbm()] * (5 + len(before)),
+        out_specs=hbm(),
         input_output_aliases={9: 0} if before else {},
         scratch_shapes=[
+            pltpu.VMEM(blocks.shape, BF16),
+            pltpu.VMEM(keys_a.shape, BF16),
+            pltpu.VMEM(keys_b.shape, BF16),
+            pltpu.VMEM((pages_a.shape[0], PAGE, HEADS * HD), BF16),
+            pltpu.VMEM((pages_b.shape[0], PAGE, HEADS * HD), BF16),
             pltpu.VMEM((count, BLOCK, HD), BF16),
             pltpu.SemaphoreType.DMA((count,)),
+            pltpu.SemaphoreType.DMA((5,)),
         ],
-        compiler_params=pltpu.CompilerParams(vmem_limit_bytes=24 << 20),
+        compiler_params=pltpu.CompilerParams(vmem_limit_bytes=62 << 20),
         cost_estimate=pl.CostEstimate(
             flops=count * HEADS * 12 * ROWS * HD * HD * 8,
             bytes_accessed=6 << 20,
@@ -218,11 +257,15 @@
     return pl.BlockSpec(memory_space=pltpu.SMEM)
 
 
+def hbm():
+    return pl.BlockSpec(memory_space=pltpu.HBM)
+
+
 def vmem():
     return pl.BlockSpec(memory_space=pltpu.VMEM)
 
 
-def own_kernel(request_col, request_row, queries, keys, values, out, total):
+def own_kernel(request_col, request_row, queries, keys, values, out_hbm, total_hbm, out, total, sems):
     token = lax.broadcasted_iota(jnp.int32, (TOK, TOK), 0)
     key = lax.broadcasted_iota(jnp.int32, (TOK, TOK), 1)
     mask = (request_col[...] == request_row[...]) & (key <= token)
@@ -239,6 +282,14 @@
         out[head] = got
         sums.append(jnp.max(jnp.where(token == key, low, NEG), axis=0, keepdims=True))
     total[...] = by_head(sums)
+    copies = [
+        pltpu.make_async_copy(out, out_hbm, sems.at[0]),
+        pltpu.make_async_copy(total, total_hbm, sems.at[1]),
+    ]
+    for copy in copies:
+        copy.start()
+    for copy in copies:
+        copy.wait()
 
 
 def own_attention(request_ids, queries, keys, values):
@@ -249,8 +300,13 @@
             jax.ShapeDtypeStruct((8, TOK), F32),
         ),
         in_specs=[vmem()] * 5,
-        out_specs=(vmem(), vmem()),
-        compiler_params=pltpu.CompilerParams(vmem_limit_bytes=16 << 20),
+        out_specs=(hbm(), hbm()),
+        scratch_shapes=[
+            pltpu.VMEM((HEADS, TOK, HD), F32),
+            pltpu.VMEM((8, TOK), F32),
+            pltpu.SemaphoreType.DMA((2,)),
+        ],
+        compiler_params=pltpu.CompilerParams(vmem_limit_bytes=62 << 20),
         cost_estimate=pl.CostEstimate(
             flops=64 << 20, bytes_accessed=1 << 20, transcendentals=HEADS * TOK * TOK
         ),
@@ -258,7 +314,21 @@
     )(request_ids[:, None], request_ids[None, :], queries, keys, values)
 
 
-def merge_kernel(codes, arrived, own, own_sums, out, acc, tiles):
+def merge_kernel(
+    codes, arrived_in, own_in, own_sums_in, out, acc, tiles, arrived, own, own_sums, sems
+):
+    part = NCHIP // MERGE_PARTS
+    loads = [
+        pltpu.make_async_copy(own_sums_in, own_sums, sems.at[0]),
+        pltpu.make_async_copy(own_in, own, sems.at[1]),
+    ] + [
+        pltpu.make_async_copy(
+            arrived_in.at[pl.ds(i * part, part)], arrived.at[pl.ds(i * part, part)], sems.at[2 + i]
+        )
+        for i in range(MERGE_PARTS)
+    ]
+    for load in loads:
+        load.start()
     row = lax.broadcasted_iota(jnp.int32, (16, TOK), 0)
     offset = lax.broadcasted_iota(jnp.int32, (16, TOK), 1) - row
     ones = jnp.ones((2 * TOK, HD), BF16)
@@ -289,7 +359,12 @@
         tiles[p] = tile
         return jnp.maximum(top, tile)
 
-    top = lax.fori_loop(0, NCHIP, collect, own_sums[...], unroll=4)
+    loads[0].wait()
+    top = own_sums[...]
+    for i in range(MERGE_PARTS):
+        loads[2 + i].wait()
+        top = lax.fori_loop(i * part, (i + 1) * part, collect, top, unroll=4)
+    loads[1].wait()
     whole = [offset == 16 * g for g in range(TOK // 16)]
     share = jnp.exp(own_sums[...] - top)
     acc[...] = own[...] * on_rows(halves(share), whole).reshape(HEADS, TOK, HD)
@@ -307,7 +382,7 @@
                 acc[head, at, :] += part * factor[start : start + 16]
         return low + share
 
-    low = lax.fori_loop(0, NCHIP, add, share)
+    low = lax.fori_loop(0, NCHIP, add, share, unroll=4)
     factor = on_rows(halves(1.0 / low), whole)
     for head in range(HEADS):
         out[:, head * HD : (head + 1) * HD] = (
@@ -319,13 +394,17 @@
     return pl.pallas_call(
         merge_kernel,
         out_shape=jax.ShapeDtypeStruct((TOK, HEADS * HD), BF16),
-        in_specs=[smem()] + [vmem()] * 3,
+        in_specs=[smem()] + [hbm()] * 3,
         out_specs=vmem(),
         scratch_shapes=[
             pltpu.VMEM((HEADS, TOK, HD), F32),
             pltpu.VMEM((NCHIP, 8, TOK), F32),
+            pltpu.VMEM((NCHIP, BLOCK, HD), BF16),
+            pltpu.VMEM((HEADS, TOK, HD), F32),
+            pltpu.VMEM((8, TOK), F32),
+            pltpu.SemaphoreType.DMA((2 + MERGE_PARTS,)),
         ],
-        compiler_params=pltpu.CompilerParams(vmem_limit_bytes=24 << 20),
+        compiler_params=pltpu.CompilerParams(vmem_limit_bytes=62 << 20),
         cost_estimate=pl.CostEstimate(
             flops=64 << 20, bytes_accessed=4 << 20, transcendentals=1 << 18
         ),
@@ -333,92 +412,139 @@
     )(codes, arrived, own, own_sums)
 
 
-def project_kernel(att, att_far, weight, weight_far, residual, gain, picks, mixed, sent, both):
+def project_kernel(
+    side, att, att_far, weight, weight_far, residual, gain, picks, mixed, sent, both, kept, rows, sems
+):
     half = residual.shape[1] // 2
+    steps, step = rows.shape[0], rows.shape[1]
     total = residual[...].astype(F32)
     total += jnp.dot(att[...], weight[...], preferred_element_type=F32)
     total += jnp.dot(att_far[...], weight_far[...], preferred_element_type=F32)
-    mixed[...] = total
+    kept[...] = jnp.where(side[0] == 0, total[:, :half], total[:, half:])
+    keep = pltpu.make_async_copy(kept, mixed, sems.at[steps])
+    keep.start()
     scale = lax.rsqrt(jnp.mean(total * total, axis=1, keepdims=True) + NORM_EPS)
     normed = (total * scale * gain[...]).astype(BF16)
     both[:TOK] = normed[:, :half]
     both[TOK:] = normed[:, half:]
-    step = 256
-    for row in range(0, sent.shape[0], step):
-        sent[row : row + step] = jnp.dot(
-            picks[row : row + step], both[...], preferred_element_type=F32
+    copies = []
+    for i in range(steps):
+        rows[i] = jnp.dot(
+            picks[i * step : (i + 1) * step], both[...], preferred_element_type=F32
         ).astype(BF16)
-
-
-def project(att, att_far, weight, weight_far, residual, gain, picks):
+        copies.append(
+            pltpu.make_async_copy(rows.at[i], sent.at[pl.ds(i * step, step)], sems.at[i])
+        )
+        copies[-1].start()
+    keep.wait()
+    for copy in copies:
+        copy.wait()
+
+
+def project(side, att, att_far, weight, weight_far, residual, gain, picks, steps=4):
     width = residual.shape[1]
+    step = picks.shape[0] // steps
     return pl.pallas_call(
         project_kernel,
         out_shape=(
-            jax.ShapeDtypeStruct((TOK, width), F32),
+            jax.ShapeDtypeStruct((TOK, width // 2), F32),
             jax.ShapeDtypeStruct((picks.shape[0], width // 2), BF16),
         ),
-        in_specs=[vmem()] * 7,
-        out_specs=(vmem(), vmem()),
-        scratch_shapes=[pltpu.VMEM((2 * TOK, width // 2), BF16)],
-        compiler_params=pltpu.CompilerParams(vmem_limit_bytes=32 << 20),
+        in_specs=[smem()] + [vmem()] * 7,
+        out_specs=(hbm(), hbm()),
+        scratch_shapes=[
+            pltpu.VMEM((2 * TOK, width // 2), BF16),
+            pltpu.VMEM((TOK, width // 2), F32),
+            pltpu.VMEM((steps, step, width // 2), BF16),
+            pltpu.SemaphoreType.DMA((steps + 1,)),
+        ],
+        compiler_params=pltpu.CompilerParams(vmem_limit_bytes=62 << 20),
         cost_estimate=pl.CostEstimate(
             flops=4 * TOK * 512 * width + 2 * picks.shape[0] * 256 * width // 2,
             bytes_accessed=10 << 20,
             transcendentals=TOK,
         ),
         name="project_dispatch",
-    )(att, att_far, weight, weight_far, residual, gain, picks)
-
-
-def expert_kernel(rows, gate, up, down, out):
-    count = rows.shape[0]
+    )(side, att, att_far, weight, weight_far, residual, gain, picks)
+
+
+def expert_kernel(rows, gate, up, down, out, rows_v, gate_v, up_v, down_v, out_v, sems, back):
+    steps, count = rows_v.shape[0], rows_v.shape[1]
     width = gate.shape[0]
     half, quarter = width // 2, width // 4
-    wide = rows[...].astype(F32)
-    upper = lax.broadcasted_iota(jnp.int32, (count // 2, 8, half), 1) < 4
-    tail = wide[:, 16:24].reshape(count // 2, 2, 8, half)
-    even, odd = tail[:, 0], tail[:, 1]
-    tail_0 = jnp.where(upper, even, pltpu.roll(odd, 4, 1))
-    tail_1 = jnp.where(upper, pltpu.roll(even, 4, 1), odd)
-    left = jnp.concatenate(
-        [wide[:, 0:8].reshape(count * 8, half), tail_0.reshape(count * 4, half)], axis=0
-    )
-    right = jnp.concatenate(
-        [wide[:, 8:16].reshape(count * 8, half), tail_1.reshape(count * 4, half)], axis=0
-    )
-    tokens = jnp.concatenate([left.astype(BF16), right.astype(BF16)], axis=1)
-    gate_act = jnp.dot(tokens, gate[...], preferred_element_type=F32)
-    up_act = jnp.dot(tokens, up[...], preferred_element_type=F32)
-    hidden = (gate_act / (1.0 + jnp.exp(-gate_act)) * up_act).astype(BF16)
-    result = jnp.dot(hidden, down[...], preferred_element_type=F32)
-    upper = lax.broadcasted_iota(jnp.int32, (count // 2, 8, quarter), 1) < 4
-    for side in range(2):
-        cols = [slice((2 * side + q) * quarter, (2 * side + q + 1) * quarter) for q in range(2)]
-        main = [result[: count * 8, c].reshape(count, 8, quarter) for c in cols]
-        tail = [result[count * 8 :, c].reshape(count // 2, 8, quarter) for c in cols]
-        even = jnp.where(upper, tail[0], pltpu.roll(tail[1], 4, 1))
-        odd = jnp.where(upper, pltpu.roll(tail[0], 4, 1), tail[1])
-        last = jnp.stack([even, odd], axis=1).reshape(count, 8, quarter)
-        out[:, side] = jnp.concatenate(main + [last], axis=1).astype(BF16)
-
-
-def run_expert(rows, gate, up, down, steps=2):
+
+    def fetch(i):
+        return pltpu.make_async_copy(rows.at[pl.ds(i * count, count)], rows_v.at[i], sems.at[i])
+
+    def send(i):
+        return pltpu.make_async_copy(out_v.at[i], out.at[pl.ds(i * count, count)], back.at[i])
+
+    loads = [
+        pltpu.make_async_copy(src, dst, sems.at[steps + n])
+        for n, (src, dst) in enumerate(((gate, gate_v), (up, up_v), (down, down_v)))
+    ]
+    fetch(0).start()
+    for load in loads:
+        load.start()
+    for i in range(1, steps):
+        fetch(i).start()
+    low_half = lax.broadcasted_iota(jnp.int32, (count // 2, 8, half), 1) < 4
+    low_quarter = lax.broadcasted_iota(jnp.int32, (count // 2, 8, quarter), 1) < 4
+    def step(i, carry):
+        fetch(i).wait()
+        wide = rows_v[i].astype(F32)
+        tail = wide[:, 16:24].reshape(count // 2, 2, 8, half)
+        even, odd = tail[:, 0], tail[:, 1]
+        tail_0 = jnp.where(low_half, even, pltpu.roll(odd, 4, 1))
+        tail_1 = jnp.where(low_half, pltpu.roll(even, 4, 1), odd)
+        left = jnp.concatenate(
+            [wide[:, 0:8].reshape(count * 8, half), tail_0.reshape(count * 4, half)], axis=0
+        )
+        right = jnp.concatenate(
+            [wide[:, 8:16].reshape(count * 8, half), tail_1.reshape(count * 4, half)], axis=0
+        )
+        tokens = jnp.concatenate([left.astype(BF16), right.astype(BF16)], axis=1)
+        pl.when(i == 0)(loads[0].wait)
+        gate_act = jnp.dot(tokens, gate_v[...], preferred_element_type=F32)
+        pl.when(i == 0)(loads[1].wait)
+        up_act = jnp.dot(tokens, up_v[...], preferred_element_type=F32)
+        hidden = (gate_act / (1.0 + jnp.exp(-gate_act)) * up_act).astype(BF16)
+        pl.when(i == 0)(loads[2].wait)
+        result = jnp.dot(hidden, down_v[...], preferred_element_type=F32)
+        for side in range(2):
+            cols = [slice((2 * side + q) * quarter, (2 * side + q + 1) * quarter) for q in range(2)]
+            main = [result[: count * 8, c].reshape(count, 8, quarter) for c in cols]
+            tail = [result[count * 8 :, c].reshape(count // 2, 8, quarter) for c in cols]
+            even = jnp.where(low_quarter, tail[0], pltpu.roll(tail[1], 4, 1))
+            odd = jnp.where(low_quarter, pltpu.roll(tail[0], 4, 1), tail[1])
+            last = jnp.stack([even, odd], axis=1).reshape(count, 8, quarter)
+            out_v[i, :, side] = jnp.concatenate(main + [last], axis=1).astype(BF16)
+        send(i).start()
+        return carry
+
+    lax.fori_loop(0, steps, step, 0)
+    for i in range(steps):
+        send(i).wait()
+
+
+def run_expert(rows, gate, up, down, steps=4):
     count = rows.shape[0] // steps
     width, hidden = gate.shape
-    once = pl.Buffered(1)
     return pl.pallas_call(
         expert_kernel,
-        grid=(steps,),
         out_shape=jax.ShapeDtypeStruct((rows.shape[0], 2, 2 * CAP, width // 4), BF16),
-        in_specs=[
-            pl.BlockSpec((count, 2 * CAP, width // 2), lambda i: (i, 0, 0)),
-            pl.BlockSpec((width, hidden), lambda i: (0, 0), pipeline_mode=once),
-            pl.BlockSpec((width, hidden), lambda i: (0, 0), pipeline_mode=once),
-            pl.BlockSpec((hidden, width), lambda i: (0, 0), pipeline_mode=once),
+        in_specs=[hbm()] * 4,
+        out_specs=hbm(),
+        scratch_shapes=[
+            pltpu.VMEM((steps, count, 2 * CAP, width // 2), BF16),
+            pltpu.VMEM((width, hidden), BF16),
+            pltpu.VMEM((width, hidden), BF16),
+            pltpu.VMEM((hidden, width), BF16),
+            pltpu.VMEM((steps, count, 2, 2 * CAP, width // 4), BF16),
+            pltpu.SemaphoreType.DMA((steps + 3,)),
+            pltpu.SemaphoreType.DMA((steps,)),
         ],
-        out_specs=pl.BlockSpec((count, 2, 2 * CAP, width // 4), lambda i: (i, 0, 0, 0)),
-        compiler_params=pltpu.CompilerParams(vmem_limit_bytes=56 << 20),
+        compiler_params=pltpu.CompilerParams(vmem_limit_bytes=62 << 20),
         cost_estimate=pl.CostEstimate(
             flops=6 * rows.shape[0] * CAP * width * hidden,
             bytes_accessed=15 << 20,
@@ -428,28 +554,50 @@
     )(rows, gate, up, down)
 
 
-def combine_kernel(mixed, shares, shares_low, rows, out):
-    total = jnp.dot(shares[...], rows[...], preferred_element_type=F32)
-    total += jnp.dot(shares_low[...], rows[...], preferred_element_type=F32)
-    width = rows.shape[1]
-    out[:, :width] = (mixed[:, :width] + total[:TOK]).astype(BF16)
-    out[:, width:] = (mixed[:, width:] + total[TOK:]).astype(BF16)
-
-
-def combine(mixed, shares, shares_low, rows):
+def combine_kernel(mixed, shares, rows, out, mixed_v, shares_v, rows_v, sems):
+    parts, depth, width = rows_v.shape
+    loads = [
+        pltpu.make_async_copy(rows.at[pl.ds(i * depth, depth)], rows_v.at[i], sems.at[i])
+        for i in range(parts)
+    ]
+    share_load = pltpu.make_async_copy(shares, shares_v, sems.at[parts])
+    mixed_load = pltpu.make_async_copy(mixed, mixed_v, sems.at[parts + 1])
+    share_load.start()
+    for load in loads:
+        load.start()
+    mixed_load.start()
+    share_load.wait()
+    total = jnp.zeros((shares_v.shape[0], width), F32)
+    for i in range(parts):
+        loads[i].wait()
+        total += jnp.dot(
+            shares_v[:, i * depth : (i + 1) * depth], rows_v[i], preferred_element_type=F32
+        )
+    mixed_load.wait()
+    out[:, :width] = (mixed_v[:, :width] + total[:TOK]).astype(BF16)
+    out[:, width:] = (mixed_v[:, width:] + total[TOK:]).astype(BF16)
+
+
+def combine(mixed, shares, rows, parts=4):
     return pl.pallas_call(
         combine_kernel,
         out_shape=jax.ShapeDtypeStruct(mixed.shape, BF16),
-        in_specs=[vmem()] * 4,
+        in_specs=[hbm()] * 3,
         out_specs=vmem(),
-        compiler_params=pltpu.CompilerParams(vmem_limit_bytes=32 << 20),
+        scratch_shapes=[
+            pltpu.VMEM(mixed.shape, F32),
+            pltpu.VMEM(shares.shape, BF16),
+            pltpu.VMEM((parts, rows.shape[0] // parts, rows.shape[1]), BF16),
+            pltpu.SemaphoreType.DMA((parts + 2,)),
+        ],
+        compiler_params=pltpu.CompilerParams(vmem_limit_bytes=62 << 20),
         cost_estimate=pl.CostEstimate(
-            flops=4 * shares.shape[0] * rows.shape[0] * rows.shape[1],
-            bytes_accessed=8 << 20,
+            flops=2 * shares.shape[0] * rows.shape[0] * rows.shape[1],
+            bytes_accessed=6 << 20,
             transcendentals=0,
         ),
         name="combine",
-    )(mixed, shares, shares_low, rows)
+    )(mixed, shares, rows)
 
 
 def slot_rows():
@@ -488,8 +636,7 @@
             col_place[:, k, None] == back_place[None, :], col_weight[:, k, None], 0.0
         )
     shares = jnp.where(back_part[None, :] == col_part[:, None], shares, 0.0)
-    high = lax.reduce_precision(shares, 8, 7)
-    return picks, high.astype(BF16), (shares - high).astype(BF16)
+    return picks, shares.astype(BF16)
 
 
 def shards(
@@ -510,7 +657,6 @@
     down_weight,
 ):
     me = lax.axis_index("req")
-    tp_index = lax.axis_index("tp")
     width = residual.shape[1]
     half = width // 2
     swap = [(0, 1), (1, 0)]
@@ -530,11 +676,9 @@
 
     note = jnp.zeros((8, queries.shape[1]), BF16)
     note = note.at[0, : NCHIP * SLOTS].set(codes.T.reshape(-1).astype(BF16))
-    pieces, weight_far = gather_blocks(
-        jnp.concatenate([queries, note], axis=0), output_weight
+    pieces, (weight_far, pages_far, sends_far) = gather_blocks(
+        jnp.concatenate([queries, note], axis=0), output_weight, page_store, page_sends
     )
-    pages_far = lax.ppermute(page_store, "req", perm_core())
-    sends_far = lax.ppermute(page_sends, "req", perm_core())
     keys_a, keys_b = turn_keys(page_store), turn_keys(pages_far)
     own, own_sums = own_attention(request_ids, queries, new_keys, new_values)
 
@@ -568,18 +712,24 @@
         parts, "req", 0, 0, tiled=True, axis_index_groups=core_groups()
     )
     attended = merge_attention(codes.reshape(-1), arrived, own, own_sums)
-    picks, shares, shares_low = routing(expert_ids, expert_weights)
+    picks, shares = routing(expert_ids, expert_weights)
     attended_far = lax.ppermute(attended, "tp", swap)
     mixed, sent = project(
-        attended, attended_far, output_weight, weight_far, residual, norm_gain[None, :], picks
+        lax.axis_index("tp")[None],
+        attended,
+        attended_far,
+        output_weight,
+        weight_far,
+        residual,
+        norm_gain[None, :],
+        picks,
     )
     rows = lax.all_to_all(sent.reshape(NREQ, 2 * CAP, half), "req", 0, 0, tiled=True)
     result = run_expert(rows, gate_weight[0], up_weight[0], down_weight[0])
     returned = lax.all_to_all(
         result.reshape(2 * NREQ, 2 * CAP, width // 4), ("req", "tp"), 0, 0, tiled=True
     )
-    mixed_half = lax.dynamic_slice_in_dim(mixed, tp_index * half, half, 1)
-    return combine(mixed_half, shares, shares_low, returned.reshape(-1, width // 4))
+    return combine(mixed, shares, returned.reshape(-1, width // 4))
 
 
 def solution(mesh):

time: 295 us -> 279 us (0.946)
  local copies, waits for them, and re-layouts: 38.1 us -> 20.9 us
  waiting for transfers between devices: 125 us -> 133 us
  starting transfers between devices: 53.2 us -> 46.4 us
    unnamed x69 -> x27, local copies, waits for them, and re-layouts: 28 us -> 8.81 us
    pallas_call x4, Pallas kernels: 34.1 us -> 26.3 us  [page_attention(): pl.pallas_call(page_kernel, out_shape=jax.ShapeDtypeStruct((NCHIP, BLOCK,...]
    ppermute x3, waiting for transfers between devices: 2.44 us -> 8.77 us  [gather_blocks(): lax.ppermute(line, 'req', perm_ring(1, step))]
    ppermute x1, waiting for transfers between devices: 7.43 us -> 3.68 us  [gather_blocks(): weight_far = lax.ppermute(weight, 'tp', [(0, 1), (1, 0)])]
    pallas_call x2, Pallas kernels: 2.38 us -> 5.86 us  [turn_keys(): pl.pallas_call(keys_kernel, out_shape=jax.ShapeDtypeStruct((count, HEADS,...]
    all_to_all x1, starting transfers between devices: 12.4 us -> 9.08 us  [shards(): lax.all_to_all(parts, 'req', 0, 0, tiled=True, axis_index_groups=core_gro...]
    all_to_all x1, waiting for transfers between devices: 33.9 us -> 36.9 us  [shards(): lax.all_to_all(parts, 'req', 0, 0, tiled=True, axis_index_groups=core_gro...]
  transfers between devices with their start and end apart: 14 -> 14, of which waited for: 9 -> 10; matrix products, arithmetic and copies ran while one was open for 10% -> 10% of each run, Pallas kernels for 10% -> 10%
where the time goes in v3:
time: 279 us; the launch traced here: 278 us
  waiting for transfers between devices  133 us (48%)
  Pallas kernels  67.2 us (24%)
  starting transfers between devices  46.4 us (17%)
  local copies, waits for them, and re-layouts  20.9 us (7%)
  other arithmetic  9.1 us (3%)
    all_to_all x1, waiting for transfers between devices, shards(): lax.all_to_all(result.reshape(2 * NREQ, 2 * CAP, width // 4), ('req', 'tp...  38.2 us
    all_to_all x1, waiting for transfers between devices, shards(): lax.all_to_all(parts, 'req', 0, 0, tiled=True, axis_index_groups=core_gro...  36.9 us
    all_to_all x1, waiting for transfers between devices, shards(): lax.all_to_all(sent.reshape(NREQ, 2 * CAP, half), 'req', 0, 0, tiled=True)  34.7 us
    pallas_call x4, Pallas kernels, page_attention(): pl.pallas_call(page_kernel, out_shape=jax.ShapeDtypeStruct((NCHIP, BLOCK,...  26.3 us
    pallas_call x1, Pallas kernels, run_expert(): pl.pallas_call(expert_kernel, out_shape=jax.ShapeDtypeStruct((rows.shape[...  14.5 us
    all_to_all x1, starting transfers between devices, shards(): lax.all_to_all(sent.reshape(NREQ, 2 * CAP, half), 'req', 0, 0, tiled=True)  9.5 us
    all_to_all x1, starting transfers between devices, shards(): lax.all_to_all(parts, 'req', 0, 0, tiled=True, axis_index_groups=core_gro...  9.08 us
    unnamed x27, local copies, waits for them, and re-layouts  8.81 us
  transfers between devices with their start and end apart: 14, of which 10 were waited for; matrix products, arithmetic and copies ran while one was open for 10% of the time, Pallas kernels for 10%

profile of v3, /device:TPU:1, one launch (start us, length us, event | category | flops | bytes accessed | tf_op | source)
XLA Modules:
  0.0 277.7 jit_solution(16468754042603475847)
XLA Ops:
  14.4 3.3 %collective-permute-start.4 = (bf16[2,136,512]{2,1,0:T(8,128)(2,1)S(1)}, bf16[2,136,512]{2,1,0:T(8,128)(2,1)S(1)}, u32[]{:S(2)}, u32[]{:S(2)}) collective-permute-start(bf16[2,136,512]{2,1,0:T(8,128)(2,1)S(1)} %get-tuple-element.40), channel_id=1, source_target_pairs={{0,64},{2,18},{4,68},{6,22},{8,72},{10,26},{12,76},{14,30},{16,80}... | collective-permute-start | bytes 835592 | tf_op jit(solution)/shard_map/ppermute | solution.py:88
  20.8 4.2 %collective-permute-done.4 = bf16[2,136,512]{2,1,0:T(8,128)(2,1)S(1)} collective-permute-done((bf16[2,136,512]{2,1,0:T(8,128)(2,1)S(1)}, bf16[2,136,512]{2,1,0:T(8,128)(2,1)S(1)}, u32[]{:S(2)}, u32[]{:S(2)}) %collective-permute-start.4) | collective-permute-done | bytes 278560 | tf_op jit(solution)/shard_map/ppermute | solution.py:88
  27.6 2.9 %turn_keys.2.keys_a_in = bf16[8,4,128,128]{3,2,1,0:T(8,128)(2,1)} custom-call(bf16[8,2,128,512]{3,2,1,0:T(8,128)(2,1)} %pages_a_in.7), custom_call_target="tpu_custom_call" | custom-call | flops 33554432 | bytes 3145728 | tf_op jit(solution)/shard_map/turn_keys/pallas_call | solution.py:120
  36.1 2.9 %turn_keys.3.keys_b_in = bf16[8,4,128,128]{3,2,1,0:T(8,128)(2,1)} custom-call(bf16[8,2,128,512]{3,2,1,0:T(8,128)(2,1)} %collective-permute-done.1.pages.pages_b_in), custom_call_target="tpu_custom_call" | custom-call | flops 33554432 | bytes 3145728 | tf_op jit(solution)/shard_map/turn_keys/pallas_call | solution.py:120
  43.2 6.6 %page_attention.4.refs_0_ = bf16[32,400,128]{2,1,0:T(8,128)(2,1)} custom-call(s32[8]{0:T(128)} %get-tuple-element.59.chip_of, s32[8]{0:T(128)} %get-tuple-element.55.page_a, s32[8]{0:T(128)} %get-tuple-element.51.page_b, s32[48]{0:T(128)} %reshape.248.codes, bf16[8,136,512]{2,1,0:T(8,128)(2,1)} %bitcast.53, bf16[8,4,128,128]{3,2,1,0:T(8,128)(2,1)} %turn_keys.2.keys_a_in, ...), custom_call_target="tpu_custom_call" | custom-call | flops 4831838208 | bytes 6291456 | tf_op jit(solution)/shard_map/page_attention/pallas_call | solution.py:229
  50.4 8.8 %collective-permute-done.8.blocks_in = bf16[8,136,512]{2,1,0:T(8,128)(2,1)} collective-permute-done((bf16[8,136,512]{2,1,0:T(8,128)(2,1)S(1)}, bf16[8,136,512]{2,1,0:T(8,128)(2,1)}, u32[]{:S(2)}, u32[]{:S(2)}) %collective-permute-start.8) | collective-permute-done | bytes 1114144 | tf_op jit(solution)/shard_map/ppermute | solution.py:91
  60.9 6.6 %page_attention.5.refs_0_ = bf16[32,400,128]{2,1,0:T(8,128)(2,1)} custom-call(s32[8]{0:T(128)} %get-tuple-element.60.chip_of, s32[8]{0:T(128)} %get-tuple-element.56.page_a, s32[8]{0:T(128)} %get-tuple-element.52.page_b, s32[48]{0:T(128)} %reshape.247.codes, bf16[8,136,512]{2,1,0:T(8,128)(2,1)} %collective-permute-done.9.blocks_in, ...), custom_call_target="tpu_custom_call", output_to_operand_aliasing={{}: (9, {})} | custom-call | flops 4831838208 | bytes 6291456 | tf_op jit(solution)/shard_map/page_attention/pallas_call | solution.py:229
  67.5 6.6 %page_attention.6.refs_0_ = bf16[32,400,128]{2,1,0:T(8,128)(2,1)} custom-call(s32[8]{0:T(128)} %get-tuple-element.61.chip_of, s32[8]{0:T(128)} %get-tuple-element.57.page_a, s32[8]{0:T(128)} %get-tuple-element.53.page_b, s32[48]{0:T(128)} %reshape.246.codes, bf16[8,136,512]{2,1,0:T(8,128)(2,1)} %collective-permute-done.8.blocks_in, ...), custom_call_target="tpu_custom_call", output_to_operand_aliasing={{}: (9, {})} | custom-call | flops 4831838208 | bytes 6291456 | tf_op jit(solution)/shard_map/page_attention/pallas_call | solution.py:229
  74.1 3.7 %collective-permute-done.7.weight_far = bf16[512,2048]{1,0:T(8,128)(2,1)} collective-permute-done((bf16[512,2048]{1,0:T(8,128)(2,1)}, bf16[512,2048]{1,0:T(8,128)(2,1)}, u32[]{:S(2)}, u32[]{:S(2)}) %collective-permute-start.7) | collective-permute-done | bytes 2097184 | tf_op jit(solution)/shard_map/ppermute | solution.py:86
  79.5 6.6 %page_attention.7 = bf16[32,400,128]{2,1,0:T(8,128)(2,1)} custom-call(s32[8]{0:T(128)} %get-tuple-element.62.chip_of, s32[8]{0:T(128)} %get-tuple-element.58.page_a, s32[8]{0:T(128)} %get-tuple-element.54.page_b, s32[48]{0:T(128)} %reshape.245.codes, bf16[8,136,512]{2,1,0:T(8,128)(2,1)} %collective-permute-done.6.blocks_in, ...), custom_call_target="tpu_custom_call", output_to_operand_aliasing={{}: (9, {})} | custom-call | flops 4831838208 | bytes 6291456 | tf_op jit(solution)/shard_map/page_attention/pallas_call | solution.py:229
  86.1 9.1 %all-to-all-start = ((bf16[32,400,128]{2,1,0:T(8,128)(2,1)}), bf16[32,400,128]{2,1,0:T(8,128)(2,1)}, u32[]{:S(2)}, u32[]{:S(2)}) async-start(bf16[32,400,128]{2,1,0:T(8,128)(2,1)} %page_attention.7), calls=%async_computation | async-start | bytes 6553600 | tf_op jit(solution)/shard_map/all_to_all | solution.py:711
  97.4 2.9 %own_attention.1 = (f32[4,128,128]{2,1,0:T(8,128)}, f32[8,128]{1,0:T(8,128)}) custom-call(s32[128,1]{1,0:T(8,128)} %copy.70.request_col, s32[1,128]{1,0:T(1,128)} %bitcast.67, bf16[128,512]{1,0:T(8,128)(2,1)} %queries.1, bf16[128,512]{1,0:T(8,128)(2,1)} %keys.1, bf16[128,512]{1,0:T(8,128)(2,1)} %values.1), custom_call_target="tpu_custom_call" | custom-call | flops 67108864 | bytes 1048576 | tf_op jit(solution)/shard_map/own_attention/pallas_call | solution.py:296
  100.3 36.9 %all-to-all-done.arrived_in = bf16[32,400,128]{2,1,0:T(8,128)(2,1)} async-done(((bf16[32,400,128]{2,1,0:T(8,128)(2,1)}), bf16[32,400,128]{2,1,0:T(8,128)(2,1)}, u32[]{:S(2)}, u32[]{:S(2)}) %all-to-all-start) | async-done | bytes 3276832 | tf_op jit(solution)/shard_map/all_to_all | solution.py:711
  137.2 8.3 %merge_attention.1.att = bf16[128,512]{1,0:T(8,128)(2,1)} custom-call(s32[192]{0:T(256)} %reshape.240.codes, bf16[32,400,128]{2,1,0:T(8,128)(2,1)} %all-to-all-done.arrived_in, f32[4,128,128]{2,1,0:T(8,128)} %get-tuple-element.32.own_in, f32[8,128]{1,0:T(8,128)} %get-tuple-element.33.own_sums_in), custom_call_target="tpu_custom_call" | custom-call | flops 67108864 | bytes 4194304 | tf_op jit(solution)/shard_map/merge_attention/pallas_call | solution.py:394
  145.5 4.5 %collective-permute-start.10 = (bf16[128,512]{1,0:T(8,128)(2,1)}, bf16[128,512]{1,0:T(8,128)(2,1)S(1)}, u32[]{:S(2)}, u32[]{:S(2)}) collective-permute-start(bf16[128,512]{1,0:T(8,128)(2,1)} %merge_attention.1.att), channel_id=1, source_target_pairs={{0,1},{1,0},{2,3},{3,2},{4,5},{5,4},{6,7},{7,6},{8,9},{9,8},{10,11... | collective-permute-start | bytes 393224 | tf_op jit(solution)/shard_map/ppermute | solution.py:716
  153.3 5.6 %project_dispatch.1 = (f32[128,1024]{1,0:T(8,128)}, bf16[1536,1024]{1,0:T(8,128)(2,1)}) custom-call(s32[1]{0:T(128)} %bitcast.side, bf16[128,512]{1,0:T(8,128)(2,1)} %merge_attention.1.att, bf16[128,512]{1,0:T(8,128)(2,1)} %copy-done.5, bf16[512,2048]{1,0:T(8,128)(2,1)} %weight.1, bf16[512,2048]{1,0:T(8,128)(2,1)} %collective-permute-done.7.weight_far, ...), custom_call_target="tpu_custom_call" | custom-call | flops 1342177280 | bytes 10485760 | tf_op jit(solution)/shard_map/project_dispatch/pallas_call | solution.py:447
  158.9 9.5 %all-to-all-start.1 = ((bf16[64,24,1024]{2,1,0:T(8,128)(2,1)}), bf16[64,24,1024]{2,1,0:T(8,128)(2,1)}, u32[]{:S(2)}, u32[]{:S(2)}) async-start(bf16[64,24,1024]{2,1,0:T(8,128)(2,1)} %bitcast.46), calls=%async_computation.1 | async-start | bytes 6291456 | tf_op jit(solution)/shard_map/all_to_all | solution.py:727
  171.3 4.6 %copy.74 = bf16[1,2048,704]{2,1,0:T(8,128)(2,1)} copy(bf16[1,2048,704]{1,2,0:T(8,128)(2,1)} %param.41) | data formatting | bytes 5767168 | tf_op args[13]
  175.9 34.7 %all-to-all-done.1.rows = bf16[64,24,1024]{2,1,0:T(8,128)(2,1)} async-done(((bf16[64,24,1024]{2,1,0:T(8,128)(2,1)}), bf16[64,24,1024]{2,1,0:T(8,128)(2,1)}, u32[]{:S(2)}, u32[]{:S(2)}) %all-to-all-start.1) | async-done | bytes 3145760 | tf_op jit(solution)/shard_map/all_to_all | solution.py:727
  210.5 14.5 %expert.1 = bf16[64,2,24,512]{3,2,1,0:T(8,128)(2,1)} custom-call(bf16[64,24,1024]{2,1,0:T(8,128)(2,1)} %all-to-all-done.1.rows, bf16[2048,704]{1,0:T(8,128)(2,1)} %bitcast.47, bf16[2048,704]{1,0:T(8,128)(2,1)} %bitcast.48, bf16[704,2048]{1,0:T(8,128)(2,1)} %bitcast.73), custom_call_target="tpu_custom_call" | custom-call | flops 6643777536 | bytes 15728640 | tf_op jit(solution)/shard_map/expert/pallas_call | solution.py:533
  225.1 7.5 %all-to-all-start.2 = ((bf16[128,24,512]{2,1,0:T(8,128)(2,1)}), bf16[128,24,512]{2,1,0:T(8,128)(2,1)}, u32[]{:S(2)}, u32[]{:S(2)}) async-start(bf16[128,24,512]{2,1,0:T(8,128)(2,1)} %bitcast.45), calls=%async_computation.2 | async-start | bytes 6291456 | tf_op jit(solution)/shard_map/all_to_all | solution.py:729
  232.7 3.0 %select_convert_fusion.shares = bf16[256,3072]{1,0:T(8,128)(2,1)} fusion(pred[256,3072]{1,0:T(32,128)(4,1)S(1)} %copy-done.3, f32[256]{0:T(256)S(1)} %bitcast.70, f32[256]{0:T(256)S(1)} %bitcast.71, f32[256]{0:T(256)S(1)} %bitcast.72, f32[256]{0:T(256)S(1)} %bitcast.69, s32[3072]{0:T(1024)S(1)} %copy-done.6, s32[256]{0:T(256)S(1)} %bitcast.61, ...), kind=kLoop, calls=%fused_computation.2 | loop fusion | flops 10223616 | bytes 2379776 | tf_op jit(solution)/shard_map/convert_element_type | solution.py:639
  235.6 38.2 %all-to-all-done.2 = bf16[128,24,512]{2,1,0:T(8,128)(2,1)} async-done(((bf16[128,24,512]{2,1,0:T(8,128)(2,1)}), bf16[128,24,512]{2,1,0:T(8,128)(2,1)}, u32[]{:S(2)}, u32[]{:S(2)}) %all-to-all-start.2) | async-done | bytes 3145760 | tf_op jit(solution)/shard_map/all_to_all | solution.py:729
  273.8 3.7 %combine.1 = bf16[128,1024]{1,0:T(8,128)(2,1)} custom-call(f32[128,1024]{1,0:T(8,128)} %get-tuple-element.35.mixed, bf16[256,3072]{1,0:T(8,128)(2,1)} %select_convert_fusion.shares, bf16[3072,512]{1,0:T(8,128)(2,1)} %bitcast.33.rows), custom_call_target="tpu_custom_call" | custom-call | flops 805306368 | bytes 6291456 | tf_op jit(solution)/shard_map/combine/pallas_call | solution.py:582
  (94 shorter events, 42.2 us)
Async XLA Ops:
  0.0 26.9 %copy-start = (s32[1,64]{1,0:T(1,128)S(1)}, s32[1,64]{1,0:T(1,128)}, u32[]{:S(2)}) copy-start(s32[1,64]{1,0:T(1,128)} %param.34) | copy-start | bytes 772
  0.0 12.6 %collective-permute-start.1 = (bf16[8,2,128,512]{3,2,1,0:T(8,128)(2,1)}, bf16[8,2,128,512]{3,2,1,0:T(8,128)(2,1)}, u32[]{:S(2)}, u32[]{:S(2)}) collective-permute-start(bf16[8,2,128,512]{3,2,1,0:T(8,128)(2,1)} %pages_a_in.7), channel_id=1, source_target_pairs={{0,2},{2,0},{4,6},{6,4},{8,10},{10,8},{12,14},{14,12},{16,18},{18,... | collective-permute-start | bytes 6291464 | tf_op jit(solution)/shard_map/ppermute | solution.py:82
  5.7 6.9 %collective-permute-start = (bf16[136,512]{1,0:T(8,128)(2,1)S(1)}, bf16[136,512]{1,0:T(8,128)(2,1)S(1)}, u32[]{:S(2)}, u32[]{:S(2)}) collective-permute-start(bf16[136,512]{1,0:T(8,128)(2,1)S(1)} %get-tuple-element.42), channel_id=1, source_target_pairs={{0,4},{2,6},{4,0},{6,2},{8,12},{10,14},{12,8},{14,10},{16,20},{18,... | collective-permute-start | bytes 417800 | tf_op jit(solution)/shard_map/ppermute | solution.py:81
  8.6 1.3 collective-permute-start.2
  12.6 8.1 %collective-permute-start.3 = (bf16[2,136,512]{2,1,0:T(8,128)(2,1)S(1)}, bf16[2,136,512]{2,1,0:T(8,128)(2,1)S(1)}, u32[]{:S(2)}, u32[]{:S(2)}) collective-permute-start(bf16[2,136,512]{2,1,0:T(8,128)(2,1)S(1)} %get-tuple-element.40), channel_id=1, source_target_pairs={{0,32},{2,10},{4,36},{6,14},{8,40},{10,18},{12,44},{14,22},{16,48}... | collective-permute-start | bytes 835592 | tf_op jit(solution)/shard_map/ppermute | solution.py:88
  14.4 10.5 %collective-permute-start.4 = (bf16[2,136,512]{2,1,0:T(8,128)(2,1)S(1)}, bf16[2,136,512]{2,1,0:T(8,128)(2,1)S(1)}, u32[]{:S(2)}, u32[]{:S(2)}) collective-permute-start(bf16[2,136,512]{2,1,0:T(8,128)(2,1)S(1)} %get-tuple-element.40), channel_id=1, source_target_pairs={{0,64},{2,18},{4,68},{6,22},{8,72},{10,26},{12,76},{14,30},{16,80}... | collective-permute-start | bytes 835592 | tf_op jit(solution)/shard_map/ppermute | solution.py:88
  17.7 7.2 %collective-permute-start.5 = (bf16[2,136,512]{2,1,0:T(8,128)(2,1)S(1)}, bf16[2,136,512]{2,1,0:T(8,128)(2,1)S(1)}, u32[]{:S(2)}, u32[]{:S(2)}) collective-permute-start(bf16[2,136,512]{2,1,0:T(8,128)(2,1)S(1)} %get-tuple-element.40), channel_id=1, source_target_pairs={{0,96},{2,26},{4,100},{6,30},{8,104},{10,2},{12,108},{14,6},{16,11... | collective-permute-start | bytes 835592 | tf_op jit(solution)/shard_map/ppermute | solution.py:88
  25.1 16.0 %copy-start.2 = (bf16[4,2,136,512]{3,2,1,0:T(8,128)(2,1)}, bf16[4,2,136,512]{3,2,1,0:T(8,128)(2,1)S(1)}, u32[]{:S(2)}) copy-start(bf16[4,2,136,512]{3,2,1,0:T(8,128)(2,1)S(1)} %pad_maximum_fusion) | copy-start | bytes 3342340
  25.1 16.1 %collective-permute-start.9 = (bf16[8,136,512]{2,1,0:T(8,128)(2,1)S(1)}, bf16[8,136,512]{2,1,0:T(8,128)(2,1)}, u32[]{:S(2)}, u32[]{:S(2)}) collective-permute-start(bf16[8,136,512]{2,1,0:T(8,128)(2,1)S(1)} %bitcast.49), channel_id=1, source_target_pairs={{0,8},{2,34},{4,12},{6,38},{8,16},{10,42},{12,20},{14,46},{16,24},... | collective-permute-start | bytes 3342344 | tf_op jit(solution)/shard_map/ppermute | solution.py:91
  31.8 45.9 %collective-permute-start.7 = (bf16[512,2048]{1,0:T(8,128)(2,1)}, bf16[512,2048]{1,0:T(8,128)(2,1)}, u32[]{:S(2)}, u32[]{:S(2)}) collective-permute-start(bf16[512,2048]{1,0:T(8,128)(2,1)} %weight.1), channel_id=1, source_target_pairs={{0,1},{1,0},{2,3},{3,2},{4,5},{5,4},{6,7},{7,6},{8,9},{9,8},{10,11... | collective-permute-start | bytes 6291464 | tf_op jit(solution)/shard_map/ppermute | solution.py:86
  33.1 26.1 %collective-permute-start.8 = (bf16[8,136,512]{2,1,0:T(8,128)(2,1)S(1)}, bf16[8,136,512]{2,1,0:T(8,128)(2,1)}, u32[]{:S(2)}, u32[]{:S(2)}) collective-permute-start(bf16[8,136,512]{2,1,0:T(8,128)(2,1)S(1)} %bitcast.50), channel_id=1, source_target_pairs={{0,24},{2,98},{4,28},{6,102},{8,0},{10,106},{12,4},{14,110},{16,8}... | collective-permute-start | bytes 3342344 | tf_op jit(solution)/shard_map/ppermute | solution.py:91
  39.7 34.4 %collective-permute-start.6 = (bf16[8,136,512]{2,1,0:T(8,128)(2,1)S(1)}, bf16[8,136,512]{2,1,0:T(8,128)(2,1)}, u32[]{:S(2)}, u32[]{:S(2)}) collective-permute-start(bf16[8,136,512]{2,1,0:T(8,128)(2,1)S(1)} %bitcast.51), channel_id=1, source_target_pairs={{0,16},{2,66},{4,20},{6,70},{8,24},{10,74},{12,28},{14,78},{16,0},... | collective-permute-start | bytes 3342344 | tf_op jit(solution)/shard_map/ppermute | solution.py:91
  86.1 9.9 %copy-start.10 = (s32[128]{0:T(128)S(1)}, s32[128]{0:T(128)}, u32[]{:S(2)}) copy-start(s32[128]{0:T(128)} %param.32) | copy-start | bytes 1540
  86.1 10.6 %copy-start.8 = (s32[128,4]{0,1:T(4,128)S(1)}, s32[128,4]{0,1:T(4,128)}, u32[]{:S(2)}) copy-start(s32[128,4]{0,1:T(4,128)} %param.36) | copy-start | bytes 6148
  86.1 51.1 %all-to-all-start = ((bf16[32,400,128]{2,1,0:T(8,128)(2,1)}), bf16[32,400,128]{2,1,0:T(8,128)(2,1)}, u32[]{:S(2)}, u32[]{:S(2)}) async-start(bf16[32,400,128]{2,1,0:T(8,128)(2,1)} %page_attention.7), calls=%async_computation | async-start | bytes 6553600 | tf_op jit(solution)/shard_map/all_to_all | solution.py:711
  95.2 54.8 %copy-start.4 = (pred[1536,256]{1,0:T(32,128)(4,1)S(1)}, pred[1536,256]{1,0:T(32,128)(4,1)}, u32[]{:S(2)}) copy-start(pred[1536,256]{1,0:T(32,128)(4,1)} %constant.108.clone) | copy-start | bytes 1179652
  95.2 54.8 %copy-start.7 = (s32[1536]{0:T(1024)S(1)}, s32[1536]{0:T(1024)}, u32[]{:S(2)}) copy-start(s32[1536]{0:T(1024)} %constant.119) | copy-start | bytes 18436
  145.5 7.1 %collective-permute-start.10 = (bf16[128,512]{1,0:T(8,128)(2,1)}, bf16[128,512]{1,0:T(8,128)(2,1)S(1)}, u32[]{:S(2)}, u32[]{:S(2)}) collective-permute-start(bf16[128,512]{1,0:T(8,128)(2,1)} %merge_attention.1.att), channel_id=1, source_target_pairs={{0,1},{1,0},{2,3},{3,2},{4,5},{5,4},{6,7},{7,6},{8,9},{9,8},{10,11... | collective-permute-start | bytes 393224 | tf_op jit(solution)/shard_map/ppermute | solution.py:716
  158.9 9.5 %copy-start.1 = (bf16[1,2048,704]{1,2,0:T(8,128)(2,1)S(1)}, bf16[1,2048,704]{1,2,0:T(8,128)(2,1)}, u32[]{:S(2)}) copy-start(bf16[1,2048,704]{1,2,0:T(8,128)(2,1)} %param.40) | copy-start | bytes 8650756
  158.9 51.7 %all-to-all-start.1 = ((bf16[64,24,1024]{2,1,0:T(8,128)(2,1)}), bf16[64,24,1024]{2,1,0:T(8,128)(2,1)}, u32[]{:S(2)}, u32[]{:S(2)}) async-start(bf16[64,24,1024]{2,1,0:T(8,128)(2,1)} %bitcast.46), calls=%async_computation.1 | async-start | bytes 6291456 | tf_op jit(solution)/shard_map/all_to_all | solution.py:727
  225.0 7.5 %copy-start.9 = (f32[128,4]{0,1:T(4,128)S(1)}, f32[128,4]{0,1:T(4,128)}, u32[]{:S(2)}) copy-start(f32[128,4]{0,1:T(4,128)} %param.37) | copy-start | bytes 6148
  225.1 7.6 %copy-start.3 = (pred[256,3072]{1,0:T(32,128)(4,1)S(1)}, pred[256,3072]{1,0:T(32,128)(4,1)}, u32[]{:S(2)}) copy-start(pred[256,3072]{1,0:T(32,128)(4,1)} %constant.110.clone) | copy-start | bytes 2359300
  225.1 7.6 %copy-start.6 = (s32[3072]{0:T(1024)S(1)}, s32[3072]{0:T(1024)}, u32[]{:S(2)}) copy-start(s32[3072]{0:T(1024)} %constant.120) | copy-start | bytes 36868
  225.1 48.7 %all-to-all-start.2 = ((bf16[128,24,512]{2,1,0:T(8,128)(2,1)}), bf16[128,24,512]{2,1,0:T(8,128)(2,1)}, u32[]{:S(2)}, u32[]{:S(2)}) async-start(bf16[128,24,512]{2,1,0:T(8,128)(2,1)} %bitcast.45), calls=%async_computation.2 | async-start | bytes 6291456 | tf_op jit(solution)/shard_map/all_to_all | solution.py:729
  (1 other events, 0.7 us)

commit v4 on v3

--- a/solution.py
+++ b/solution.py
@@ -77,19 +77,21 @@
     return [[chip * NC + core for chip in range(NCHIP)] for core in range(NC)]
 
 
-def gather_blocks(block, weight, pages, sends):
-    near = lax.ppermute(block, "req", perm_x())
+def gather_near(queries, note, pages, sends):
+    near = lax.ppermute(queries, "req", perm_x())
+    near_note = lax.ppermute(note, "req", perm_x())
     pages = lax.ppermute(pages, "req", perm_core())
     sends = lax.ppermute(sends, "req", perm_core())
-    near, weight, pages, sends = lax.optimization_barrier((near, weight, pages, sends))
-    pair = jnp.stack([block, near])
-    weight_far = lax.ppermute(weight, "tp", [(0, 1), (1, 0)])
-    line = jnp.stack(
-        [pair] + [lax.ppermute(pair, "req", perm_ring(0, step)) for step in (1, 2, 3)]
-    ).reshape(8, *block.shape)
-    return [line] + [
-        lax.ppermute(line, "req", perm_ring(1, step)) for step in (1, 3, 2)
-    ], (weight_far, pages, sends)
+    return near, near_note, pages, sends
+
+
+def gather_line(pair):
+    line = [pair] + [lax.ppermute(pair, "req", perm_ring(0, step)) for step in (1, 2, 3)]
+    return jnp.stack(line).reshape(8, *pair.shape[1:])
+
+
+def gather_rest(line):
+    return [line] + [lax.ppermute(line, "req", perm_ring(1, step)) for step in (1, 3, 2)]
 
 
 def attend(query, key_t, value_1, shift):
@@ -110,9 +112,12 @@
 
 
 def keys_kernel(pages, out):
-    for page in range(pages.shape[0]):
+    def step(page, carry):
         for head in range(HEADS):
             out[page, head] = pages[page, 0, :, head * HD : (head + 1) * HD].T
+        return carry
+
+    lax.fori_loop(0, pages.shape[0], step, 0, unroll=2)
 
 
 def turn_keys(pages):
@@ -120,7 +125,7 @@
     return pl.pallas_call(
         keys_kernel,
         out_shape=jax.ShapeDtypeStruct((count, HEADS, HD, PAGE), BF16),
-        in_specs=[pl.BlockSpec(pages.shape, lambda i: (0, 0, 0, 0))],
+        in_specs=[pl.BlockSpec((count, 1, PAGE, HEADS * HD), lambda i: (0, 0, 0, 0))],
         out_specs=pl.BlockSpec((count, HEADS, HD, PAGE), lambda i: (0, 0, 0, 0)),
         grid=(1,),
         cost_estimate=pl.CostEstimate(
@@ -245,8 +250,8 @@
         ],
         compiler_params=pltpu.CompilerParams(vmem_limit_bytes=62 << 20),
         cost_estimate=pl.CostEstimate(
-            flops=count * HEADS * 12 * ROWS * HD * HD * 8,
-            bytes_accessed=6 << 20,
+            flops=count * HEADS * 16 * ROWS * HD * HD,
+            bytes_accessed=5 << 20,
             transcendentals=count * HEADS * ROWS * 2 * PAGE,
         ),
         name="page_attention",
@@ -504,12 +509,15 @@
             [wide[:, 8:16].reshape(count * 8, half), tail_1.reshape(count * 4, half)], axis=0
         )
         tokens = jnp.concatenate([left.astype(BF16), right.astype(BF16)], axis=1)
-        pl.when(i == 0)(loads[0].wait)
+        if i == 0:
+            loads[0].wait()
         gate_act = jnp.dot(tokens, gate_v[...], preferred_element_type=F32)
-        pl.when(i == 0)(loads[1].wait)
+        if i == 0:
+            loads[1].wait()
         up_act = jnp.dot(tokens, up_v[...], preferred_element_type=F32)
         hidden = (gate_act / (1.0 + jnp.exp(-gate_act)) * up_act).astype(BF16)
-        pl.when(i == 0)(loads[2].wait)
+        if i == 0:
+            loads[2].wait()
         result = jnp.dot(hidden, down_v[...], preferred_element_type=F32)
         for side in range(2):
             cols = [slice((2 * side + q) * quarter, (2 * side + q + 1) * quarter) for q in range(2)]
@@ -522,12 +530,13 @@
         send(i).start()
         return carry
 
-    lax.fori_loop(0, steps, step, 0)
+    for i in range(steps):
+        step(i, 0)
     for i in range(steps):
         send(i).wait()
 
 
-def run_expert(rows, gate, up, down, steps=4):
+def run_expert(rows, gate, up, down, steps=2):
     count = rows.shape[0] // steps
     width, hidden = gate.shape
     return pl.pallas_call(
@@ -676,11 +685,15 @@
 
     note = jnp.zeros((8, queries.shape[1]), BF16)
     note = note.at[0, : NCHIP * SLOTS].set(codes.T.reshape(-1).astype(BF16))
-    pieces, (weight_far, pages_far, sends_far) = gather_blocks(
-        jnp.concatenate([queries, note], axis=0), output_weight, page_store, page_sends
-    )
-    keys_a, keys_b = turn_keys(page_store), turn_keys(pages_far)
-    own, own_sums = own_attention(request_ids, queries, new_keys, new_values)
+    near, near_note, pages_far, sends_far = gather_near(queries, note, page_store, page_sends)
+    near, near_note, far_in, pages_far, sends_far = lax.optimization_barrier(
+        (near, near_note, output_weight, pages_far, sends_far)
+    )
+    weight_far = lax.ppermute(far_in, "tp", swap)
+    pair = jnp.stack(
+        [jnp.concatenate([queries, note], axis=0), jnp.concatenate([near, near_note], axis=0)]
+    )
+    line = gather_line(pair)
 
     table = chip_table()
     order = np.array([0, 1, 3, 2])
@@ -689,10 +702,19 @@
     )
     page_a = page_sends[0][chips * NC + core]
     page_b = sends_far[0][chips * NC + core]
+    keys_a, keys_b = turn_keys(page_store), turn_keys(pages_far)
+    line, keys_a, keys_b, chips, page_a, page_b = lax.optimization_barrier(
+        (line, keys_a, keys_b, chips, page_a, page_b)
+    )
+    pieces = gather_rest(line)
+    own, own_sums = own_attention(request_ids, queries, new_keys, new_values)
+
     parts = None
     for index, piece in enumerate(pieces):
         if index == 3:
-            piece, weight_far = lax.optimization_barrier((piece, weight_far))
+            piece, parts, weight_far = lax.optimization_barrier((piece, parts, weight_far))
+        elif index > 0:
+            piece, parts = lax.optimization_barrier((piece, parts))
         asked = piece[:, TOK, : NCHIP * SLOTS].reshape(8, SLOTS, NCHIP)
         asked = lax.dynamic_index_in_dim(asked, me // NC, 2, keepdims=False)
         rows = slice(8 * index, 8 * index + 8)

time: 279 us -> 270 us (0.968)
  waiting for transfers between devices: 133 us -> 117 us
  starting transfers between devices: 46.4 us -> 54.9 us
    ppermute x10 -> x11, waiting for transfers between devices: 22.6 us -> 7.86 us  [the longest x3 5.47 us: gather_rest(): lax.ppermute(line, 'req', perm_ring(1, step))]
    all_to_all x1, starting transfers between devices: 9.08 us -> 14.4 us  [shards(): lax.all_to_all(parts, 'req', 0, 0, tiled=True, axis_index_groups=core_gro...]
    ppermute x10 -> x11, starting transfers between devices: 15.8 us -> 15.5 us  [the longest x3 5.74 us: gather_line(): lax.ppermute(pair, 'req', perm_ring(0, step))]
  transfers between devices with their start and end apart: 14 -> 15, of which waited for: 10 -> 7; matrix products, arithmetic and copies ran while one was open for 10% -> 11% of each run, Pallas kernels for 10% -> 10%
where the time goes in v4:
time: 270 us; the launch traced here: 269 us
  waiting for transfers between devices  117 us (43%)
  Pallas kernels  64.7 us (24%)
  starting transfers between devices  54.9 us (20%)
  local copies, waits for them, and re-layouts  21.6 us (8%)
  other arithmetic  10.2 us (4%)
    all_to_all x1, waiting for transfers between devices, shards(): lax.all_to_all(result.reshape(2 * NREQ, 2 * CAP, width // 4), ('req', 'tp...  38.2 us
    all_to_all x1, waiting for transfers between devices, shards(): lax.all_to_all(parts, 'req', 0, 0, tiled=True, axis_index_groups=core_gro...  34.8 us
    all_to_all x1, waiting for transfers between devices, shards(): lax.all_to_all(sent.reshape(NREQ, 2 * CAP, half), 'req', 0, 0, tiled=True)  34.7 us
    pallas_call x4, Pallas kernels, page_attention(): pl.pallas_call(page_kernel, out_shape=jax.ShapeDtypeStruct((NCHIP, BLOCK,...  26.3 us
    all_to_all x1, starting transfers between devices, shards(): lax.all_to_all(parts, 'req', 0, 0, tiled=True, axis_index_groups=core_gro...  14.4 us
    pallas_call x1, Pallas kernels, run_expert(): pl.pallas_call(expert_kernel, out_shape=jax.ShapeDtypeStruct((rows.shape[...  12.4 us
    all_to_all x1, starting transfers between devices, shards(): lax.all_to_all(sent.reshape(NREQ, 2 * CAP, half), 'req', 0, 0, tiled=True)  11 us
    unnamed x27, local copies, waits for them, and re-layouts  9.53 us
  transfers between devices with their start and end apart: 15, of which 7 were waited for; matrix products, arithmetic and copies ran while one was open for 11% of the time, Pallas kernels for 10%

profile of v4, /device:TPU:1, one launch (start us, length us, event | category | flops | bytes accessed | tf_op | source)
XLA Modules:
  0.0 268.7 jit_solution(13964194449362431526)
XLA Ops:
  1.4 2.8 %collective-permute-start = (bf16[128,512]{1,0:T(8,128)(2,1)}, bf16[128,512]{1,0:T(8,128)(2,1)S(1)}, u32[]{:S(2)}, u32[]{:S(2)}) collective-permute-start(bf16[128,512]{1,0:T(8,128)(2,1)} %queries.1), channel_id=1, source_target_pairs={{0,4},{2,6},{4,0},{6,2},{8,12},{10,14},{12,8},{14,10},{16,20},{18,... | collective-permute-start | bytes 393224 | tf_op jit(solution)/shard_map/ppermute | solution.py:81
  13.8 3.3 %collective-permute-start.5 = (bf16[2,136,512]{2,1,0:T(8,128)(2,1)S(1)}, bf16[2,136,512]{2,1,0:T(8,128)(2,1)S(1)}, u32[]{:S(2)}, u32[]{:S(2)}) collective-permute-start(bf16[2,136,512]{2,1,0:T(8,128)(2,1)S(1)} %get-tuple-element.64), channel_id=1, source_target_pairs={{0,64},{2,18},{4,68},{6,22},{8,72},{10,26},{12,76},{14,30},{16,80}... | collective-permute-start | bytes 835592 | tf_op jit(solution)/shard_map/ppermute | solution.py:89
  19.9 2.7 %turn_keys.2.keys_a_in = bf16[8,4,128,128]{3,2,1,0:T(8,128)(2,1)} custom-call(bf16[8,2,128,512]{3,2,1,0:T(8,128)(2,1)} %pages_a_in.7), custom_call_target="tpu_custom_call" | custom-call | flops 33554432 | bytes 3145728 | tf_op jit(solution)/shard_map/turn_keys/pallas_call | solution.py:125
  24.0 2.7 %turn_keys.3.keys_b_in = bf16[8,4,128,128]{3,2,1,0:T(8,128)(2,1)} custom-call(bf16[8,2,128,512]{3,2,1,0:T(8,128)(2,1)} %collective-permute-done.2.pages.pages_b_in), custom_call_target="tpu_custom_call" | custom-call | flops 33554432 | bytes 3145728 | tf_op jit(solution)/shard_map/turn_keys/pallas_call | solution.py:125
  35.4 6.6 %page_attention.4.refs_0_ = bf16[32,400,128]{2,1,0:T(8,128)(2,1)} custom-call(s32[8]{0:T(128)} %get-tuple-element.81.chip_of, s32[8]{0:T(128)} %get-tuple-element.88.page_a, s32[8]{0:T(128)} %get-tuple-element.73.page_b, s32[48]{0:T(128)} %reshape.241.codes, bf16[8,136,512]{2,1,0:T(8,128)(2,1)} %bitcast.44, bf16[8,4,128,128]{3,2,1,0:T(8,128)(2,1)} %turn_keys.2.keys_a_in, ...), custom_call_target="tpu_custom_call" | custom-call | flops 805306368 | bytes 5242880 | tf_op jit(solution)/shard_map/page_attention/pallas_call | solution.py:234
  46.4 6.6 %page_attention.5.refs_0_ = bf16[32,400,128]{2,1,0:T(8,128)(2,1)} custom-call(s32[8]{0:T(128)} %get-tuple-element.82.chip_of, s32[8]{0:T(128)} %get-tuple-element.87.page_a, s32[8]{0:T(128)} %get-tuple-element.74.page_b, s32[48]{0:T(128)} %reshape.242.codes, bf16[8,136,512]{2,1,0:T(8,128)(2,1)} %collective-permute-done.9.blocks_in, ...), custom_call_target="tpu_custom_call", output_to_operand_aliasing={{}: (9, {})} | custom-call | flops 805306368 | bytes 5242880 | tf_op jit(solution)/shard_map/page_attention/pallas_call | solution.py:234
  53.0 2.8 %collective-permute-done.8.blocks_in = bf16[8,136,512]{2,1,0:T(8,128)(2,1)} collective-permute-done((bf16[8,136,512]{2,1,0:T(8,128)(2,1)S(1)}, bf16[8,136,512]{2,1,0:T(8,128)(2,1)}, u32[]{:S(2)}, u32[]{:S(2)}) %collective-permute-start.8) | collective-permute-done | bytes 1114144 | tf_op jit(solution)/shard_map/ppermute | solution.py:94
  57.6 6.6 %page_attention.6.refs_0_ = bf16[32,400,128]{2,1,0:T(8,128)(2,1)} custom-call(s32[8]{0:T(128)} %get-tuple-element.83.chip_of, s32[8]{0:T(128)} %get-tuple-element.86.page_a, s32[8]{0:T(128)} %get-tuple-element.75.page_b, s32[48]{0:T(128)} %reshape.243.codes, bf16[8,136,512]{2,1,0:T(8,128)(2,1)} %collective-permute-done.8.blocks_in, ...), custom_call_target="tpu_custom_call", output_to_operand_aliasing={{}: (9, {})} | custom-call | flops 805306368 | bytes 5242880 | tf_op jit(solution)/shard_map/page_attention/pallas_call | solution.py:234
  66.0 6.6 %page_attention.7 = bf16[32,400,128]{2,1,0:T(8,128)(2,1)} custom-call(s32[8]{0:T(128)} %get-tuple-element.84.chip_of, s32[8]{0:T(128)} %get-tuple-element.85.page_a, s32[8]{0:T(128)} %get-tuple-element.76.page_b, s32[48]{0:T(128)} %reshape.244.codes, bf16[8,136,512]{2,1,0:T(8,128)(2,1)} %collective-permute-done.7.blocks_in, ...), custom_call_target="tpu_custom_call", output_to_operand_aliasing={{}: (9, {})} | custom-call | flops 805306368 | bytes 5242880 | tf_op jit(solution)/shard_map/page_attention/pallas_call | solution.py:234
  72.6 14.4 %all-to-all-start = ((bf16[32,400,128]{2,1,0:T(8,128)(2,1)}), bf16[32,400,128]{2,1,0:T(8,128)(2,1)}, u32[]{:S(2)}, u32[]{:S(2)}) async-start(bf16[32,400,128]{2,1,0:T(8,128)(2,1)} %page_attention.7), calls=%async_computation | async-start | bytes 6553600 | tf_op jit(solution)/shard_map/all_to_all | solution.py:733
  89.2 2.9 %own_attention.1 = (f32[4,128,128]{2,1,0:T(8,128)}, f32[8,128]{1,0:T(8,128)}) custom-call(s32[128,1]{1,0:T(8,128)} %copy.70.request_col, s32[1,128]{1,0:T(1,128)} %bitcast.61, bf16[128,512]{1,0:T(8,128)(2,1)} %queries.1, bf16[128,512]{1,0:T(8,128)(2,1)} %keys.1, bf16[128,512]{1,0:T(8,128)(2,1)} %values.1), custom_call_target="tpu_custom_call" | custom-call | flops 67108864 | bytes 1048576 | tf_op jit(solution)/shard_map/own_attention/pallas_call | solution.py:301
  92.1 34.8 %all-to-all-done.arrived_in = bf16[32,400,128]{2,1,0:T(8,128)(2,1)} async-done(((bf16[32,400,128]{2,1,0:T(8,128)(2,1)}), bf16[32,400,128]{2,1,0:T(8,128)(2,1)}, u32[]{:S(2)}, u32[]{:S(2)}) %all-to-all-start) | async-done | bytes 3276832 | tf_op jit(solution)/shard_map/all_to_all | solution.py:733
  126.9 8.3 %merge_attention.1.att = bf16[128,512]{1,0:T(8,128)(2,1)} custom-call(s32[192]{0:T(256)} %reshape.236.codes, bf16[32,400,128]{2,1,0:T(8,128)(2,1)} %all-to-all-done.arrived_in, f32[4,128,128]{2,1,0:T(8,128)} %get-tuple-element.56.own_in, f32[8,128]{1,0:T(8,128)} %get-tuple-element.57.own_sums_in), custom_call_target="tpu_custom_call" | custom-call | flops 67108864 | bytes 4194304 | tf_op jit(solution)/shard_map/merge_attention/pallas_call | solution.py:399
  135.3 6.4 %collective-permute-start.11 = (bf16[128,512]{1,0:T(8,128)(2,1)}, bf16[128,512]{1,0:T(8,128)(2,1)S(1)}, u32[]{:S(2)}, u32[]{:S(2)}) collective-permute-start(bf16[128,512]{1,0:T(8,128)(2,1)} %merge_attention.1.att), channel_id=1, source_target_pairs={{0,1},{1,0},{2,3},{3,2},{4,5},{5,4},{6,7},{7,6},{8,9},{9,8},{10,11... | collective-permute-start | bytes 393224 | tf_op jit(solution)/shard_map/ppermute | solution.py:738
  144.9 5.6 %project_dispatch.1 = (f32[128,1024]{1,0:T(8,128)}, bf16[1536,1024]{1,0:T(8,128)(2,1)}) custom-call(s32[1]{0:T(128)} %bitcast.side, bf16[128,512]{1,0:T(8,128)(2,1)} %merge_attention.1.att, bf16[128,512]{1,0:T(8,128)(2,1)} %copy-done.5, bf16[512,2048]{1,0:T(8,128)(2,1)} %weight.1, bf16[512,2048]{1,0:T(8,128)(2,1)} %collective-permute-done.10.weight_far, ...), custom_call_target="tpu_custom_call" | custom-call | flops 1342177280 | bytes 10485760 | tf_op jit(solution)/shard_map/project_dispatch/pallas_call | solution.py:452
  150.5 11.0 %all-to-all-start.1 = ((bf16[64,24,1024]{2,1,0:T(8,128)(2,1)}), bf16[64,24,1024]{2,1,0:T(8,128)(2,1)}, u32[]{:S(2)}, u32[]{:S(2)}) async-start(bf16[64,24,1024]{2,1,0:T(8,128)(2,1)} %bitcast.46), calls=%async_computation.1 | async-start | bytes 6291456 | tf_op jit(solution)/shard_map/all_to_all | solution.py:749
  161.5 2.9 %copy.73 = bf16[1,2048,704]{2,1,0:T(8,128)(2,1)} copy(bf16[1,2048,704]{1,2,0:T(8,128)(2,1)S(1)} %copy-done.1) | data formatting | bytes 5767168 | tf_op args[12]
  164.4 4.6 %copy.74 = bf16[1,2048,704]{2,1,0:T(8,128)(2,1)} copy(bf16[1,2048,704]{1,2,0:T(8,128)(2,1)} %param.41) | data formatting | bytes 5767168 | tf_op args[13]
  169.0 34.7 %all-to-all-done.1.rows = bf16[64,24,1024]{2,1,0:T(8,128)(2,1)} async-done(((bf16[64,24,1024]{2,1,0:T(8,128)(2,1)}), bf16[64,24,1024]{2,1,0:T(8,128)(2,1)}, u32[]{:S(2)}, u32[]{:S(2)}) %all-to-all-start.1) | async-done | bytes 3145760 | tf_op jit(solution)/shard_map/all_to_all | solution.py:749
  203.7 12.4 %expert.1 = bf16[64,2,24,512]{3,2,1,0:T(8,128)(2,1)} custom-call(bf16[64,24,1024]{2,1,0:T(8,128)(2,1)} %all-to-all-done.1.rows, bf16[2048,704]{1,0:T(8,128)(2,1)} %bitcast.47, bf16[2048,704]{1,0:T(8,128)(2,1)} %bitcast.48, bf16[704,2048]{1,0:T(8,128)(2,1)} %bitcast.67), custom_call_target="tpu_custom_call" | custom-call | flops 6643777536 | bytes 15728640 | tf_op jit(solution)/shard_map/expert/pallas_call | solution.py:542
  216.1 7.5 %all-to-all-start.2 = ((bf16[128,24,512]{2,1,0:T(8,128)(2,1)}), bf16[128,24,512]{2,1,0:T(8,128)(2,1)}, u32[]{:S(2)}, u32[]{:S(2)}) async-start(bf16[128,24,512]{2,1,0:T(8,128)(2,1)} %bitcast.45), calls=%async_computation.2 | async-start | bytes 6291456 | tf_op jit(solution)/shard_map/all_to_all | solution.py:751
  223.7 3.0 %select_convert_fusion.shares = bf16[256,3072]{1,0:T(8,128)(2,1)} fusion(pred[256,3072]{1,0:T(32,128)(4,1)S(1)} %copy-done.2, f32[256]{0:T(256)S(1)} %bitcast.64, f32[256]{0:T(256)S(1)} %bitcast.65, f32[256]{0:T(256)S(1)} %bitcast.66, f32[256]{0:T(256)S(1)} %bitcast.63, s32[3072]{0:T(1024)S(1)} %copy-done.6, s32[256]{0:T(256)S(1)} %bitcast.55, ...), kind=kLoop, calls=%fused_computation.2 | loop fusion | flops 10223616 | bytes 2379776 | tf_op jit(solution)/shard_map/convert_element_type | solution.py:648
  226.6 38.2 %all-to-all-done.2 = bf16[128,24,512]{2,1,0:T(8,128)(2,1)} async-done(((bf16[128,24,512]{2,1,0:T(8,128)(2,1)}), bf16[128,24,512]{2,1,0:T(8,128)(2,1)}, u32[]{:S(2)}, u32[]{:S(2)}) %all-to-all-start.2) | async-done | bytes 3145760 | tf_op jit(solution)/shard_map/all_to_all | solution.py:751
  264.8 3.7 %combine.1 = bf16[128,1024]{1,0:T(8,128)(2,1)} custom-call(f32[128,1024]{1,0:T(8,128)} %get-tuple-element.59.mixed, bf16[256,3072]{1,0:T(8,128)(2,1)} %select_convert_fusion.shares, bf16[3072,512]{1,0:T(8,128)(2,1)} %bitcast.30.rows), custom_call_target="tpu_custom_call" | custom-call | flops 805306368 | bytes 6291456 | tf_op jit(solution)/shard_map/combine/pallas_call | solution.py:591
  (98 shorter events, 37.1 us)
Async XLA Ops:
  0.0 11.7 %collective-permute-start.2 = (bf16[8,2,128,512]{3,2,1,0:T(8,128)(2,1)}, bf16[8,2,128,512]{3,2,1,0:T(8,128)(2,1)}, u32[]{:S(2)}, u32[]{:S(2)}) collective-permute-start(bf16[8,2,128,512]{3,2,1,0:T(8,128)(2,1)} %pages_a_in.7), channel_id=1, source_target_pairs={{0,2},{2,0},{4,6},{6,4},{8,10},{10,8},{12,14},{14,12},{16,18},{18,... | collective-permute-start | bytes 6291464 | tf_op jit(solution)/shard_map/ppermute | solution.py:83
  1.4 10.3 %collective-permute-start = (bf16[128,512]{1,0:T(8,128)(2,1)}, bf16[128,512]{1,0:T(8,128)(2,1)S(1)}, u32[]{:S(2)}, u32[]{:S(2)}) collective-permute-start(bf16[128,512]{1,0:T(8,128)(2,1)} %queries.1), channel_id=1, source_target_pairs={{0,4},{2,6},{4,0},{6,2},{8,12},{10,14},{12,8},{14,10},{16,20},{18,... | collective-permute-start | bytes 393224 | tf_op jit(solution)/shard_map/ppermute | solution.py:81
  7.6 4.1 %collective-permute-start.1 = (bf16[8,512]{1,0:T(8,128)(2,1)S(1)}, bf16[8,512]{1,0:T(8,128)(2,1)S(1)}, u32[]{:S(2)}, u32[]{:S(2)}) collective-permute-start(bf16[8,512]{1,0:T(8,128)(2,1)S(1)} %scatter.4), channel_id=1, source_target_pairs={{0,4},{2,6},{4,0},{6,2},{8,12},{10,14},{12,8},{14,10},{16,20},{18,... | collective-permute-start | bytes 24584 | tf_op jit(solution)/shard_map/ppermute | solution.py:82
  7.8 1.5 collective-permute-start.3
  11.7 52.5 %collective-permute-start.10 = (bf16[512,2048]{1,0:T(8,128)(2,1)}, bf16[512,2048]{1,0:T(8,128)(2,1)}, u32[]{:S(2)}, u32[]{:S(2)}) collective-permute-start(bf16[512,2048]{1,0:T(8,128)(2,1)} %weight.1), channel_id=1, source_target_pairs={{0,1},{1,0},{2,3},{3,2},{4,5},{5,4},{6,7},{7,6},{8,9},{9,8},{10,11... | collective-permute-start | bytes 6291464 | tf_op jit(solution)/shard_map/ppermute | solution.py:692
  12.1 14.7 %collective-permute-start.4 = (bf16[2,136,512]{2,1,0:T(8,128)(2,1)S(1)}, bf16[2,136,512]{2,1,0:T(8,128)(2,1)S(1)}, u32[]{:S(2)}, u32[]{:S(2)}) collective-permute-start(bf16[2,136,512]{2,1,0:T(8,128)(2,1)S(1)} %get-tuple-element.64), channel_id=1, source_target_pairs={{0,32},{2,10},{4,36},{6,14},{8,40},{10,18},{12,44},{14,22},{16,48}... | collective-permute-start | bytes 835592 | tf_op jit(solution)/shard_map/ppermute | solution.py:89
  13.8 12.9 %collective-permute-start.5 = (bf16[2,136,512]{2,1,0:T(8,128)(2,1)S(1)}, bf16[2,136,512]{2,1,0:T(8,128)(2,1)S(1)}, u32[]{:S(2)}, u32[]{:S(2)}) collective-permute-start(bf16[2,136,512]{2,1,0:T(8,128)(2,1)S(1)} %get-tuple-element.64), channel_id=1, source_target_pairs={{0,64},{2,18},{4,68},{6,22},{8,72},{10,26},{12,76},{14,30},{16,80}... | collective-permute-start | bytes 835592 | tf_op jit(solution)/shard_map/ppermute | solution.py:89
  17.1 9.6 %collective-permute-start.6 = (bf16[2,136,512]{2,1,0:T(8,128)(2,1)S(1)}, bf16[2,136,512]{2,1,0:T(8,128)(2,1)S(1)}, u32[]{:S(2)}, u32[]{:S(2)}) collective-permute-start(bf16[2,136,512]{2,1,0:T(8,128)(2,1)S(1)} %get-tuple-element.64), channel_id=1, source_target_pairs={{0,96},{2,26},{4,100},{6,30},{8,104},{10,2},{12,108},{14,6},{16,11... | collective-permute-start | bytes 835592 | tf_op jit(solution)/shard_map/ppermute | solution.py:89
  28.6 6.9 %copy-start = (bf16[4,2,136,512]{3,2,1,0:T(8,128)(2,1)}, bf16[4,2,136,512]{3,2,1,0:T(8,128)(2,1)S(1)}, u32[]{:S(2)}) copy-start(bf16[4,2,136,512]{3,2,1,0:T(8,128)(2,1)S(1)} %pad_maximum_fusion) | copy-start | bytes 3342340
  28.6 16.1 %collective-permute-start.9 = (bf16[8,136,512]{2,1,0:T(8,128)(2,1)S(1)}, bf16[8,136,512]{2,1,0:T(8,128)(2,1)}, u32[]{:S(2)}, u32[]{:S(2)}) collective-permute-start(bf16[8,136,512]{2,1,0:T(8,128)(2,1)S(1)} %bitcast.40), channel_id=1, source_target_pairs={{0,8},{2,34},{4,12},{6,38},{8,16},{10,42},{12,20},{14,46},{16,24},... | collective-permute-start | bytes 3342344 | tf_op jit(solution)/shard_map/ppermute | solution.py:94
  29.9 25.9 %collective-permute-start.8 = (bf16[8,136,512]{2,1,0:T(8,128)(2,1)S(1)}, bf16[8,136,512]{2,1,0:T(8,128)(2,1)}, u32[]{:S(2)}, u32[]{:S(2)}) collective-permute-start(bf16[8,136,512]{2,1,0:T(8,128)(2,1)S(1)} %bitcast.41), channel_id=1, source_target_pairs={{0,24},{2,98},{4,28},{6,102},{8,0},{10,106},{12,4},{14,110},{16,8}... | collective-permute-start | bytes 3342344 | tf_op jit(solution)/shard_map/ppermute | solution.py:94
  31.4 32.7 %collective-permute-start.7 = (bf16[8,136,512]{2,1,0:T(8,128)(2,1)S(1)}, bf16[8,136,512]{2,1,0:T(8,128)(2,1)}, u32[]{:S(2)}, u32[]{:S(2)}) collective-permute-start(bf16[8,136,512]{2,1,0:T(8,128)(2,1)S(1)} %bitcast.42), channel_id=1, source_target_pairs={{0,16},{2,66},{4,20},{6,70},{8,24},{10,74},{12,28},{14,78},{16,0},... | collective-permute-start | bytes 3342344 | tf_op jit(solution)/shard_map/ppermute | solution.py:94
  72.5 15.2 %copy-start.10 = (s32[128]{0:T(128)S(1)}, s32[128]{0:T(128)}, u32[]{:S(2)}) copy-start(s32[128]{0:T(128)} %param.32) | copy-start | bytes 1540
  72.6 15.9 %copy-start.8 = (s32[128,4]{0,1:T(4,128)S(1)}, s32[128,4]{0,1:T(4,128)}, u32[]{:S(2)}) copy-start(s32[128,4]{0,1:T(4,128)} %param.36) | copy-start | bytes 6148
  72.6 54.4 %all-to-all-start = ((bf16[32,400,128]{2,1,0:T(8,128)(2,1)}), bf16[32,400,128]{2,1,0:T(8,128)(2,1)}, u32[]{:S(2)}, u32[]{:S(2)}) async-start(bf16[32,400,128]{2,1,0:T(8,128)(2,1)} %page_attention.7), calls=%async_computation | async-start | bytes 6553600 | tf_op jit(solution)/shard_map/all_to_all | solution.py:733
  87.0 54.6 %copy-start.3 = (pred[1536,256]{1,0:T(32,128)(4,1)S(1)}, pred[1536,256]{1,0:T(32,128)(4,1)}, u32[]{:S(2)}) copy-start(pred[1536,256]{1,0:T(32,128)(4,1)} %constant.108.clone) | copy-start | bytes 1179652
  87.0 54.6 %copy-start.7 = (s32[1536]{0:T(1024)S(1)}, s32[1536]{0:T(1024)}, u32[]{:S(2)}) copy-start(s32[1536]{0:T(1024)} %constant.119) | copy-start | bytes 18436
  135.3 9.0 %collective-permute-start.11 = (bf16[128,512]{1,0:T(8,128)(2,1)}, bf16[128,512]{1,0:T(8,128)(2,1)S(1)}, u32[]{:S(2)}, u32[]{:S(2)}) collective-permute-start(bf16[128,512]{1,0:T(8,128)(2,1)} %merge_attention.1.att), channel_id=1, source_target_pairs={{0,1},{1,0},{2,3},{3,2},{4,5},{5,4},{6,7},{7,6},{8,9},{9,8},{10,11... | collective-permute-start | bytes 393224 | tf_op jit(solution)/shard_map/ppermute | solution.py:738
  150.5 11.0 %copy-start.1 = (bf16[1,2048,704]{1,2,0:T(8,128)(2,1)S(1)}, bf16[1,2048,704]{1,2,0:T(8,128)(2,1)}, u32[]{:S(2)}) copy-start(bf16[1,2048,704]{1,2,0:T(8,128)(2,1)} %param.40) | copy-start | bytes 8650756
  150.5 53.2 %all-to-all-start.1 = ((bf16[64,24,1024]{2,1,0:T(8,128)(2,1)}), bf16[64,24,1024]{2,1,0:T(8,128)(2,1)}, u32[]{:S(2)}, u32[]{:S(2)}) async-start(bf16[64,24,1024]{2,1,0:T(8,128)(2,1)} %bitcast.46), calls=%async_computation.1 | async-start | bytes 6291456 | tf_op jit(solution)/shard_map/all_to_all | solution.py:749
  216.0 7.5 %copy-start.9 = (f32[128,4]{0,1:T(4,128)S(1)}, f32[128,4]{0,1:T(4,128)}, u32[]{:S(2)}) copy-start(f32[128,4]{0,1:T(4,128)} %param.37) | copy-start | bytes 6148
  216.1 7.6 %copy-start.2 = (pred[256,3072]{1,0:T(32,128)(4,1)S(1)}, pred[256,3072]{1,0:T(32,128)(4,1)}, u32[]{:S(2)}) copy-start(pred[256,3072]{1,0:T(32,128)(4,1)} %constant.110.clone) | copy-start | bytes 2359300
  216.1 7.6 %copy-start.6 = (s32[3072]{0:T(1024)S(1)}, s32[3072]{0:T(1024)}, u32[]{:S(2)}) copy-start(s32[3072]{0:T(1024)} %constant.120) | copy-start | bytes 36868
  216.1 48.8 %all-to-all-start.2 = ((bf16[128,24,512]{2,1,0:T(8,128)(2,1)}), bf16[128,24,512]{2,1,0:T(8,128)(2,1)}, u32[]{:S(2)}, u32[]{:S(2)}) async-start(bf16[128,24,512]{2,1,0:T(8,128)(2,1)} %bitcast.45), calls=%async_computation.2 | async-start | bytes 6291456 | tf_op jit(solution)/shard_map/all_to_all | solution.py:751
  (2 other events, 1.4 us)

commit v5 on v4

--- a/solution.py
+++ b/solution.py
@@ -77,14 +77,6 @@
     return [[chip * NC + core for chip in range(NCHIP)] for core in range(NC)]
 
 
-def gather_near(queries, note, pages, sends):
-    near = lax.ppermute(queries, "req", perm_x())
-    near_note = lax.ppermute(note, "req", perm_x())
-    pages = lax.ppermute(pages, "req", perm_core())
-    sends = lax.ppermute(sends, "req", perm_core())
-    return near, near_note, pages, sends
-
-
 def gather_line(pair):
     line = [pair] + [lax.ppermute(pair, "req", perm_ring(0, step)) for step in (1, 2, 3)]
     return jnp.stack(line).reshape(8, *pair.shape[1:])
@@ -111,43 +103,15 @@
     return jnp.where(head == 3, rows[3], tile)
 
 
-def keys_kernel(pages, out):
-    def step(page, carry):
-        for head in range(HEADS):
-            out[page, head] = pages[page, 0, :, head * HD : (head + 1) * HD].T
-        return carry
-
-    lax.fori_loop(0, pages.shape[0], step, 0, unroll=2)
-
-
-def turn_keys(pages):
-    count = pages.shape[0]
-    return pl.pallas_call(
-        keys_kernel,
-        out_shape=jax.ShapeDtypeStruct((count, HEADS, HD, PAGE), BF16),
-        in_specs=[pl.BlockSpec((count, 1, PAGE, HEADS * HD), lambda i: (0, 0, 0, 0))],
-        out_specs=pl.BlockSpec((count, HEADS, HD, PAGE), lambda i: (0, 0, 0, 0)),
-        grid=(1,),
-        cost_estimate=pl.CostEstimate(
-            flops=32 << 20, bytes_accessed=3 << 20, transcendentals=0
-        ),
-        compiler_params=pltpu.CompilerParams(vmem_limit_bytes=62 << 20),
-        name="turn_keys",
-    )(pages)
-
-
-def page_kernel(chip_of, page_a, page_b, codes, blocks_in, keys_a_in, keys_b_in, pages_a_in, pages_b_in, *refs):
-    out, blocks, keys_a, keys_b, values_a, values_b, held, sems, load_sems = refs[-9:]
+def page_kernel(chip_of, page_a, page_b, codes, pages_a_in, pages_b_in, *refs):
+    out, blocks, pages_a, pages_b, held, sems, load_sems = refs[-7:]
+    count = held.shape[0]
+    pieces = refs[: count // 8]
     loads = [
         pltpu.make_async_copy(source, target, load_sems.at[n])
         for n, (source, target) in enumerate(
-            (
-                (keys_a_in, keys_a),
-                (keys_b_in, keys_b),
-                (blocks_in, blocks),
-                (pages_a_in.at[:, 1], values_a),
-                (pages_b_in.at[:, 1], values_b),
-            )
+            [(pages_a_in, pages_a), (pages_b_in, pages_b)]
+            + [(piece, blocks.at[pl.ds(8 * n, 8)]) for n, piece in enumerate(pieces)]
         )
     ]
     for load in loads:
@@ -186,8 +150,13 @@
             query = jnp.concatenate(
                 [blocks[i, pl.ds(first[j], 16), cols] for j in range(SLOTS)], axis=0
             )
-            key_t = jnp.concatenate([keys_a[pa, head], keys_b[pb, head]], axis=1)
-            scores.append(jnp.dot(query, key_t, preferred_element_type=F32) + bias)
+            key = jnp.concatenate([pages_a[pa, 0, :, cols], pages_b[pb, 0, :, cols]], axis=0)
+            scores.append(
+                lax.dot_general(
+                    query, key, (((1,), (1,)), ((), ())), preferred_element_type=F32
+                )
+                + bias
+            )
         tops = [jnp.max(s, axis=1, keepdims=True) for s in scores]
         probs = [
             jnp.exp2((s - t) * (SCALE * LOG2E)).astype(BF16) for s, t in zip(scores, tops)
@@ -197,8 +166,8 @@
             cols = slice(head * HD, (head + 1) * HD)
             value_1 = jnp.concatenate(
                 [
-                    jnp.concatenate([values_a[pa, :, cols], ones], axis=1),
-                    jnp.concatenate([values_b[pb, :, cols], ones], axis=1),
+                    jnp.concatenate([pages_a[pa, 1, :, cols], ones], axis=1),
+                    jnp.concatenate([pages_b[pb, 1, :, cols], ones], axis=1),
                 ],
                 axis=0,
             )
@@ -223,30 +192,26 @@
         copy(i).start()
         return carry
 
-    count = blocks.shape[0]
     lax.fori_loop(0, count, step, 0, unroll=4)
     lax.fori_loop(0, count, lambda i, carry: (copy(i).wait(), carry)[1], 0)
 
 
-def page_attention(chip_of, page_a, page_b, codes, blocks, keys_a, keys_b, pages_a, pages_b, last):
-    count = blocks.shape[0]
+def page_attention(chip_of, page_a, page_b, codes, pages_a, pages_b, pieces, last):
+    count = 8 * len(pieces)
     before = [] if last is None else [last]
     return pl.pallas_call(
         page_kernel,
         out_shape=jax.ShapeDtypeStruct((NCHIP, BLOCK, HD), BF16),
-        in_specs=[smem()] * 4
-        + [hbm()] * (5 + len(before)),
+        in_specs=[smem()] * 4 + [hbm()] * (2 + len(pieces) + len(before)),
         out_specs=hbm(),
-        input_output_aliases={9: 0} if before else {},
+        input_output_aliases={6 + len(pieces): 0} if before else {},
         scratch_shapes=[
-            pltpu.VMEM(blocks.shape, BF16),
-            pltpu.VMEM(keys_a.shape, BF16),
-            pltpu.VMEM(keys_b.shape, BF16),
-            pltpu.VMEM((pages_a.shape[0], PAGE, HEADS * HD), BF16),
-            pltpu.VMEM((pages_b.shape[0], PAGE, HEADS * HD), BF16),
+            pltpu.VMEM((count, *pieces[0].shape[1:]), BF16),
+            pltpu.VMEM(pages_a.shape, BF16),
+            pltpu.VMEM(pages_b.shape, BF16),
             pltpu.VMEM((count, BLOCK, HD), BF16),
             pltpu.SemaphoreType.DMA((count,)),
-            pltpu.SemaphoreType.DMA((5,)),
+            pltpu.SemaphoreType.DMA((2 + len(pieces),)),
         ],
         compiler_params=pltpu.CompilerParams(vmem_limit_bytes=62 << 20),
         cost_estimate=pl.CostEstimate(
@@ -255,7 +220,7 @@
             transcendentals=count * HEADS * ROWS * 2 * PAGE,
         ),
         name="page_attention",
-    )(chip_of, page_a, page_b, codes, blocks, keys_a, keys_b, pages_a, pages_b, *before)
+    )(chip_of, page_a, page_b, codes, pages_a, pages_b, *pieces, *before)
 
 
 def smem():
@@ -336,7 +301,6 @@
         load.start()
     row = lax.broadcasted_iota(jnp.int32, (16, TOK), 0)
     offset = lax.broadcasted_iota(jnp.int32, (16, TOK), 1) - row
-    ones = jnp.ones((2 * TOK, HD), BF16)
 
     def halves(tile):
         high = tile.astype(BF16).astype(F32)
@@ -356,6 +320,7 @@
                     )
                 )
         picked = jnp.concatenate(blocks, axis=0).astype(BF16)
+        ones = jnp.ones((len(parts) * TOK, HD), BF16)
         return jnp.dot(picked, ones, preferred_element_type=F32)
 
     def collect(p, top):
@@ -375,10 +340,10 @@
     acc[...] = own[...] * on_rows(halves(share), whole).reshape(HEADS, TOK, HD)
 
     def add(p, low):
-        share = jnp.exp(tiles[p] - top)
+        share = jnp.exp(tiles[p] - top).astype(BF16).astype(F32)
         code = [codes[p * SLOTS + j] for j in range(SLOTS)]
         masks = [offset == jnp.where(c >= 8, (c & 7) * 16, -1024) for c in code]
-        factor = on_rows(halves(share), masks)
+        factor = on_rows((share,), masks)
         for j in range(SLOTS):
             at = pl.ds(pl.multiple_of((code[j] & 7) * 16, 16), 16)
             for head in range(HEADS):
@@ -418,12 +383,46 @@
 
 
 def project_kernel(
-    side, att, att_far, weight, weight_far, residual, gain, picks, mixed, sent, both, kept, rows, sems
+    side,
+    att,
+    att_far,
+    weight_in,
+    weight_far_in,
+    residual_in,
+    gain,
+    picks_in,
+    mixed,
+    sent,
+    both,
+    kept,
+    rows,
+    weight,
+    weight_far,
+    residual,
+    picks,
+    load_sems,
+    sems,
 ):
+    loads = [
+        pltpu.make_async_copy(source, target, load_sems.at[n])
+        for n, (source, target) in enumerate(
+            (
+                (weight_in, weight),
+                (residual_in, residual),
+                (weight_far_in, weight_far),
+                (picks_in, picks),
+            )
+        )
+    ]
+    for load in loads:
+        load.start()
     half = residual.shape[1] // 2
     steps, step = rows.shape[0], rows.shape[1]
-    total = residual[...].astype(F32)
-    total += jnp.dot(att[...], weight[...], preferred_element_type=F32)
+    loads[0].wait()
+    total = jnp.dot(att[...], weight[...], preferred_element_type=F32)
+    loads[1].wait()
+    total += residual[...].astype(F32)
+    loads[2].wait()
     total += jnp.dot(att_far[...], weight_far[...], preferred_element_type=F32)
     kept[...] = jnp.where(side[0] == 0, total[:, :half], total[:, half:])
     keep = pltpu.make_async_copy(kept, mixed, sems.at[steps])
@@ -433,6 +432,7 @@
     both[:TOK] = normed[:, :half]
     both[TOK:] = normed[:, half:]
     copies = []
+    loads[3].wait()
     for i in range(steps):
         rows[i] = jnp.dot(
             picks[i * step : (i + 1) * step], both[...], preferred_element_type=F32
@@ -455,12 +455,17 @@
             jax.ShapeDtypeStruct((TOK, width // 2), F32),
             jax.ShapeDtypeStruct((picks.shape[0], width // 2), BF16),
         ),
-        in_specs=[smem()] + [vmem()] * 7,
+        in_specs=[smem(), vmem(), vmem(), hbm(), hbm(), hbm(), vmem(), hbm()],
         out_specs=(hbm(), hbm()),
         scratch_shapes=[
             pltpu.VMEM((2 * TOK, width // 2), BF16),
             pltpu.VMEM((TOK, width // 2), F32),
             pltpu.VMEM((steps, step, width // 2), BF16),
+            pltpu.VMEM(weight.shape, BF16),
+            pltpu.VMEM(weight_far.shape, BF16),
+            pltpu.VMEM(residual.shape, BF16),
+            pltpu.VMEM(picks.shape, BF16),
+            pltpu.SemaphoreType.DMA((4,)),
             pltpu.SemaphoreType.DMA((steps + 1,)),
         ],
         compiler_params=pltpu.CompilerParams(vmem_limit_bytes=62 << 20),
@@ -648,6 +653,22 @@
     return picks, shares.astype(BF16)
 
 
+def group_codes(users, ids, core):
+    users = users.reshape(-1, NCHIP, NC)
+    user_a = jnp.where(core == 0, users[..., 0], users[..., 1])[..., None]
+    user_b = jnp.where(core == 0, users[..., 1], users[..., 0])[..., None]
+    group = jnp.arange(TOK // 16, dtype=jnp.int32)
+    group_user = ids.reshape(-1, 1, TOK // 16, 16)[..., 0]
+    hit_a, hit_b = group_user == user_a, group_user == user_b
+    needed = (hit_a | hit_b).astype(jnp.int32)
+    rank = jnp.sum(needed[..., None, :] * (group[None, :] < group[:, None]), axis=-1)
+    value = needed * (group + 8 * hit_a + 16 * hit_b)
+    slot = jnp.arange(SLOTS, dtype=jnp.int32)
+    return jnp.sum(
+        jnp.where(rank[..., None, :] == slot[:, None], value[..., None, :], 0), axis=-1
+    )
+
+
 def shards(
     residual,
     queries,
@@ -670,29 +691,22 @@
     half = width // 2
     swap = [(0, 1), (1, 0)]
 
-    core = me % NC
-    users = page_users[0].reshape(NCHIP, NC)
-    user_a = jnp.where(core == 0, users[:, 0], users[:, 1])[:, None]
-    user_b = jnp.where(core == 0, users[:, 1], users[:, 0])[:, None]
-    group = jnp.arange(TOK // 16, dtype=jnp.int32)
-    group_user = request_ids.reshape(TOK // 16, 16)[:, 0][None, :]
-    hit_a, hit_b = group_user == user_a, group_user == user_b
-    needed = (hit_a | hit_b).astype(jnp.int32)
-    rank = jnp.sum(needed[:, None, :] * (group[None, :] < group[:, None]), axis=2)
-    value = needed * (group[None, :] + 8 * hit_a + 16 * hit_b)
-    slot = jnp.arange(SLOTS, dtype=jnp.int32)
-    codes = jnp.sum(jnp.where(rank[:, None, :] == slot[None, :, None], value[:, None, :], 0), 2)
-
-    note = jnp.zeros((8, queries.shape[1]), BF16)
-    note = note.at[0, : NCHIP * SLOTS].set(codes.T.reshape(-1).astype(BF16))
-    near, near_note, pages_far, sends_far = gather_near(queries, note, page_store, page_sends)
-    near, near_note, far_in, pages_far, sends_far = lax.optimization_barrier(
-        (near, near_note, output_weight, pages_far, sends_far)
+    near, users, ids = [
+        jnp.stack([own, lax.ppermute(own, "req", perm_x())])
+        for own in (queries, page_users[0], request_ids)
+    ]
+    pages_far = lax.ppermute(page_store, "req", perm_core())
+    sends_far = lax.ppermute(page_sends, "req", perm_core())
+    codes = group_codes(users, ids, me % NC)
+    note = jnp.zeros((2, 8, queries.shape[1]), BF16)
+    note = note.at[:, 0, : NCHIP * SLOTS].set(
+        codes.transpose(0, 2, 1).reshape(2, NCHIP * SLOTS).astype(BF16)
+    )
+    pair = jnp.concatenate([near, note], axis=1)
+    pair, far_in, pages_far, sends_far = lax.optimization_barrier(
+        (pair, output_weight, pages_far, sends_far)
     )
     weight_far = lax.ppermute(far_in, "tp", swap)
-    pair = jnp.stack(
-        [jnp.concatenate([queries, note], axis=0), jnp.concatenate([near, near_note], axis=0)]
-    )
     line = gather_line(pair)
 
     table = chip_table()
@@ -700,41 +714,38 @@
     chips = lax.dynamic_index_in_dim(
         jnp.asarray(table.reshape(NREQ, 4, 8)[:, order].reshape(NREQ, NCHIP)), me, 0, keepdims=False
     )
+    core = me % NC
     page_a = page_sends[0][chips * NC + core]
     page_b = sends_far[0][chips * NC + core]
-    keys_a, keys_b = turn_keys(page_store), turn_keys(pages_far)
-    line, keys_a, keys_b, chips, page_a, page_b = lax.optimization_barrier(
-        (line, keys_a, keys_b, chips, page_a, page_b)
-    )
+    line, chips, page_a, page_b = lax.optimization_barrier((line, chips, page_a, page_b))
     pieces = gather_rest(line)
     own, own_sums = own_attention(request_ids, queries, new_keys, new_values)
+    picks, shares = routing(expert_ids, expert_weights)
+    own, picks = lax.optimization_barrier((own, picks))
 
     parts = None
-    for index, piece in enumerate(pieces):
-        if index == 3:
-            piece, parts, weight_far = lax.optimization_barrier((piece, parts, weight_far))
-        elif index > 0:
-            piece, parts = lax.optimization_barrier((piece, parts))
-        asked = piece[:, TOK, : NCHIP * SLOTS].reshape(8, SLOTS, NCHIP)
+    for first, last in ((0, 1), (1, 4)):
+        group = pieces[first:last]
+        if first:
+            group, parts, weight_far = lax.optimization_barrier((group, parts, weight_far))
+        asked = jnp.concatenate([piece[:, TOK, : NCHIP * SLOTS] for piece in group], axis=0)
+        asked = asked.reshape(-1, SLOTS, NCHIP)
         asked = lax.dynamic_index_in_dim(asked, me // NC, 2, keepdims=False)
-        rows = slice(8 * index, 8 * index + 8)
+        rows = slice(8 * first, 8 * last)
         parts = page_attention(
             chips[rows],
             page_a[rows],
             page_b[rows],
             asked.astype(jnp.int32).reshape(-1),
-            piece,
-            keys_a,
-            keys_b,
             page_store,
             pages_far,
+            group,
             parts,
         )
     arrived = lax.all_to_all(
         parts, "req", 0, 0, tiled=True, axis_index_groups=core_groups()
     )
-    attended = merge_attention(codes.reshape(-1), arrived, own, own_sums)
-    picks, shares = routing(expert_ids, expert_weights)
+    attended = merge_attention(codes[0].reshape(-1), arrived, own, own_sums)
     attended_far = lax.ppermute(attended, "tp", swap)
     mixed, sent = project(
         lax.axis_index("tp")[None],

time: 270 us -> 266 us (0.985)
  waiting for transfers between devices: 117 us -> 133 us
  Pallas kernels: 64.7 us -> 52 us
  starting transfers between devices: 54.9 us -> 48.8 us
    ppermute x3, waiting for transfers between devices: 5.47 us -> 13.5 us  [gather_rest(): lax.ppermute(line, 'req', perm_ring(1, step))]
    pallas_call x4 -> x2, Pallas kernels: 26.3 us -> 19.7 us  [page_attention(): pl.pallas_call(page_kernel, out_shape=jax.ShapeDtypeStruct((NCHIP, BLOCK,...]
    all_to_all x1, starting transfers between devices: 14.4 us -> 8.61 us  [shards(): lax.all_to_all(parts, 'req', 0, 0, tiled=True, axis_index_groups=core_gro...]
    pallas_call x2 -> x0, Pallas kernels: 5.46 us -> none  [turn_keys(): pl.pallas_call(keys_kernel, out_shape=jax.ShapeDtypeStruct((count, HEADS,...]
    ppermute x3, waiting for transfers between devices: 0.01 us -> 5.1 us  [gather_line(): lax.ppermute(pair, 'req', perm_ring(0, step))]
    ppermute x4 -> x5, starting transfers between devices: 5.03 us -> 8.08 us  [the longest x3 5.8 us: shards(): lax.ppermute(own, 'req', perm_x())]
    ppermute x1, waiting for transfers between devices: 0.01 us -> 3.03 us  [shards(): weight_far = lax.ppermute(far_in, 'tp', swap)]
    unnamed x27 -> x35, local copies, waits for them, and re-layouts: 9.53 us -> 9.54 us
  transfers between devices with their start and end apart: 15 -> 16, of which waited for: 7 -> 9; matrix products, arithmetic and copies ran while one was open for 11% -> 10% of each run, Pallas kernels for 10% -> 4%
where the time goes in v5:
time: 266 us; the launch traced here: 265 us
  waiting for transfers between devices  133 us (50%)
  Pallas kernels  52 us (20%)
  starting transfers between devices  48.8 us (18%)
  local copies, waits for them, and re-layouts  20.4 us (8%)
  other arithmetic  9.96 us (4%)
    all_to_all x1, waiting for transfers between devices, shards(): lax.all_to_all(result.reshape(2 * NREQ, 2 * CAP, width // 4), ('req', 'tp...  38.2 us
    all_to_all x1, waiting for transfers between devices, shards(): lax.all_to_all(parts, 'req', 0, 0, tiled=True, axis_index_groups=core_gro...  36.3 us
    all_to_all x1, waiting for transfers between devices, shards(): lax.all_to_all(sent.reshape(NREQ, 2 * CAP, half), 'req', 0, 0, tiled=True)  34.8 us
    pallas_call x2, Pallas kernels, page_attention(): pl.pallas_call(page_kernel, out_shape=jax.ShapeDtypeStruct((NCHIP, BLOCK,...  19.7 us
    ppermute x3, waiting for transfers between devices, gather_rest(): lax.ppermute(line, 'req', perm_ring(1, step))  13.5 us
    pallas_call x1, Pallas kernels, run_expert(): pl.pallas_call(expert_kernel, out_shape=jax.ShapeDtypeStruct((rows.shape[...  12.4 us
    unnamed x35, local copies, waits for them, and re-layouts  9.54 us
    all_to_all x1, starting transfers between devices, shards(): lax.all_to_all(sent.reshape(NREQ, 2 * CAP, half), 'req', 0, 0, tiled=True)  9.26 us
  transfers between devices with their start and end apart: 16, of which 9 were waited for; matrix products, arithmetic and copies ran while one was open for 10% of the time, Pallas kernels for 4%

profile of v5, /device:TPU:1, one launch (start us, length us, event | category | flops | bytes accessed | tf_op | source)
XLA Modules:
  0.0 265.4 jit_solution(7912533842279473904)
XLA Ops:
  1.4 2.8 %collective-permute-start.1 = (s32[64]{0:T(128)}, s32[64]{0:T(128)S(1)}, u32[]{:S(2)}, u32[]{:S(2)}) collective-permute-start(s32[64]{0:T(128)} %bitcast.81), channel_id=1, source_target_pairs={{0,4},{2,6},{4,0},{6,2},{8,12},{10,14},{12,8},{14,10},{16,20},{18,... | collective-permute-start | bytes 776 | tf_op jit(solution)/shard_map/ppermute | solution.py:695
  4.4 2.8 %collective-permute-start.2 = (bf16[128,512]{1,0:T(8,128)(2,1)}, bf16[128,512]{1,0:T(8,128)(2,1)S(1)}, u32[]{:S(2)}, u32[]{:S(2)}) collective-permute-start(bf16[128,512]{1,0:T(8,128)(2,1)} %queries.1), channel_id=1, source_target_pairs={{0,4},{2,6},{4,0},{6,2},{8,12},{10,14},{12,8},{14,10},{16,20},{18,... | collective-permute-start | bytes 393224 | tf_op jit(solution)/shard_map/ppermute | solution.py:695
  13.0 3.8 %collective-permute-start.7 = (bf16[2,136,512]{2,1,0:T(8,128)(2,1)S(1)}, bf16[2,136,512]{2,1,0:T(8,128)(2,1)S(1)}, u32[]{:S(2)}, u32[]{:S(2)}) collective-permute-start(bf16[2,136,512]{2,1,0:T(8,128)(2,1)S(1)} %fusion.2), channel_id=1, source_target_pairs={{0,96},{2,26},{4,100},{6,30},{8,104},{10,2},{12,108},{14,6},{16,11... | collective-permute-start | bytes 835592 | tf_op jit(solution)/shard_map/ppermute | solution.py:81
  21.6 5.1 %collective-permute-done.5 = bf16[2,136,512]{2,1,0:T(8,128)(2,1)S(1)} collective-permute-done((bf16[2,136,512]{2,1,0:T(8,128)(2,1)S(1)}, bf16[2,136,512]{2,1,0:T(8,128)(2,1)S(1)}, u32[]{:S(2)}, u32[]{:S(2)}) %collective-permute-start.5) | collective-permute-done | bytes 278560 | tf_op jit(solution)/shard_map/ppermute | solution.py:81
  28.5 2.7 %collective-permute-start.10 = (bf16[8,136,512]{2,1,0:T(8,128)(2,1)S(1)}, bf16[8,136,512]{2,1,0:T(8,128)(2,1)}, u32[]{:S(2)}, u32[]{:S(2)}) collective-permute-start(bf16[8,136,512]{2,1,0:T(8,128)(2,1)S(1)} %bitcast.43), channel_id=1, source_target_pairs={{0,16},{2,66},{4,20},{6,70},{8,24},{10,74},{12,28},{14,78},{16,0},... | collective-permute-start | bytes 3342344 | tf_op jit(solution)/shard_map/ppermute | solution.py:86
  36.7 6.7 %page_attention.2.refs_3_ = bf16[32,400,128]{2,1,0:T(8,128)(2,1)} custom-call(s32[8]{0:T(128)} %bitcast.79, s32[8]{0:T(128)} %bitcast.77, s32[8]{0:T(128)} %bitcast.78, s32[48]{0:T(128)} %reshape.146.codes, bf16[8,2,128,512]{3,2,1,0:T(8,128)(2,1)} %pages_a_in.3, bf16[8,2,128,512]{3,2,1,0:T(8,128)(2,1)} %copy-done, bf16[8,136,512]{2,1,0:T(8,128)(2,1)} %bitcast.47), custom_call_target="tpu_custom_call" | custom-call | flops 805306368 | bytes 5242880 | tf_op jit(solution)/shard_map/page_attention/pallas_call | solution.py:202
  44.9 11.9 %collective-permute-done.8.refs_0_ = bf16[8,136,512]{2,1,0:T(8,128)(2,1)} collective-permute-done((bf16[8,136,512]{2,1,0:T(8,128)(2,1)S(1)}, bf16[8,136,512]{2,1,0:T(8,128)(2,1)}, u32[]{:S(2)}, u32[]{:S(2)}) %collective-permute-start.8) | collective-permute-done | bytes 1114144 | tf_op jit(solution)/shard_map/ppermute | solution.py:86
  56.8 3.0 %collective-permute-done.11.weight_far_in = bf16[512,2048]{1,0:T(8,128)(2,1)} collective-permute-done((bf16[512,2048]{1,0:T(8,128)(2,1)}, bf16[512,2048]{1,0:T(8,128)(2,1)}, u32[]{:S(2)}, u32[]{:S(2)}) %collective-permute-start.11) | collective-permute-done | bytes 2097184 | tf_op jit(solution)/shard_map/ppermute | solution.py:709
  63.0 13.1 %page_attention.3 = bf16[32,400,128]{2,1,0:T(8,128)(2,1)} custom-call(s32[24]{0:T(128)} %slice.99.chip_of, s32[24]{0:T(128)} %slice.100.page_a, s32[24]{0:T(128)} %slice.101.page_b, s32[144]{0:T(256)} %reshape.147.codes, bf16[8,2,128,512]{3,2,1,0:T(8,128)(2,1)} %pages_a_in.3, bf16[8,2,128,512]{3,2,1,0:T(8,128)(2,1)} %copy-done, ...), custom_call_target="tpu_custom_call", output_to_operand_aliasing={{}: (9, {})} | custom-call | flops 2415919104 | bytes 5242880 | tf_op jit(solution)/shard_map/page_attention/pallas_call | solution.py:202
  76.1 8.6 %all-to-all-start = ((bf16[32,400,128]{2,1,0:T(8,128)(2,1)}), bf16[32,400,128]{2,1,0:T(8,128)(2,1)}, u32[]{:S(2)}, u32[]{:S(2)}) async-start(bf16[32,400,128]{2,1,0:T(8,128)(2,1)} %page_attention.3), calls=%async_computation | async-start | bytes 6553600 | tf_op jit(solution)/shard_map/all_to_all | solution.py:745
  86.2 2.9 %own_attention.1 = (f32[4,128,128]{2,1,0:T(8,128)}, f32[8,128]{1,0:T(8,128)}) custom-call(s32[128,1]{1,0:T(8,128)} %copy.76.request_col, s32[1,128]{1,0:T(1,128)} %bitcast.71, bf16[128,512]{1,0:T(8,128)(2,1)} %queries.1, bf16[128,512]{1,0:T(8,128)(2,1)} %keys.1, bf16[128,512]{1,0:T(8,128)(2,1)} %values.1), custom_call_target="tpu_custom_call" | custom-call | flops 67108864 | bytes 1048576 | tf_op jit(solution)/shard_map/own_attention/pallas_call | solution.py:266
  91.6 36.3 %all-to-all-done.arrived_in = bf16[32,400,128]{2,1,0:T(8,128)(2,1)} async-done(((bf16[32,400,128]{2,1,0:T(8,128)(2,1)}), bf16[32,400,128]{2,1,0:T(8,128)(2,1)}, u32[]{:S(2)}, u32[]{:S(2)}) %all-to-all-start) | async-done | bytes 3276832 | tf_op jit(solution)/shard_map/all_to_all | solution.py:745
  127.8 7.1 %merge_attention.1.att = bf16[128,512]{1,0:T(8,128)(2,1)} custom-call(s32[192]{0:T(256)} %reshape_squeeze.6.codes, bf16[32,400,128]{2,1,0:T(8,128)(2,1)} %all-to-all-done.arrived_in, f32[4,128,128]{2,1,0:T(8,128)} %get-tuple-element.49.own_in, f32[8,128]{1,0:T(8,128)} %get-tuple-element.50.own_sums_in), custom_call_target="tpu_custom_call" | custom-call | flops 67108864 | bytes 4194304 | tf_op jit(solution)/shard_map/merge_attention/pallas_call | solution.py:364
  135.0 4.4 %collective-permute-start.12 = (bf16[128,512]{1,0:T(8,128)(2,1)}, bf16[128,512]{1,0:T(8,128)(2,1)S(1)}, u32[]{:S(2)}, u32[]{:S(2)}) collective-permute-start(bf16[128,512]{1,0:T(8,128)(2,1)} %merge_attention.1.att), channel_id=1, source_target_pairs={{0,1},{1,0},{2,3},{3,2},{4,5},{5,4},{6,7},{7,6},{8,9},{9,8},{10,11... | collective-permute-start | bytes 393224 | tf_op jit(solution)/shard_map/ppermute | solution.py:749
  142.7 6.1 %project_dispatch.1 = (f32[128,1024]{1,0:T(8,128)}, bf16[1536,1024]{1,0:T(8,128)(2,1)}) custom-call(s32[1]{0:T(128)} %bitcast.side, bf16[128,512]{1,0:T(8,128)(2,1)} %merge_attention.1.att, bf16[128,512]{1,0:T(8,128)(2,1)} %copy-done.6, bf16[512,2048]{1,0:T(8,128)(2,1)} %weight_in.1, bf16[512,2048]{1,0:T(8,128)(2,1)} %collective-permute-done.11.weight_far_in, ...), custom_call_target="tpu_custom_call" | custom-call | flops 1342177280 | bytes 10485760 | tf_op jit(solution)/shard_map/project_dispatch/pallas_call | solution.py:452
  148.7 9.3 %all-to-all-start.1 = ((bf16[64,24,1024]{2,1,0:T(8,128)(2,1)}), bf16[64,24,1024]{2,1,0:T(8,128)(2,1)}, u32[]{:S(2)}, u32[]{:S(2)}) async-start(bf16[64,24,1024]{2,1,0:T(8,128)(2,1)} %bitcast.49), calls=%async_computation.1 | async-start | bytes 6291456 | tf_op jit(solution)/shard_map/all_to_all | solution.py:760
  158.0 2.9 %copy.79 = bf16[1,2048,704]{2,1,0:T(8,128)(2,1)} copy(bf16[1,2048,704]{1,2,0:T(8,128)(2,1)S(1)} %copy-done.2) | data formatting | bytes 5767168 | tf_op args[12]
  160.9 4.6 %copy.80 = bf16[1,2048,704]{2,1,0:T(8,128)(2,1)} copy(bf16[1,2048,704]{1,2,0:T(8,128)(2,1)} %param.41) | data formatting | bytes 5767168 | tf_op args[13]
  165.5 34.8 %all-to-all-done.1.rows = bf16[64,24,1024]{2,1,0:T(8,128)(2,1)} async-done(((bf16[64,24,1024]{2,1,0:T(8,128)(2,1)}), bf16[64,24,1024]{2,1,0:T(8,128)(2,1)}, u32[]{:S(2)}, u32[]{:S(2)}) %all-to-all-start.1) | async-done | bytes 3145760 | tf_op jit(solution)/shard_map/all_to_all | solution.py:760
  200.2 12.4 %expert.1 = bf16[64,2,24,512]{3,2,1,0:T(8,128)(2,1)} custom-call(bf16[64,24,1024]{2,1,0:T(8,128)(2,1)} %all-to-all-done.1.rows, bf16[2048,704]{1,0:T(8,128)(2,1)} %bitcast.50, bf16[2048,704]{1,0:T(8,128)(2,1)} %bitcast.51, bf16[704,2048]{1,0:T(8,128)(2,1)} %bitcast.80), custom_call_target="tpu_custom_call" | custom-call | flops 6643777536 | bytes 15728640 | tf_op jit(solution)/shard_map/expert/pallas_call | solution.py:547
  212.7 7.6 %all-to-all-start.2 = ((bf16[128,24,512]{2,1,0:T(8,128)(2,1)}), bf16[128,24,512]{2,1,0:T(8,128)(2,1)}, u32[]{:S(2)}, u32[]{:S(2)}) async-start(bf16[128,24,512]{2,1,0:T(8,128)(2,1)} %bitcast.48), calls=%async_computation.2 | async-start | bytes 6291456 | tf_op jit(solution)/shard_map/all_to_all | solution.py:762
  220.3 3.0 %select_convert_fusion.shares = bf16[256,3072]{1,0:T(8,128)(2,1)} fusion(pred[256,3072]{1,0:T(32,128)(4,1)S(1)} %copy-done.3, f32[256]{0:T(256)S(1)} %bitcast.74, f32[256]{0:T(256)S(1)} %bitcast.75, f32[256]{0:T(256)S(1)} %bitcast.76, f32[256]{0:T(256)S(1)} %bitcast.73, s32[3072]{0:T(1024)S(1)} %copy-done.7, s32[256]{0:T(256)S(1)} %bitcast.61, ...), kind=kLoop, calls=%fused_computation.2 | loop fusion | flops 10223616 | bytes 2379776 | tf_op jit(solution)/shard_map/convert_element_type | solution.py:653
  223.3 38.2 %all-to-all-done.2 = bf16[128,24,512]{2,1,0:T(8,128)(2,1)} async-done(((bf16[128,24,512]{2,1,0:T(8,128)(2,1)}), bf16[128,24,512]{2,1,0:T(8,128)(2,1)}, u32[]{:S(2)}, u32[]{:S(2)}) %all-to-all-start.2) | async-done | bytes 3145760 | tf_op jit(solution)/shard_map/all_to_all | solution.py:762
  261.5 3.7 %combine.1 = bf16[128,1024]{1,0:T(8,128)(2,1)} custom-call(f32[128,1024]{1,0:T(8,128)} %get-tuple-element.53.mixed, bf16[256,3072]{1,0:T(8,128)(2,1)} %select_convert_fusion.shares, bf16[3072,512]{1,0:T(8,128)(2,1)} %bitcast.33.rows), custom_call_target="tpu_custom_call" | custom-call | flops 805306368 | bytes 6291456 | tf_op jit(solution)/shard_map/combine/pallas_call | solution.py:596
  (102 shorter events, 31.2 us)
Async XLA Ops:
  0.0 12.6 %collective-permute-start.3 = (bf16[8,2,128,512]{3,2,1,0:T(8,128)(2,1)}, bf16[8,2,128,512]{3,2,1,0:T(8,128)(2,1)S(1)}, u32[]{:S(2)}, u32[]{:S(2)}) collective-permute-start(bf16[8,2,128,512]{3,2,1,0:T(8,128)(2,1)} %pages_a_in.3), channel_id=1, source_target_pairs={{0,2},{2,0},{4,6},{6,4},{8,10},{10,8},{12,14},{14,12},{16,18},{18,... | collective-permute-start | bytes 6291464 | tf_op jit(solution)/shard_map/ppermute | solution.py:698
  1.4 9.4 %collective-permute-start.1 = (s32[64]{0:T(128)}, s32[64]{0:T(128)S(1)}, u32[]{:S(2)}, u32[]{:S(2)}) collective-permute-start(s32[64]{0:T(128)} %bitcast.81), channel_id=1, source_target_pairs={{0,4},{2,6},{4,0},{6,2},{8,12},{10,14},{12,8},{14,10},{16,20},{18,... | collective-permute-start | bytes 776 | tf_op jit(solution)/shard_map/ppermute | solution.py:695
  4.2 6.8 %collective-permute-start = (s32[128]{0:T(128)}, s32[128]{0:T(128)S(1)}, u32[]{:S(2)}, u32[]{:S(2)}) collective-permute-start(s32[128]{0:T(128)} %param.32), channel_id=1, source_target_pairs={{0,4},{2,6},{4,0},{6,2},{8,12},{10,14},{12,8},{14,10},{16,20},{18,... | collective-permute-start | bytes 1544 | tf_op jit(solution)/shard_map/ppermute | solution.py:695
  4.4 7.3 %collective-permute-start.2 = (bf16[128,512]{1,0:T(8,128)(2,1)}, bf16[128,512]{1,0:T(8,128)(2,1)S(1)}, u32[]{:S(2)}, u32[]{:S(2)}) collective-permute-start(bf16[128,512]{1,0:T(8,128)(2,1)} %queries.1), channel_id=1, source_target_pairs={{0,4},{2,6},{4,0},{6,2},{8,12},{10,14},{12,8},{14,10},{16,20},{18,... | collective-permute-start | bytes 393224 | tf_op jit(solution)/shard_map/ppermute | solution.py:695
  7.2 5.4 %collective-permute-start.4 = (s32[1,64]{1,0:T(1,128)}, s32[1,64]{1,0:T(1,128)S(1)}, u32[]{:S(2)}, u32[]{:S(2)}) collective-permute-start(s32[1,64]{1,0:T(1,128)} %param.34), channel_id=1, source_target_pairs={{0,2},{2,0},{4,6},{6,4},{8,10},{10,8},{12,14},{14,12},{16,18},{18,... | collective-permute-start | bytes 776 | tf_op jit(solution)/shard_map/ppermute | solution.py:699
  12.6 8.9 %copy-start = (bf16[8,2,128,512]{3,2,1,0:T(8,128)(2,1)}, bf16[8,2,128,512]{3,2,1,0:T(8,128)(2,1)S(1)}, u32[]{:S(2)}) copy-start(bf16[8,2,128,512]{3,2,1,0:T(8,128)(2,1)S(1)} %collective-permute-done.3.pages_b_in) | copy-start | bytes 6291460
  12.6 47.3 %collective-permute-start.11 = (bf16[512,2048]{1,0:T(8,128)(2,1)}, bf16[512,2048]{1,0:T(8,128)(2,1)}, u32[]{:S(2)}, u32[]{:S(2)}) collective-permute-start(bf16[512,2048]{1,0:T(8,128)(2,1)} %weight_in.1), channel_id=1, source_target_pairs={{0,1},{1,0},{2,3},{3,2},{4,5},{5,4},{6,7},{7,6},{8,9},{9,8},{10,11... | collective-permute-start | bytes 6291464 | tf_op jit(solution)/shard_map/ppermute | solution.py:709
  13.0 8.5 %collective-permute-start.7 = (bf16[2,136,512]{2,1,0:T(8,128)(2,1)S(1)}, bf16[2,136,512]{2,1,0:T(8,128)(2,1)S(1)}, u32[]{:S(2)}, u32[]{:S(2)}) collective-permute-start(bf16[2,136,512]{2,1,0:T(8,128)(2,1)S(1)} %fusion.2), channel_id=1, source_target_pairs={{0,96},{2,26},{4,100},{6,30},{8,104},{10,2},{12,108},{14,6},{16,11... | collective-permute-start | bytes 835592 | tf_op jit(solution)/shard_map/ppermute | solution.py:81
  16.8 9.9 %collective-permute-start.5 = (bf16[2,136,512]{2,1,0:T(8,128)(2,1)S(1)}, bf16[2,136,512]{2,1,0:T(8,128)(2,1)S(1)}, u32[]{:S(2)}, u32[]{:S(2)}) collective-permute-start(bf16[2,136,512]{2,1,0:T(8,128)(2,1)S(1)} %fusion.2), channel_id=1, source_target_pairs={{0,32},{2,10},{4,36},{6,14},{8,40},{10,18},{12,44},{14,22},{16,48}... | collective-permute-start | bytes 835592 | tf_op jit(solution)/shard_map/ppermute | solution.py:81
  16.8 9.9 %collective-permute-start.6 = (bf16[2,136,512]{2,1,0:T(8,128)(2,1)S(1)}, bf16[2,136,512]{2,1,0:T(8,128)(2,1)S(1)}, u32[]{:S(2)}, u32[]{:S(2)}) collective-permute-start(bf16[2,136,512]{2,1,0:T(8,128)(2,1)S(1)} %fusion.2), channel_id=1, source_target_pairs={{0,64},{2,18},{4,68},{6,22},{8,72},{10,26},{12,76},{14,30},{16,80}... | collective-permute-start | bytes 835592 | tf_op jit(solution)/shard_map/ppermute | solution.py:81
  20.1 16.6 %copy-start.12 = (s32[32]{0:T(128)}, s32[32]{0:T(128)S(1)}, u32[]{:S(2)}) copy-start(s32[32]{0:T(128)S(1)} %gather_fusion) | copy-start | bytes 388
  20.8 15.9 %copy-start.14 = (s32[32]{0:T(128)}, s32[32]{0:T(128)S(1)}, u32[]{:S(2)}) copy-start(s32[32]{0:T(128)S(1)} %fusion.16) | copy-start | bytes 388
  21.5 15.2 %copy-start.13 = (s32[32]{0:T(128)}, s32[32]{0:T(128)S(1)}, u32[]{:S(2)}) copy-start(s32[32]{0:T(128)S(1)} %gather_fusion.1) | copy-start | bytes 388
  28.5 16.4 %collective-permute-start.10 = (bf16[8,136,512]{2,1,0:T(8,128)(2,1)S(1)}, bf16[8,136,512]{2,1,0:T(8,128)(2,1)}, u32[]{:S(2)}, u32[]{:S(2)}) collective-permute-start(bf16[8,136,512]{2,1,0:T(8,128)(2,1)S(1)} %bitcast.43), channel_id=1, source_target_pairs={{0,16},{2,66},{4,20},{6,70},{8,24},{10,74},{12,28},{14,78},{16,0},... | collective-permute-start | bytes 3342344 | tf_op jit(solution)/shard_map/ppermute | solution.py:86
  31.2 25.6 %collective-permute-start.8 = (bf16[8,136,512]{2,1,0:T(8,128)(2,1)S(1)}, bf16[8,136,512]{2,1,0:T(8,128)(2,1)}, u32[]{:S(2)}, u32[]{:S(2)}) collective-permute-start(bf16[8,136,512]{2,1,0:T(8,128)(2,1)S(1)} %bitcast.44), channel_id=1, source_target_pairs={{0,8},{2,34},{4,12},{6,38},{8,16},{10,42},{12,20},{14,46},{16,24},... | collective-permute-start | bytes 3342344 | tf_op jit(solution)/shard_map/ppermute | solution.py:86
  31.6 25.3 %collective-permute-start.9 = (bf16[8,136,512]{2,1,0:T(8,128)(2,1)S(1)}, bf16[8,136,512]{2,1,0:T(8,128)(2,1)}, u32[]{:S(2)}, u32[]{:S(2)}) collective-permute-start(bf16[8,136,512]{2,1,0:T(8,128)(2,1)S(1)} %bitcast.45), channel_id=1, source_target_pairs={{0,24},{2,98},{4,28},{6,102},{8,0},{10,106},{12,4},{14,110},{16,8}... | collective-permute-start | bytes 3342344 | tf_op jit(solution)/shard_map/ppermute | solution.py:86
  76.1 9.4 %copy-start.11 = (s32[128]{0:T(128)S(1)}, s32[128]{0:T(128)}, u32[]{:S(2)}) copy-start(s32[128]{0:T(128)} %param.32) | copy-start | bytes 1540
  76.1 13.0 %copy-start.4 = (pred[1536,256]{1,0:T(32,128)(4,1)S(1)}, pred[1536,256]{1,0:T(32,128)(4,1)}, u32[]{:S(2)}) copy-start(pred[1536,256]{1,0:T(32,128)(4,1)} %constant.107.clone) | copy-start | bytes 1179652
  76.1 13.0 %copy-start.8 = (s32[1536]{0:T(1024)S(1)}, s32[1536]{0:T(1024)}, u32[]{:S(2)}) copy-start(s32[1536]{0:T(1024)} %constant.118) | copy-start | bytes 18436
  76.1 51.7 %all-to-all-start = ((bf16[32,400,128]{2,1,0:T(8,128)(2,1)}), bf16[32,400,128]{2,1,0:T(8,128)(2,1)}, u32[]{:S(2)}, u32[]{:S(2)}) async-start(bf16[32,400,128]{2,1,0:T(8,128)(2,1)} %page_attention.3), calls=%async_computation | async-start | bytes 6553600 | tf_op jit(solution)/shard_map/all_to_all | solution.py:745
  135.0 7.0 %collective-permute-start.12 = (bf16[128,512]{1,0:T(8,128)(2,1)}, bf16[128,512]{1,0:T(8,128)(2,1)S(1)}, u32[]{:S(2)}, u32[]{:S(2)}) collective-permute-start(bf16[128,512]{1,0:T(8,128)(2,1)} %merge_attention.1.att), channel_id=1, source_target_pairs={{0,1},{1,0},{2,3},{3,2},{4,5},{5,4},{6,7},{7,6},{8,9},{9,8},{10,11... | collective-permute-start | bytes 393224 | tf_op jit(solution)/shard_map/ppermute | solution.py:749
  148.7 9.3 %copy-start.2 = (bf16[1,2048,704]{1,2,0:T(8,128)(2,1)S(1)}, bf16[1,2048,704]{1,2,0:T(8,128)(2,1)}, u32[]{:S(2)}) copy-start(bf16[1,2048,704]{1,2,0:T(8,128)(2,1)} %param.40) | copy-start | bytes 8650756
  148.7 51.5 %all-to-all-start.1 = ((bf16[64,24,1024]{2,1,0:T(8,128)(2,1)}), bf16[64,24,1024]{2,1,0:T(8,128)(2,1)}, u32[]{:S(2)}, u32[]{:S(2)}) async-start(bf16[64,24,1024]{2,1,0:T(8,128)(2,1)} %bitcast.49), calls=%async_computation.1 | async-start | bytes 6291456 | tf_op jit(solution)/shard_map/all_to_all | solution.py:760
  212.7 48.8 %all-to-all-start.2 = ((bf16[128,24,512]{2,1,0:T(8,128)(2,1)}), bf16[128,24,512]{2,1,0:T(8,128)(2,1)}, u32[]{:S(2)}, u32[]{:S(2)}) async-start(bf16[128,24,512]{2,1,0:T(8,128)(2,1)} %bitcast.48), calls=%async_computation.2 | async-start | bytes 6291456 | tf_op jit(solution)/shard_map/all_to_all | solution.py:762
  (7 other events, 41.2 us)

commit v6 on v5

--- a/solution.py
+++ b/solution.py
@@ -60,15 +60,17 @@
     return pairs
 
 
+PIECES = tuple((step, far) for step in (0, 1, 3, 2) for far in (0, 1))
+
+
 def chip_table():
     table = np.zeros((NREQ, NCHIP), np.int32)
     for y, z, x, c in all_coords():
         row = []
-        for d1 in range(4):
+        for d1, dx in PIECES:
             for d0 in range(4):
-                for dx in range(2):
-                    dy, dz = (d0, d1) if c == 0 else (d1, d0)
-                    row.append(req_index((y - dy) % NY, (z - dz) % NZ, x ^ dx, 0) // NC)
+                dy, dz = (d0, d1) if c == 0 else (d1, d0)
+                row.append(req_index((y - dy) % NY, (z - dz) % NZ, x ^ dx, 0) // NC)
         table[req_index(y, z, x, c)] = row
     return table
 
@@ -77,13 +79,12 @@
     return [[chip * NC + core for chip in range(NCHIP)] for core in range(NC)]
 
 
-def gather_line(pair):
-    line = [pair] + [lax.ppermute(pair, "req", perm_ring(0, step)) for step in (1, 2, 3)]
-    return jnp.stack(line).reshape(8, *pair.shape[1:])
-
-
-def gather_rest(line):
-    return [line] + [lax.ppermute(line, "req", perm_ring(1, step)) for step in (1, 3, 2)]
+def ring_line(block):
+    return [block] + [lax.ppermute(block, "req", perm_ring(0, step)) for step in (1, 2, 3)]
+
+
+def ring_rest(line):
+    return [lax.ppermute(line, "req", perm_ring(1, step)) for step in (1, 3, 2)]
 
 
 def attend(query, key_t, value_1, shift):
@@ -103,15 +104,15 @@
     return jnp.where(head == 3, rows[3], tile)
 
 
-def page_kernel(chip_of, page_a, page_b, codes, pages_a_in, pages_b_in, *refs):
-    out, blocks, pages_a, pages_b, held, sems, load_sems = refs[-7:]
+def page_kernel(here, chip_of, page_a, page_b, pages_a_in, pages_b_in, *refs):
+    out, blocks, pages_a, pages_b, held, notes, codes, sems, load_sems, note_sem = refs[-10:]
     count = held.shape[0]
     pieces = refs[: count // 8]
     loads = [
         pltpu.make_async_copy(source, target, load_sems.at[n])
         for n, (source, target) in enumerate(
-            [(pages_a_in, pages_a), (pages_b_in, pages_b)]
-            + [(piece, blocks.at[pl.ds(8 * n, 8)]) for n, piece in enumerate(pieces)]
+            [(piece, blocks.at[pl.ds(8 * n, 8)]) for n, piece in enumerate(pieces)]
+            + [(pages_a_in, pages_a), (pages_b_in, pages_b)]
         )
     ]
     for load in loads:
@@ -120,15 +121,25 @@
     offset = lax.broadcasted_iota(jnp.int32, (16, 128), 1) - row
     sub = lax.broadcasted_iota(jnp.int32, (8, 128), 0)
     ones = jnp.ones((PAGE, HD), BF16)
-    for load in loads:
+    for load in loads[: len(pieces)]:
         load.wait()
+    width = notes.shape[1]
+    for i in range(count):
+        words = blocks[i, TOK : TOK + 8, :width].astype(F32).astype(jnp.int32)
+        notes[i : i + 1, :] = words[:1]
+    note_copy = pltpu.make_async_copy(notes, codes, note_sem)
+    note_copy.start()
+    for load in loads[len(pieces) :]:
+        load.wait()
+    note_copy.wait()
+    chip = here[0]
 
     def copy(i):
         return pltpu.make_async_copy(held.at[i], out.at[chip_of[i]], sems.at[i])
 
     def step(i, carry):
         pa, pb = page_a[i], page_b[i]
-        code = [codes[i * SLOTS + j] for j in range(SLOTS)]
+        code = [codes[i, j * NCHIP + chip] for j in range(SLOTS)]
         first = [pl.multiple_of((c & 7) * 16, 16) for c in code]
         bias = jnp.concatenate(
             [
@@ -196,8 +207,9 @@
     lax.fori_loop(0, count, lambda i, carry: (copy(i).wait(), carry)[1], 0)
 
 
-def page_attention(chip_of, page_a, page_b, codes, pages_a, pages_b, pieces, last):
+def page_attention(here, chip_of, page_a, page_b, pages_a, pages_b, pieces, last):
     count = 8 * len(pieces)
+    width = -(-NCHIP * SLOTS // 128) * 128
     before = [] if last is None else [last]
     return pl.pallas_call(
         page_kernel,
@@ -210,8 +222,11 @@
             pltpu.VMEM(pages_a.shape, BF16),
             pltpu.VMEM(pages_b.shape, BF16),
             pltpu.VMEM((count, BLOCK, HD), BF16),
+            pltpu.VMEM((count, width), jnp.int32),
+            pltpu.SMEM((count, width), jnp.int32),
             pltpu.SemaphoreType.DMA((count,)),
             pltpu.SemaphoreType.DMA((2 + len(pieces),)),
+            pltpu.SemaphoreType.DMA,
         ],
         compiler_params=pltpu.CompilerParams(vmem_limit_bytes=62 << 20),
         cost_estimate=pl.CostEstimate(
@@ -220,7 +235,7 @@
             transcendentals=count * HEADS * ROWS * 2 * PAGE,
         ),
         name="page_attention",
-    )(chip_of, page_a, page_b, codes, pages_a, pages_b, *pieces, *before)
+    )(here, chip_of, page_a, page_b, pages_a, pages_b, *pieces, *before)
 
 
 def smem():
@@ -387,7 +402,8 @@
     att,
     att_far,
     weight_in,
-    weight_far_in,
+    weight_mine,
+    weight_other,
     residual_in,
     gain,
     picks_in,
@@ -403,13 +419,15 @@
     load_sems,
     sems,
 ):
+    part = weight_mine.shape[0]
     loads = [
         pltpu.make_async_copy(source, target, load_sems.at[n])
         for n, (source, target) in enumerate(
             (
                 (weight_in, weight),
                 (residual_in, residual),
-                (weight_far_in, weight_far),
+                (weight_mine, weight_far.at[pl.ds(pl.multiple_of(side[1] * part, part), part)]),
+                (weight_other, weight_far.at[pl.ds(pl.multiple_of(side[2] * part, part), part)]),
                 (picks_in, picks),
             )
         )
@@ -423,6 +441,7 @@
     loads[1].wait()
     total += residual[...].astype(F32)
     loads[2].wait()
+    loads[3].wait()
     total += jnp.dot(att_far[...], weight_far[...], preferred_element_type=F32)
     kept[...] = jnp.where(side[0] == 0, total[:, :half], total[:, half:])
     keep = pltpu.make_async_copy(kept, mixed, sems.at[steps])
@@ -432,7 +451,7 @@
     both[:TOK] = normed[:, :half]
     both[TOK:] = normed[:, half:]
     copies = []
-    loads[3].wait()
+    loads[4].wait()
     for i in range(steps):
         rows[i] = jnp.dot(
             picks[i * step : (i + 1) * step], both[...], preferred_element_type=F32
@@ -446,7 +465,7 @@
         copy.wait()
 
 
-def project(side, att, att_far, weight, weight_far, residual, gain, picks, steps=4):
+def project(side, att, att_far, weight, weight_mine, weight_other, residual, gain, picks, steps=4):
     width = residual.shape[1]
     step = picks.shape[0] // steps
     return pl.pallas_call(
@@ -455,17 +474,17 @@
             jax.ShapeDtypeStruct((TOK, width // 2), F32),
             jax.ShapeDtypeStruct((picks.shape[0], width // 2), BF16),
         ),
-        in_specs=[smem(), vmem(), vmem(), hbm(), hbm(), hbm(), vmem(), hbm()],
+        in_specs=[smem(), vmem(), vmem(), hbm(), hbm(), hbm(), hbm(), vmem(), hbm()],
         out_specs=(hbm(), hbm()),
         scratch_shapes=[
             pltpu.VMEM((2 * TOK, width // 2), BF16),
             pltpu.VMEM((TOK, width // 2), F32),
             pltpu.VMEM((steps, step, width // 2), BF16),
             pltpu.VMEM(weight.shape, BF16),
-            pltpu.VMEM(weight_far.shape, BF16),
+            pltpu.VMEM((2 * weight_mine.shape[0], width), BF16),
             pltpu.VMEM(residual.shape, BF16),
             pltpu.VMEM(picks.shape, BF16),
-            pltpu.SemaphoreType.DMA((4,)),
+            pltpu.SemaphoreType.DMA((5,)),
             pltpu.SemaphoreType.DMA((steps + 1,)),
         ],
         compiler_params=pltpu.CompilerParams(vmem_limit_bytes=62 << 20),
@@ -475,7 +494,7 @@
             transcendentals=TOK,
         ),
         name="project_dispatch",
-    )(side, att, att_far, weight, weight_far, residual, gain, picks)
+    )(side, att, att_far, weight, weight_mine, weight_other, residual, gain, picks)
 
 
 def expert_kernel(rows, gate, up, down, out, rows_v, gate_v, up_v, down_v, out_v, sems, back):
@@ -654,19 +673,17 @@
 
 
 def group_codes(users, ids, core):
-    users = users.reshape(-1, NCHIP, NC)
-    user_a = jnp.where(core == 0, users[..., 0], users[..., 1])[..., None]
-    user_b = jnp.where(core == 0, users[..., 1], users[..., 0])[..., None]
+    users = users.reshape(NCHIP, NC)
+    user_a = jnp.where(core == 0, users[:, 0], users[:, 1])[:, None]
+    user_b = jnp.where(core == 0, users[:, 1], users[:, 0])[:, None]
     group = jnp.arange(TOK // 16, dtype=jnp.int32)
-    group_user = ids.reshape(-1, 1, TOK // 16, 16)[..., 0]
+    group_user = ids.reshape(1, TOK // 16, 16)[..., 0]
     hit_a, hit_b = group_user == user_a, group_user == user_b
     needed = (hit_a | hit_b).astype(jnp.int32)
-    rank = jnp.sum(needed[..., None, :] * (group[None, :] < group[:, None]), axis=-1)
+    rank = jnp.sum(needed[:, None, :] * (group[None, :] < group[:, None]), axis=2)
     value = needed * (group + 8 * hit_a + 16 * hit_b)
     slot = jnp.arange(SLOTS, dtype=jnp.int32)
-    return jnp.sum(
-        jnp.where(rank[..., None, :] == slot[:, None], value[..., None, :], 0), axis=-1
-    )
+    return jnp.sum(jnp.where(rank[:, None, :] == slot[:, None], value[:, None, :], 0), axis=2)
 
 
 def shards(
@@ -691,34 +708,29 @@
     half = width // 2
     swap = [(0, 1), (1, 0)]
 
-    near, users, ids = [
-        jnp.stack([own, lax.ppermute(own, "req", perm_x())])
-        for own in (queries, page_users[0], request_ids)
-    ]
+    core = me % NC
     pages_far = lax.ppermute(page_store, "req", perm_core())
     sends_far = lax.ppermute(page_sends, "req", perm_core())
-    codes = group_codes(users, ids, me % NC)
-    note = jnp.zeros((2, 8, queries.shape[1]), BF16)
-    note = note.at[:, 0, : NCHIP * SLOTS].set(
-        codes.transpose(0, 2, 1).reshape(2, NCHIP * SLOTS).astype(BF16)
+    codes = group_codes(page_users[0], request_ids, core)
+    note = jnp.zeros((8, queries.shape[1]), BF16)
+    note = note.at[0, : NCHIP * SLOTS].set(codes.T.reshape(-1).astype(BF16))
+    block = jnp.concatenate([queries, note], axis=0)
+    far_rows = output_weight.shape[0] // NC
+    far_part = lax.dynamic_slice_in_dim(output_weight, core * far_rows, far_rows, 0)
+    near = lax.ppermute(block, "req", perm_x())
+    line_a = ring_line(block)
+    near, line_a, pages_far, sends_far, far_part = lax.optimization_barrier(
+        (near, line_a, pages_far, sends_far, far_part)
     )
-    pair = jnp.concatenate([near, note], axis=1)
-    pair, far_in, pages_far, sends_far = lax.optimization_barrier(
-        (pair, output_weight, pages_far, sends_far)
-    )
-    weight_far = lax.ppermute(far_in, "tp", swap)
-    line = gather_line(pair)
-
-    table = chip_table()
-    order = np.array([0, 1, 3, 2])
-    chips = lax.dynamic_index_in_dim(
-        jnp.asarray(table.reshape(NREQ, 4, 8)[:, order].reshape(NREQ, NCHIP)), me, 0, keepdims=False
-    )
-    core = me % NC
+    weight_mine = lax.ppermute(far_part, "tp", swap)
+    line = jnp.stack(line_a + ring_line(near))
+
+    chips = lax.dynamic_index_in_dim(jnp.asarray(chip_table()), me, 0, keepdims=False)
     page_a = page_sends[0][chips * NC + core]
     page_b = sends_far[0][chips * NC + core]
     line, chips, page_a, page_b = lax.optimization_barrier((line, chips, page_a, page_b))
-    pieces = gather_rest(line)
+    pieces = [line] + ring_rest(line)
+    here = me // NC
     own, own_sums = own_attention(request_ids, queries, new_keys, new_values)
     picks, shares = routing(expert_ids, expert_weights)
     own, picks = lax.optimization_barrier((own, picks))
@@ -727,32 +739,26 @@
     for first, last in ((0, 1), (1, 4)):
         group = pieces[first:last]
         if first:
-            group, parts, weight_far = lax.optimization_barrier((group, parts, weight_far))
-        asked = jnp.concatenate([piece[:, TOK, : NCHIP * SLOTS] for piece in group], axis=0)
-        asked = asked.reshape(-1, SLOTS, NCHIP)
-        asked = lax.dynamic_index_in_dim(asked, me // NC, 2, keepdims=False)
+            weight_other = lax.ppermute(weight_mine, "req", perm_core())
+            group, parts, weight_mine, weight_other = lax.optimization_barrier(
+                (group, parts, weight_mine, weight_other)
+            )
         rows = slice(8 * first, 8 * last)
         parts = page_attention(
-            chips[rows],
-            page_a[rows],
-            page_b[rows],
-            asked.astype(jnp.int32).reshape(-1),
-            page_store,
-            pages_far,
-            group,
-            parts,
+            here[None], chips[rows], page_a[rows], page_b[rows], page_store, pages_far, group, parts
         )
     arrived = lax.all_to_all(
         parts, "req", 0, 0, tiled=True, axis_index_groups=core_groups()
     )
-    attended = merge_attention(codes[0].reshape(-1), arrived, own, own_sums)
+    attended = merge_attention(codes.reshape(-1), arrived, own, own_sums)
     attended_far = lax.ppermute(attended, "tp", swap)
     mixed, sent = project(
-        lax.axis_index("tp")[None],
+        jnp.stack([lax.axis_index("tp"), core, 1 - core]),
         attended,
         attended_far,
         output_weight,
-        weight_far,
+        weight_mine,
+        weight_other,
         residual,
         norm_gain[None, :],
         picks,

time: 266 us -> 263 us (0.989)
  waiting for transfers between devices: 133 us -> 125 us
  starting transfers between devices: 48.8 us -> 52.2 us
  local copies, waits for them, and re-layouts: 20.4 us -> 23.4 us
    ppermute x10 -> x12, waiting for transfers between devices: 21.6 us -> 16.8 us  [the longest x1 14.8 us: shards(): weight_mine = lax.ppermute(far_part, 'tp', swap)]
    ppermute x10 -> x12, starting transfers between devices: 16.6 us -> 20.8 us  [the longest x6 13 us: ring_line(): lax.ppermute(block, 'req', perm_ring(0, step))]
    unnamed x35 -> x48, local copies, waits for them, and re-layouts: 9.54 us -> 13.4 us
    all_to_all x1, starting transfers between devices: 8.61 us -> 4.96 us  [shards(): lax.all_to_all(parts, 'req', 0, 0, tiled=True, axis_index_groups=core_gro...]
    ppermute x1, starting transfers between devices: 4.43 us -> 7.91 us  [shards(): attended_far = lax.ppermute(attended, 'tp', swap)]
    all_to_all x1, waiting for transfers between devices: 36.3 us -> 33.6 us  [shards(): lax.all_to_all(parts, 'req', 0, 0, tiled=True, axis_index_groups=core_gro...]
  transfers between devices with their start and end apart: 16 -> 18, of which waited for: 9 -> 7; matrix products, arithmetic and copies ran while one was open for 10% -> 12% of each run, Pallas kernels for 4% -> 4%
where the time goes in v6:
time: 263 us; the launch traced here: 262 us
  waiting for transfers between devices  125 us (48%)
  starting transfers between devices  52.2 us (20%)
  Pallas kernels  52.1 us (20%)
  local copies, waits for them, and re-layouts  23.4 us (9%)
  other arithmetic  8.58 us (3%)
    all_to_all x1, waiting for transfers between devices, shards(): lax.all_to_all(result.reshape(2 * NREQ, 2 * CAP, width // 4), ('req', 'tp...  38.2 us
    all_to_all x1, waiting for transfers between devices, shards(): lax.all_to_all(sent.reshape(NREQ, 2 * CAP, half), 'req', 0, 0, tiled=True)  34.7 us
    all_to_all x1, waiting for transfers between devices, shards(): lax.all_to_all(parts, 'req', 0, 0, tiled=True, axis_index_groups=core_gro...  33.6 us
    pallas_call x2, Pallas kernels, page_attention(): pl.pallas_call(page_kernel, out_shape=jax.ShapeDtypeStruct((NCHIP, BLOCK,...  19.9 us
    ppermute x1, waiting for transfers between devices, shards(): weight_mine = lax.ppermute(far_part, 'tp', swap)  14.8 us
    unnamed x48, local copies, waits for them, and re-layouts  13.4 us
    ppermute x6, starting transfers between devices, ring_line(): lax.ppermute(block, 'req', perm_ring(0, step))  13 us
    pallas_call x1, Pallas kernels, run_expert(): pl.pallas_call(expert_kernel, out_shape=jax.ShapeDtypeStruct((rows.shape[...  12.4 us
  transfers between devices with their start and end apart: 18, of which 7 were waited for; matrix products, arithmetic and copies ran while one was open for 12% of the time, Pallas kernels for 4%

profile of v6, /device:TPU:1, one launch (start us, length us, event | category | flops | bytes accessed | tf_op | source)
XLA Modules:
  0.0 262.3 jit_solution(896755269736433793)
XLA Ops:
  5.7 2.9 %collective-permute-start = (bf16[136,512]{1,0:T(8,128)(2,1)S(1)}, bf16[136,512]{1,0:T(8,128)(2,1)S(1)}, u32[]{:S(2)}, u32[]{:S(2)}) collective-permute-start(bf16[136,512]{1,0:T(8,128)(2,1)S(1)} %fusion.2), channel_id=1, source_target_pairs={{0,4},{2,6},{4,0},{6,2},{8,12},{10,14},{12,8},{14,10},{16,20},{18,... | collective-permute-start | bytes 417800 | tf_op jit(solution)/shard_map/ppermute | solution.py:720
  10.2 3.3 %collective-permute-start.2 = (bf16[136,512]{1,0:T(8,128)(2,1)S(1)}, bf16[136,512]{1,0:T(8,128)(2,1)S(1)}, u32[]{:S(2)}, u32[]{:S(2)}) collective-permute-start(bf16[136,512]{1,0:T(8,128)(2,1)S(1)} %fusion.2), channel_id=1, source_target_pairs={{0,64},{2,18},{4,68},{6,22},{8,72},{10,26},{12,76},{14,30},{16,80}... | collective-permute-start | bytes 417800 | tf_op jit(solution)/shard_map/ppermute | solution.py:83
  13.5 2.3 constant_dynamic-slice_fusion.1
  16.6 3.6 %collective-permute-start.3 = (bf16[136,512]{1,0:T(8,128)(2,1)S(1)}, bf16[136,512]{1,0:T(8,128)(2,1)S(1)}, u32[]{:S(2)}, u32[]{:S(2)}) collective-permute-start(bf16[136,512]{1,0:T(8,128)(2,1)S(1)} %fusion.2), channel_id=1, source_target_pairs={{0,96},{2,26},{4,100},{6,30},{8,104},{10,2},{12,108},{14,6},{16,11... | collective-permute-start | bytes 417800 | tf_op jit(solution)/shard_map/ppermute | solution.py:83
  22.5 4.0 %collective-permute-start.7 = (bf16[136,512]{1,0:T(8,128)(2,1)S(1)}, bf16[136,512]{1,0:T(8,128)(2,1)}, u32[]{:S(2)}, u32[]{:S(2)}) collective-permute-start(bf16[136,512]{1,0:T(8,128)(2,1)S(1)} %collective-permute-done), channel_id=1, source_target_pairs={{0,64},{2,18},{4,68},{6,22},{8,72},{10,26},{12,76},{14,30},{16,80}... | collective-permute-start | bytes 417800 | tf_op jit(solution)/shard_map/ppermute | solution.py:83
  35.5 14.8 %collective-permute-done.12.weight_mine = bf16[256,2048]{1,0:T(8,128)(2,1)} collective-permute-done((bf16[256,2048]{1,0:T(8,128)(2,1)}, bf16[256,2048]{1,0:T(8,128)(2,1)}, u32[]{:S(2)}, u32[]{:S(2)}) %collective-permute-start.12) | collective-permute-done | bytes 1048608 | tf_op jit(solution)/shard_map/ppermute | solution.py:725
  50.2 2.4 collective-permute-start.13
  54.4 6.8 %page_attention.2.refs_3_ = bf16[32,400,128]{2,1,0:T(8,128)(2,1)} custom-call(s32[1]{0:T(128)} %bitcast.3.here, s32[8]{0:T(128)} %bitcast.73, s32[8]{0:T(128)} %bitcast.71, s32[8]{0:T(128)} %bitcast.72, bf16[8,2,128,512]{3,2,1,0:T(8,128)(2,1)} %pages_a_in.3, bf16[8,2,128,512]{3,2,1,0:T(8,128)(2,1)} %copy-done.1, bf16[8,136,512]{2,1,0:T(8,128)(2,1)} %copy-done.3), custom_call_target="tpu_custom_call" | custom-call | flops 805306368 | bytes 5242880 | tf_op jit(solution)/shard_map/page_attention/pallas_call | solution.py:214
  62.7 13.1 %page_attention.3 = bf16[32,400,128]{2,1,0:T(8,128)(2,1)} custom-call(s32[1]{0:T(128)} %bitcast.3.here, s32[24]{0:T(128)} %slice.76.chip_of, s32[24]{0:T(128)} %slice.77.page_a, s32[24]{0:T(128)} %slice.78.page_b, bf16[8,2,128,512]{3,2,1,0:T(8,128)(2,1)} %pages_a_in.3, bf16[8,2,128,512]{3,2,1,0:T(8,128)(2,1)} %copy-done.1, ...), custom_call_target="tpu_custom_call", output_to_operand_aliasing={{}: (9, {})} | custom-call | flops 2415919104 | bytes 5242880 | tf_op jit(solution)/shard_map/page_attention/pallas_call | solution.py:214
  75.9 5.0 %all-to-all-start = ((bf16[32,400,128]{2,1,0:T(8,128)(2,1)}), bf16[32,400,128]{2,1,0:T(8,128)(2,1)}, u32[]{:S(2)}, u32[]{:S(2)}) async-start(bf16[32,400,128]{2,1,0:T(8,128)(2,1)} %page_attention.3), calls=%async_computation | async-start | bytes 6553600 | tf_op jit(solution)/shard_map/all_to_all | solution.py:750
  83.1 2.9 %own_attention.1 = (f32[4,128,128]{2,1,0:T(8,128)}, f32[8,128]{1,0:T(8,128)}) custom-call(s32[128,1]{1,0:T(8,128)} %copy.64.request_col, s32[1,128]{1,0:T(1,128)} %bitcast.65, bf16[128,512]{1,0:T(8,128)(2,1)} %queries.1, bf16[128,512]{1,0:T(8,128)(2,1)} %keys.1, bf16[128,512]{1,0:T(8,128)(2,1)} %values.1), custom_call_target="tpu_custom_call" | custom-call | flops 67108864 | bytes 1048576 | tf_op jit(solution)/shard_map/own_attention/pallas_call | solution.py:281
  87.6 33.6 %all-to-all-done.arrived_in = bf16[32,400,128]{2,1,0:T(8,128)(2,1)} async-done(((bf16[32,400,128]{2,1,0:T(8,128)(2,1)}), bf16[32,400,128]{2,1,0:T(8,128)(2,1)}, u32[]{:S(2)}, u32[]{:S(2)}) %all-to-all-start) | async-done | bytes 3276832 | tf_op jit(solution)/shard_map/all_to_all | solution.py:750
  121.2 7.2 %merge_attention.1.att = bf16[128,512]{1,0:T(8,128)(2,1)} custom-call(s32[192]{0:T(256)} %reshape.217.codes, bf16[32,400,128]{2,1,0:T(8,128)(2,1)} %all-to-all-done.arrived_in, f32[4,128,128]{2,1,0:T(8,128)} %get-tuple-element.58.own_in, f32[8,128]{1,0:T(8,128)} %get-tuple-element.59.own_sums_in), custom_call_target="tpu_custom_call" | custom-call | flops 67108864 | bytes 4194304 | tf_op jit(solution)/shard_map/merge_attention/pallas_call | solution.py:379
  128.4 7.9 %collective-permute-start.14 = (bf16[128,512]{1,0:T(8,128)(2,1)}, bf16[128,512]{1,0:T(8,128)(2,1)S(1)}, u32[]{:S(2)}, u32[]{:S(2)}) collective-permute-start(bf16[128,512]{1,0:T(8,128)(2,1)} %merge_attention.1.att), channel_id=1, source_target_pairs={{0,1},{1,0},{2,3},{3,2},{4,5},{5,4},{6,7},{7,6},{8,9},{9,8},{10,11... | collective-permute-start | bytes 393224 | tf_op jit(solution)/shard_map/ppermute | solution.py:754
  139.5 6.0 %project_dispatch.1 = (f32[128,1024]{1,0:T(8,128)}, bf16[1536,1024]{1,0:T(8,128)(2,1)}) custom-call(s32[3]{0:T(128)} %pad_add_fusion.1.side, bf16[128,512]{1,0:T(8,128)(2,1)} %merge_attention.1.att, bf16[128,512]{1,0:T(8,128)(2,1)} %copy-done.9, bf16[512,2048]{1,0:T(8,128)(2,1)} %weight_in.1, bf16[256,2048]{1,0:T(8,128)(2,1)} %collective-permute-done.12.weight_mine, ...), custom_call_target="tpu_custom_call" | custom-call | flops 1342177280 | bytes 10485760 | tf_op jit(solution)/shard_map/project_dispatch/pallas_call | solution.py:471
  145.5 9.9 %all-to-all-start.1 = ((bf16[64,24,1024]{2,1,0:T(8,128)(2,1)}), bf16[64,24,1024]{2,1,0:T(8,128)(2,1)}, u32[]{:S(2)}, u32[]{:S(2)}) async-start(bf16[64,24,1024]{2,1,0:T(8,128)(2,1)} %bitcast.53), calls=%async_computation.1 | async-start | bytes 6291456 | tf_op jit(solution)/shard_map/all_to_all | solution.py:766
  155.5 2.9 %copy.67 = bf16[1,2048,704]{2,1,0:T(8,128)(2,1)} copy(bf16[1,2048,704]{1,2,0:T(8,128)(2,1)S(1)} %copy-done.2) | data formatting | bytes 5767168 | tf_op args[12]
  158.3 4.6 %copy.68 = bf16[1,2048,704]{2,1,0:T(8,128)(2,1)} copy(bf16[1,2048,704]{1,2,0:T(8,128)(2,1)} %param.41) | data formatting | bytes 5767168 | tf_op args[13]
  162.9 34.7 %all-to-all-done.1.rows = bf16[64,24,1024]{2,1,0:T(8,128)(2,1)} async-done(((bf16[64,24,1024]{2,1,0:T(8,128)(2,1)}), bf16[64,24,1024]{2,1,0:T(8,128)(2,1)}, u32[]{:S(2)}, u32[]{:S(2)}) %all-to-all-start.1) | async-done | bytes 3145760 | tf_op jit(solution)/shard_map/all_to_all | solution.py:766
  197.6 12.4 %expert.1 = bf16[64,2,24,512]{3,2,1,0:T(8,128)(2,1)} custom-call(bf16[64,24,1024]{2,1,0:T(8,128)(2,1)} %all-to-all-done.1.rows, bf16[2048,704]{1,0:T(8,128)(2,1)} %bitcast.54, bf16[2048,704]{1,0:T(8,128)(2,1)} %bitcast.55, bf16[704,2048]{1,0:T(8,128)(2,1)} %bitcast.74), custom_call_target="tpu_custom_call" | custom-call | flops 6643777536 | bytes 15728640 | tf_op jit(solution)/shard_map/expert/pallas_call | solution.py:566
  210.0 7.2 %all-to-all-start.2 = ((bf16[128,24,512]{2,1,0:T(8,128)(2,1)}), bf16[128,24,512]{2,1,0:T(8,128)(2,1)}, u32[]{:S(2)}, u32[]{:S(2)}) async-start(bf16[128,24,512]{2,1,0:T(8,128)(2,1)} %bitcast.52), calls=%async_computation.2 | async-start | bytes 6291456 | tf_op jit(solution)/shard_map/all_to_all | solution.py:768
  217.3 3.0 %select_convert_fusion.shares = bf16[256,3072]{1,0:T(8,128)(2,1)} fusion(pred[256,3072]{1,0:T(32,128)(4,1)S(1)} %copy-done.4, f32[256]{0:T(256)S(1)} %bitcast.68, f32[256]{0:T(256)S(1)} %bitcast.69, f32[256]{0:T(256)S(1)} %bitcast.70, f32[256]{0:T(256)S(1)} %bitcast.67, s32[3072]{0:T(1024)S(1)} %copy-done.10, s32[256]{0:T(256)S(1)} %bitcast.59, ...), kind=kLoop, calls=%fused_computation.2 | loop fusion | flops 10223616 | bytes 2379776 | tf_op jit(solution)/shard_map/convert_element_type | solution.py:672
  220.3 38.2 %all-to-all-done.2 = bf16[128,24,512]{2,1,0:T(8,128)(2,1)} async-done(((bf16[128,24,512]{2,1,0:T(8,128)(2,1)}), bf16[128,24,512]{2,1,0:T(8,128)(2,1)}, u32[]{:S(2)}, u32[]{:S(2)}) %all-to-all-start.2) | async-done | bytes 3145760 | tf_op jit(solution)/shard_map/all_to_all | solution.py:768
  258.5 3.7 %combine.1 = bf16[128,1024]{1,0:T(8,128)(2,1)} custom-call(f32[128,1024]{1,0:T(8,128)} %get-tuple-element.63.mixed, bf16[256,3072]{1,0:T(8,128)(2,1)} %select_convert_fusion.shares, bf16[3072,512]{1,0:T(8,128)(2,1)} %bitcast.34.rows), custom_call_target="tpu_custom_call" | custom-call | flops 805306368 | bytes 6291456 | tf_op jit(solution)/shard_map/combine/pallas_call | solution.py:615
  (105 shorter events, 29.4 us)
Async XLA Ops:
  0.0 20.2 %copy-start = (s32[1,64]{1,0:T(1,128)S(1)}, s32[1,64]{1,0:T(1,128)}, u32[]{:S(2)}) copy-start(s32[1,64]{1,0:T(1,128)} %param.34) | copy-start | bytes 772
  0.0 22.2 %collective-permute-start.4 = (bf16[8,2,128,512]{3,2,1,0:T(8,128)(2,1)}, bf16[8,2,128,512]{3,2,1,0:T(8,128)(2,1)S(1)}, u32[]{:S(2)}, u32[]{:S(2)}) collective-permute-start(bf16[8,2,128,512]{3,2,1,0:T(8,128)(2,1)} %pages_a_in.3), channel_id=1, source_target_pairs={{0,2},{2,0},{4,6},{6,4},{8,10},{10,8},{12,14},{14,12},{16,18},{18,... | collective-permute-start | bytes 6291464 | tf_op jit(solution)/shard_map/ppermute | solution.py:712
  5.7 15.9 %collective-permute-start = (bf16[136,512]{1,0:T(8,128)(2,1)S(1)}, bf16[136,512]{1,0:T(8,128)(2,1)S(1)}, u32[]{:S(2)}, u32[]{:S(2)}) collective-permute-start(bf16[136,512]{1,0:T(8,128)(2,1)S(1)} %fusion.2), channel_id=1, source_target_pairs={{0,4},{2,6},{4,0},{6,2},{8,12},{10,14},{12,8},{14,10},{16,20},{18,... | collective-permute-start | bytes 417800 | tf_op jit(solution)/shard_map/ppermute | solution.py:720
  8.6 13.0 %collective-permute-start.1 = (bf16[136,512]{1,0:T(8,128)(2,1)S(1)}, bf16[136,512]{1,0:T(8,128)(2,1)S(1)}, u32[]{:S(2)}, u32[]{:S(2)}) collective-permute-start(bf16[136,512]{1,0:T(8,128)(2,1)S(1)} %fusion.2), channel_id=1, source_target_pairs={{0,32},{2,10},{4,36},{6,14},{8,40},{10,18},{12,44},{14,22},{16,48}... | collective-permute-start | bytes 417800 | tf_op jit(solution)/shard_map/ppermute | solution.py:83
  10.2 11.4 %collective-permute-start.2 = (bf16[136,512]{1,0:T(8,128)(2,1)S(1)}, bf16[136,512]{1,0:T(8,128)(2,1)S(1)}, u32[]{:S(2)}, u32[]{:S(2)}) collective-permute-start(bf16[136,512]{1,0:T(8,128)(2,1)S(1)} %fusion.2), channel_id=1, source_target_pairs={{0,64},{2,18},{4,68},{6,22},{8,72},{10,26},{12,76},{14,30},{16,80}... | collective-permute-start | bytes 417800 | tf_op jit(solution)/shard_map/ppermute | solution.py:83
  13.5 3.0 %collective-permute-start.5 = (s32[1,64]{1,0:T(1,128)}, s32[1,64]{1,0:T(1,128)S(1)}, u32[]{:S(2)}, u32[]{:S(2)}) collective-permute-start(s32[1,64]{1,0:T(1,128)} %param.34), channel_id=1, source_target_pairs={{0,2},{2,0},{4,6},{6,4},{8,10},{10,8},{12,14},{14,12},{16,18},{18,... | collective-permute-start | bytes 776 | tf_op jit(solution)/shard_map/ppermute | solution.py:713
  16.6 5.7 %collective-permute-start.3 = (bf16[136,512]{1,0:T(8,128)(2,1)S(1)}, bf16[136,512]{1,0:T(8,128)(2,1)S(1)}, u32[]{:S(2)}, u32[]{:S(2)}) collective-permute-start(bf16[136,512]{1,0:T(8,128)(2,1)S(1)} %fusion.2), channel_id=1, source_target_pairs={{0,96},{2,26},{4,100},{6,30},{8,104},{10,2},{12,108},{14,6},{16,11... | collective-permute-start | bytes 417800 | tf_op jit(solution)/shard_map/ppermute | solution.py:83
  20.9 33.5 %copy-start.15 = (s32[32]{0:T(128)}, s32[32]{0:T(128)S(1)}, u32[]{:S(2)}) copy-start(s32[32]{0:T(128)S(1)} %gather_fusion) | copy-start | bytes 388
  21.6 32.8 %copy-start.17 = (s32[32]{0:T(128)}, s32[32]{0:T(128)S(1)}, u32[]{:S(2)}) copy-start(s32[32]{0:T(128)S(1)} %fusion.14) | copy-start | bytes 388
  22.2 8.3 %collective-permute-start.6 = (bf16[136,512]{1,0:T(8,128)(2,1)S(1)}, bf16[136,512]{1,0:T(8,128)(2,1)}, u32[]{:S(2)}, u32[]{:S(2)}) collective-permute-start(bf16[136,512]{1,0:T(8,128)(2,1)S(1)} %collective-permute-done), channel_id=1, source_target_pairs={{0,32},{2,10},{4,36},{6,14},{8,40},{10,18},{12,44},{14,22},{16,48}... | collective-permute-start | bytes 417800 | tf_op jit(solution)/shard_map/ppermute | solution.py:83
  22.5 9.0 %collective-permute-start.7 = (bf16[136,512]{1,0:T(8,128)(2,1)S(1)}, bf16[136,512]{1,0:T(8,128)(2,1)}, u32[]{:S(2)}, u32[]{:S(2)}) collective-permute-start(bf16[136,512]{1,0:T(8,128)(2,1)S(1)} %collective-permute-done), channel_id=1, source_target_pairs={{0,64},{2,18},{4,68},{6,22},{8,72},{10,26},{12,76},{14,30},{16,80}... | collective-permute-start | bytes 417800 | tf_op jit(solution)/shard_map/ppermute | solution.py:83
  26.6 5.8 %collective-permute-start.8 = (bf16[136,512]{1,0:T(8,128)(2,1)S(1)}, bf16[136,512]{1,0:T(8,128)(2,1)}, u32[]{:S(2)}, u32[]{:S(2)}) collective-permute-start(bf16[136,512]{1,0:T(8,128)(2,1)S(1)} %collective-permute-done), channel_id=1, source_target_pairs={{0,96},{2,26},{4,100},{6,30},{8,104},{10,2},{12,108},{14,6},{16,11... | collective-permute-start | bytes 417800 | tf_op jit(solution)/shard_map/ppermute | solution.py:83
  26.7 23.6 %collective-permute-start.12 = (bf16[256,2048]{1,0:T(8,128)(2,1)}, bf16[256,2048]{1,0:T(8,128)(2,1)}, u32[]{:S(2)}, u32[]{:S(2)}) collective-permute-start(bf16[256,2048]{1,0:T(8,128)(2,1)} %constant_dynamic-slice_fusion.1), channel_id=1, source_target_pairs={{0,1},{1,0},{2,3},{3,2},{4,5},{5,4},{6,7},{7,6},{8,9},{9,8},{10,11... | collective-permute-start | bytes 3145736 | tf_op jit(solution)/shard_map/ppermute | solution.py:725
  30.5 23.9 %copy-start.16 = (s32[32]{0:T(128)}, s32[32]{0:T(128)S(1)}, u32[]{:S(2)}) copy-start(s32[32]{0:T(128)S(1)} %gather_fusion.1) | copy-start | bytes 388
  33.4 21.1 %copy-start.3 = (bf16[8,136,512]{2,1,0:T(8,128)(2,1)}, bf16[8,136,512]{2,1,0:T(8,128)(2,1)S(1)}, u32[]{:S(2)}) copy-start(bf16[8,136,512]{2,1,0:T(8,128)(2,1)S(1)} %bitcast_dynamic-update-slice_fusion.refs_0_) | copy-start | bytes 3342340
  33.4 27.9 %collective-permute-start.10 = (bf16[8,136,512]{2,1,0:T(8,128)(2,1)S(1)}, bf16[8,136,512]{2,1,0:T(8,128)(2,1)}, u32[]{:S(2)}, u32[]{:S(2)}) collective-permute-start(bf16[8,136,512]{2,1,0:T(8,128)(2,1)S(1)} %bitcast_dynamic-update-slice_fusion.refs_0_), channel_id=1, source_target_pairs={{0,24},{2,98},{4,28},{6,102},{8,0},{10,106},{12,4},{14,110},{16,8}... | collective-permute-start | bytes 3342344 | tf_op jit(solution)/shard_map/ppermute | solution.py:87
  34.8 26.5 %collective-permute-start.11 = (bf16[8,136,512]{2,1,0:T(8,128)(2,1)S(1)}, bf16[8,136,512]{2,1,0:T(8,128)(2,1)}, u32[]{:S(2)}, u32[]{:S(2)}) collective-permute-start(bf16[8,136,512]{2,1,0:T(8,128)(2,1)S(1)} %bitcast_dynamic-update-slice_fusion.refs_0_), channel_id=1, source_target_pairs={{0,16},{2,66},{4,20},{6,70},{8,24},{10,74},{12,28},{14,78},{16,0},... | collective-permute-start | bytes 3342344 | tf_op jit(solution)/shard_map/ppermute | solution.py:87
  34.8 27.9 %collective-permute-start.9 = (bf16[8,136,512]{2,1,0:T(8,128)(2,1)S(1)}, bf16[8,136,512]{2,1,0:T(8,128)(2,1)}, u32[]{:S(2)}, u32[]{:S(2)}) collective-permute-start(bf16[8,136,512]{2,1,0:T(8,128)(2,1)S(1)} %bitcast_dynamic-update-slice_fusion.refs_0_), channel_id=1, source_target_pairs={{0,8},{2,34},{4,12},{6,38},{8,16},{10,42},{12,20},{14,46},{16,24},... | collective-permute-start | bytes 3342344 | tf_op jit(solution)/shard_map/ppermute | solution.py:87
  50.2 12.5 %collective-permute-start.13 = (bf16[256,2048]{1,0:T(8,128)(2,1)}, bf16[256,2048]{1,0:T(8,128)(2,1)}, u32[]{:S(2)}, u32[]{:S(2)}) collective-permute-start(bf16[256,2048]{1,0:T(8,128)(2,1)} %collective-permute-done.12.weight_mine), channel_id=1, source_target_pairs={{0,2},{2,0},{4,6},{6,4},{8,10},{10,8},{12,14},{14,12},{16,18},{18,... | collective-permute-start | bytes 3145736 | tf_op jit(solution)/shard_map/ppermute | solution.py:742
  75.9 10.1 %copy-start.5 = (pred[1536,256]{1,0:T(32,128)(4,1)S(1)}, pred[1536,256]{1,0:T(32,128)(4,1)}, u32[]{:S(2)}) copy-start(pred[1536,256]{1,0:T(32,128)(4,1)} %constant.96.clone) | copy-start | bytes 1179652
  75.9 45.3 %all-to-all-start = ((bf16[32,400,128]{2,1,0:T(8,128)(2,1)}), bf16[32,400,128]{2,1,0:T(8,128)(2,1)}, u32[]{:S(2)}, u32[]{:S(2)}) async-start(bf16[32,400,128]{2,1,0:T(8,128)(2,1)} %page_attention.3), calls=%async_computation | async-start | bytes 6553600 | tf_op jit(solution)/shard_map/all_to_all | solution.py:750
  128.4 10.5 %collective-permute-start.14 = (bf16[128,512]{1,0:T(8,128)(2,1)}, bf16[128,512]{1,0:T(8,128)(2,1)S(1)}, u32[]{:S(2)}, u32[]{:S(2)}) collective-permute-start(bf16[128,512]{1,0:T(8,128)(2,1)} %merge_attention.1.att), channel_id=1, source_target_pairs={{0,1},{1,0},{2,3},{3,2},{4,5},{5,4},{6,7},{7,6},{8,9},{9,8},{10,11... | collective-permute-start | bytes 393224 | tf_op jit(solution)/shard_map/ppermute | solution.py:754
  145.5 52.1 %all-to-all-start.1 = ((bf16[64,24,1024]{2,1,0:T(8,128)(2,1)}), bf16[64,24,1024]{2,1,0:T(8,128)(2,1)}, u32[]{:S(2)}, u32[]{:S(2)}) async-start(bf16[64,24,1024]{2,1,0:T(8,128)(2,1)} %bitcast.53), calls=%async_computation.1 | async-start | bytes 6291456 | tf_op jit(solution)/shard_map/all_to_all | solution.py:766
  210.0 48.4 %all-to-all-start.2 = ((bf16[128,24,512]{2,1,0:T(8,128)(2,1)}), bf16[128,24,512]{2,1,0:T(8,128)(2,1)}, u32[]{:S(2)}, u32[]{:S(2)}) async-start(bf16[128,24,512]{2,1,0:T(8,128)(2,1)} %bitcast.52), calls=%async_computation.2 | async-start | bytes 6291456 | tf_op jit(solution)/shard_map/all_to_all | solution.py:768
  (12 other events, 77.3 us)

commit v7 on v6

--- a/solution.py
+++ b/solution.py
@@ -81,6 +81,34 @@
 
 def ring_line(block):
     return [block] + [lax.ppermute(block, "req", perm_ring(0, step)) for step in (1, 2, 3)]
+
+
+def stack_kernel(*refs):
+    out, sems = refs[-2:]
+    copies = [
+        pltpu.make_async_copy(block, out.at[i], sems.at[i]) for i, block in enumerate(refs[:-2])
+    ]
+    for copy in copies:
+        copy.start()
+    for copy in copies:
+        copy.wait()
+
+
+def stack_blocks(blocks):
+    count = len(blocks)
+    size = math.prod(blocks[0].shape) * 2
+    return pl.pallas_call(
+        stack_kernel,
+        out_shape=jax.ShapeDtypeStruct((count, *blocks[0].shape), BF16),
+        in_specs=[pl.BlockSpec(memory_space=pl.ANY)] * count,
+        out_specs=pl.BlockSpec(memory_space=pl.ANY),
+        scratch_shapes=[pltpu.SemaphoreType.DMA((count,))],
+        compiler_params=pltpu.CompilerParams(vmem_limit_bytes=8 << 20),
+        cost_estimate=pl.CostEstimate(
+            flops=0, bytes_accessed=2 * count * size, transcendentals=0
+        ),
+        name="stack_blocks",
+    )(*blocks)
 
 
 def ring_rest(line):
@@ -715,15 +743,15 @@
     note = jnp.zeros((8, queries.shape[1]), BF16)
     note = note.at[0, : NCHIP * SLOTS].set(codes.T.reshape(-1).astype(BF16))
     block = jnp.concatenate([queries, note], axis=0)
-    far_rows = output_weight.shape[0] // NC
-    far_part = lax.dynamic_slice_in_dim(output_weight, core * far_rows, far_rows, 0)
     near = lax.ppermute(block, "req", perm_x())
     line_a = ring_line(block)
-    near, line_a, pages_far, sends_far, far_part = lax.optimization_barrier(
-        (near, line_a, pages_far, sends_far, far_part)
+    near, line_a, pages_far, sends_far, weight = lax.optimization_barrier(
+        (near, line_a, pages_far, sends_far, output_weight)
     )
+    line = stack_blocks(line_a + ring_line(near))
+    far_rows = weight.shape[0] // NC
+    far_part = lax.dynamic_slice_in_dim(weight, core * far_rows, far_rows, 0)
     weight_mine = lax.ppermute(far_part, "tp", swap)
-    line = jnp.stack(line_a + ring_line(near))
 
     chips = lax.dynamic_index_in_dim(jnp.asarray(chip_table()), me, 0, keepdims=False)
     page_a = page_sends[0][chips * NC + core]
@@ -733,23 +761,22 @@
     here = me // NC
     own, own_sums = own_attention(request_ids, queries, new_keys, new_values)
     picks, shares = routing(expert_ids, expert_weights)
-    own, picks = lax.optimization_barrier((own, picks))
 
     parts = None
     for first, last in ((0, 1), (1, 4)):
         group = pieces[first:last]
         if first:
-            weight_other = lax.ppermute(weight_mine, "req", perm_core())
-            group, parts, weight_mine, weight_other = lax.optimization_barrier(
-                (group, parts, weight_mine, weight_other)
-            )
+            group, parts = lax.optimization_barrier((group, parts))
         rows = slice(8 * first, 8 * last)
         parts = page_attention(
             here[None], chips[rows], page_a[rows], page_b[rows], page_store, pages_far, group, parts
         )
+    parts, weight_mine = lax.optimization_barrier((parts, weight_mine))
+    weight_other = lax.ppermute(weight_mine, "req", perm_core())
     arrived = lax.all_to_all(
         parts, "req", 0, 0, tiled=True, axis_index_groups=core_groups()
     )
+    own, picks, weight_other = lax.optimization_barrier((own, picks, weight_other))
     attended = merge_attention(codes.reshape(-1), arrived, own, own_sums)
     attended_far = lax.ppermute(attended, "tp", swap)
     mixed, sent = project(

time: 263 us -> 257 us (0.977)
  local copies, waits for them, and re-layouts: 23.4 us -> 18.5 us
    ppermute x1, waiting for transfers between devices: 14.8 us -> 0.01 us  [shards(): weight_mine = lax.ppermute(far_part, 'tp', swap)]
    ppermute x3, waiting for transfers between devices: 1.45 us -> 16 us  [ring_rest(): return [lax.ppermute(line, 'req', perm_ring(1, step)) for step in (1, 3, 2)]]
    ppermute x1, starting transfers between devices: 7.91 us -> 2.53 us  [shards(): attended_far = lax.ppermute(attended, 'tp', swap)]
    unnamed x48 -> x33, local copies, waits for them, and re-layouts: 13.4 us -> 8.83 us
    ppermute x6, starting transfers between devices: 13 us -> 9.4 us  [ring_line(): lax.ppermute(block, 'req', perm_ring(0, step))]
    all_to_all x1, waiting for transfers between devices: 33.6 us -> 30.4 us  [shards(): lax.all_to_all(parts, 'req', 0, 0, tiled=True, axis_index_groups=core_gro...]
    ppermute x6, waiting for transfers between devices: 0.58 us -> 3.48 us  [ring_line(): lax.ppermute(block, 'req', perm_ring(0, step))]
  transfers between devices with their start and end apart: 18 -> 18, of which waited for: 7 -> 10; matrix products, arithmetic and copies ran while one was open for 12% -> 10% of each run, Pallas kernels for 4% -> 9%
where the time goes in v7:
time: 257 us; the launch traced here: 256 us
  waiting for transfers between devices  125 us (49%)
  Pallas kernels  53.5 us (21%)
  starting transfers between devices  50 us (19%)
  local copies, waits for them, and re-layouts  18.5 us (7%)
  other arithmetic  8.66 us (3%)
    all_to_all x1, waiting for transfers between devices, shards(): lax.all_to_all(result.reshape(2 * NREQ, 2 * CAP, width // 4), ('req', 'tp...  38.2 us
    all_to_all x1, waiting for transfers between devices, shards(): lax.all_to_all(sent.reshape(NREQ, 2 * CAP, half), 'req', 0, 0, tiled=True)  34.7 us
    all_to_all x1, waiting for transfers between devices, shards(): lax.all_to_all(parts, 'req', 0, 0, tiled=True, axis_index_groups=core_gro...  30.4 us
    pallas_call x2, Pallas kernels, page_attention(): pl.pallas_call(page_kernel, out_shape=jax.ShapeDtypeStruct((NCHIP, BLOCK,...  19.9 us
    ppermute x3, waiting for transfers between devices, ring_rest(): return [lax.ppermute(line, 'req', perm_ring(1, step)) for step in (1, 3, 2)]  16 us
    pallas_call x1, Pallas kernels, run_expert(): pl.pallas_call(expert_kernel, out_shape=jax.ShapeDtypeStruct((rows.shape[...  12.4 us
    all_to_all x1, starting transfers between devices, shards(): lax.all_to_all(sent.reshape(NREQ, 2 * CAP, half), 'req', 0, 0, tiled=True)  12.3 us
    ppermute x6, starting transfers between devices, ring_line(): lax.ppermute(block, 'req', perm_ring(0, step))  9.4 us
  transfers between devices with their start and end apart: 18, of which 10 were waited for; matrix products, arithmetic and copies ran while one was open for 10% of the time, Pallas kernels for 9%

profile of v7, /device:TPU:1, one launch (start us, length us, event | category | flops | bytes accessed | tf_op | source)
XLA Modules:
  0.0 256.3 jit_solution(10094848570027927652)
XLA Ops:
  5.7 2.9 %collective-permute-start = (bf16[136,512]{1,0:T(8,128)(2,1)S(1)}, bf16[136,512]{1,0:T(8,128)(2,1)S(1)}, u32[]{:S(2)}, u32[]{:S(2)}) collective-permute-start(bf16[136,512]{1,0:T(8,128)(2,1)S(1)} %fusion.2.refs_0_), channel_id=1, source_target_pairs={{0,4},{2,6},{4,0},{6,2},{8,12},{10,14},{12,8},{14,10},{16,20},{18,... | collective-permute-start | bytes 417800 | tf_op jit(solution)/shard_map/ppermute | solution.py:746
  10.2 3.3 %collective-permute-start.2 = (bf16[136,512]{1,0:T(8,128)(2,1)S(1)}, bf16[136,512]{1,0:T(8,128)(2,1)S(1)}, u32[]{:S(2)}, u32[]{:S(2)}) collective-permute-start(bf16[136,512]{1,0:T(8,128)(2,1)S(1)} %fusion.2.refs_0_), channel_id=1, source_target_pairs={{0,64},{2,18},{4,68},{6,22},{8,72},{10,26},{12,76},{14,30},{16,80}... | collective-permute-start | bytes 417800 | tf_op jit(solution)/shard_map/ppermute | solution.py:83
  15.1 2.7 %collective-permute-done.2.refs_2_ = bf16[136,512]{1,0:T(8,128)(2,1)S(1)} collective-permute-done((bf16[136,512]{1,0:T(8,128)(2,1)S(1)}, bf16[136,512]{1,0:T(8,128)(2,1)S(1)}, u32[]{:S(2)}, u32[]{:S(2)}) %collective-permute-start.2) | collective-permute-done | bytes 139296 | tf_op jit(solution)/shard_map/ppermute | solution.py:83
  26.5 3.1 %collective-permute-start.10 = (bf16[8,136,512]{2,1,0:T(8,128)(2,1)S(1)}, bf16[8,136,512]{2,1,0:T(8,128)(2,1)}, u32[]{:S(2)}, u32[]{:S(2)}) collective-permute-start(bf16[8,136,512]{2,1,0:T(8,128)(2,1)S(1)} %stack_blocks.1.refs_0_), channel_id=1, source_target_pairs={{0,24},{2,98},{4,28},{6,102},{8,0},{10,106},{12,4},{14,110},{16,8}... | collective-permute-start | bytes 3342344 | tf_op jit(solution)/shard_map/ppermute | solution.py:115
  34.9 6.8 %page_attention.2.refs_3_ = bf16[32,400,128]{2,1,0:T(8,128)(2,1)} custom-call(s32[1]{0:T(128)} %bitcast.3.here, s32[8]{0:T(128)} %bitcast.57, s32[8]{0:T(128)} %bitcast.55, s32[8]{0:T(128)} %bitcast.56, bf16[8,2,128,512]{3,2,1,0:T(8,128)(2,1)} %pages_a_in.3, bf16[8,2,128,512]{3,2,1,0:T(8,128)(2,1)} %collective-permute-done.4.pages_b_in, ...), custom_call_target="tpu_custom_call" | custom-call | flops 805306368 | bytes 5242880 | tf_op jit(solution)/shard_map/page_attention/pallas_call | solution.py:242
  41.7 12.2 %collective-permute-done.10.refs_1_ = bf16[8,136,512]{2,1,0:T(8,128)(2,1)} collective-permute-done((bf16[8,136,512]{2,1,0:T(8,128)(2,1)S(1)}, bf16[8,136,512]{2,1,0:T(8,128)(2,1)}, u32[]{:S(2)}, u32[]{:S(2)}) %collective-permute-start.10) | collective-permute-done | bytes 1114144 | tf_op jit(solution)/shard_map/ppermute | solution.py:115
  53.9 3.8 %collective-permute-done.9.refs_0_ = bf16[8,136,512]{2,1,0:T(8,128)(2,1)} collective-permute-done((bf16[8,136,512]{2,1,0:T(8,128)(2,1)S(1)}, bf16[8,136,512]{2,1,0:T(8,128)(2,1)}, u32[]{:S(2)}, u32[]{:S(2)}) %collective-permute-start.9) | collective-permute-done | bytes 1114144 | tf_op jit(solution)/shard_map/ppermute | solution.py:115
  57.7 13.1 %page_attention.3 = bf16[32,400,128]{2,1,0:T(8,128)(2,1)} custom-call(s32[1]{0:T(128)} %bitcast.3.here, s32[24]{0:T(128)} %slice.76.chip_of, s32[24]{0:T(128)} %slice.77.page_a, s32[24]{0:T(128)} %slice.78.page_b, bf16[8,2,128,512]{3,2,1,0:T(8,128)(2,1)} %pages_a_in.3, ...), custom_call_target="tpu_custom_call", output_to_operand_aliasing={{}: (9, {})} | custom-call | flops 2415919104 | bytes 5242880 | tf_op jit(solution)/shard_map/page_attention/pallas_call | solution.py:242
  70.9 5.0 %all-to-all-start = ((bf16[32,400,128]{2,1,0:T(8,128)(2,1)}), bf16[32,400,128]{2,1,0:T(8,128)(2,1)}, u32[]{:S(2)}, u32[]{:S(2)}) async-start(bf16[32,400,128]{2,1,0:T(8,128)(2,1)} %page_attention.3), calls=%async_computation | async-start | bytes 6553600 | tf_op jit(solution)/shard_map/all_to_all | solution.py:776
  75.9 4.7 %collective-permute-start.13 = (bf16[256,2048]{1,0:T(8,128)(2,1)}, bf16[256,2048]{1,0:T(8,128)(2,1)S(1)}, u32[]{:S(2)}, u32[]{:S(2)}) collective-permute-start(bf16[256,2048]{1,0:T(8,128)(2,1)} %collective-permute-done.12.weight_mine), channel_id=1, source_target_pairs={{0,2},{2,0},{4,6},{6,4},{8,10},{10,8},{12,14},{14,12},{16,18},{18,... | collective-permute-start | bytes 3145736 | tf_op jit(solution)/shard_map/ppermute | solution.py:775
  82.8 2.9 %own_attention.1 = (f32[4,128,128]{2,1,0:T(8,128)}, f32[8,128]{1,0:T(8,128)}) custom-call(s32[128,1]{1,0:T(8,128)} %copy.64.request_col, s32[1,128]{1,0:T(1,128)} %bitcast.49, bf16[128,512]{1,0:T(8,128)(2,1)} %queries.1, bf16[128,512]{1,0:T(8,128)(2,1)} %keys.1, bf16[128,512]{1,0:T(8,128)(2,1)} %values.1), custom_call_target="tpu_custom_call" | custom-call | flops 67108864 | bytes 1048576 | tf_op jit(solution)/shard_map/own_attention/pallas_call | solution.py:309
  87.4 30.4 %all-to-all-done.arrived_in = bf16[32,400,128]{2,1,0:T(8,128)(2,1)} async-done(((bf16[32,400,128]{2,1,0:T(8,128)(2,1)}), bf16[32,400,128]{2,1,0:T(8,128)(2,1)}, u32[]{:S(2)}, u32[]{:S(2)}) %all-to-all-start) | async-done | bytes 3276832 | tf_op jit(solution)/shard_map/all_to_all | solution.py:776
  117.8 7.2 %merge_attention.1.att = bf16[128,512]{1,0:T(8,128)(2,1)} custom-call(s32[192]{0:T(256)} %reshape.217.codes, bf16[32,400,128]{2,1,0:T(8,128)(2,1)} %all-to-all-done.arrived_in, f32[4,128,128]{2,1,0:T(8,128)} %get-tuple-element.61.own_in, f32[8,128]{1,0:T(8,128)} %get-tuple-element.62.own_sums_in), custom_call_target="tpu_custom_call" | custom-call | flops 67108864 | bytes 4194304 | tf_op jit(solution)/shard_map/merge_attention/pallas_call | solution.py:407
  125.0 2.5 collective-permute-start.14
  130.8 6.0 %project_dispatch.1 = (f32[128,1024]{1,0:T(8,128)}, bf16[1536,1024]{1,0:T(8,128)(2,1)}) custom-call(s32[3]{0:T(128)} %pad_add_fusion.1.side, bf16[128,512]{1,0:T(8,128)(2,1)} %merge_attention.1.att, bf16[128,512]{1,0:T(8,128)(2,1)} %copy-done.5, bf16[512,2048]{1,0:T(8,128)(2,1)} %weight_in.1, bf16[256,2048]{1,0:T(8,128)(2,1)} %collective-permute-done.12.weight_mine, ...), custom_call_target="tpu_custom_call" | custom-call | flops 1342177280 | bytes 10485760 | tf_op jit(solution)/shard_map/project_dispatch/pallas_call | solution.py:499
  136.8 12.3 %all-to-all-start.1 = ((bf16[64,24,1024]{2,1,0:T(8,128)(2,1)}), bf16[64,24,1024]{2,1,0:T(8,128)(2,1)}, u32[]{:S(2)}, u32[]{:S(2)}) async-start(bf16[64,24,1024]{2,1,0:T(8,128)(2,1)} %bitcast.37), calls=%async_computation.1 | async-start | bytes 6291456 | tf_op jit(solution)/shard_map/all_to_all | solution.py:793
  149.1 2.9 %copy.67 = bf16[1,2048,704]{2,1,0:T(8,128)(2,1)} copy(bf16[1,2048,704]{1,2,0:T(8,128)(2,1)S(1)} %copy-done.1) | data formatting | bytes 5767168 | tf_op args[12]
  152.0 4.6 %copy.68 = bf16[1,2048,704]{2,1,0:T(8,128)(2,1)} copy(bf16[1,2048,704]{1,2,0:T(8,128)(2,1)} %param.41) | data formatting | bytes 5767168 | tf_op args[13]
  156.6 34.7 %all-to-all-done.1.rows = bf16[64,24,1024]{2,1,0:T(8,128)(2,1)} async-done(((bf16[64,24,1024]{2,1,0:T(8,128)(2,1)}), bf16[64,24,1024]{2,1,0:T(8,128)(2,1)}, u32[]{:S(2)}, u32[]{:S(2)}) %all-to-all-start.1) | async-done | bytes 3145760 | tf_op jit(solution)/shard_map/all_to_all | solution.py:793
  191.2 12.4 %expert.1 = bf16[64,2,24,512]{3,2,1,0:T(8,128)(2,1)} custom-call(bf16[64,24,1024]{2,1,0:T(8,128)(2,1)} %all-to-all-done.1.rows, bf16[2048,704]{1,0:T(8,128)(2,1)} %bitcast.38, bf16[2048,704]{1,0:T(8,128)(2,1)} %bitcast.39, bf16[704,2048]{1,0:T(8,128)(2,1)} %bitcast.58), custom_call_target="tpu_custom_call" | custom-call | flops 6643777536 | bytes 15728640 | tf_op jit(solution)/shard_map/expert/pallas_call | solution.py:594
  203.6 7.5 %all-to-all-start.2 = ((bf16[128,24,512]{2,1,0:T(8,128)(2,1)}), bf16[128,24,512]{2,1,0:T(8,128)(2,1)}, u32[]{:S(2)}, u32[]{:S(2)}) async-start(bf16[128,24,512]{2,1,0:T(8,128)(2,1)} %bitcast.36), calls=%async_computation.2 | async-start | bytes 6291456 | tf_op jit(solution)/shard_map/all_to_all | solution.py:795
  211.2 3.0 %select_convert_fusion.shares = bf16[256,3072]{1,0:T(8,128)(2,1)} fusion(pred[256,3072]{1,0:T(32,128)(4,1)S(1)} %copy-done.3, f32[256]{0:T(256)S(1)} %bitcast.52, f32[256]{0:T(256)S(1)} %bitcast.53, f32[256]{0:T(256)S(1)} %bitcast.54, f32[256]{0:T(256)S(1)} %bitcast.51, s32[3072]{0:T(1024)S(1)} %copy-done.6, s32[256]{0:T(256)S(1)} %bitcast.43, ...), kind=kLoop, calls=%fused_computation.2 | loop fusion | flops 10223616 | bytes 2379776 | tf_op jit(solution)/shard_map/convert_element_type | solution.py:700
  214.2 38.2 %all-to-all-done.2 = bf16[128,24,512]{2,1,0:T(8,128)(2,1)} async-done(((bf16[128,24,512]{2,1,0:T(8,128)(2,1)}), bf16[128,24,512]{2,1,0:T(8,128)(2,1)}, u32[]{:S(2)}, u32[]{:S(2)}) %all-to-all-start.2) | async-done | bytes 3145760 | tf_op jit(solution)/shard_map/all_to_all | solution.py:795
  252.4 3.7 %combine.1 = bf16[128,1024]{1,0:T(8,128)(2,1)} custom-call(f32[128,1024]{1,0:T(8,128)} %get-tuple-element.65.mixed, bf16[256,3072]{1,0:T(8,128)(2,1)} %select_convert_fusion.shares, bf16[3072,512]{1,0:T(8,128)(2,1)} %bitcast.26.rows), custom_call_target="tpu_custom_call" | custom-call | flops 805306368 | bytes 6291456 | tf_op jit(solution)/shard_map/combine/pallas_call | solution.py:643
  (90 shorter events, 30.0 us)
Async XLA Ops:
  0.0 17.8 %collective-permute-start.4 = (bf16[8,2,128,512]{3,2,1,0:T(8,128)(2,1)}, bf16[8,2,128,512]{3,2,1,0:T(8,128)(2,1)}, u32[]{:S(2)}, u32[]{:S(2)}) collective-permute-start(bf16[8,2,128,512]{3,2,1,0:T(8,128)(2,1)} %pages_a_in.3), channel_id=1, source_target_pairs={{0,2},{2,0},{4,6},{6,4},{8,10},{10,8},{12,14},{14,12},{16,18},{18,... | collective-permute-start | bytes 6291464 | tf_op jit(solution)/shard_map/ppermute | solution.py:740
  1.4 12.1 %collective-permute-start.5 = (s32[1,64]{1,0:T(1,128)}, s32[1,64]{1,0:T(1,128)S(1)}, u32[]{:S(2)}, u32[]{:S(2)}) collective-permute-start(s32[1,64]{1,0:T(1,128)} %param.34), channel_id=1, source_target_pairs={{0,2},{2,0},{4,6},{6,4},{8,10},{10,8},{12,14},{14,12},{16,18},{18,... | collective-permute-start | bytes 776 | tf_op jit(solution)/shard_map/ppermute | solution.py:741
  5.7 9.3 %collective-permute-start = (bf16[136,512]{1,0:T(8,128)(2,1)S(1)}, bf16[136,512]{1,0:T(8,128)(2,1)S(1)}, u32[]{:S(2)}, u32[]{:S(2)}) collective-permute-start(bf16[136,512]{1,0:T(8,128)(2,1)S(1)} %fusion.2.refs_0_), channel_id=1, source_target_pairs={{0,4},{2,6},{4,0},{6,2},{8,12},{10,14},{12,8},{14,10},{16,20},{18,... | collective-permute-start | bytes 417800 | tf_op jit(solution)/shard_map/ppermute | solution.py:746
  8.6 6.5 %collective-permute-start.1 = (bf16[136,512]{1,0:T(8,128)(2,1)S(1)}, bf16[136,512]{1,0:T(8,128)(2,1)S(1)}, u32[]{:S(2)}, u32[]{:S(2)}) collective-permute-start(bf16[136,512]{1,0:T(8,128)(2,1)S(1)} %fusion.2.refs_0_), channel_id=1, source_target_pairs={{0,32},{2,10},{4,36},{6,14},{8,40},{10,18},{12,44},{14,22},{16,48}... | collective-permute-start | bytes 417800 | tf_op jit(solution)/shard_map/ppermute | solution.py:83
  10.2 7.5 %collective-permute-start.2 = (bf16[136,512]{1,0:T(8,128)(2,1)S(1)}, bf16[136,512]{1,0:T(8,128)(2,1)S(1)}, u32[]{:S(2)}, u32[]{:S(2)}) collective-permute-start(bf16[136,512]{1,0:T(8,128)(2,1)S(1)} %fusion.2.refs_0_), channel_id=1, source_target_pairs={{0,64},{2,18},{4,68},{6,22},{8,72},{10,26},{12,76},{14,30},{16,80}... | collective-permute-start | bytes 417800 | tf_op jit(solution)/shard_map/ppermute | solution.py:83
  13.5 4.2 %collective-permute-start.3 = (bf16[136,512]{1,0:T(8,128)(2,1)S(1)}, bf16[136,512]{1,0:T(8,128)(2,1)S(1)}, u32[]{:S(2)}, u32[]{:S(2)}) collective-permute-start(bf16[136,512]{1,0:T(8,128)(2,1)S(1)} %fusion.2.refs_0_), channel_id=1, source_target_pairs={{0,96},{2,26},{4,100},{6,30},{8,104},{10,2},{12,108},{14,6},{16,11... | collective-permute-start | bytes 417800 | tf_op jit(solution)/shard_map/ppermute | solution.py:83
  17.8 6.5 %collective-permute-start.6 = (bf16[136,512]{1,0:T(8,128)(2,1)S(1)}, bf16[136,512]{1,0:T(8,128)(2,1)S(1)}, u32[]{:S(2)}, u32[]{:S(2)}) collective-permute-start(bf16[136,512]{1,0:T(8,128)(2,1)S(1)} %collective-permute-done.refs_4_), channel_id=1, source_target_pairs={{0,32},{2,10},{4,36},{6,14},{8,40},{10,18},{12,44},{14,22},{16,48}... | collective-permute-start | bytes 417800 | tf_op jit(solution)/shard_map/ppermute | solution.py:83
  18.6 5.9 %collective-permute-start.7 = (bf16[136,512]{1,0:T(8,128)(2,1)S(1)}, bf16[136,512]{1,0:T(8,128)(2,1)S(1)}, u32[]{:S(2)}, u32[]{:S(2)}) collective-permute-start(bf16[136,512]{1,0:T(8,128)(2,1)S(1)} %collective-permute-done.refs_4_), channel_id=1, source_target_pairs={{0,64},{2,18},{4,68},{6,22},{8,72},{10,26},{12,76},{14,30},{16,80}... | collective-permute-start | bytes 417800 | tf_op jit(solution)/shard_map/ppermute | solution.py:83
  20.6 4.4 %collective-permute-start.8 = (bf16[136,512]{1,0:T(8,128)(2,1)S(1)}, bf16[136,512]{1,0:T(8,128)(2,1)S(1)}, u32[]{:S(2)}, u32[]{:S(2)}) collective-permute-start(bf16[136,512]{1,0:T(8,128)(2,1)S(1)} %collective-permute-done.refs_4_), channel_id=1, source_target_pairs={{0,96},{2,26},{4,100},{6,30},{8,104},{10,2},{12,108},{14,6},{16,11... | collective-permute-start | bytes 417800 | tf_op jit(solution)/shard_map/ppermute | solution.py:83
  22.9 12.1 %copy-start.11 = (s32[32]{0:T(128)}, s32[32]{0:T(128)S(1)}, u32[]{:S(2)}) copy-start(s32[32]{0:T(128)S(1)} %gather_fusion) | copy-start | bytes 388
  23.6 11.4 %copy-start.13 = (s32[32]{0:T(128)}, s32[32]{0:T(128)S(1)}, u32[]{:S(2)}) copy-start(s32[32]{0:T(128)S(1)} %fusion.14) | copy-start | bytes 388
  26.5 27.5 %collective-permute-start.10 = (bf16[8,136,512]{2,1,0:T(8,128)(2,1)S(1)}, bf16[8,136,512]{2,1,0:T(8,128)(2,1)}, u32[]{:S(2)}, u32[]{:S(2)}) collective-permute-start(bf16[8,136,512]{2,1,0:T(8,128)(2,1)S(1)} %stack_blocks.1.refs_0_), channel_id=1, source_target_pairs={{0,24},{2,98},{4,28},{6,102},{8,0},{10,106},{12,4},{14,110},{16,8}... | collective-permute-start | bytes 3342344 | tf_op jit(solution)/shard_map/ppermute | solution.py:115
  29.5 24.4 %collective-permute-start.11 = (bf16[8,136,512]{2,1,0:T(8,128)(2,1)S(1)}, bf16[8,136,512]{2,1,0:T(8,128)(2,1)}, u32[]{:S(2)}, u32[]{:S(2)}) collective-permute-start(bf16[8,136,512]{2,1,0:T(8,128)(2,1)S(1)} %stack_blocks.1.refs_0_), channel_id=1, source_target_pairs={{0,16},{2,66},{4,20},{6,70},{8,24},{10,74},{12,28},{14,78},{16,0},... | collective-permute-start | bytes 3342344 | tf_op jit(solution)/shard_map/ppermute | solution.py:115
  29.9 27.8 %collective-permute-start.9 = (bf16[8,136,512]{2,1,0:T(8,128)(2,1)S(1)}, bf16[8,136,512]{2,1,0:T(8,128)(2,1)}, u32[]{:S(2)}, u32[]{:S(2)}) collective-permute-start(bf16[8,136,512]{2,1,0:T(8,128)(2,1)S(1)} %stack_blocks.1.refs_0_), channel_id=1, source_target_pairs={{0,8},{2,34},{4,12},{6,38},{8,16},{10,42},{12,20},{14,46},{16,24},... | collective-permute-start | bytes 3342344 | tf_op jit(solution)/shard_map/ppermute | solution.py:115
  32.8 38.1 %collective-permute-start.12 = (bf16[256,2048]{1,0:T(8,128)(2,1)}, bf16[256,2048]{1,0:T(8,128)(2,1)}, u32[]{:S(2)}, u32[]{:S(2)}) collective-permute-start(bf16[256,2048]{1,0:T(8,128)(2,1)} %constant_dynamic-slice_fusion), channel_id=1, source_target_pairs={{0,1},{1,0},{2,3},{3,2},{4,5},{5,4},{6,7},{7,6},{8,9},{9,8},{10,11... | collective-permute-start | bytes 3145736 | tf_op jit(solution)/shard_map/ppermute | solution.py:754
  70.9 14.9 %copy-start.4 = (pred[1536,256]{1,0:T(32,128)(4,1)S(1)}, pred[1536,256]{1,0:T(32,128)(4,1)}, u32[]{:S(2)}) copy-start(pred[1536,256]{1,0:T(32,128)(4,1)} %constant.96.clone) | copy-start | bytes 1179652
  70.9 14.9 %copy-start.7 = (s32[1536]{0:T(1024)S(1)}, s32[1536]{0:T(1024)}, u32[]{:S(2)}) copy-start(s32[1536]{0:T(1024)} %constant.107) | copy-start | bytes 18436
  70.9 46.9 %all-to-all-start = ((bf16[32,400,128]{2,1,0:T(8,128)(2,1)}), bf16[32,400,128]{2,1,0:T(8,128)(2,1)}, u32[]{:S(2)}, u32[]{:S(2)}) async-start(bf16[32,400,128]{2,1,0:T(8,128)(2,1)} %page_attention.3), calls=%async_computation | async-start | bytes 6553600 | tf_op jit(solution)/shard_map/all_to_all | solution.py:776
  75.9 11.5 %collective-permute-start.13 = (bf16[256,2048]{1,0:T(8,128)(2,1)}, bf16[256,2048]{1,0:T(8,128)(2,1)S(1)}, u32[]{:S(2)}, u32[]{:S(2)}) collective-permute-start(bf16[256,2048]{1,0:T(8,128)(2,1)} %collective-permute-done.12.weight_mine), channel_id=1, source_target_pairs={{0,2},{2,0},{4,6},{6,4},{8,10},{10,8},{12,14},{14,12},{16,18},{18,... | collective-permute-start | bytes 3145736 | tf_op jit(solution)/shard_map/ppermute | solution.py:775
  87.4 42.7 %copy-start.2 = (bf16[256,2048]{1,0:T(8,128)(2,1)}, bf16[256,2048]{1,0:T(8,128)(2,1)S(1)}, u32[]{:S(2)}) copy-start(bf16[256,2048]{1,0:T(8,128)(2,1)S(1)} %collective-permute-done.13.weight_other) | copy-start | bytes 3145732
  125.0 5.1 %collective-permute-start.14 = (bf16[128,512]{1,0:T(8,128)(2,1)}, bf16[128,512]{1,0:T(8,128)(2,1)S(1)}, u32[]{:S(2)}, u32[]{:S(2)}) collective-permute-start(bf16[128,512]{1,0:T(8,128)(2,1)} %merge_attention.1.att), channel_id=1, source_target_pairs={{0,1},{1,0},{2,3},{3,2},{4,5},{5,4},{6,7},{7,6},{8,9},{9,8},{10,11... | collective-permute-start | bytes 393224 | tf_op jit(solution)/shard_map/ppermute | solution.py:781
  136.8 12.3 %copy-start.1 = (bf16[1,2048,704]{1,2,0:T(8,128)(2,1)S(1)}, bf16[1,2048,704]{1,2,0:T(8,128)(2,1)}, u32[]{:S(2)}) copy-start(bf16[1,2048,704]{1,2,0:T(8,128)(2,1)} %param.40) | copy-start | bytes 8650756
  136.8 54.4 %all-to-all-start.1 = ((bf16[64,24,1024]{2,1,0:T(8,128)(2,1)}), bf16[64,24,1024]{2,1,0:T(8,128)(2,1)}, u32[]{:S(2)}, u32[]{:S(2)}) async-start(bf16[64,24,1024]{2,1,0:T(8,128)(2,1)} %bitcast.37), calls=%async_computation.1 | async-start | bytes 6291456 | tf_op jit(solution)/shard_map/all_to_all | solution.py:793
  203.6 48.7 %all-to-all-start.2 = ((bf16[128,24,512]{2,1,0:T(8,128)(2,1)}), bf16[128,24,512]{2,1,0:T(8,128)(2,1)}, u32[]{:S(2)}, u32[]{:S(2)}) async-start(bf16[128,24,512]{2,1,0:T(8,128)(2,1)} %bitcast.36), calls=%async_computation.2 | async-start | bytes 6291456 | tf_op jit(solution)/shard_map/all_to_all | solution.py:795
  (8 other events, 62.9 us)

commit v8 on v7

--- a/solution.py
+++ b/solution.py
@@ -132,7 +132,7 @@
     return jnp.where(head == 3, rows[3], tile)
 
 
-def page_kernel(here, chip_of, page_a, page_b, pages_a_in, pages_b_in, *refs):
+def page_kernel(place, chip_of, page_a, page_b, pages_a_in, pages_b_in, *refs):
     out, blocks, pages_a, pages_b, held, notes, codes, sems, load_sems, note_sem = refs[-10:]
     count = held.shape[0]
     pieces = refs[: count // 8]
@@ -151,23 +151,21 @@
     ones = jnp.ones((PAGE, HD), BF16)
     for load in loads[: len(pieces)]:
         load.wait()
-    width = notes.shape[1]
     for i in range(count):
-        words = blocks[i, TOK : TOK + 8, :width].astype(F32).astype(jnp.int32)
-        notes[i : i + 1, :] = words[:1]
+        words = blocks[i, TOK : TOK + 8, :128].astype(F32).astype(jnp.int32)
+        notes[8 * i : 8 * i + 8, :] = words
     note_copy = pltpu.make_async_copy(notes, codes, note_sem)
     note_copy.start()
     for load in loads[len(pieces) :]:
         load.wait()
     note_copy.wait()
-    chip = here[0]
 
     def copy(i):
         return pltpu.make_async_copy(held.at[i], out.at[chip_of[i]], sems.at[i])
 
     def step(i, carry):
         pa, pb = page_a[i], page_b[i]
-        code = [codes[i, j * NCHIP + chip] for j in range(SLOTS)]
+        code = [codes[i * 8 + j, place[0]] for j in range(SLOTS)]
         first = [pl.multiple_of((c & 7) * 16, 16) for c in code]
         bias = jnp.concatenate(
             [
@@ -237,7 +235,6 @@
 
 def page_attention(here, chip_of, page_a, page_b, pages_a, pages_b, pieces, last):
     count = 8 * len(pieces)
-    width = -(-NCHIP * SLOTS // 128) * 128
     before = [] if last is None else [last]
     return pl.pallas_call(
         page_kernel,
@@ -250,8 +247,8 @@
             pltpu.VMEM(pages_a.shape, BF16),
             pltpu.VMEM(pages_b.shape, BF16),
             pltpu.VMEM((count, BLOCK, HD), BF16),
-            pltpu.VMEM((count, width), jnp.int32),
-            pltpu.SMEM((count, width), jnp.int32),
+            pltpu.VMEM((count * 8, 128), jnp.int32),
+            pltpu.SMEM((count * 8, 128), jnp.int32),
             pltpu.SemaphoreType.DMA((count,)),
             pltpu.SemaphoreType.DMA((2 + len(pieces),)),
             pltpu.SemaphoreType.DMA,
@@ -328,7 +325,7 @@
 
 
 def merge_kernel(
-    codes, arrived_in, own_in, own_sums_in, out, acc, tiles, arrived, own, own_sums, sems
+    here, codes, arrived_in, own_in, own_sums_in, out, acc, tiles, arrived, own, own_sums, sems
 ):
     part = NCHIP // MERGE_PARTS
     loads = [
@@ -384,7 +381,7 @@
 
     def add(p, low):
         share = jnp.exp(tiles[p] - top).astype(BF16).astype(F32)
-        code = [codes[p * SLOTS + j] for j in range(SLOTS)]
+        code = [codes[j, p * NC + here[0] % NC] for j in range(SLOTS)]
         masks = [offset == jnp.where(c >= 8, (c & 7) * 16, -1024) for c in code]
         factor = on_rows((share,), masks)
         for j in range(SLOTS):
@@ -403,11 +400,11 @@
         ).astype(BF16)
 
 
-def merge_attention(codes, arrived, own, own_sums):
+def merge_attention(here, codes, arrived, own, own_sums):
     return pl.pallas_call(
         merge_kernel,
         out_shape=jax.ShapeDtypeStruct((TOK, HEADS * HD), BF16),
-        in_specs=[smem()] + [hbm()] * 3,
+        in_specs=[smem()] * 2 + [hbm()] * 3,
         out_specs=vmem(),
         scratch_shapes=[
             pltpu.VMEM((HEADS, TOK, HD), F32),
@@ -422,7 +419,7 @@
             flops=64 << 20, bytes_accessed=4 << 20, transcendentals=1 << 18
         ),
         name="merge_attention",
-    )(codes, arrived, own, own_sums)
+    )(here, codes, arrived, own, own_sums)
 
 
 def project_kernel(
@@ -700,18 +697,39 @@
     return picks, shares.astype(BF16)
 
 
-def group_codes(users, ids, core):
-    users = users.reshape(NCHIP, NC)
-    user_a = jnp.where(core == 0, users[:, 0], users[:, 1])[:, None]
-    user_b = jnp.where(core == 0, users[:, 1], users[:, 0])[:, None]
-    group = jnp.arange(TOK // 16, dtype=jnp.int32)
-    group_user = ids.reshape(1, TOK // 16, 16)[..., 0]
-    hit_a, hit_b = group_user == user_a, group_user == user_b
-    needed = (hit_a | hit_b).astype(jnp.int32)
-    rank = jnp.sum(needed[:, None, :] * (group[None, :] < group[:, None]), axis=2)
-    value = needed * (group + 8 * hit_a + 16 * hit_b)
-    slot = jnp.arange(SLOTS, dtype=jnp.int32)
-    return jnp.sum(jnp.where(rank[:, None, :] == slot[:, None], value[:, None, :], 0), axis=2)
+def note_kernel(ids, users, queries, block, codes):
+    lane = lax.broadcasted_iota(jnp.int32, (8, 128), 1)
+    slot = lax.broadcasted_iota(jnp.int32, (8, 128), 0)
+    user = jnp.broadcast_to(users[...], (8, 128))
+    other = jnp.where(lane % 2 == 0, pltpu.roll(user, 127, 1), pltpu.roll(user, 1, 1))
+    rank = jnp.zeros((8, 128), jnp.int32)
+    total = jnp.zeros((8, 128), jnp.int32)
+    for group in range(TOK // 16):
+        mine = user == ids[group * 16]
+        theirs = other == ids[group * 16]
+        value = group + jnp.where(mine, 8, 0) + jnp.where(theirs, 16, 0)
+        needed = mine | theirs
+        total = jnp.where(needed & (rank == slot), value, total)
+        rank = rank + jnp.where(needed, 1, 0)
+    codes[...] = total
+    block[:TOK] = queries[...]
+    block[TOK:] = jnp.zeros((8, block.shape[1]), BF16)
+    block[TOK:, :128] = total.astype(F32).astype(BF16)
+
+
+def make_block(ids, users, queries):
+    return pl.pallas_call(
+        note_kernel,
+        out_shape=(
+            jax.ShapeDtypeStruct((TOK + 8, queries.shape[1]), BF16),
+            jax.ShapeDtypeStruct((8, 128), jnp.int32),
+        ),
+        in_specs=[smem(), vmem(), vmem()],
+        out_specs=(vmem(), vmem()),
+        compiler_params=pltpu.CompilerParams(vmem_limit_bytes=62 << 20),
+        cost_estimate=pl.CostEstimate(flops=1 << 16, bytes_accessed=1 << 18, transcendentals=0),
+        name="make_block",
+    )(ids, users, queries)
 
 
 def shards(
@@ -739,10 +757,8 @@
     core = me % NC
     pages_far = lax.ppermute(page_store, "req", perm_core())
     sends_far = lax.ppermute(page_sends, "req", perm_core())
-    codes = group_codes(page_users[0], request_ids, core)
-    note = jnp.zeros((8, queries.shape[1]), BF16)
-    note = note.at[0, : NCHIP * SLOTS].set(codes.T.reshape(-1).astype(BF16))
-    block = jnp.concatenate([queries, note], axis=0)
+    users = jnp.pad(page_users, ((0, 0), (0, 128 - NREQ)), constant_values=-1)
+    block, codes = make_block(request_ids, users, queries)
     near = lax.ppermute(block, "req", perm_x())
     line_a = ring_line(block)
     near, line_a, pages_far, sends_far, weight = lax.optimization_barrier(
@@ -758,7 +774,6 @@
     page_b = sends_far[0][chips * NC + core]
     line, chips, page_a, page_b = lax.optimization_barrier((line, chips, page_a, page_b))
     pieces = [line] + ring_rest(line)
-    here = me // NC
     own, own_sums = own_attention(request_ids, queries, new_keys, new_values)
     picks, shares = routing(expert_ids, expert_weights)
 
@@ -769,7 +784,7 @@
             group, parts = lax.optimization_barrier((group, parts))
         rows = slice(8 * first, 8 * last)
         parts = page_attention(
-            here[None], chips[rows], page_a[rows], page_b[rows], page_store, pages_far, group, parts
+            me[None], chips[rows], page_a[rows], page_b[rows], page_store, pages_far, group, parts
         )
     parts, weight_mine = lax.optimization_barrier((parts, weight_mine))
     weight_other = lax.ppermute(weight_mine, "req", perm_core())
@@ -777,7 +792,7 @@
         parts, "req", 0, 0, tiled=True, axis_index_groups=core_groups()
     )
     own, picks, weight_other = lax.optimization_barrier((own, picks, weight_other))
-    attended = merge_attention(codes.reshape(-1), arrived, own, own_sums)
+    attended = merge_attention(me[None], codes, arrived, own, own_sums)
     attended_far = lax.ppermute(attended, "tp", swap)
     mixed, sent = project(
         jnp.stack([lax.axis_index("tp"), core, 1 - core]),

time: 257 us -> 258 us (level)
  Pallas kernels: 53.5 us -> 56.2 us
  other arithmetic: 8.66 us -> 6.02 us
    unnamed x33 -> x34, local copies, waits for them, and re-layouts: 8.83 us -> 9.22 us
  transfers between devices with their start and end apart: 18 -> 18, of which waited for: 10 -> 10; matrix products, arithmetic and copies ran while one was open for 10% -> 9% of each run, Pallas kernels for 9% -> 10%
where the time goes in v8:
time: 258 us; the launch traced here: 257 us
  waiting for transfers between devices  125 us (48%)
  Pallas kernels  56.2 us (22%)
  starting transfers between devices  50 us (19%)
  local copies, waits for them, and re-layouts  18.4 us (7%)
  other arithmetic  6.02 us (2%)
    all_to_all x1, waiting for transfers between devices, shards(): lax.all_to_all(result.reshape(2 * NREQ, 2 * CAP, width // 4), ('req', 'tp...  38.1 us
    all_to_all x1, waiting for transfers between devices, shards(): lax.all_to_all(sent.reshape(NREQ, 2 * CAP, half), 'req', 0, 0, tiled=True)  34.7 us
    all_to_all x1, waiting for transfers between devices, shards(): lax.all_to_all(parts, 'req', 0, 0, tiled=True, axis_index_groups=core_gro...  31.1 us
    pallas_call x2, Pallas kernels, page_attention(): pl.pallas_call(page_kernel, out_shape=jax.ShapeDtypeStruct((NCHIP, BLOCK,...  20.7 us
    ppermute x3, waiting for transfers between devices, ring_rest(): return [lax.ppermute(line, 'req', perm_ring(1, step)) for step in (1, 3, 2)]  15.9 us
    pallas_call x1, Pallas kernels, run_expert(): pl.pallas_call(expert_kernel, out_shape=jax.ShapeDtypeStruct((rows.shape[...  12.4 us
    all_to_all x1, starting transfers between devices, shards(): lax.all_to_all(sent.reshape(NREQ, 2 * CAP, half), 'req', 0, 0, tiled=True)  12.3 us
    ppermute x6, starting transfers between devices, ring_line(): lax.ppermute(block, 'req', perm_ring(0, step))  9.4 us
  transfers between devices with their start and end apart: 18, of which 10 were waited for; matrix products, arithmetic and copies ran while one was open for 9% of the time, Pallas kernels for 10%

profile of v8, /device:TPU:1, one launch (start us, length us, event | category | flops | bytes accessed | tf_op | source)
XLA Modules:
  0.0 256.9 jit_solution(16432435072103710383)
XLA Ops:
  4.3 2.8 %collective-permute-start = (bf16[136,512]{1,0:T(8,128)(2,1)}, bf16[136,512]{1,0:T(8,128)(2,1)S(1)}, u32[]{:S(2)}, u32[]{:S(2)}) collective-permute-start(bf16[136,512]{1,0:T(8,128)(2,1)} %get-tuple-element.34.refs_0_), channel_id=1, source_target_pairs={{0,4},{2,6},{4,0},{6,2},{8,12},{10,14},{12,8},{14,10},{16,20},{18,... | collective-permute-start | bytes 417800 | tf_op jit(solution)/shard_map/ppermute | solution.py:762
  8.7 3.3 %collective-permute-start.2 = (bf16[136,512]{1,0:T(8,128)(2,1)}, bf16[136,512]{1,0:T(8,128)(2,1)S(1)}, u32[]{:S(2)}, u32[]{:S(2)}) collective-permute-start(bf16[136,512]{1,0:T(8,128)(2,1)} %get-tuple-element.34.refs_0_), channel_id=1, source_target_pairs={{0,64},{2,18},{4,68},{6,22},{8,72},{10,26},{12,76},{14,30},{16,80}... | collective-permute-start | bytes 417800 | tf_op jit(solution)/shard_map/ppermute | solution.py:83
  13.8 2.6 %collective-permute-done.2.refs_2_ = bf16[136,512]{1,0:T(8,128)(2,1)S(1)} collective-permute-done((bf16[136,512]{1,0:T(8,128)(2,1)}, bf16[136,512]{1,0:T(8,128)(2,1)S(1)}, u32[]{:S(2)}, u32[]{:S(2)}) %collective-permute-start.2) | collective-permute-done | bytes 139296 | tf_op jit(solution)/shard_map/ppermute | solution.py:83
  26.1 3.1 %collective-permute-start.10 = (bf16[8,136,512]{2,1,0:T(8,128)(2,1)S(1)}, bf16[8,136,512]{2,1,0:T(8,128)(2,1)}, u32[]{:S(2)}, u32[]{:S(2)}) collective-permute-start(bf16[8,136,512]{2,1,0:T(8,128)(2,1)S(1)} %stack_blocks.1.refs_0_), channel_id=1, source_target_pairs={{0,24},{2,98},{4,28},{6,102},{8,0},{10,106},{12,4},{14,110},{16,8}... | collective-permute-start | bytes 3342344 | tf_op jit(solution)/shard_map/ppermute | solution.py:115
  34.6 6.8 %page_attention.2.refs_3_ = bf16[32,400,128]{2,1,0:T(8,128)(2,1)} custom-call(s32[1]{0:T(128)} %bitcast.3.place.here, s32[8]{0:T(128)} %bitcast.55, s32[8]{0:T(128)} %bitcast.53, s32[8]{0:T(128)} %bitcast.54, bf16[8,2,128,512]{3,2,1,0:T(8,128)(2,1)} %pages_a_in.3, bf16[8,2,128,512]{3,2,1,0:T(8,128)(2,1)} %collective-permute-done.4.pages_b_in, ...), custom_call_target="tpu_custom_call" | custom-call | flops 805306368 | bytes 5242880 | tf_op jit(solution)/shard_map/page_attention/pallas_call | solution.py:239
  41.4 12.1 %collective-permute-done.10.refs_1_ = bf16[8,136,512]{2,1,0:T(8,128)(2,1)} collective-permute-done((bf16[8,136,512]{2,1,0:T(8,128)(2,1)S(1)}, bf16[8,136,512]{2,1,0:T(8,128)(2,1)}, u32[]{:S(2)}, u32[]{:S(2)}) %collective-permute-start.10) | collective-permute-done | bytes 1114144 | tf_op jit(solution)/shard_map/ppermute | solution.py:115
  53.5 3.8 %collective-permute-done.9.refs_0_ = bf16[8,136,512]{2,1,0:T(8,128)(2,1)} collective-permute-done((bf16[8,136,512]{2,1,0:T(8,128)(2,1)S(1)}, bf16[8,136,512]{2,1,0:T(8,128)(2,1)}, u32[]{:S(2)}, u32[]{:S(2)}) %collective-permute-start.9) | collective-permute-done | bytes 1114144 | tf_op jit(solution)/shard_map/ppermute | solution.py:115
  57.3 13.9 %page_attention.3 = bf16[32,400,128]{2,1,0:T(8,128)(2,1)} custom-call(s32[1]{0:T(128)} %bitcast.3.place.here, s32[24]{0:T(128)} %slice.46.chip_of, s32[24]{0:T(128)} %slice.47.page_a, s32[24]{0:T(128)} %slice.48.page_b, bf16[8,2,128,512]{3,2,1,0:T(8,128)(2,1)} %pages_a_in.3, ...), custom_call_target="tpu_custom_call", output_to_operand_aliasing={{}: (9, {})} | custom-call | flops 2415919104 | bytes 5242880 | tf_op jit(solution)/shard_map/page_attention/pallas_call | solution.py:239
  71.3 5.0 %all-to-all-start = ((bf16[32,400,128]{2,1,0:T(8,128)(2,1)}), bf16[32,400,128]{2,1,0:T(8,128)(2,1)}, u32[]{:S(2)}, u32[]{:S(2)}) async-start(bf16[32,400,128]{2,1,0:T(8,128)(2,1)} %page_attention.3), calls=%async_computation | async-start | bytes 6553600 | tf_op jit(solution)/shard_map/all_to_all | solution.py:791
  76.3 4.8 %collective-permute-start.13 = (bf16[256,2048]{1,0:T(8,128)(2,1)}, bf16[256,2048]{1,0:T(8,128)(2,1)S(1)}, u32[]{:S(2)}, u32[]{:S(2)}) collective-permute-start(bf16[256,2048]{1,0:T(8,128)(2,1)} %collective-permute-done.12.weight_mine), channel_id=1, source_target_pairs={{0,2},{2,0},{4,6},{6,4},{8,10},{10,8},{12,14},{14,12},{16,18},{18,... | collective-permute-start | bytes 3145736 | tf_op jit(solution)/shard_map/ppermute | solution.py:790
  82.5 2.9 %own_attention.1 = (f32[4,128,128]{2,1,0:T(8,128)}, f32[8,128]{1,0:T(8,128)}) custom-call(s32[128,1]{1,0:T(8,128)} %copy.51.request_col, s32[1,128]{1,0:T(1,128)} %bitcast.47, bf16[128,512]{1,0:T(8,128)(2,1)} %queries.3, bf16[128,512]{1,0:T(8,128)(2,1)} %keys.1, bf16[128,512]{1,0:T(8,128)(2,1)} %values.1), custom_call_target="tpu_custom_call" | custom-call | flops 67108864 | bytes 1048576 | tf_op jit(solution)/shard_map/own_attention/pallas_call | solution.py:306
  87.1 31.1 %all-to-all-done.arrived_in = bf16[32,400,128]{2,1,0:T(8,128)(2,1)} async-done(((bf16[32,400,128]{2,1,0:T(8,128)(2,1)}), bf16[32,400,128]{2,1,0:T(8,128)(2,1)}, u32[]{:S(2)}, u32[]{:S(2)}) %all-to-all-start) | async-done | bytes 3276832 | tf_op jit(solution)/shard_map/all_to_all | solution.py:791
  118.2 7.3 %merge_attention.1.att = bf16[128,512]{1,0:T(8,128)(2,1)} custom-call(s32[1]{0:T(128)} %bitcast.3.place.here, s32[8,128]{1,0:T(8,128)} %get-tuple-element.32.codes, bf16[32,400,128]{2,1,0:T(8,128)(2,1)} %all-to-all-done.arrived_in, f32[4,128,128]{2,1,0:T(8,128)} %get-tuple-element.53.own_in, f32[8,128]{1,0:T(8,128)} %get-tuple-element.54.own_sums_in), custom_call_target="tpu_custom_call" | custom-call | flops 67108864 | bytes 4194304 | tf_op jit(solution)/shard_map/merge_attention/pallas_call | solution.py:404
  125.6 2.6 %collective-permute-start.14 = (bf16[128,512]{1,0:T(8,128)(2,1)}, bf16[128,512]{1,0:T(8,128)(2,1)S(1)}, u32[]{:S(2)}, u32[]{:S(2)}) collective-permute-start(bf16[128,512]{1,0:T(8,128)(2,1)} %merge_attention.1.att), channel_id=1, source_target_pairs={{0,1},{1,0},{2,3},{3,2},{4,5},{5,4},{6,7},{7,6},{8,9},{9,8},{10,11... | collective-permute-start | bytes 393224 | tf_op jit(solution)/shard_map/ppermute | solution.py:796
  131.4 6.0 %project_dispatch.1 = (f32[128,1024]{1,0:T(8,128)}, bf16[1536,1024]{1,0:T(8,128)(2,1)}) custom-call(s32[3]{0:T(128)} %pad_add_fusion.1.side, bf16[128,512]{1,0:T(8,128)(2,1)} %merge_attention.1.att, bf16[128,512]{1,0:T(8,128)(2,1)} %copy-done.6, bf16[512,2048]{1,0:T(8,128)(2,1)} %weight_in.1, bf16[256,2048]{1,0:T(8,128)(2,1)} %collective-permute-done.12.weight_mine, ...), custom_call_target="tpu_custom_call" | custom-call | flops 1342177280 | bytes 10485760 | tf_op jit(solution)/shard_map/project_dispatch/pallas_call | solution.py:496
  137.4 12.3 %all-to-all-start.1 = ((bf16[64,24,1024]{2,1,0:T(8,128)(2,1)}), bf16[64,24,1024]{2,1,0:T(8,128)(2,1)}, u32[]{:S(2)}, u32[]{:S(2)}) async-start(bf16[64,24,1024]{2,1,0:T(8,128)(2,1)} %bitcast.35), calls=%async_computation.1 | async-start | bytes 6291456 | tf_op jit(solution)/shard_map/all_to_all | solution.py:808
  149.7 2.8 %copy.54 = bf16[1,2048,704]{2,1,0:T(8,128)(2,1)} copy(bf16[1,2048,704]{1,2,0:T(8,128)(2,1)S(1)} %copy-done.2) | data formatting | bytes 5767168 | tf_op args[12]
  152.5 4.6 %copy.55 = bf16[1,2048,704]{2,1,0:T(8,128)(2,1)} copy(bf16[1,2048,704]{1,2,0:T(8,128)(2,1)} %param.39) | data formatting | bytes 5767168 | tf_op args[13]
  157.2 34.7 %all-to-all-done.1.rows = bf16[64,24,1024]{2,1,0:T(8,128)(2,1)} async-done(((bf16[64,24,1024]{2,1,0:T(8,128)(2,1)}), bf16[64,24,1024]{2,1,0:T(8,128)(2,1)}, u32[]{:S(2)}, u32[]{:S(2)}) %all-to-all-start.1) | async-done | bytes 3145760 | tf_op jit(solution)/shard_map/all_to_all | solution.py:808
  191.8 12.4 %expert.1 = bf16[64,2,24,512]{3,2,1,0:T(8,128)(2,1)} custom-call(bf16[64,24,1024]{2,1,0:T(8,128)(2,1)} %all-to-all-done.1.rows, bf16[2048,704]{1,0:T(8,128)(2,1)} %bitcast.36, bf16[2048,704]{1,0:T(8,128)(2,1)} %bitcast.37, bf16[704,2048]{1,0:T(8,128)(2,1)} %bitcast.56), custom_call_target="tpu_custom_call" | custom-call | flops 6643777536 | bytes 15728640 | tf_op jit(solution)/shard_map/expert/pallas_call | solution.py:591
  204.3 7.5 %all-to-all-start.2 = ((bf16[128,24,512]{2,1,0:T(8,128)(2,1)}), bf16[128,24,512]{2,1,0:T(8,128)(2,1)}, u32[]{:S(2)}, u32[]{:S(2)}) async-start(bf16[128,24,512]{2,1,0:T(8,128)(2,1)} %bitcast.34), calls=%async_computation.2 | async-start | bytes 6291456 | tf_op jit(solution)/shard_map/all_to_all | solution.py:810
  211.8 3.0 %select_convert_fusion.shares = bf16[256,3072]{1,0:T(8,128)(2,1)} fusion(pred[256,3072]{1,0:T(32,128)(4,1)S(1)} %copy-done.4, f32[256]{0:T(256)S(1)} %bitcast.50, f32[256]{0:T(256)S(1)} %bitcast.51, f32[256]{0:T(256)S(1)} %bitcast.52, f32[256]{0:T(256)S(1)} %bitcast.49, s32[3072]{0:T(1024)S(1)} %copy-done.7, s32[256]{0:T(256)S(1)} %bitcast.41, ...), kind=kLoop, calls=%fused_computation.2 | loop fusion | flops 10223616 | bytes 2379776 | tf_op jit(solution)/shard_map/convert_element_type | solution.py:697
  214.9 38.1 %all-to-all-done.2 = bf16[128,24,512]{2,1,0:T(8,128)(2,1)} async-done(((bf16[128,24,512]{2,1,0:T(8,128)(2,1)}), bf16[128,24,512]{2,1,0:T(8,128)(2,1)}, u32[]{:S(2)}, u32[]{:S(2)}) %all-to-all-start.2) | async-done | bytes 3145760 | tf_op jit(solution)/shard_map/all_to_all | solution.py:810
  253.0 3.7 %combine.1 = bf16[128,1024]{1,0:T(8,128)(2,1)} custom-call(f32[128,1024]{1,0:T(8,128)} %get-tuple-element.57.mixed, bf16[256,3072]{1,0:T(8,128)(2,1)} %select_convert_fusion.shares, bf16[3072,512]{1,0:T(8,128)(2,1)} %bitcast.25.rows), custom_call_target="tpu_custom_call" | custom-call | flops 805306368 | bytes 6291456 | tf_op jit(solution)/shard_map/combine/pallas_call | solution.py:640
  (78 shorter events, 29.1 us)
Async XLA Ops:
  0.0 16.5 %collective-permute-start.4 = (bf16[8,2,128,512]{3,2,1,0:T(8,128)(2,1)}, bf16[8,2,128,512]{3,2,1,0:T(8,128)(2,1)}, u32[]{:S(2)}, u32[]{:S(2)}) collective-permute-start(bf16[8,2,128,512]{3,2,1,0:T(8,128)(2,1)} %pages_a_in.3), channel_id=1, source_target_pairs={{0,2},{2,0},{4,6},{6,4},{8,10},{10,8},{12,14},{14,12},{16,18},{18,... | collective-permute-start | bytes 6291464 | tf_op jit(solution)/shard_map/ppermute | solution.py:758
  1.4 10.6 %collective-permute-start.5 = (s32[1,64]{1,0:T(1,128)}, s32[1,64]{1,0:T(1,128)S(1)}, u32[]{:S(2)}, u32[]{:S(2)}) collective-permute-start(s32[1,64]{1,0:T(1,128)} %param.32), channel_id=1, source_target_pairs={{0,2},{2,0},{4,6},{6,4},{8,10},{10,8},{12,14},{14,12},{16,18},{18,... | collective-permute-start | bytes 776 | tf_op jit(solution)/shard_map/ppermute | solution.py:759
  4.3 9.2 %collective-permute-start = (bf16[136,512]{1,0:T(8,128)(2,1)}, bf16[136,512]{1,0:T(8,128)(2,1)S(1)}, u32[]{:S(2)}, u32[]{:S(2)}) collective-permute-start(bf16[136,512]{1,0:T(8,128)(2,1)} %get-tuple-element.34.refs_0_), channel_id=1, source_target_pairs={{0,4},{2,6},{4,0},{6,2},{8,12},{10,14},{12,8},{14,10},{16,20},{18,... | collective-permute-start | bytes 417800 | tf_op jit(solution)/shard_map/ppermute | solution.py:762
  7.1 6.7 %collective-permute-start.1 = (bf16[136,512]{1,0:T(8,128)(2,1)}, bf16[136,512]{1,0:T(8,128)(2,1)S(1)}, u32[]{:S(2)}, u32[]{:S(2)}) collective-permute-start(bf16[136,512]{1,0:T(8,128)(2,1)} %get-tuple-element.34.refs_0_), channel_id=1, source_target_pairs={{0,32},{2,10},{4,36},{6,14},{8,40},{10,18},{12,44},{14,22},{16,48}... | collective-permute-start | bytes 417800 | tf_op jit(solution)/shard_map/ppermute | solution.py:83
  8.7 7.7 %collective-permute-start.2 = (bf16[136,512]{1,0:T(8,128)(2,1)}, bf16[136,512]{1,0:T(8,128)(2,1)S(1)}, u32[]{:S(2)}, u32[]{:S(2)}) collective-permute-start(bf16[136,512]{1,0:T(8,128)(2,1)} %get-tuple-element.34.refs_0_), channel_id=1, source_target_pairs={{0,64},{2,18},{4,68},{6,22},{8,72},{10,26},{12,76},{14,30},{16,80}... | collective-permute-start | bytes 417800 | tf_op jit(solution)/shard_map/ppermute | solution.py:83
  12.0 4.4 %collective-permute-start.3 = (bf16[136,512]{1,0:T(8,128)(2,1)}, bf16[136,512]{1,0:T(8,128)(2,1)S(1)}, u32[]{:S(2)}, u32[]{:S(2)}) collective-permute-start(bf16[136,512]{1,0:T(8,128)(2,1)} %get-tuple-element.34.refs_0_), channel_id=1, source_target_pairs={{0,96},{2,26},{4,100},{6,30},{8,104},{10,2},{12,108},{14,6},{16,11... | collective-permute-start | bytes 417800 | tf_op jit(solution)/shard_map/ppermute | solution.py:83
  16.5 6.5 %collective-permute-start.6 = (bf16[136,512]{1,0:T(8,128)(2,1)S(1)}, bf16[136,512]{1,0:T(8,128)(2,1)S(1)}, u32[]{:S(2)}, u32[]{:S(2)}) collective-permute-start(bf16[136,512]{1,0:T(8,128)(2,1)S(1)} %collective-permute-done.refs_4_), channel_id=1, source_target_pairs={{0,32},{2,10},{4,36},{6,14},{8,40},{10,18},{12,44},{14,22},{16,48}... | collective-permute-start | bytes 417800 | tf_op jit(solution)/shard_map/ppermute | solution.py:83
  17.3 5.9 %collective-permute-start.7 = (bf16[136,512]{1,0:T(8,128)(2,1)S(1)}, bf16[136,512]{1,0:T(8,128)(2,1)S(1)}, u32[]{:S(2)}, u32[]{:S(2)}) collective-permute-start(bf16[136,512]{1,0:T(8,128)(2,1)S(1)} %collective-permute-done.refs_4_), channel_id=1, source_target_pairs={{0,64},{2,18},{4,68},{6,22},{8,72},{10,26},{12,76},{14,30},{16,80}... | collective-permute-start | bytes 417800 | tf_op jit(solution)/shard_map/ppermute | solution.py:83
  19.3 4.4 %collective-permute-start.8 = (bf16[136,512]{1,0:T(8,128)(2,1)S(1)}, bf16[136,512]{1,0:T(8,128)(2,1)S(1)}, u32[]{:S(2)}, u32[]{:S(2)}) collective-permute-start(bf16[136,512]{1,0:T(8,128)(2,1)S(1)} %collective-permute-done.refs_4_), channel_id=1, source_target_pairs={{0,96},{2,26},{4,100},{6,30},{8,104},{10,2},{12,108},{14,6},{16,11... | collective-permute-start | bytes 417800 | tf_op jit(solution)/shard_map/ppermute | solution.py:83
  21.6 13.0 %copy-start.12 = (s32[32]{0:T(128)}, s32[32]{0:T(128)S(1)}, u32[]{:S(2)}) copy-start(s32[32]{0:T(128)S(1)} %gather_fusion) | copy-start | bytes 388
  22.3 12.3 %copy-start.14 = (s32[32]{0:T(128)}, s32[32]{0:T(128)S(1)}, u32[]{:S(2)}) copy-start(s32[32]{0:T(128)S(1)} %fusion.7) | copy-start | bytes 388
  26.1 27.5 %collective-permute-start.10 = (bf16[8,136,512]{2,1,0:T(8,128)(2,1)S(1)}, bf16[8,136,512]{2,1,0:T(8,128)(2,1)}, u32[]{:S(2)}, u32[]{:S(2)}) collective-permute-start(bf16[8,136,512]{2,1,0:T(8,128)(2,1)S(1)} %stack_blocks.1.refs_0_), channel_id=1, source_target_pairs={{0,24},{2,98},{4,28},{6,102},{8,0},{10,106},{12,4},{14,110},{16,8}... | collective-permute-start | bytes 3342344 | tf_op jit(solution)/shard_map/ppermute | solution.py:115
  29.1 24.4 %collective-permute-start.11 = (bf16[8,136,512]{2,1,0:T(8,128)(2,1)S(1)}, bf16[8,136,512]{2,1,0:T(8,128)(2,1)}, u32[]{:S(2)}, u32[]{:S(2)}) collective-permute-start(bf16[8,136,512]{2,1,0:T(8,128)(2,1)S(1)} %stack_blocks.1.refs_0_), channel_id=1, source_target_pairs={{0,16},{2,66},{4,20},{6,70},{8,24},{10,74},{12,28},{14,78},{16,0},... | collective-permute-start | bytes 3342344 | tf_op jit(solution)/shard_map/ppermute | solution.py:115
  29.5 27.8 %collective-permute-start.9 = (bf16[8,136,512]{2,1,0:T(8,128)(2,1)S(1)}, bf16[8,136,512]{2,1,0:T(8,128)(2,1)}, u32[]{:S(2)}, u32[]{:S(2)}) collective-permute-start(bf16[8,136,512]{2,1,0:T(8,128)(2,1)S(1)} %stack_blocks.1.refs_0_), channel_id=1, source_target_pairs={{0,8},{2,34},{4,12},{6,38},{8,16},{10,42},{12,20},{14,46},{16,24},... | collective-permute-start | bytes 3342344 | tf_op jit(solution)/shard_map/ppermute | solution.py:115
  32.4 38.9 %collective-permute-start.12 = (bf16[256,2048]{1,0:T(8,128)(2,1)}, bf16[256,2048]{1,0:T(8,128)(2,1)}, u32[]{:S(2)}, u32[]{:S(2)}) collective-permute-start(bf16[256,2048]{1,0:T(8,128)(2,1)} %constant_dynamic-slice_fusion), channel_id=1, source_target_pairs={{0,1},{1,0},{2,3},{3,2},{4,5},{5,4},{6,7},{7,6},{8,9},{9,8},{10,11... | collective-permute-start | bytes 3145736 | tf_op jit(solution)/shard_map/ppermute | solution.py:770
  71.3 14.1 %copy-start.5 = (pred[1536,256]{1,0:T(32,128)(4,1)S(1)}, pred[1536,256]{1,0:T(32,128)(4,1)}, u32[]{:S(2)}) copy-start(pred[1536,256]{1,0:T(32,128)(4,1)} %constant.53.clone) | copy-start | bytes 1179652
  71.3 14.1 %copy-start.8 = (s32[1536]{0:T(1024)S(1)}, s32[1536]{0:T(1024)}, u32[]{:S(2)}) copy-start(s32[1536]{0:T(1024)} %constant.64) | copy-start | bytes 18436
  71.3 46.9 %all-to-all-start = ((bf16[32,400,128]{2,1,0:T(8,128)(2,1)}), bf16[32,400,128]{2,1,0:T(8,128)(2,1)}, u32[]{:S(2)}, u32[]{:S(2)}) async-start(bf16[32,400,128]{2,1,0:T(8,128)(2,1)} %page_attention.3), calls=%async_computation | async-start | bytes 6553600 | tf_op jit(solution)/shard_map/all_to_all | solution.py:791
  76.3 10.8 %collective-permute-start.13 = (bf16[256,2048]{1,0:T(8,128)(2,1)}, bf16[256,2048]{1,0:T(8,128)(2,1)S(1)}, u32[]{:S(2)}, u32[]{:S(2)}) collective-permute-start(bf16[256,2048]{1,0:T(8,128)(2,1)} %collective-permute-done.12.weight_mine), channel_id=1, source_target_pairs={{0,2},{2,0},{4,6},{6,4},{8,10},{10,8},{12,14},{14,12},{16,18},{18,... | collective-permute-start | bytes 3145736 | tf_op jit(solution)/shard_map/ppermute | solution.py:790
  87.1 43.6 %copy-start.3 = (bf16[256,2048]{1,0:T(8,128)(2,1)}, bf16[256,2048]{1,0:T(8,128)(2,1)S(1)}, u32[]{:S(2)}) copy-start(bf16[256,2048]{1,0:T(8,128)(2,1)S(1)} %collective-permute-done.13.weight_other) | copy-start | bytes 3145732
  125.6 5.1 %collective-permute-start.14 = (bf16[128,512]{1,0:T(8,128)(2,1)}, bf16[128,512]{1,0:T(8,128)(2,1)S(1)}, u32[]{:S(2)}, u32[]{:S(2)}) collective-permute-start(bf16[128,512]{1,0:T(8,128)(2,1)} %merge_attention.1.att), channel_id=1, source_target_pairs={{0,1},{1,0},{2,3},{3,2},{4,5},{5,4},{6,7},{7,6},{8,9},{9,8},{10,11... | collective-permute-start | bytes 393224 | tf_op jit(solution)/shard_map/ppermute | solution.py:796
  137.4 12.3 %copy-start.2 = (bf16[1,2048,704]{1,2,0:T(8,128)(2,1)S(1)}, bf16[1,2048,704]{1,2,0:T(8,128)(2,1)}, u32[]{:S(2)}) copy-start(bf16[1,2048,704]{1,2,0:T(8,128)(2,1)} %param.38) | copy-start | bytes 8650756
  137.4 54.4 %all-to-all-start.1 = ((bf16[64,24,1024]{2,1,0:T(8,128)(2,1)}), bf16[64,24,1024]{2,1,0:T(8,128)(2,1)}, u32[]{:S(2)}, u32[]{:S(2)}) async-start(bf16[64,24,1024]{2,1,0:T(8,128)(2,1)} %bitcast.35), calls=%async_computation.1 | async-start | bytes 6291456 | tf_op jit(solution)/shard_map/all_to_all | solution.py:808
  204.3 48.7 %all-to-all-start.2 = ((bf16[128,24,512]{2,1,0:T(8,128)(2,1)}), bf16[128,24,512]{2,1,0:T(8,128)(2,1)}, u32[]{:S(2)}, u32[]{:S(2)}) async-start(bf16[128,24,512]{2,1,0:T(8,128)(2,1)} %bitcast.34), calls=%async_computation.2 | async-start | bytes 6291456 | tf_op jit(solution)/shard_map/all_to_all | solution.py:810
  (9 other events, 64.7 us)

commit v9 on v8

--- a/solution.py
+++ b/solution.py
@@ -100,7 +100,7 @@
     return pl.pallas_call(
         stack_kernel,
         out_shape=jax.ShapeDtypeStruct((count, *blocks[0].shape), BF16),
-        in_specs=[pl.BlockSpec(memory_space=pl.ANY)] * count,
+        in_specs=[hbm()] + [pl.BlockSpec(memory_space=pl.ANY)] * (count - 1),
         out_specs=pl.BlockSpec(memory_space=pl.ANY),
         scratch_shapes=[pltpu.SemaphoreType.DMA((count,))],
         compiler_params=pltpu.CompilerParams(vmem_limit_bytes=8 << 20),
@@ -151,9 +151,13 @@
     ones = jnp.ones((PAGE, HD), BF16)
     for load in loads[: len(pieces)]:
         load.wait()
+    lane = lax.broadcasted_iota(jnp.int32, (8, 128), 1)
+    words = jnp.zeros((8, 128), F32)
     for i in range(count):
-        words = blocks[i, TOK : TOK + 8, :128].astype(F32).astype(jnp.int32)
-        notes[8 * i : 8 * i + 8, :] = words
+        sent = blocks[i, TOK : TOK + 8, :128].astype(F32)
+        mine = jnp.sum(jnp.where(lane == place[0], sent, 0.0), axis=1, keepdims=True)
+        words = jnp.where(lane == i, mine, words)
+    notes[...] = words.astype(jnp.int32)
     note_copy = pltpu.make_async_copy(notes, codes, note_sem)
     note_copy.start()
     for load in loads[len(pieces) :]:
@@ -165,7 +169,7 @@
 
     def step(i, carry):
         pa, pb = page_a[i], page_b[i]
-        code = [codes[i * 8 + j, place[0]] for j in range(SLOTS)]
+        code = [codes[j, i] for j in range(SLOTS)]
         first = [pl.multiple_of((c & 7) * 16, 16) for c in code]
         bias = jnp.concatenate(
             [
@@ -247,8 +251,8 @@
             pltpu.VMEM(pages_a.shape, BF16),
             pltpu.VMEM(pages_b.shape, BF16),
             pltpu.VMEM((count, BLOCK, HD), BF16),
-            pltpu.VMEM((count * 8, 128), jnp.int32),
-            pltpu.SMEM((count * 8, 128), jnp.int32),
+            pltpu.VMEM((8, 128), jnp.int32),
+            pltpu.SMEM((8, 128), jnp.int32),
             pltpu.SemaphoreType.DMA((count,)),
             pltpu.SemaphoreType.DMA((2 + len(pieces),)),
             pltpu.SemaphoreType.DMA,
@@ -697,10 +701,12 @@
     return picks, shares.astype(BF16)
 
 
-def note_kernel(ids, users, queries, block, codes):
+def note_kernel(ids, users, queries, block, codes, wide):
     lane = lax.broadcasted_iota(jnp.int32, (8, 128), 1)
     slot = lax.broadcasted_iota(jnp.int32, (8, 128), 0)
-    user = jnp.broadcast_to(users[...], (8, 128))
+    wide[...] = jnp.full((8, 128), -1, jnp.int32)
+    wide[:1, : users.shape[1]] = users[...]
+    user = jnp.broadcast_to(wide[:1], (8, 128))
     other = jnp.where(lane % 2 == 0, pltpu.roll(user, 127, 1), pltpu.roll(user, 1, 1))
     rank = jnp.zeros((8, 128), jnp.int32)
     total = jnp.zeros((8, 128), jnp.int32)
@@ -726,6 +732,7 @@
         ),
         in_specs=[smem(), vmem(), vmem()],
         out_specs=(vmem(), vmem()),
+        scratch_shapes=[pltpu.VMEM((8, 128), jnp.int32)],
         compiler_params=pltpu.CompilerParams(vmem_limit_bytes=62 << 20),
         cost_estimate=pl.CostEstimate(flops=1 << 16, bytes_accessed=1 << 18, transcendentals=0),
         name="make_block",
@@ -757,8 +764,7 @@
     core = me % NC
     pages_far = lax.ppermute(page_store, "req", perm_core())
     sends_far = lax.ppermute(page_sends, "req", perm_core())
-    users = jnp.pad(page_users, ((0, 0), (0, 128 - NREQ)), constant_values=-1)
-    block, codes = make_block(request_ids, users, queries)
+    block, codes = make_block(request_ids, page_users, queries)
     near = lax.ppermute(block, "req", perm_x())
     line_a = ring_line(block)
     near, line_a, pages_far, sends_far, weight = lax.optimization_barrier(

time: 258 us -> 256 us (level)
  no operation moved by 1% of the time
where the time goes in v9:
time: 256 us; the launch traced here: 255 us
  waiting for transfers between devices  125 us (49%)
  Pallas kernels  55.4 us (22%)
  starting transfers between devices  50 us (20%)
  local copies, waits for them, and re-layouts  17.2 us (7%)
  other arithmetic  6.02 us (2%)
    all_to_all x1, waiting for transfers between devices, shards(): lax.all_to_all(result.reshape(2 * NREQ, 2 * CAP, width // 4), ('req', 'tp...  38.1 us
    all_to_all x1, waiting for transfers between devices, shards(): lax.all_to_all(sent.reshape(NREQ, 2 * CAP, half), 'req', 0, 0, tiled=True)  34.7 us
    all_to_all x1, waiting for transfers between devices, shards(): lax.all_to_all(parts, 'req', 0, 0, tiled=True, axis_index_groups=core_gro...  31.1 us
    pallas_call x2, Pallas kernels, page_attention(): pl.pallas_call(page_kernel, out_shape=jax.ShapeDtypeStruct((NCHIP, BLOCK,...  19.9 us
    ppermute x3, waiting for transfers between devices, ring_rest(): return [lax.ppermute(line, 'req', perm_ring(1, step)) for step in (1, 3, 2)]  15.9 us
    pallas_call x1, Pallas kernels, run_expert(): pl.pallas_call(expert_kernel, out_shape=jax.ShapeDtypeStruct((rows.shape[...  12.4 us
    all_to_all x1, starting transfers between devices, shards(): lax.all_to_all(sent.reshape(NREQ, 2 * CAP, half), 'req', 0, 0, tiled=True)  12.2 us
    ppermute x6, starting transfers between devices, ring_line(): lax.ppermute(block, 'req', perm_ring(0, step))  9.4 us
  transfers between devices with their start and end apart: 18, of which 10 were waited for; matrix products, arithmetic and copies ran while one was open for 9% of the time, Pallas kernels for 10%

profile of v9, /device:TPU:1, one launch (start us, length us, event | category | flops | bytes accessed | tf_op | source)
XLA Modules:
  0.0 254.8 jit_solution(7620229983619551431)
XLA Ops:
  3.1 2.8 %collective-permute-start = (bf16[136,512]{1,0:T(8,128)(2,1)}, bf16[136,512]{1,0:T(8,128)(2,1)S(1)}, u32[]{:S(2)}, u32[]{:S(2)}) collective-permute-start(bf16[136,512]{1,0:T(8,128)(2,1)} %get-tuple-element.34.refs_0_), channel_id=1, source_target_pairs={{0,4},{2,6},{4,0},{6,2},{8,12},{10,14},{12,8},{14,10},{16,20},{18,... | collective-permute-start | bytes 417800 | tf_op jit(solution)/shard_map/ppermute | solution.py:768
  7.6 3.3 %collective-permute-start.2 = (bf16[136,512]{1,0:T(8,128)(2,1)}, bf16[136,512]{1,0:T(8,128)(2,1)S(1)}, u32[]{:S(2)}, u32[]{:S(2)}) collective-permute-start(bf16[136,512]{1,0:T(8,128)(2,1)} %get-tuple-element.34.refs_0_), channel_id=1, source_target_pairs={{0,64},{2,18},{4,68},{6,22},{8,72},{10,26},{12,76},{14,30},{16,80}... | collective-permute-start | bytes 417800 | tf_op jit(solution)/shard_map/ppermute | solution.py:83
  12.7 2.6 %collective-permute-done.2.refs_2_ = bf16[136,512]{1,0:T(8,128)(2,1)S(1)} collective-permute-done((bf16[136,512]{1,0:T(8,128)(2,1)}, bf16[136,512]{1,0:T(8,128)(2,1)S(1)}, u32[]{:S(2)}, u32[]{:S(2)}) %collective-permute-start.2) | collective-permute-done | bytes 139296 | tf_op jit(solution)/shard_map/ppermute | solution.py:83
  24.9 3.1 %collective-permute-start.10 = (bf16[8,136,512]{2,1,0:T(8,128)(2,1)S(1)}, bf16[8,136,512]{2,1,0:T(8,128)(2,1)}, u32[]{:S(2)}, u32[]{:S(2)}) collective-permute-start(bf16[8,136,512]{2,1,0:T(8,128)(2,1)S(1)} %stack_blocks.1.refs_0_), channel_id=1, source_target_pairs={{0,24},{2,98},{4,28},{6,102},{8,0},{10,106},{12,4},{14,110},{16,8}... | collective-permute-start | bytes 3342344 | tf_op jit(solution)/shard_map/ppermute | solution.py:115
  33.5 6.8 %page_attention.2.refs_3_ = bf16[32,400,128]{2,1,0:T(8,128)(2,1)} custom-call(s32[1]{0:T(128)} %bitcast.3.place.here, s32[8]{0:T(128)} %bitcast.55, s32[8]{0:T(128)} %bitcast.53, s32[8]{0:T(128)} %bitcast.54, bf16[8,2,128,512]{3,2,1,0:T(8,128)(2,1)} %pages_a_in.3, bf16[8,2,128,512]{3,2,1,0:T(8,128)(2,1)} %collective-permute-done.4.pages_b_in, ...), custom_call_target="tpu_custom_call" | custom-call | flops 805306368 | bytes 5242880 | tf_op jit(solution)/shard_map/page_attention/pallas_call | solution.py:243
  40.3 12.1 %collective-permute-done.10.refs_1_ = bf16[8,136,512]{2,1,0:T(8,128)(2,1)} collective-permute-done((bf16[8,136,512]{2,1,0:T(8,128)(2,1)S(1)}, bf16[8,136,512]{2,1,0:T(8,128)(2,1)}, u32[]{:S(2)}, u32[]{:S(2)}) %collective-permute-start.10) | collective-permute-done | bytes 1114144 | tf_op jit(solution)/shard_map/ppermute | solution.py:115
  52.4 3.8 %collective-permute-done.9.refs_0_ = bf16[8,136,512]{2,1,0:T(8,128)(2,1)} collective-permute-done((bf16[8,136,512]{2,1,0:T(8,128)(2,1)S(1)}, bf16[8,136,512]{2,1,0:T(8,128)(2,1)}, u32[]{:S(2)}, u32[]{:S(2)}) %collective-permute-start.9) | collective-permute-done | bytes 1114144 | tf_op jit(solution)/shard_map/ppermute | solution.py:115
  56.2 13.1 %page_attention.3 = bf16[32,400,128]{2,1,0:T(8,128)(2,1)} custom-call(s32[1]{0:T(128)} %bitcast.3.place.here, s32[24]{0:T(128)} %slice.46.chip_of, s32[24]{0:T(128)} %slice.47.page_a, s32[24]{0:T(128)} %slice.48.page_b, bf16[8,2,128,512]{3,2,1,0:T(8,128)(2,1)} %pages_a_in.3, ...), custom_call_target="tpu_custom_call", output_to_operand_aliasing={{}: (9, {})} | custom-call | flops 2415919104 | bytes 5242880 | tf_op jit(solution)/shard_map/page_attention/pallas_call | solution.py:243
  69.4 5.0 %all-to-all-start = ((bf16[32,400,128]{2,1,0:T(8,128)(2,1)}), bf16[32,400,128]{2,1,0:T(8,128)(2,1)}, u32[]{:S(2)}, u32[]{:S(2)}) async-start(bf16[32,400,128]{2,1,0:T(8,128)(2,1)} %page_attention.3), calls=%async_computation | async-start | bytes 6553600 | tf_op jit(solution)/shard_map/all_to_all | solution.py:797
  74.3 4.7 %collective-permute-start.13 = (bf16[256,2048]{1,0:T(8,128)(2,1)}, bf16[256,2048]{1,0:T(8,128)(2,1)S(1)}, u32[]{:S(2)}, u32[]{:S(2)}) collective-permute-start(bf16[256,2048]{1,0:T(8,128)(2,1)} %collective-permute-done.12.weight_mine), channel_id=1, source_target_pairs={{0,2},{2,0},{4,6},{6,4},{8,10},{10,8},{12,14},{14,12},{16,18},{18,... | collective-permute-start | bytes 3145736 | tf_op jit(solution)/shard_map/ppermute | solution.py:796
  80.5 2.9 %own_attention.1 = (f32[4,128,128]{2,1,0:T(8,128)}, f32[8,128]{1,0:T(8,128)}) custom-call(s32[128,1]{1,0:T(8,128)} %copy.51.request_col, s32[1,128]{1,0:T(1,128)} %bitcast.47, bf16[128,512]{1,0:T(8,128)(2,1)} %queries.3, bf16[128,512]{1,0:T(8,128)(2,1)} %keys.1, bf16[128,512]{1,0:T(8,128)(2,1)} %values.1), custom_call_target="tpu_custom_call" | custom-call | flops 67108864 | bytes 1048576 | tf_op jit(solution)/shard_map/own_attention/pallas_call | solution.py:310
  85.1 31.1 %all-to-all-done.arrived_in = bf16[32,400,128]{2,1,0:T(8,128)(2,1)} async-done(((bf16[32,400,128]{2,1,0:T(8,128)(2,1)}), bf16[32,400,128]{2,1,0:T(8,128)(2,1)}, u32[]{:S(2)}, u32[]{:S(2)}) %all-to-all-start) | async-done | bytes 3276832 | tf_op jit(solution)/shard_map/all_to_all | solution.py:797
  116.2 7.3 %merge_attention.1.att = bf16[128,512]{1,0:T(8,128)(2,1)} custom-call(s32[1]{0:T(128)} %bitcast.3.place.here, s32[8,128]{1,0:T(8,128)} %get-tuple-element.32.codes, bf16[32,400,128]{2,1,0:T(8,128)(2,1)} %all-to-all-done.arrived_in, f32[4,128,128]{2,1,0:T(8,128)} %get-tuple-element.53.own_in, f32[8,128]{1,0:T(8,128)} %get-tuple-element.54.own_sums_in), custom_call_target="tpu_custom_call" | custom-call | flops 67108864 | bytes 4194304 | tf_op jit(solution)/shard_map/merge_attention/pallas_call | solution.py:408
  123.6 2.6 %collective-permute-start.14 = (bf16[128,512]{1,0:T(8,128)(2,1)}, bf16[128,512]{1,0:T(8,128)(2,1)S(1)}, u32[]{:S(2)}, u32[]{:S(2)}) collective-permute-start(bf16[128,512]{1,0:T(8,128)(2,1)} %merge_attention.1.att), channel_id=1, source_target_pairs={{0,1},{1,0},{2,3},{3,2},{4,5},{5,4},{6,7},{7,6},{8,9},{9,8},{10,11... | collective-permute-start | bytes 393224 | tf_op jit(solution)/shard_map/ppermute | solution.py:802
  129.4 6.0 %project_dispatch.1 = (f32[128,1024]{1,0:T(8,128)}, bf16[1536,1024]{1,0:T(8,128)(2,1)}) custom-call(s32[3]{0:T(128)} %pad_add_fusion.1.side, bf16[128,512]{1,0:T(8,128)(2,1)} %merge_attention.1.att, bf16[128,512]{1,0:T(8,128)(2,1)} %copy-done.6, bf16[512,2048]{1,0:T(8,128)(2,1)} %weight_in.1, bf16[256,2048]{1,0:T(8,128)(2,1)} %collective-permute-done.12.weight_mine, ...), custom_call_target="tpu_custom_call" | custom-call | flops 1342177280 | bytes 10485760 | tf_op jit(solution)/shard_map/project_dispatch/pallas_call | solution.py:500
  135.5 12.2 %all-to-all-start.1 = ((bf16[64,24,1024]{2,1,0:T(8,128)(2,1)}), bf16[64,24,1024]{2,1,0:T(8,128)(2,1)}, u32[]{:S(2)}, u32[]{:S(2)}) async-start(bf16[64,24,1024]{2,1,0:T(8,128)(2,1)} %bitcast.35), calls=%async_computation.1 | async-start | bytes 6291456 | tf_op jit(solution)/shard_map/all_to_all | solution.py:814
  147.6 2.8 %copy.54 = bf16[1,2048,704]{2,1,0:T(8,128)(2,1)} copy(bf16[1,2048,704]{1,2,0:T(8,128)(2,1)S(1)} %copy-done.2) | data formatting | bytes 5767168 | tf_op args[12]
  150.5 4.6 %copy.55 = bf16[1,2048,704]{2,1,0:T(8,128)(2,1)} copy(bf16[1,2048,704]{1,2,0:T(8,128)(2,1)} %param.39) | data formatting | bytes 5767168 | tf_op args[13]
  155.1 34.7 %all-to-all-done.1.rows = bf16[64,24,1024]{2,1,0:T(8,128)(2,1)} async-done(((bf16[64,24,1024]{2,1,0:T(8,128)(2,1)}), bf16[64,24,1024]{2,1,0:T(8,128)(2,1)}, u32[]{:S(2)}, u32[]{:S(2)}) %all-to-all-start.1) | async-done | bytes 3145760 | tf_op jit(solution)/shard_map/all_to_all | solution.py:814
  189.8 12.4 %expert.1 = bf16[64,2,24,512]{3,2,1,0:T(8,128)(2,1)} custom-call(bf16[64,24,1024]{2,1,0:T(8,128)(2,1)} %all-to-all-done.1.rows, bf16[2048,704]{1,0:T(8,128)(2,1)} %bitcast.36, bf16[2048,704]{1,0:T(8,128)(2,1)} %bitcast.37, bf16[704,2048]{1,0:T(8,128)(2,1)} %bitcast.56), custom_call_target="tpu_custom_call" | custom-call | flops 6643777536 | bytes 15728640 | tf_op jit(solution)/shard_map/expert/pallas_call | solution.py:595
  202.2 7.5 %all-to-all-start.2 = ((bf16[128,24,512]{2,1,0:T(8,128)(2,1)}), bf16[128,24,512]{2,1,0:T(8,128)(2,1)}, u32[]{:S(2)}, u32[]{:S(2)}) async-start(bf16[128,24,512]{2,1,0:T(8,128)(2,1)} %bitcast.34), calls=%async_computation.2 | async-start | bytes 6291456 | tf_op jit(solution)/shard_map/all_to_all | solution.py:816
  209.8 3.0 %select_convert_fusion.shares = bf16[256,3072]{1,0:T(8,128)(2,1)} fusion(pred[256,3072]{1,0:T(32,128)(4,1)S(1)} %copy-done.4, f32[256]{0:T(256)S(1)} %bitcast.50, f32[256]{0:T(256)S(1)} %bitcast.51, f32[256]{0:T(256)S(1)} %bitcast.52, f32[256]{0:T(256)S(1)} %bitcast.49, s32[3072]{0:T(1024)S(1)} %copy-done.7, s32[256]{0:T(256)S(1)} %bitcast.41, ...), kind=kLoop, calls=%fused_computation.2 | loop fusion | flops 10223616 | bytes 2379776 | tf_op jit(solution)/shard_map/convert_element_type | solution.py:701
  212.8 38.1 %all-to-all-done.2 = bf16[128,24,512]{2,1,0:T(8,128)(2,1)} async-done(((bf16[128,24,512]{2,1,0:T(8,128)(2,1)}), bf16[128,24,512]{2,1,0:T(8,128)(2,1)}, u32[]{:S(2)}, u32[]{:S(2)}) %all-to-all-start.2) | async-done | bytes 3145760 | tf_op jit(solution)/shard_map/all_to_all | solution.py:816
  251.0 3.7 %combine.1 = bf16[128,1024]{1,0:T(8,128)(2,1)} custom-call(f32[128,1024]{1,0:T(8,128)} %get-tuple-element.57.mixed, bf16[256,3072]{1,0:T(8,128)(2,1)} %select_convert_fusion.shares, bf16[3072,512]{1,0:T(8,128)(2,1)} %bitcast.25.rows), custom_call_target="tpu_custom_call" | custom-call | flops 805306368 | bytes 6291456 | tf_op jit(solution)/shard_map/combine/pallas_call | solution.py:644
  (77 shorter events, 27.9 us)
Async XLA Ops:
  0.0 15.3 %collective-permute-start.4 = (bf16[8,2,128,512]{3,2,1,0:T(8,128)(2,1)}, bf16[8,2,128,512]{3,2,1,0:T(8,128)(2,1)}, u32[]{:S(2)}, u32[]{:S(2)}) collective-permute-start(bf16[8,2,128,512]{3,2,1,0:T(8,128)(2,1)} %pages_a_in.3), channel_id=1, source_target_pairs={{0,2},{2,0},{4,6},{6,4},{8,10},{10,8},{12,14},{14,12},{16,18},{18,... | collective-permute-start | bytes 6291464 | tf_op jit(solution)/shard_map/ppermute | solution.py:765
  1.4 9.5 %collective-permute-start.5 = (s32[1,64]{1,0:T(1,128)}, s32[1,64]{1,0:T(1,128)S(1)}, u32[]{:S(2)}, u32[]{:S(2)}) collective-permute-start(s32[1,64]{1,0:T(1,128)} %param.32), channel_id=1, source_target_pairs={{0,2},{2,0},{4,6},{6,4},{8,10},{10,8},{12,14},{14,12},{16,18},{18,... | collective-permute-start | bytes 776 | tf_op jit(solution)/shard_map/ppermute | solution.py:766
  3.1 9.2 %collective-permute-start = (bf16[136,512]{1,0:T(8,128)(2,1)}, bf16[136,512]{1,0:T(8,128)(2,1)S(1)}, u32[]{:S(2)}, u32[]{:S(2)}) collective-permute-start(bf16[136,512]{1,0:T(8,128)(2,1)} %get-tuple-element.34.refs_0_), channel_id=1, source_target_pairs={{0,4},{2,6},{4,0},{6,2},{8,12},{10,14},{12,8},{14,10},{16,20},{18,... | collective-permute-start | bytes 417800 | tf_op jit(solution)/shard_map/ppermute | solution.py:768
  5.9 6.7 %collective-permute-start.1 = (bf16[136,512]{1,0:T(8,128)(2,1)}, bf16[136,512]{1,0:T(8,128)(2,1)S(1)}, u32[]{:S(2)}, u32[]{:S(2)}) collective-permute-start(bf16[136,512]{1,0:T(8,128)(2,1)} %get-tuple-element.34.refs_0_), channel_id=1, source_target_pairs={{0,32},{2,10},{4,36},{6,14},{8,40},{10,18},{12,44},{14,22},{16,48}... | collective-permute-start | bytes 417800 | tf_op jit(solution)/shard_map/ppermute | solution.py:83
  7.6 7.7 %collective-permute-start.2 = (bf16[136,512]{1,0:T(8,128)(2,1)}, bf16[136,512]{1,0:T(8,128)(2,1)S(1)}, u32[]{:S(2)}, u32[]{:S(2)}) collective-permute-start(bf16[136,512]{1,0:T(8,128)(2,1)} %get-tuple-element.34.refs_0_), channel_id=1, source_target_pairs={{0,64},{2,18},{4,68},{6,22},{8,72},{10,26},{12,76},{14,30},{16,80}... | collective-permute-start | bytes 417800 | tf_op jit(solution)/shard_map/ppermute | solution.py:83
  10.9 4.4 %collective-permute-start.3 = (bf16[136,512]{1,0:T(8,128)(2,1)}, bf16[136,512]{1,0:T(8,128)(2,1)S(1)}, u32[]{:S(2)}, u32[]{:S(2)}) collective-permute-start(bf16[136,512]{1,0:T(8,128)(2,1)} %get-tuple-element.34.refs_0_), channel_id=1, source_target_pairs={{0,96},{2,26},{4,100},{6,30},{8,104},{10,2},{12,108},{14,6},{16,11... | collective-permute-start | bytes 417800 | tf_op jit(solution)/shard_map/ppermute | solution.py:83
  15.3 6.5 %collective-permute-start.6 = (bf16[136,512]{1,0:T(8,128)(2,1)S(1)}, bf16[136,512]{1,0:T(8,128)(2,1)S(1)}, u32[]{:S(2)}, u32[]{:S(2)}) collective-permute-start(bf16[136,512]{1,0:T(8,128)(2,1)S(1)} %collective-permute-done.refs_4_), channel_id=1, source_target_pairs={{0,32},{2,10},{4,36},{6,14},{8,40},{10,18},{12,44},{14,22},{16,48}... | collective-permute-start | bytes 417800 | tf_op jit(solution)/shard_map/ppermute | solution.py:83
  16.2 5.9 %collective-permute-start.7 = (bf16[136,512]{1,0:T(8,128)(2,1)S(1)}, bf16[136,512]{1,0:T(8,128)(2,1)S(1)}, u32[]{:S(2)}, u32[]{:S(2)}) collective-permute-start(bf16[136,512]{1,0:T(8,128)(2,1)S(1)} %collective-permute-done.refs_4_), channel_id=1, source_target_pairs={{0,64},{2,18},{4,68},{6,22},{8,72},{10,26},{12,76},{14,30},{16,80}... | collective-permute-start | bytes 417800 | tf_op jit(solution)/shard_map/ppermute | solution.py:83
  18.1 4.4 %collective-permute-start.8 = (bf16[136,512]{1,0:T(8,128)(2,1)S(1)}, bf16[136,512]{1,0:T(8,128)(2,1)S(1)}, u32[]{:S(2)}, u32[]{:S(2)}) collective-permute-start(bf16[136,512]{1,0:T(8,128)(2,1)S(1)} %collective-permute-done.refs_4_), channel_id=1, source_target_pairs={{0,96},{2,26},{4,100},{6,30},{8,104},{10,2},{12,108},{14,6},{16,11... | collective-permute-start | bytes 417800 | tf_op jit(solution)/shard_map/ppermute | solution.py:83
  20.4 13.0 %copy-start.12 = (s32[32]{0:T(128)}, s32[32]{0:T(128)S(1)}, u32[]{:S(2)}) copy-start(s32[32]{0:T(128)S(1)} %gather_fusion) | copy-start | bytes 388
  21.1 12.3 %copy-start.14 = (s32[32]{0:T(128)}, s32[32]{0:T(128)S(1)}, u32[]{:S(2)}) copy-start(s32[32]{0:T(128)S(1)} %fusion.7) | copy-start | bytes 388
  24.9 27.5 %collective-permute-start.10 = (bf16[8,136,512]{2,1,0:T(8,128)(2,1)S(1)}, bf16[8,136,512]{2,1,0:T(8,128)(2,1)}, u32[]{:S(2)}, u32[]{:S(2)}) collective-permute-start(bf16[8,136,512]{2,1,0:T(8,128)(2,1)S(1)} %stack_blocks.1.refs_0_), channel_id=1, source_target_pairs={{0,24},{2,98},{4,28},{6,102},{8,0},{10,106},{12,4},{14,110},{16,8}... | collective-permute-start | bytes 3342344 | tf_op jit(solution)/shard_map/ppermute | solution.py:115
  28.0 24.4 %collective-permute-start.11 = (bf16[8,136,512]{2,1,0:T(8,128)(2,1)S(1)}, bf16[8,136,512]{2,1,0:T(8,128)(2,1)}, u32[]{:S(2)}, u32[]{:S(2)}) collective-permute-start(bf16[8,136,512]{2,1,0:T(8,128)(2,1)S(1)} %stack_blocks.1.refs_0_), channel_id=1, source_target_pairs={{0,16},{2,66},{4,20},{6,70},{8,24},{10,74},{12,28},{14,78},{16,0},... | collective-permute-start | bytes 3342344 | tf_op jit(solution)/shard_map/ppermute | solution.py:115
  28.3 27.8 %collective-permute-start.9 = (bf16[8,136,512]{2,1,0:T(8,128)(2,1)S(1)}, bf16[8,136,512]{2,1,0:T(8,128)(2,1)}, u32[]{:S(2)}, u32[]{:S(2)}) collective-permute-start(bf16[8,136,512]{2,1,0:T(8,128)(2,1)S(1)} %stack_blocks.1.refs_0_), channel_id=1, source_target_pairs={{0,8},{2,34},{4,12},{6,38},{8,16},{10,42},{12,20},{14,46},{16,24},... | collective-permute-start | bytes 3342344 | tf_op jit(solution)/shard_map/ppermute | solution.py:115
  31.2 38.1 %collective-permute-start.12 = (bf16[256,2048]{1,0:T(8,128)(2,1)}, bf16[256,2048]{1,0:T(8,128)(2,1)}, u32[]{:S(2)}, u32[]{:S(2)}) collective-permute-start(bf16[256,2048]{1,0:T(8,128)(2,1)} %constant_dynamic-slice_fusion), channel_id=1, source_target_pairs={{0,1},{1,0},{2,3},{3,2},{4,5},{5,4},{6,7},{7,6},{8,9},{9,8},{10,11... | collective-permute-start | bytes 3145736 | tf_op jit(solution)/shard_map/ppermute | solution.py:776
  69.3 14.1 %copy-start.5 = (pred[1536,256]{1,0:T(32,128)(4,1)S(1)}, pred[1536,256]{1,0:T(32,128)(4,1)}, u32[]{:S(2)}) copy-start(pred[1536,256]{1,0:T(32,128)(4,1)} %constant.51.clone) | copy-start | bytes 1179652
  69.3 14.1 %copy-start.8 = (s32[1536]{0:T(1024)S(1)}, s32[1536]{0:T(1024)}, u32[]{:S(2)}) copy-start(s32[1536]{0:T(1024)} %constant.60) | copy-start | bytes 18436
  69.4 46.9 %all-to-all-start = ((bf16[32,400,128]{2,1,0:T(8,128)(2,1)}), bf16[32,400,128]{2,1,0:T(8,128)(2,1)}, u32[]{:S(2)}, u32[]{:S(2)}) async-start(bf16[32,400,128]{2,1,0:T(8,128)(2,1)} %page_attention.3), calls=%async_computation | async-start | bytes 6553600 | tf_op jit(solution)/shard_map/all_to_all | solution.py:797
  74.3 10.8 %collective-permute-start.13 = (bf16[256,2048]{1,0:T(8,128)(2,1)}, bf16[256,2048]{1,0:T(8,128)(2,1)S(1)}, u32[]{:S(2)}, u32[]{:S(2)}) collective-permute-start(bf16[256,2048]{1,0:T(8,128)(2,1)} %collective-permute-done.12.weight_mine), channel_id=1, source_target_pairs={{0,2},{2,0},{4,6},{6,4},{8,10},{10,8},{12,14},{14,12},{16,18},{18,... | collective-permute-start | bytes 3145736 | tf_op jit(solution)/shard_map/ppermute | solution.py:796
  85.1 43.7 %copy-start.3 = (bf16[256,2048]{1,0:T(8,128)(2,1)}, bf16[256,2048]{1,0:T(8,128)(2,1)S(1)}, u32[]{:S(2)}) copy-start(bf16[256,2048]{1,0:T(8,128)(2,1)S(1)} %collective-permute-done.13.weight_other) | copy-start | bytes 3145732
  123.6 5.2 %collective-permute-start.14 = (bf16[128,512]{1,0:T(8,128)(2,1)}, bf16[128,512]{1,0:T(8,128)(2,1)S(1)}, u32[]{:S(2)}, u32[]{:S(2)}) collective-permute-start(bf16[128,512]{1,0:T(8,128)(2,1)} %merge_attention.1.att), channel_id=1, source_target_pairs={{0,1},{1,0},{2,3},{3,2},{4,5},{5,4},{6,7},{7,6},{8,9},{9,8},{10,11... | collective-permute-start | bytes 393224 | tf_op jit(solution)/shard_map/ppermute | solution.py:802
  135.4 12.2 %copy-start.2 = (bf16[1,2048,704]{1,2,0:T(8,128)(2,1)S(1)}, bf16[1,2048,704]{1,2,0:T(8,128)(2,1)}, u32[]{:S(2)}) copy-start(bf16[1,2048,704]{1,2,0:T(8,128)(2,1)} %param.38) | copy-start | bytes 8650756
  135.5 54.3 %all-to-all-start.1 = ((bf16[64,24,1024]{2,1,0:T(8,128)(2,1)}), bf16[64,24,1024]{2,1,0:T(8,128)(2,1)}, u32[]{:S(2)}, u32[]{:S(2)}) async-start(bf16[64,24,1024]{2,1,0:T(8,128)(2,1)} %bitcast.35), calls=%async_computation.1 | async-start | bytes 6291456 | tf_op jit(solution)/shard_map/all_to_all | solution.py:814
  202.2 48.7 %all-to-all-start.2 = ((bf16[128,24,512]{2,1,0:T(8,128)(2,1)}), bf16[128,24,512]{2,1,0:T(8,128)(2,1)}, u32[]{:S(2)}, u32[]{:S(2)}) async-start(bf16[128,24,512]{2,1,0:T(8,128)(2,1)} %bitcast.34), calls=%async_computation.2 | async-start | bytes 6291456 | tf_op jit(solution)/shard_map/all_to_all | solution.py:816
  (9 other events, 64.7 us)

commit v10 on v9

--- a/solution.py
+++ b/solution.py
@@ -396,7 +396,7 @@
                 acc[head, at, :] += part * factor[start : start + 16]
         return low + share
 
-    low = lax.fori_loop(0, NCHIP, add, share, unroll=4)
+    low = lax.fori_loop(0, NCHIP, add, share, unroll=8)
     factor = on_rows(halves(1.0 / low), whole)
     for head in range(HEADS):
         out[:, head * HD : (head + 1) * HD] = (
@@ -589,7 +589,7 @@
         send(i).wait()
 
 
-def run_expert(rows, gate, up, down, steps=2):
+def run_expert(rows, gate, up, down, steps=4):
     count = rows.shape[0] // steps
     width, hidden = gate.shape
     return pl.pallas_call(

time: 256 us -> 255 us (level)
  no operation moved by 1% of the time
where the time goes in v10:
time: 255 us; the launch traced here: 254 us
  waiting for transfers between devices  125 us (49%)
  Pallas kernels  54.9 us (22%)
  starting transfers between devices  50 us (20%)
  local copies, waits for them, and re-layouts  17.2 us (7%)
  other arithmetic  6.02 us (2%)
    all_to_all x1, waiting for transfers between devices, shards(): lax.all_to_all(result.reshape(2 * NREQ, 2 * CAP, width // 4), ('req', 'tp...  38.1 us
    all_to_all x1, waiting for transfers between devices, shards(): lax.all_to_all(sent.reshape(NREQ, 2 * CAP, half), 'req', 0, 0, tiled=True)  34.7 us
    all_to_all x1, waiting for transfers between devices, shards(): lax.all_to_all(parts, 'req', 0, 0, tiled=True, axis_index_groups=core_gro...  31.1 us
    pallas_call x2, Pallas kernels, page_attention(): pl.pallas_call(page_kernel, out_shape=jax.ShapeDtypeStruct((NCHIP, BLOCK,...  19.9 us
    ppermute x3, waiting for transfers between devices, ring_rest(): return [lax.ppermute(line, 'req', perm_ring(1, step)) for step in (1, 3, 2)]  15.9 us
    all_to_all x1, starting transfers between devices, shards(): lax.all_to_all(sent.reshape(NREQ, 2 * CAP, half), 'req', 0, 0, tiled=True)  12.2 us
    pallas_call x1, Pallas kernels, run_expert(): pl.pallas_call(expert_kernel, out_shape=jax.ShapeDtypeStruct((rows.shape[...  12.1 us
    ppermute x6, starting transfers between devices, ring_line(): lax.ppermute(block, 'req', perm_ring(0, step))  9.4 us
  transfers between devices with their start and end apart: 18, of which 10 were waited for; matrix products, arithmetic and copies ran while one was open for 9% of the time, Pallas kernels for 10%

profile of v10, /device:TPU:1, one launch (start us, length us, event | category | flops | bytes accessed | tf_op | source)
XLA Modules:
  0.0 254.3 jit_solution(8083863669979881390)
XLA Ops:
  3.1 2.8 %collective-permute-start = (bf16[136,512]{1,0:T(8,128)(2,1)}, bf16[136,512]{1,0:T(8,128)(2,1)S(1)}, u32[]{:S(2)}, u32[]{:S(2)}) collective-permute-start(bf16[136,512]{1,0:T(8,128)(2,1)} %get-tuple-element.34.refs_0_), channel_id=1, source_target_pairs={{0,4},{2,6},{4,0},{6,2},{8,12},{10,14},{12,8},{14,10},{16,20},{18,... | collective-permute-start | bytes 417800 | tf_op jit(solution)/shard_map/ppermute | solution.py:768
  7.6 3.3 %collective-permute-start.2 = (bf16[136,512]{1,0:T(8,128)(2,1)}, bf16[136,512]{1,0:T(8,128)(2,1)S(1)}, u32[]{:S(2)}, u32[]{:S(2)}) collective-permute-start(bf16[136,512]{1,0:T(8,128)(2,1)} %get-tuple-element.34.refs_0_), channel_id=1, source_target_pairs={{0,64},{2,18},{4,68},{6,22},{8,72},{10,26},{12,76},{14,30},{16,80}... | collective-permute-start | bytes 417800 | tf_op jit(solution)/shard_map/ppermute | solution.py:83
  12.7 2.6 %collective-permute-done.2.refs_2_ = bf16[136,512]{1,0:T(8,128)(2,1)S(1)} collective-permute-done((bf16[136,512]{1,0:T(8,128)(2,1)}, bf16[136,512]{1,0:T(8,128)(2,1)S(1)}, u32[]{:S(2)}, u32[]{:S(2)}) %collective-permute-start.2) | collective-permute-done | bytes 139296 | tf_op jit(solution)/shard_map/ppermute | solution.py:83
  24.9 3.1 %collective-permute-start.10 = (bf16[8,136,512]{2,1,0:T(8,128)(2,1)S(1)}, bf16[8,136,512]{2,1,0:T(8,128)(2,1)}, u32[]{:S(2)}, u32[]{:S(2)}) collective-permute-start(bf16[8,136,512]{2,1,0:T(8,128)(2,1)S(1)} %stack_blocks.1.refs_0_), channel_id=1, source_target_pairs={{0,24},{2,98},{4,28},{6,102},{8,0},{10,106},{12,4},{14,110},{16,8}... | collective-permute-start | bytes 3342344 | tf_op jit(solution)/shard_map/ppermute | solution.py:115
  33.5 6.8 %page_attention.2.refs_3_ = bf16[32,400,128]{2,1,0:T(8,128)(2,1)} custom-call(s32[1]{0:T(128)} %bitcast.3.place.here, s32[8]{0:T(128)} %bitcast.55, s32[8]{0:T(128)} %bitcast.53, s32[8]{0:T(128)} %bitcast.54, bf16[8,2,128,512]{3,2,1,0:T(8,128)(2,1)} %pages_a_in.3, bf16[8,2,128,512]{3,2,1,0:T(8,128)(2,1)} %collective-permute-done.4.pages_b_in, ...), custom_call_target="tpu_custom_call" | custom-call | flops 805306368 | bytes 5242880 | tf_op jit(solution)/shard_map/page_attention/pallas_call | solution.py:243
  40.3 12.1 %collective-permute-done.10.refs_1_ = bf16[8,136,512]{2,1,0:T(8,128)(2,1)} collective-permute-done((bf16[8,136,512]{2,1,0:T(8,128)(2,1)S(1)}, bf16[8,136,512]{2,1,0:T(8,128)(2,1)}, u32[]{:S(2)}, u32[]{:S(2)}) %collective-permute-start.10) | collective-permute-done | bytes 1114144 | tf_op jit(solution)/shard_map/ppermute | solution.py:115
  52.4 3.8 %collective-permute-done.9.refs_0_ = bf16[8,136,512]{2,1,0:T(8,128)(2,1)} collective-permute-done((bf16[8,136,512]{2,1,0:T(8,128)(2,1)S(1)}, bf16[8,136,512]{2,1,0:T(8,128)(2,1)}, u32[]{:S(2)}, u32[]{:S(2)}) %collective-permute-start.9) | collective-permute-done | bytes 1114144 | tf_op jit(solution)/shard_map/ppermute | solution.py:115
  56.2 13.1 %page_attention.3 = bf16[32,400,128]{2,1,0:T(8,128)(2,1)} custom-call(s32[1]{0:T(128)} %bitcast.3.place.here, s32[24]{0:T(128)} %slice.46.chip_of, s32[24]{0:T(128)} %slice.47.page_a, s32[24]{0:T(128)} %slice.48.page_b, bf16[8,2,128,512]{3,2,1,0:T(8,128)(2,1)} %pages_a_in.3, ...), custom_call_target="tpu_custom_call", output_to_operand_aliasing={{}: (9, {})} | custom-call | flops 2415919104 | bytes 5242880 | tf_op jit(solution)/shard_map/page_attention/pallas_call | solution.py:243
  69.4 5.0 %all-to-all-start = ((bf16[32,400,128]{2,1,0:T(8,128)(2,1)}), bf16[32,400,128]{2,1,0:T(8,128)(2,1)}, u32[]{:S(2)}, u32[]{:S(2)}) async-start(bf16[32,400,128]{2,1,0:T(8,128)(2,1)} %page_attention.3), calls=%async_computation | async-start | bytes 6553600 | tf_op jit(solution)/shard_map/all_to_all | solution.py:797
  74.3 4.7 %collective-permute-start.13 = (bf16[256,2048]{1,0:T(8,128)(2,1)}, bf16[256,2048]{1,0:T(8,128)(2,1)S(1)}, u32[]{:S(2)}, u32[]{:S(2)}) collective-permute-start(bf16[256,2048]{1,0:T(8,128)(2,1)} %collective-permute-done.12.weight_mine), channel_id=1, source_target_pairs={{0,2},{2,0},{4,6},{6,4},{8,10},{10,8},{12,14},{14,12},{16,18},{18,... | collective-permute-start | bytes 3145736 | tf_op jit(solution)/shard_map/ppermute | solution.py:796
  80.5 2.9 %own_attention.1 = (f32[4,128,128]{2,1,0:T(8,128)}, f32[8,128]{1,0:T(8,128)}) custom-call(s32[128,1]{1,0:T(8,128)} %copy.51.request_col, s32[1,128]{1,0:T(1,128)} %bitcast.47, bf16[128,512]{1,0:T(8,128)(2,1)} %queries.3, bf16[128,512]{1,0:T(8,128)(2,1)} %keys.1, bf16[128,512]{1,0:T(8,128)(2,1)} %values.1), custom_call_target="tpu_custom_call" | custom-call | flops 67108864 | bytes 1048576 | tf_op jit(solution)/shard_map/own_attention/pallas_call | solution.py:310
  85.1 31.1 %all-to-all-done.arrived_in = bf16[32,400,128]{2,1,0:T(8,128)(2,1)} async-done(((bf16[32,400,128]{2,1,0:T(8,128)(2,1)}), bf16[32,400,128]{2,1,0:T(8,128)(2,1)}, u32[]{:S(2)}, u32[]{:S(2)}) %all-to-all-start) | async-done | bytes 3276832 | tf_op jit(solution)/shard_map/all_to_all | solution.py:797
  116.2 7.1 %merge_attention.1.att = bf16[128,512]{1,0:T(8,128)(2,1)} custom-call(s32[1]{0:T(128)} %bitcast.3.place.here, s32[8,128]{1,0:T(8,128)} %get-tuple-element.32.codes, bf16[32,400,128]{2,1,0:T(8,128)(2,1)} %all-to-all-done.arrived_in, f32[4,128,128]{2,1,0:T(8,128)} %get-tuple-element.53.own_in, f32[8,128]{1,0:T(8,128)} %get-tuple-element.54.own_sums_in), custom_call_target="tpu_custom_call" | custom-call | flops 67108864 | bytes 4194304 | tf_op jit(solution)/shard_map/merge_attention/pallas_call | solution.py:408
  123.3 2.6 %collective-permute-start.14 = (bf16[128,512]{1,0:T(8,128)(2,1)}, bf16[128,512]{1,0:T(8,128)(2,1)S(1)}, u32[]{:S(2)}, u32[]{:S(2)}) collective-permute-start(bf16[128,512]{1,0:T(8,128)(2,1)} %merge_attention.1.att), channel_id=1, source_target_pairs={{0,1},{1,0},{2,3},{3,2},{4,5},{5,4},{6,7},{7,6},{8,9},{9,8},{10,11... | collective-permute-start | bytes 393224 | tf_op jit(solution)/shard_map/ppermute | solution.py:802
  129.2 6.0 %project_dispatch.1 = (f32[128,1024]{1,0:T(8,128)}, bf16[1536,1024]{1,0:T(8,128)(2,1)}) custom-call(s32[3]{0:T(128)} %pad_add_fusion.1.side, bf16[128,512]{1,0:T(8,128)(2,1)} %merge_attention.1.att, bf16[128,512]{1,0:T(8,128)(2,1)} %copy-done.6, bf16[512,2048]{1,0:T(8,128)(2,1)} %weight_in.1, bf16[256,2048]{1,0:T(8,128)(2,1)} %collective-permute-done.12.weight_mine, ...), custom_call_target="tpu_custom_call" | custom-call | flops 1342177280 | bytes 10485760 | tf_op jit(solution)/shard_map/project_dispatch/pallas_call | solution.py:500
  135.2 12.2 %all-to-all-start.1 = ((bf16[64,24,1024]{2,1,0:T(8,128)(2,1)}), bf16[64,24,1024]{2,1,0:T(8,128)(2,1)}, u32[]{:S(2)}, u32[]{:S(2)}) async-start(bf16[64,24,1024]{2,1,0:T(8,128)(2,1)} %bitcast.35), calls=%async_computation.1 | async-start | bytes 6291456 | tf_op jit(solution)/shard_map/all_to_all | solution.py:814
  147.4 2.8 %copy.54 = bf16[1,2048,704]{2,1,0:T(8,128)(2,1)} copy(bf16[1,2048,704]{1,2,0:T(8,128)(2,1)S(1)} %copy-done.2) | data formatting | bytes 5767168 | tf_op args[12]
  150.2 4.6 %copy.55 = bf16[1,2048,704]{2,1,0:T(8,128)(2,1)} copy(bf16[1,2048,704]{1,2,0:T(8,128)(2,1)} %param.39) | data formatting | bytes 5767168 | tf_op args[13]
  154.9 34.7 %all-to-all-done.1.rows = bf16[64,24,1024]{2,1,0:T(8,128)(2,1)} async-done(((bf16[64,24,1024]{2,1,0:T(8,128)(2,1)}), bf16[64,24,1024]{2,1,0:T(8,128)(2,1)}, u32[]{:S(2)}, u32[]{:S(2)}) %all-to-all-start.1) | async-done | bytes 3145760 | tf_op jit(solution)/shard_map/all_to_all | solution.py:814
  189.6 12.1 %expert.1 = bf16[64,2,24,512]{3,2,1,0:T(8,128)(2,1)} custom-call(bf16[64,24,1024]{2,1,0:T(8,128)(2,1)} %all-to-all-done.1.rows, bf16[2048,704]{1,0:T(8,128)(2,1)} %bitcast.36, bf16[2048,704]{1,0:T(8,128)(2,1)} %bitcast.37, bf16[704,2048]{1,0:T(8,128)(2,1)} %bitcast.56), custom_call_target="tpu_custom_call" | custom-call | flops 6643777536 | bytes 15728640 | tf_op jit(solution)/shard_map/expert/pallas_call | solution.py:595
  201.7 7.5 %all-to-all-start.2 = ((bf16[128,24,512]{2,1,0:T(8,128)(2,1)}), bf16[128,24,512]{2,1,0:T(8,128)(2,1)}, u32[]{:S(2)}, u32[]{:S(2)}) async-start(bf16[128,24,512]{2,1,0:T(8,128)(2,1)} %bitcast.34), calls=%async_computation.2 | async-start | bytes 6291456 | tf_op jit(solution)/shard_map/all_to_all | solution.py:816
  209.3 3.0 %select_convert_fusion.shares = bf16[256,3072]{1,0:T(8,128)(2,1)} fusion(pred[256,3072]{1,0:T(32,128)(4,1)S(1)} %copy-done.4, f32[256]{0:T(256)S(1)} %bitcast.50, f32[256]{0:T(256)S(1)} %bitcast.51, f32[256]{0:T(256)S(1)} %bitcast.52, f32[256]{0:T(256)S(1)} %bitcast.49, s32[3072]{0:T(1024)S(1)} %copy-done.7, s32[256]{0:T(256)S(1)} %bitcast.41, ...), kind=kLoop, calls=%fused_computation.2 | loop fusion | flops 10223616 | bytes 2379776 | tf_op jit(solution)/shard_map/convert_element_type | solution.py:701
  212.3 38.1 %all-to-all-done.2 = bf16[128,24,512]{2,1,0:T(8,128)(2,1)} async-done(((bf16[128,24,512]{2,1,0:T(8,128)(2,1)}), bf16[128,24,512]{2,1,0:T(8,128)(2,1)}, u32[]{:S(2)}, u32[]{:S(2)}) %all-to-all-start.2) | async-done | bytes 3145760 | tf_op jit(solution)/shard_map/all_to_all | solution.py:816
  250.4 3.7 %combine.1 = bf16[128,1024]{1,0:T(8,128)(2,1)} custom-call(f32[128,1024]{1,0:T(8,128)} %get-tuple-element.57.mixed, bf16[256,3072]{1,0:T(8,128)(2,1)} %select_convert_fusion.shares, bf16[3072,512]{1,0:T(8,128)(2,1)} %bitcast.25.rows), custom_call_target="tpu_custom_call" | custom-call | flops 805306368 | bytes 6291456 | tf_op jit(solution)/shard_map/combine/pallas_call | solution.py:644
  (77 shorter events, 27.9 us)
Async XLA Ops:
  0.0 15.3 %collective-permute-start.4 = (bf16[8,2,128,512]{3,2,1,0:T(8,128)(2,1)}, bf16[8,2,128,512]{3,2,1,0:T(8,128)(2,1)}, u32[]{:S(2)}, u32[]{:S(2)}) collective-permute-start(bf16[8,2,128,512]{3,2,1,0:T(8,128)(2,1)} %pages_a_in.3), channel_id=1, source_target_pairs={{0,2},{2,0},{4,6},{6,4},{8,10},{10,8},{12,14},{14,12},{16,18},{18,... | collective-permute-start | bytes 6291464 | tf_op jit(solution)/shard_map/ppermute | solution.py:765
  1.4 9.5 %collective-permute-start.5 = (s32[1,64]{1,0:T(1,128)}, s32[1,64]{1,0:T(1,128)S(1)}, u32[]{:S(2)}, u32[]{:S(2)}) collective-permute-start(s32[1,64]{1,0:T(1,128)} %param.32), channel_id=1, source_target_pairs={{0,2},{2,0},{4,6},{6,4},{8,10},{10,8},{12,14},{14,12},{16,18},{18,... | collective-permute-start | bytes 776 | tf_op jit(solution)/shard_map/ppermute | solution.py:766
  3.1 9.2 %collective-permute-start = (bf16[136,512]{1,0:T(8,128)(2,1)}, bf16[136,512]{1,0:T(8,128)(2,1)S(1)}, u32[]{:S(2)}, u32[]{:S(2)}) collective-permute-start(bf16[136,512]{1,0:T(8,128)(2,1)} %get-tuple-element.34.refs_0_), channel_id=1, source_target_pairs={{0,4},{2,6},{4,0},{6,2},{8,12},{10,14},{12,8},{14,10},{16,20},{18,... | collective-permute-start | bytes 417800 | tf_op jit(solution)/shard_map/ppermute | solution.py:768
  5.9 6.7 %collective-permute-start.1 = (bf16[136,512]{1,0:T(8,128)(2,1)}, bf16[136,512]{1,0:T(8,128)(2,1)S(1)}, u32[]{:S(2)}, u32[]{:S(2)}) collective-permute-start(bf16[136,512]{1,0:T(8,128)(2,1)} %get-tuple-element.34.refs_0_), channel_id=1, source_target_pairs={{0,32},{2,10},{4,36},{6,14},{8,40},{10,18},{12,44},{14,22},{16,48}... | collective-permute-start | bytes 417800 | tf_op jit(solution)/shard_map/ppermute | solution.py:83
  7.6 7.7 %collective-permute-start.2 = (bf16[136,512]{1,0:T(8,128)(2,1)}, bf16[136,512]{1,0:T(8,128)(2,1)S(1)}, u32[]{:S(2)}, u32[]{:S(2)}) collective-permute-start(bf16[136,512]{1,0:T(8,128)(2,1)} %get-tuple-element.34.refs_0_), channel_id=1, source_target_pairs={{0,64},{2,18},{4,68},{6,22},{8,72},{10,26},{12,76},{14,30},{16,80}... | collective-permute-start | bytes 417800 | tf_op jit(solution)/shard_map/ppermute | solution.py:83
  10.9 4.4 %collective-permute-start.3 = (bf16[136,512]{1,0:T(8,128)(2,1)}, bf16[136,512]{1,0:T(8,128)(2,1)S(1)}, u32[]{:S(2)}, u32[]{:S(2)}) collective-permute-start(bf16[136,512]{1,0:T(8,128)(2,1)} %get-tuple-element.34.refs_0_), channel_id=1, source_target_pairs={{0,96},{2,26},{4,100},{6,30},{8,104},{10,2},{12,108},{14,6},{16,11... | collective-permute-start | bytes 417800 | tf_op jit(solution)/shard_map/ppermute | solution.py:83
  15.3 6.5 %collective-permute-start.6 = (bf16[136,512]{1,0:T(8,128)(2,1)S(1)}, bf16[136,512]{1,0:T(8,128)(2,1)S(1)}, u32[]{:S(2)}, u32[]{:S(2)}) collective-permute-start(bf16[136,512]{1,0:T(8,128)(2,1)S(1)} %collective-permute-done.refs_4_), channel_id=1, source_target_pairs={{0,32},{2,10},{4,36},{6,14},{8,40},{10,18},{12,44},{14,22},{16,48}... | collective-permute-start | bytes 417800 | tf_op jit(solution)/shard_map/ppermute | solution.py:83
  16.2 5.9 %collective-permute-start.7 = (bf16[136,512]{1,0:T(8,128)(2,1)S(1)}, bf16[136,512]{1,0:T(8,128)(2,1)S(1)}, u32[]{:S(2)}, u32[]{:S(2)}) collective-permute-start(bf16[136,512]{1,0:T(8,128)(2,1)S(1)} %collective-permute-done.refs_4_), channel_id=1, source_target_pairs={{0,64},{2,18},{4,68},{6,22},{8,72},{10,26},{12,76},{14,30},{16,80}... | collective-permute-start | bytes 417800 | tf_op jit(solution)/shard_map/ppermute | solution.py:83
  18.1 4.4 %collective-permute-start.8 = (bf16[136,512]{1,0:T(8,128)(2,1)S(1)}, bf16[136,512]{1,0:T(8,128)(2,1)S(1)}, u32[]{:S(2)}, u32[]{:S(2)}) collective-permute-start(bf16[136,512]{1,0:T(8,128)(2,1)S(1)} %collective-permute-done.refs_4_), channel_id=1, source_target_pairs={{0,96},{2,26},{4,100},{6,30},{8,104},{10,2},{12,108},{14,6},{16,11... | collective-permute-start | bytes 417800 | tf_op jit(solution)/shard_map/ppermute | solution.py:83
  20.4 13.0 %copy-start.12 = (s32[32]{0:T(128)}, s32[32]{0:T(128)S(1)}, u32[]{:S(2)}) copy-start(s32[32]{0:T(128)S(1)} %gather_fusion) | copy-start | bytes 388
  21.1 12.3 %copy-start.14 = (s32[32]{0:T(128)}, s32[32]{0:T(128)S(1)}, u32[]{:S(2)}) copy-start(s32[32]{0:T(128)S(1)} %fusion.7) | copy-start | bytes 388
  24.9 27.5 %collective-permute-start.10 = (bf16[8,136,512]{2,1,0:T(8,128)(2,1)S(1)}, bf16[8,136,512]{2,1,0:T(8,128)(2,1)}, u32[]{:S(2)}, u32[]{:S(2)}) collective-permute-start(bf16[8,136,512]{2,1,0:T(8,128)(2,1)S(1)} %stack_blocks.1.refs_0_), channel_id=1, source_target_pairs={{0,24},{2,98},{4,28},{6,102},{8,0},{10,106},{12,4},{14,110},{16,8}... | collective-permute-start | bytes 3342344 | tf_op jit(solution)/shard_map/ppermute | solution.py:115
  28.0 24.4 %collective-permute-start.11 = (bf16[8,136,512]{2,1,0:T(8,128)(2,1)S(1)}, bf16[8,136,512]{2,1,0:T(8,128)(2,1)}, u32[]{:S(2)}, u32[]{:S(2)}) collective-permute-start(bf16[8,136,512]{2,1,0:T(8,128)(2,1)S(1)} %stack_blocks.1.refs_0_), channel_id=1, source_target_pairs={{0,16},{2,66},{4,20},{6,70},{8,24},{10,74},{12,28},{14,78},{16,0},... | collective-permute-start | bytes 3342344 | tf_op jit(solution)/shard_map/ppermute | solution.py:115
  28.3 27.8 %collective-permute-start.9 = (bf16[8,136,512]{2,1,0:T(8,128)(2,1)S(1)}, bf16[8,136,512]{2,1,0:T(8,128)(2,1)}, u32[]{:S(2)}, u32[]{:S(2)}) collective-permute-start(bf16[8,136,512]{2,1,0:T(8,128)(2,1)S(1)} %stack_blocks.1.refs_0_), channel_id=1, source_target_pairs={{0,8},{2,34},{4,12},{6,38},{8,16},{10,42},{12,20},{14,46},{16,24},... | collective-permute-start | bytes 3342344 | tf_op jit(solution)/shard_map/ppermute | solution.py:115
  31.2 38.1 %collective-permute-start.12 = (bf16[256,2048]{1,0:T(8,128)(2,1)}, bf16[256,2048]{1,0:T(8,128)(2,1)}, u32[]{:S(2)}, u32[]{:S(2)}) collective-permute-start(bf16[256,2048]{1,0:T(8,128)(2,1)} %constant_dynamic-slice_fusion), channel_id=1, source_target_pairs={{0,1},{1,0},{2,3},{3,2},{4,5},{5,4},{6,7},{7,6},{8,9},{9,8},{10,11... | collective-permute-start | bytes 3145736 | tf_op jit(solution)/shard_map/ppermute | solution.py:776
  69.3 14.1 %copy-start.5 = (pred[1536,256]{1,0:T(32,128)(4,1)S(1)}, pred[1536,256]{1,0:T(32,128)(4,1)}, u32[]{:S(2)}) copy-start(pred[1536,256]{1,0:T(32,128)(4,1)} %constant.51.clone) | copy-start | bytes 1179652
  69.3 14.1 %copy-start.8 = (s32[1536]{0:T(1024)S(1)}, s32[1536]{0:T(1024)}, u32[]{:S(2)}) copy-start(s32[1536]{0:T(1024)} %constant.60) | copy-start | bytes 18436
  69.4 46.9 %all-to-all-start = ((bf16[32,400,128]{2,1,0:T(8,128)(2,1)}), bf16[32,400,128]{2,1,0:T(8,128)(2,1)}, u32[]{:S(2)}, u32[]{:S(2)}) async-start(bf16[32,400,128]{2,1,0:T(8,128)(2,1)} %page_attention.3), calls=%async_computation | async-start | bytes 6553600 | tf_op jit(solution)/shard_map/all_to_all | solution.py:797
  74.3 10.8 %collective-permute-start.13 = (bf16[256,2048]{1,0:T(8,128)(2,1)}, bf16[256,2048]{1,0:T(8,128)(2,1)S(1)}, u32[]{:S(2)}, u32[]{:S(2)}) collective-permute-start(bf16[256,2048]{1,0:T(8,128)(2,1)} %collective-permute-done.12.weight_mine), channel_id=1, source_target_pairs={{0,2},{2,0},{4,6},{6,4},{8,10},{10,8},{12,14},{14,12},{16,18},{18,... | collective-permute-start | bytes 3145736 | tf_op jit(solution)/shard_map/ppermute | solution.py:796
  85.1 43.4 %copy-start.3 = (bf16[256,2048]{1,0:T(8,128)(2,1)}, bf16[256,2048]{1,0:T(8,128)(2,1)S(1)}, u32[]{:S(2)}) copy-start(bf16[256,2048]{1,0:T(8,128)(2,1)S(1)} %collective-permute-done.13.weight_other) | copy-start | bytes 3145732
  123.3 5.2 %collective-permute-start.14 = (bf16[128,512]{1,0:T(8,128)(2,1)}, bf16[128,512]{1,0:T(8,128)(2,1)S(1)}, u32[]{:S(2)}, u32[]{:S(2)}) collective-permute-start(bf16[128,512]{1,0:T(8,128)(2,1)} %merge_attention.1.att), channel_id=1, source_target_pairs={{0,1},{1,0},{2,3},{3,2},{4,5},{5,4},{6,7},{7,6},{8,9},{9,8},{10,11... | collective-permute-start | bytes 393224 | tf_op jit(solution)/shard_map/ppermute | solution.py:802
  135.2 12.2 %copy-start.2 = (bf16[1,2048,704]{1,2,0:T(8,128)(2,1)S(1)}, bf16[1,2048,704]{1,2,0:T(8,128)(2,1)}, u32[]{:S(2)}) copy-start(bf16[1,2048,704]{1,2,0:T(8,128)(2,1)} %param.38) | copy-start | bytes 8650756
  135.2 54.3 %all-to-all-start.1 = ((bf16[64,24,1024]{2,1,0:T(8,128)(2,1)}), bf16[64,24,1024]{2,1,0:T(8,128)(2,1)}, u32[]{:S(2)}, u32[]{:S(2)}) async-start(bf16[64,24,1024]{2,1,0:T(8,128)(2,1)} %bitcast.35), calls=%async_computation.1 | async-start | bytes 6291456 | tf_op jit(solution)/shard_map/all_to_all | solution.py:814
  201.7 48.8 %all-to-all-start.2 = ((bf16[128,24,512]{2,1,0:T(8,128)(2,1)}), bf16[128,24,512]{2,1,0:T(8,128)(2,1)}, u32[]{:S(2)}, u32[]{:S(2)}) async-start(bf16[128,24,512]{2,1,0:T(8,128)(2,1)} %bitcast.34), calls=%async_computation.2 | async-start | bytes 6291456 | tf_op jit(solution)/shard_map/all_to_all | solution.py:816
  (9 other events, 64.7 us)

commit v11 on v10

--- a/solution.py
+++ b/solution.py
@@ -60,7 +60,7 @@
     return pairs
 
 
-PIECES = tuple((step, far) for step in (0, 1, 3, 2) for far in (0, 1))
+PIECES = tuple((step, far) for step in (0, 2, 1, 3) for far in (0, 1))
 
 
 def chip_table():
@@ -112,7 +112,7 @@
 
 
 def ring_rest(line):
-    return [lax.ppermute(line, "req", perm_ring(1, step)) for step in (1, 3, 2)]
+    return [lax.ppermute(line, "req", perm_ring(1, step)) for step in (2, 1, 3)]
 
 
 def attend(query, key_t, value_1, shift):

time: 255 us -> 255 us (level)
  starting transfers between devices: 50 us -> 52.8 us
  transfers between devices with their start and end apart: 18 -> 18, of which waited for: 10 -> 11; matrix products, arithmetic and copies ran while one was open for 9% -> 9% of each run, Pallas kernels for 10% -> 10%
where the time goes in v11:
time: 255 us; the launch traced here: 254 us
  waiting for transfers between devices  123 us (48%)
  Pallas kernels  54.9 us (22%)
  starting transfers between devices  52.8 us (21%)
  local copies, waits for them, and re-layouts  17.2 us (7%)
  other arithmetic  6.02 us (2%)
    all_to_all x1, waiting for transfers between devices, shards(): lax.all_to_all(result.reshape(2 * NREQ, 2 * CAP, width // 4), ('req', 'tp...  38.1 us
    all_to_all x1, waiting for transfers between devices, shards(): lax.all_to_all(sent.reshape(NREQ, 2 * CAP, half), 'req', 0, 0, tiled=True)  34.7 us
    all_to_all x1, waiting for transfers between devices, shards(): lax.all_to_all(parts, 'req', 0, 0, tiled=True, axis_index_groups=core_gro...  30.6 us
    pallas_call x2, Pallas kernels, page_attention(): pl.pallas_call(page_kernel, out_shape=jax.ShapeDtypeStruct((NCHIP, BLOCK,...  19.9 us
    ppermute x3, waiting for transfers between devices, ring_rest(): return [lax.ppermute(line, 'req', perm_ring(1, step)) for step in (2, 1, 3)]  13.5 us
    all_to_all x1, starting transfers between devices, shards(): lax.all_to_all(sent.reshape(NREQ, 2 * CAP, half), 'req', 0, 0, tiled=True)  12.5 us
    pallas_call x1, Pallas kernels, run_expert(): pl.pallas_call(expert_kernel, out_shape=jax.ShapeDtypeStruct((rows.shape[...  12.1 us
    ppermute x6, starting transfers between devices, ring_line(): lax.ppermute(block, 'req', perm_ring(0, step))  9.4 us
  transfers between devices with their start and end apart: 18, of which 11 were waited for; matrix products, arithmetic and copies ran while one was open for 9% of the time, Pallas kernels for 10%

profile of v11, /device:TPU:1, one launch (start us, length us, event | category | flops | bytes accessed | tf_op | source)
XLA Modules:
  0.0 254.2 jit_solution(6756462309592914628)
XLA Ops:
  3.1 2.8 %collective-permute-start = (bf16[136,512]{1,0:T(8,128)(2,1)}, bf16[136,512]{1,0:T(8,128)(2,1)S(1)}, u32[]{:S(2)}, u32[]{:S(2)}) collective-permute-start(bf16[136,512]{1,0:T(8,128)(2,1)} %get-tuple-element.34.refs_0_), channel_id=1, source_target_pairs={{0,4},{2,6},{4,0},{6,2},{8,12},{10,14},{12,8},{14,10},{16,20},{18,... | collective-permute-start | bytes 417800 | tf_op jit(solution)/shard_map/ppermute | solution.py:768
  7.6 3.3 %collective-permute-start.2 = (bf16[136,512]{1,0:T(8,128)(2,1)}, bf16[136,512]{1,0:T(8,128)(2,1)S(1)}, u32[]{:S(2)}, u32[]{:S(2)}) collective-permute-start(bf16[136,512]{1,0:T(8,128)(2,1)} %get-tuple-element.34.refs_0_), channel_id=1, source_target_pairs={{0,64},{2,18},{4,68},{6,22},{8,72},{10,26},{12,76},{14,30},{16,80}... | collective-permute-start | bytes 417800 | tf_op jit(solution)/shard_map/ppermute | solution.py:83
  12.7 2.6 %collective-permute-done.2.refs_2_ = bf16[136,512]{1,0:T(8,128)(2,1)S(1)} collective-permute-done((bf16[136,512]{1,0:T(8,128)(2,1)}, bf16[136,512]{1,0:T(8,128)(2,1)S(1)}, u32[]{:S(2)}, u32[]{:S(2)}) %collective-permute-start.2) | collective-permute-done | bytes 139296 | tf_op jit(solution)/shard_map/ppermute | solution.py:83
  29.5 2.3 constant_dynamic-slice_fusion
  34.1 6.8 %page_attention.2.refs_3_ = bf16[32,400,128]{2,1,0:T(8,128)(2,1)} custom-call(s32[1]{0:T(128)} %bitcast.3.place.here, s32[8]{0:T(128)} %bitcast.55, s32[8]{0:T(128)} %bitcast.53, s32[8]{0:T(128)} %bitcast.54, bf16[8,2,128,512]{3,2,1,0:T(8,128)(2,1)} %pages_a_in.3, bf16[8,2,128,512]{3,2,1,0:T(8,128)(2,1)} %collective-permute-done.4.pages_b_in, ...), custom_call_target="tpu_custom_call" | custom-call | flops 805306368 | bytes 5242880 | tf_op jit(solution)/shard_map/page_attention/pallas_call | solution.py:243
  41.3 11.2 %collective-permute-done.11.refs_2_ = bf16[8,136,512]{2,1,0:T(8,128)(2,1)} collective-permute-done((bf16[8,136,512]{2,1,0:T(8,128)(2,1)S(1)}, bf16[8,136,512]{2,1,0:T(8,128)(2,1)}, u32[]{:S(2)}, u32[]{:S(2)}) %collective-permute-start.11) | collective-permute-done | bytes 1114144 | tf_op jit(solution)/shard_map/ppermute | solution.py:115
  52.5 1.9 collective-permute-done.9.refs_0_
  54.4 13.1 %page_attention.3 = bf16[32,400,128]{2,1,0:T(8,128)(2,1)} custom-call(s32[1]{0:T(128)} %bitcast.3.place.here, s32[24]{0:T(128)} %slice.46.chip_of, s32[24]{0:T(128)} %slice.47.page_a, s32[24]{0:T(128)} %slice.48.page_b, bf16[8,2,128,512]{3,2,1,0:T(8,128)(2,1)} %pages_a_in.3, ...), custom_call_target="tpu_custom_call", output_to_operand_aliasing={{}: (9, {})} | custom-call | flops 2415919104 | bytes 5242880 | tf_op jit(solution)/shard_map/page_attention/pallas_call | solution.py:243
  67.6 5.6 %all-to-all-start = ((bf16[32,400,128]{2,1,0:T(8,128)(2,1)}), bf16[32,400,128]{2,1,0:T(8,128)(2,1)}, u32[]{:S(2)}, u32[]{:S(2)}) async-start(bf16[32,400,128]{2,1,0:T(8,128)(2,1)} %page_attention.3), calls=%async_computation | async-start | bytes 6553600 | tf_op jit(solution)/shard_map/all_to_all | solution.py:797
  73.2 4.5 %collective-permute-start.13 = (bf16[256,2048]{1,0:T(8,128)(2,1)}, bf16[256,2048]{1,0:T(8,128)(2,1)S(1)}, u32[]{:S(2)}, u32[]{:S(2)}) collective-permute-start(bf16[256,2048]{1,0:T(8,128)(2,1)} %collective-permute-done.12.weight_mine), channel_id=1, source_target_pairs={{0,2},{2,0},{4,6},{6,4},{8,10},{10,8},{12,14},{14,12},{16,18},{18,... | collective-permute-start | bytes 3145736 | tf_op jit(solution)/shard_map/ppermute | solution.py:796
  79.2 2.9 %own_attention.1 = (f32[4,128,128]{2,1,0:T(8,128)}, f32[8,128]{1,0:T(8,128)}) custom-call(s32[128,1]{1,0:T(8,128)} %copy.51.request_col, s32[1,128]{1,0:T(1,128)} %bitcast.47, bf16[128,512]{1,0:T(8,128)(2,1)} %queries.3, bf16[128,512]{1,0:T(8,128)(2,1)} %keys.1, bf16[128,512]{1,0:T(8,128)(2,1)} %values.1), custom_call_target="tpu_custom_call" | custom-call | flops 67108864 | bytes 1048576 | tf_op jit(solution)/shard_map/own_attention/pallas_call | solution.py:310
  83.8 30.6 %all-to-all-done.arrived_in = bf16[32,400,128]{2,1,0:T(8,128)(2,1)} async-done(((bf16[32,400,128]{2,1,0:T(8,128)(2,1)}), bf16[32,400,128]{2,1,0:T(8,128)(2,1)}, u32[]{:S(2)}, u32[]{:S(2)}) %all-to-all-start) | async-done | bytes 3276832 | tf_op jit(solution)/shard_map/all_to_all | solution.py:797
  114.4 7.1 %merge_attention.1.att = bf16[128,512]{1,0:T(8,128)(2,1)} custom-call(s32[1]{0:T(128)} %bitcast.3.place.here, s32[8,128]{1,0:T(8,128)} %get-tuple-element.32.codes, bf16[32,400,128]{2,1,0:T(8,128)(2,1)} %all-to-all-done.arrived_in, f32[4,128,128]{2,1,0:T(8,128)} %get-tuple-element.53.own_in, f32[8,128]{1,0:T(8,128)} %get-tuple-element.54.own_sums_in), custom_call_target="tpu_custom_call" | custom-call | flops 67108864 | bytes 4194304 | tf_op jit(solution)/shard_map/merge_attention/pallas_call | solution.py:408
  121.5 4.0 %collective-permute-start.14 = (bf16[128,512]{1,0:T(8,128)(2,1)}, bf16[128,512]{1,0:T(8,128)(2,1)S(1)}, u32[]{:S(2)}, u32[]{:S(2)}) collective-permute-start(bf16[128,512]{1,0:T(8,128)(2,1)} %merge_attention.1.att), channel_id=1, source_target_pairs={{0,1},{1,0},{2,3},{3,2},{4,5},{5,4},{6,7},{7,6},{8,9},{9,8},{10,11... | collective-permute-start | bytes 393224 | tf_op jit(solution)/shard_map/ppermute | solution.py:802
  128.7 6.0 %project_dispatch.1 = (f32[128,1024]{1,0:T(8,128)}, bf16[1536,1024]{1,0:T(8,128)(2,1)}) custom-call(s32[3]{0:T(128)} %pad_add_fusion.1.side, bf16[128,512]{1,0:T(8,128)(2,1)} %merge_attention.1.att, bf16[128,512]{1,0:T(8,128)(2,1)} %copy-done.6, bf16[512,2048]{1,0:T(8,128)(2,1)} %weight_in.1, bf16[256,2048]{1,0:T(8,128)(2,1)} %collective-permute-done.12.weight_mine, ...), custom_call_target="tpu_custom_call" | custom-call | flops 1342177280 | bytes 10485760 | tf_op jit(solution)/shard_map/project_dispatch/pallas_call | solution.py:500
  134.8 12.5 %all-to-all-start.1 = ((bf16[64,24,1024]{2,1,0:T(8,128)(2,1)}), bf16[64,24,1024]{2,1,0:T(8,128)(2,1)}, u32[]{:S(2)}, u32[]{:S(2)}) async-start(bf16[64,24,1024]{2,1,0:T(8,128)(2,1)} %bitcast.35), calls=%async_computation.1 | async-start | bytes 6291456 | tf_op jit(solution)/shard_map/all_to_all | solution.py:814
  147.3 2.8 %copy.54 = bf16[1,2048,704]{2,1,0:T(8,128)(2,1)} copy(bf16[1,2048,704]{1,2,0:T(8,128)(2,1)S(1)} %copy-done.2) | data formatting | bytes 5767168 | tf_op args[12]
  150.2 4.6 %copy.55 = bf16[1,2048,704]{2,1,0:T(8,128)(2,1)} copy(bf16[1,2048,704]{1,2,0:T(8,128)(2,1)} %param.39) | data formatting | bytes 5767168 | tf_op args[13]
  154.8 34.7 %all-to-all-done.1.rows = bf16[64,24,1024]{2,1,0:T(8,128)(2,1)} async-done(((bf16[64,24,1024]{2,1,0:T(8,128)(2,1)}), bf16[64,24,1024]{2,1,0:T(8,128)(2,1)}, u32[]{:S(2)}, u32[]{:S(2)}) %all-to-all-start.1) | async-done | bytes 3145760 | tf_op jit(solution)/shard_map/all_to_all | solution.py:814
  189.5 12.1 %expert.1 = bf16[64,2,24,512]{3,2,1,0:T(8,128)(2,1)} custom-call(bf16[64,24,1024]{2,1,0:T(8,128)(2,1)} %all-to-all-done.1.rows, bf16[2048,704]{1,0:T(8,128)(2,1)} %bitcast.36, bf16[2048,704]{1,0:T(8,128)(2,1)} %bitcast.37, bf16[704,2048]{1,0:T(8,128)(2,1)} %bitcast.56), custom_call_target="tpu_custom_call" | custom-call | flops 6643777536 | bytes 15728640 | tf_op jit(solution)/shard_map/expert/pallas_call | solution.py:595
  201.6 7.5 %all-to-all-start.2 = ((bf16[128,24,512]{2,1,0:T(8,128)(2,1)}), bf16[128,24,512]{2,1,0:T(8,128)(2,1)}, u32[]{:S(2)}, u32[]{:S(2)}) async-start(bf16[128,24,512]{2,1,0:T(8,128)(2,1)} %bitcast.34), calls=%async_computation.2 | async-start | bytes 6291456 | tf_op jit(solution)/shard_map/all_to_all | solution.py:816
  209.2 3.0 %select_convert_fusion.shares = bf16[256,3072]{1,0:T(8,128)(2,1)} fusion(pred[256,3072]{1,0:T(32,128)(4,1)S(1)} %copy-done.4, f32[256]{0:T(256)S(1)} %bitcast.50, f32[256]{0:T(256)S(1)} %bitcast.51, f32[256]{0:T(256)S(1)} %bitcast.52, f32[256]{0:T(256)S(1)} %bitcast.49, s32[3072]{0:T(1024)S(1)} %copy-done.7, s32[256]{0:T(256)S(1)} %bitcast.41, ...), kind=kLoop, calls=%fused_computation.2 | loop fusion | flops 10223616 | bytes 2379776 | tf_op jit(solution)/shard_map/convert_element_type | solution.py:701
  212.2 38.1 %all-to-all-done.2 = bf16[128,24,512]{2,1,0:T(8,128)(2,1)} async-done(((bf16[128,24,512]{2,1,0:T(8,128)(2,1)}), bf16[128,24,512]{2,1,0:T(8,128)(2,1)}, u32[]{:S(2)}, u32[]{:S(2)}) %all-to-all-start.2) | async-done | bytes 3145760 | tf_op jit(solution)/shard_map/all_to_all | solution.py:816
  250.4 3.7 %combine.1 = bf16[128,1024]{1,0:T(8,128)(2,1)} custom-call(f32[128,1024]{1,0:T(8,128)} %get-tuple-element.57.mixed, bf16[256,3072]{1,0:T(8,128)(2,1)} %select_convert_fusion.shares, bf16[3072,512]{1,0:T(8,128)(2,1)} %bitcast.25.rows), custom_call_target="tpu_custom_call" | custom-call | flops 805306368 | bytes 6291456 | tf_op jit(solution)/shard_map/combine/pallas_call | solution.py:644
  (77 shorter events, 29.7 us)
Async XLA Ops:
  0.0 15.3 %collective-permute-start.4 = (bf16[8,2,128,512]{3,2,1,0:T(8,128)(2,1)}, bf16[8,2,128,512]{3,2,1,0:T(8,128)(2,1)}, u32[]{:S(2)}, u32[]{:S(2)}) collective-permute-start(bf16[8,2,128,512]{3,2,1,0:T(8,128)(2,1)} %pages_a_in.3), channel_id=1, source_target_pairs={{0,2},{2,0},{4,6},{6,4},{8,10},{10,8},{12,14},{14,12},{16,18},{18,... | collective-permute-start | bytes 6291464 | tf_op jit(solution)/shard_map/ppermute | solution.py:765
  1.4 9.5 %collective-permute-start.5 = (s32[1,64]{1,0:T(1,128)}, s32[1,64]{1,0:T(1,128)S(1)}, u32[]{:S(2)}, u32[]{:S(2)}) collective-permute-start(s32[1,64]{1,0:T(1,128)} %param.32), channel_id=1, source_target_pairs={{0,2},{2,0},{4,6},{6,4},{8,10},{10,8},{12,14},{14,12},{16,18},{18,... | collective-permute-start | bytes 776 | tf_op jit(solution)/shard_map/ppermute | solution.py:766
  3.1 9.2 %collective-permute-start = (bf16[136,512]{1,0:T(8,128)(2,1)}, bf16[136,512]{1,0:T(8,128)(2,1)S(1)}, u32[]{:S(2)}, u32[]{:S(2)}) collective-permute-start(bf16[136,512]{1,0:T(8,128)(2,1)} %get-tuple-element.34.refs_0_), channel_id=1, source_target_pairs={{0,4},{2,6},{4,0},{6,2},{8,12},{10,14},{12,8},{14,10},{16,20},{18,... | collective-permute-start | bytes 417800 | tf_op jit(solution)/shard_map/ppermute | solution.py:768
  5.9 6.7 %collective-permute-start.1 = (bf16[136,512]{1,0:T(8,128)(2,1)}, bf16[136,512]{1,0:T(8,128)(2,1)S(1)}, u32[]{:S(2)}, u32[]{:S(2)}) collective-permute-start(bf16[136,512]{1,0:T(8,128)(2,1)} %get-tuple-element.34.refs_0_), channel_id=1, source_target_pairs={{0,32},{2,10},{4,36},{6,14},{8,40},{10,18},{12,44},{14,22},{16,48}... | collective-permute-start | bytes 417800 | tf_op jit(solution)/shard_map/ppermute | solution.py:83
  7.6 7.7 %collective-permute-start.2 = (bf16[136,512]{1,0:T(8,128)(2,1)}, bf16[136,512]{1,0:T(8,128)(2,1)S(1)}, u32[]{:S(2)}, u32[]{:S(2)}) collective-permute-start(bf16[136,512]{1,0:T(8,128)(2,1)} %get-tuple-element.34.refs_0_), channel_id=1, source_target_pairs={{0,64},{2,18},{4,68},{6,22},{8,72},{10,26},{12,76},{14,30},{16,80}... | collective-permute-start | bytes 417800 | tf_op jit(solution)/shard_map/ppermute | solution.py:83
  10.9 4.4 %collective-permute-start.3 = (bf16[136,512]{1,0:T(8,128)(2,1)}, bf16[136,512]{1,0:T(8,128)(2,1)S(1)}, u32[]{:S(2)}, u32[]{:S(2)}) collective-permute-start(bf16[136,512]{1,0:T(8,128)(2,1)} %get-tuple-element.34.refs_0_), channel_id=1, source_target_pairs={{0,96},{2,26},{4,100},{6,30},{8,104},{10,2},{12,108},{14,6},{16,11... | collective-permute-start | bytes 417800 | tf_op jit(solution)/shard_map/ppermute | solution.py:83
  15.3 6.5 %collective-permute-start.6 = (bf16[136,512]{1,0:T(8,128)(2,1)S(1)}, bf16[136,512]{1,0:T(8,128)(2,1)S(1)}, u32[]{:S(2)}, u32[]{:S(2)}) collective-permute-start(bf16[136,512]{1,0:T(8,128)(2,1)S(1)} %collective-permute-done.refs_4_), channel_id=1, source_target_pairs={{0,32},{2,10},{4,36},{6,14},{8,40},{10,18},{12,44},{14,22},{16,48}... | collective-permute-start | bytes 417800 | tf_op jit(solution)/shard_map/ppermute | solution.py:83
  16.2 5.9 %collective-permute-start.7 = (bf16[136,512]{1,0:T(8,128)(2,1)S(1)}, bf16[136,512]{1,0:T(8,128)(2,1)S(1)}, u32[]{:S(2)}, u32[]{:S(2)}) collective-permute-start(bf16[136,512]{1,0:T(8,128)(2,1)S(1)} %collective-permute-done.refs_4_), channel_id=1, source_target_pairs={{0,64},{2,18},{4,68},{6,22},{8,72},{10,26},{12,76},{14,30},{16,80}... | collective-permute-start | bytes 417800 | tf_op jit(solution)/shard_map/ppermute | solution.py:83
  18.1 4.4 %collective-permute-start.8 = (bf16[136,512]{1,0:T(8,128)(2,1)S(1)}, bf16[136,512]{1,0:T(8,128)(2,1)S(1)}, u32[]{:S(2)}, u32[]{:S(2)}) collective-permute-start(bf16[136,512]{1,0:T(8,128)(2,1)S(1)} %collective-permute-done.refs_4_), channel_id=1, source_target_pairs={{0,96},{2,26},{4,100},{6,30},{8,104},{10,2},{12,108},{14,6},{16,11... | collective-permute-start | bytes 417800 | tf_op jit(solution)/shard_map/ppermute | solution.py:83
  20.4 13.6 %copy-start.12 = (s32[32]{0:T(128)}, s32[32]{0:T(128)S(1)}, u32[]{:S(2)}) copy-start(s32[32]{0:T(128)S(1)} %gather_fusion) | copy-start | bytes 388
  21.1 12.9 %copy-start.14 = (s32[32]{0:T(128)}, s32[32]{0:T(128)S(1)}, u32[]{:S(2)}) copy-start(s32[32]{0:T(128)S(1)} %fusion.7) | copy-start | bytes 388
  24.9 16.4 %collective-permute-start.10 = (bf16[8,136,512]{2,1,0:T(8,128)(2,1)S(1)}, bf16[8,136,512]{2,1,0:T(8,128)(2,1)}, u32[]{:S(2)}, u32[]{:S(2)}) collective-permute-start(bf16[8,136,512]{2,1,0:T(8,128)(2,1)S(1)} %stack_blocks.1.refs_0_), channel_id=1, source_target_pairs={{0,8},{2,34},{4,12},{6,38},{8,16},{10,42},{12,20},{14,46},{16,24},... | collective-permute-start | bytes 3342344 | tf_op jit(solution)/shard_map/ppermute | solution.py:115
  26.6 25.9 %collective-permute-start.11 = (bf16[8,136,512]{2,1,0:T(8,128)(2,1)S(1)}, bf16[8,136,512]{2,1,0:T(8,128)(2,1)}, u32[]{:S(2)}, u32[]{:S(2)}) collective-permute-start(bf16[8,136,512]{2,1,0:T(8,128)(2,1)S(1)} %stack_blocks.1.refs_0_), channel_id=1, source_target_pairs={{0,24},{2,98},{4,28},{6,102},{8,0},{10,106},{12,4},{14,110},{16,8}... | collective-permute-start | bytes 3342344 | tf_op jit(solution)/shard_map/ppermute | solution.py:115
  28.1 26.3 %collective-permute-start.9 = (bf16[8,136,512]{2,1,0:T(8,128)(2,1)S(1)}, bf16[8,136,512]{2,1,0:T(8,128)(2,1)}, u32[]{:S(2)}, u32[]{:S(2)}) collective-permute-start(bf16[8,136,512]{2,1,0:T(8,128)(2,1)S(1)} %stack_blocks.1.refs_0_), channel_id=1, source_target_pairs={{0,16},{2,66},{4,20},{6,70},{8,24},{10,74},{12,28},{14,78},{16,0},... | collective-permute-start | bytes 3342344 | tf_op jit(solution)/shard_map/ppermute | solution.py:115
  31.9 35.7 %collective-permute-start.12 = (bf16[256,2048]{1,0:T(8,128)(2,1)}, bf16[256,2048]{1,0:T(8,128)(2,1)}, u32[]{:S(2)}, u32[]{:S(2)}) collective-permute-start(bf16[256,2048]{1,0:T(8,128)(2,1)} %constant_dynamic-slice_fusion), channel_id=1, source_target_pairs={{0,1},{1,0},{2,3},{3,2},{4,5},{5,4},{6,7},{7,6},{8,9},{9,8},{10,11... | collective-permute-start | bytes 3145736 | tf_op jit(solution)/shard_map/ppermute | solution.py:776
  67.6 14.6 %copy-start.5 = (pred[1536,256]{1,0:T(32,128)(4,1)S(1)}, pred[1536,256]{1,0:T(32,128)(4,1)}, u32[]{:S(2)}) copy-start(pred[1536,256]{1,0:T(32,128)(4,1)} %constant.51.clone) | copy-start | bytes 1179652
  67.6 14.6 %copy-start.8 = (s32[1536]{0:T(1024)S(1)}, s32[1536]{0:T(1024)}, u32[]{:S(2)}) copy-start(s32[1536]{0:T(1024)} %constant.60) | copy-start | bytes 18436
  67.6 46.8 %all-to-all-start = ((bf16[32,400,128]{2,1,0:T(8,128)(2,1)}), bf16[32,400,128]{2,1,0:T(8,128)(2,1)}, u32[]{:S(2)}, u32[]{:S(2)}) async-start(bf16[32,400,128]{2,1,0:T(8,128)(2,1)} %page_attention.3), calls=%async_computation | async-start | bytes 6553600 | tf_op jit(solution)/shard_map/all_to_all | solution.py:797
  73.2 10.6 %collective-permute-start.13 = (bf16[256,2048]{1,0:T(8,128)(2,1)}, bf16[256,2048]{1,0:T(8,128)(2,1)S(1)}, u32[]{:S(2)}, u32[]{:S(2)}) collective-permute-start(bf16[256,2048]{1,0:T(8,128)(2,1)} %collective-permute-done.12.weight_mine), channel_id=1, source_target_pairs={{0,2},{2,0},{4,6},{6,4},{8,10},{10,8},{12,14},{14,12},{16,18},{18,... | collective-permute-start | bytes 3145736 | tf_op jit(solution)/shard_map/ppermute | solution.py:796
  83.8 44.3 %copy-start.3 = (bf16[256,2048]{1,0:T(8,128)(2,1)}, bf16[256,2048]{1,0:T(8,128)(2,1)S(1)}, u32[]{:S(2)}) copy-start(bf16[256,2048]{1,0:T(8,128)(2,1)S(1)} %collective-permute-done.13.weight_other) | copy-start | bytes 3145732
  121.5 6.6 %collective-permute-start.14 = (bf16[128,512]{1,0:T(8,128)(2,1)}, bf16[128,512]{1,0:T(8,128)(2,1)S(1)}, u32[]{:S(2)}, u32[]{:S(2)}) collective-permute-start(bf16[128,512]{1,0:T(8,128)(2,1)} %merge_attention.1.att), channel_id=1, source_target_pairs={{0,1},{1,0},{2,3},{3,2},{4,5},{5,4},{6,7},{7,6},{8,9},{9,8},{10,11... | collective-permute-start | bytes 393224 | tf_op jit(solution)/shard_map/ppermute | solution.py:802
  134.8 12.6 %copy-start.2 = (bf16[1,2048,704]{1,2,0:T(8,128)(2,1)S(1)}, bf16[1,2048,704]{1,2,0:T(8,128)(2,1)}, u32[]{:S(2)}) copy-start(bf16[1,2048,704]{1,2,0:T(8,128)(2,1)} %param.38) | copy-start | bytes 8650756
  134.8 54.7 %all-to-all-start.1 = ((bf16[64,24,1024]{2,1,0:T(8,128)(2,1)}), bf16[64,24,1024]{2,1,0:T(8,128)(2,1)}, u32[]{:S(2)}, u32[]{:S(2)}) async-start(bf16[64,24,1024]{2,1,0:T(8,128)(2,1)} %bitcast.35), calls=%async_computation.1 | async-start | bytes 6291456 | tf_op jit(solution)/shard_map/all_to_all | solution.py:814
  201.6 48.8 %all-to-all-start.2 = ((bf16[128,24,512]{2,1,0:T(8,128)(2,1)}), bf16[128,24,512]{2,1,0:T(8,128)(2,1)}, u32[]{:S(2)}, u32[]{:S(2)}) async-start(bf16[128,24,512]{2,1,0:T(8,128)(2,1)} %bitcast.34), calls=%async_computation.2 | async-start | bytes 6291456 | tf_op jit(solution)/shard_map/all_to_all | solution.py:816
  (9 other events, 66.8 us)
